TPU v7x, 512 devices: a whole 4x4x16 slice. The times are simulated.
512 devices in a mesh: depth: 4 (over x), row: 8 (over y, core), col: 16 (over z).
Axes of the slice: x: 4, y: 4, z: 16, core: 2. Of those that a mesh axis runs over, the one named last changes fastest.
Arguments:
- species: float32 [2, 64, 256, 2048], P(None, 'depth', 'row', 'col'), may hold values from -6 to 6
- diffusivity: float32 [64, 256, 2048], P('depth', 'row', 'col'), may hold values from 0.05 to 0.4
- reaction_rate: float32 [64, 256, 2048], P('depth', 'row', 'col'), may hold values from 0.2 to 2
- shear_rate: float32 [16], replicated, may hold values from -0.08 to 0.08
- colour_weight: float32 [16, 4, 2], replicated, may hold values from -4 to 4
- colour_bias: float32 [16, 4], replicated, may hold values from -1 to 1
- slab_order: int32 [16, 4], replicated, may hold values from 0 to 3, each once within a row
- lengths: int32 [16, 16, 256], P('depth', 'col', 'row'), may hold values from 1 to 128
- owners: int32 [16, 16, 256, 1], P('depth', 'col', 'row'), may hold values from 0 to 15; in each aligned block of 32 rows (0 to 31, 32 to 63, ..., all dimensions but the last counted through in order) at most 4 rows name the same one
- warp_matrix: bfloat16 [16, 128, 128], replicated, may hold values from -0.5 to 0.5
Outputs:
- species_out: float32 [2, 64, 256, 2048], P(None, 'depth', 'row', 'col')
- frame: float32 [16, 256, 4, 2048], P('depth', 'row', None, 'col')
Inputs may be any that keep to these rules, and one draw needn't show every extreme that they name: `slab_order`: each row names each of the 4 slabs once. `owners`: for one view, the 32 scanlines of one device (aligned blocks of 32 along the third dimension) name any one owner at most 4 times.
All inputs are finite; a program needn't handle non-finite values.
Results may differ from a plain program's by a relative error of at most 0.001.
The roundings to bfloat16 on the way count: a program that leaves them out, or rounds other values in their place, can miss the bound.
Values may be sent and summed in bfloat16 or wider, within the bound.
No kernel may reach another device: no remote copies, remote signals or barrier semaphores. Data moves between devices by JAX's collectives and lax.ppermute only.
A program may use at most 64 MiB of HBM per device.

v0:
```python
import jax
import jax.numpy as jnp
from jax import lax
from jax.sharding import PartitionSpec as P

TIME_STEP = 0.1
RAY_STEP = 0.02
VEL_DEPTH = 0.3
VEL_ROW = 0.2
VEL_COL = 0.4


def with_halo(cells, sides, width):
    for axis, dim in sides:
        count = lax.axis_size(axis)
        ends = count - 1
        head = lax.slice_in_dim(cells, 0, width, axis=dim)
        tail = lax.slice_in_dim(cells, cells.shape[dim] - width, cells.shape[dim], axis=dim)
        cells = jnp.concatenate(
            [
                lax.ppermute(tail, axis, [(i, (i + 1) % count) for i in range(ends)]),
                cells,
                lax.ppermute(head, axis, [((i + 1) % count, i) for i in range(ends)]),
            ],
            axis=dim,
        )
    return cells


def tendency_of(padded, diffusivity, reaction_rate):
    centre = padded[:, 1:-1, 1:-1, 1:-1]
    below_depth = padded[:, :-2, 1:-1, 1:-1]
    above_depth = padded[:, 2:, 1:-1, 1:-1]
    below_row = padded[:, 1:-1, :-2, 1:-1]
    above_row = padded[:, 1:-1, 2:, 1:-1]
    below_col = padded[:, 1:-1, 1:-1, :-2]
    above_col = padded[:, 1:-1, 1:-1, 2:]
    laplace = (
        below_depth + above_depth + below_row + above_row + below_col + above_col - 6.0 * centre
    )
    advect = (
        VEL_DEPTH * (centre - below_depth)
        + VEL_ROW * (centre - below_row)
        + VEL_COL * (centre - below_col)
    )
    heat_part = centre[1]
    burned = reaction_rate * centre[0] * heat_part * heat_part / (1.0 + heat_part * heat_part)
    source = jnp.stack([-burned, burned])
    return diffusivity * laplace - advect + source


def with_faces(fields):
    return with_halo(fields.astype(jnp.bfloat16), (("depth", 1), ("row", 2), ("col", 3)), 1).astype(
        fields.dtype
    )


def advance(species, diffusivity, reaction_rate):
    first = species + TIME_STEP * tendency_of(with_faces(species), diffusivity, reaction_rate)
    second = 0.75 * species + 0.25 * (
        first + TIME_STEP * tendency_of(with_faces(first), diffusivity, reaction_rate)
    )
    return species / 3.0 + 2.0 / 3.0 * (
        second + TIME_STEP * tendency_of(with_faces(second), diffusivity, reaction_rate)
    )


def slot_plan(owner_rows, tiles):
    onehot = (owner_rows[..., None] == jnp.arange(tiles, dtype=jnp.int32)).astype(jnp.int32)
    running = jnp.cumsum(onehot, axis=-2)
    return jnp.sum(running * onehot, axis=-1) - 1


def body(
    species,
    diffusivity,
    reaction_rate,
    shear_rate,
    colour_weight,
    colour_bias,
    slab_order,
    lengths,
    owners,
    warp_matrix,
):
    depth_cells = species.shape[1]
    rows = species.shape[2]
    width = species.shape[3]
    depth_devices = lax.axis_size("depth")
    depth_total = depth_cells * depth_devices
    rim_width = (4 * depth_total + 99) // 100
    species_out = advance(species, diffusivity, reaction_rate)
    rimmed = with_halo(species_out, (("col", 3),), rim_width)
    slab_first = lax.axis_index("depth") * depth_cells
    views = shear_rate.shape[0]
    padded_width = width + 2 * rim_width
    rows_in = jnp.arange(padded_width, dtype=jnp.int32)[None, :, None]
    cols_out = jnp.arange(width, dtype=jnp.int32)[None, None, :]

    def march(state_pair, local_depth):
        colour, through = state_pair
        depth_index = slab_first + local_depth
        offset = shear_rate * (depth_index.astype(jnp.float32) + 0.5 - 0.5 * depth_total)
        floor_part = jnp.floor(offset)
        fraction = offset - floor_part
        start = floor_part.astype(jnp.int32) + rim_width
        target = cols_out + start[:, None, None]
        resample = jnp.where(rows_in == target, (1.0 - fraction)[:, None, None], 0.0) + jnp.where(
            rows_in == target + 1, fraction[:, None, None], 0.0
        )
        depth_plane = lax.dynamic_index_in_dim(rimmed, local_depth, 1, keepdims=False)
        samples = jnp.einsum(
            "fyp,vpx->vfyx", depth_plane, resample, precision=lax.Precision.HIGHEST
        )
        logits = (
            colour_weight[:, None, :, 0, None] * samples[:, 0][:, :, None, :]
            + colour_weight[:, None, :, 1, None] * samples[:, 1][:, :, None, :]
            + colour_bias[:, None, :, None]
        )
        colours = jax.nn.sigmoid(logits[:, :, :3, :])
        fading = jnp.exp(-RAY_STEP * jax.nn.softplus(logits[:, :, 3, :]))
        colour = colour + (through * (1.0 - fading))[:, :, None, :] * colours
        return ((colour, through * fading), None)

    start_state = (
        jnp.zeros((views, rows, 3, width), jnp.float32),
        jnp.ones((views, rows, width), jnp.float32),
    )
    (colour, through), unused = lax.scan(
        march, start_state, jnp.arange(depth_cells, dtype=jnp.int32)
    )
    slab = jnp.concatenate([colour, (1.0 - through)[:, :, None, :]], axis=2)
    view_count = views // depth_devices
    view_first = lax.axis_index("depth") * view_count
    everything = lax.all_gather(slab[None], "depth", axis=0, tiled=True)
    stack = lax.dynamic_slice_in_dim(everything, view_first, view_count, 1)
    own_order = lax.dynamic_slice_in_dim(slab_order, view_first, view_count, 0)
    slab_ids = jnp.arange(depth_devices, dtype=jnp.int32)

    def pick(position):
        chooser = (own_order[:, position][None, :] == slab_ids[:, None]).astype(jnp.float32)
        return jnp.sum(chooser[:, :, None, None, None] * stack, axis=0)

    result = pick(0)
    for position in range(1, depth_devices):
        result = result + (1.0 - result[:, :, 3:4, :]) * pick(position)
    picture = result.astype(jnp.bfloat16)
    column = jnp.arange(width, dtype=jnp.int32)
    keep = column[None, None, :] < lengths[:, 0, :, None]
    pieces = jnp.where(keep[:, :, None, :], picture, jnp.zeros((), jnp.bfloat16))
    tiles = lax.axis_size("col")
    capacity = 2 * rows // tiles
    mine = owners[:, 0, :, 0]
    slot_rank = slot_plan(mine, tiles)
    tile_ids = jnp.arange(tiles, dtype=jnp.int32)
    slot_ids = jnp.arange(capacity, dtype=jnp.int32)
    select = (mine[:, None, None, :] == tile_ids[None, :, None, None]) & (
        slot_rank[:, None, None, :] == slot_ids[None, None, :, None]
    )
    outgoing = jnp.einsum(
        "vosy,vycx->voscx", select.astype(jnp.bfloat16), pieces, preferred_element_type=jnp.float32
    ).astype(jnp.bfloat16)
    incoming = lax.all_to_all(outgoing, "col", split_axis=1, concat_axis=1, tiled=True)
    this_tile = lax.axis_index("col")
    owner_map = lax.all_gather(owners, "col", axis=1, tiled=True)[:, :, :, 0]
    source_rank = slot_plan(owner_map, tiles)
    place = (owner_map[:, :, None, :] == this_tile) & (
        source_rank[:, :, None, :] == slot_ids[None, None, :, None]
    )
    warp_own = lax.dynamic_slice_in_dim(warp_matrix, view_first, view_count, 0)
    warped = jnp.einsum("vtscx,vxz->vtscz", incoming, warp_own, preferred_element_type=jnp.float32)
    frame = jnp.einsum(
        "vtsy,vtscz->vycz", place.astype(jnp.float32), warped, precision=lax.Precision.HIGHEST
    )
    return (species_out, frame)


def solution(mesh):
    in_specs = (
        P(None, "depth", "row", "col"),
        P("depth", "row", "col"),
        P("depth", "row", "col"),
        P(),
        P(),
        P(),
        P(),
        P("depth", "col", "row"),
        P("depth", "col", "row", None),
        P(),
    )
    out_specs = (P(None, "depth", "row", "col"), P("depth", "row", None, "col"))
    return jax.shard_map(body, mesh=mesh, in_specs=in_specs, out_specs=out_specs, check_vma=False)
```

profile of v0, /device:TPU:6, one launch (start us, length us, event | category | flops | bytes accessed | tf_op | source)
XLA Modules:
  0.0 361.8 jit_solution(12064472902889304858)
XLA Ops:
  8.4 1.3 collective-permute-start
  9.7 4.5 %collective-permute-start.1 = (bf16[2,1,32,128]{3,2,1,0:T(8,128)(2,1)S(1)}, bf16[2,1,32,128]{3,2,1,0:T(8,128)(2,1)S(1)}, u32[]{:S(2)}, u32[]{:S(2)}) collective-permute-start(bf16[2,1,32,128]{3,2,1,0:T(8,128)(2,1)S(1)} %get-tuple-element.426), channel_id=1, source_target_pairs={{128,0},{256,128},{384,256},{129,1},{257,129},{385,257},{130,2},{2... | collective-permute-start | bytes 49160 | tf_op jit(solution)/shard_map/ppermute | solution.py:23
  14.2 1.4 collective-permute-done.1
  15.7 1.3 collective-permute-start.2
  17.0 1.3 collective-permute-start.3
  18.3 3.6 collective-permute-done.3
  22.3 4.0 %collective-permute-start.4 = (bf16[2,18,34,1]{3,2,1,0:T(8,128)(2,1)S(1)}, bf16[2,18,34,1]{3,2,1,0:T(8,128)(2,1)S(1)}, u32[]{:S(2)}, u32[]{:S(2)}) collective-permute-start(bf16[2,18,34,1]{3,2,1,0:T(8,128)(2,1)S(1)} %get-tuple-element.413), channel_id=1, source_target_pairs={{0,1},{1,2},{2,3},{3,4},{4,5},{5,6},{6,7},{7,8},{8,9},{9,10},{10,1... | collective-permute-start | bytes 7352 | tf_op jit(solution)/shard_map/ppermute | solution.py:21
  26.3 1.4 collective-permute-start.5
  27.7 6.0 %collective-permute-done.4 = bf16[2,18,34,1]{3,2,1,0:T(8,128)(2,1)S(1)} collective-permute-done((bf16[2,18,34,1]{3,2,1,0:T(8,128)(2,1)S(1)}, bf16[2,18,34,1]{3,2,1,0:T(8,128)(2,1)S(1)}, u32[]{:S(2)}, u32[]{:S(2)}) %collective-permute-start.4) | collective-permute-done | bytes 2480 | tf_op jit(solution)/shard_map/ppermute | solution.py:21
  33.7 4.7 %collective-permute-done.5 = bf16[2,18,34,1]{3,2,1,0:T(8,128)(2,1)S(1)} collective-permute-done((bf16[2,18,34,1]{3,2,1,0:T(8,128)(2,1)S(1)}, bf16[2,18,34,1]{3,2,1,0:T(8,128)(2,1)S(1)}, u32[]{:S(2)}, u32[]{:S(2)}) %collective-permute-start.5) | collective-permute-done | bytes 2480 | tf_op jit(solution)/shard_map/ppermute | solution.py:23
  40.1 1.3 collective-permute-start.6
  41.4 4.8 %collective-permute-start.7 = (bf16[2,1,32,128]{3,2,1,0:T(8,128)(2,1)S(1)}, bf16[2,1,32,128]{3,2,1,0:T(8,128)(2,1)S(1)}, u32[]{:S(2)}, u32[]{:S(2)}) collective-permute-start(bf16[2,1,32,128]{3,2,1,0:T(8,128)(2,1)S(1)} %get-tuple-element.424), channel_id=1, source_target_pairs={{128,0},{256,128},{384,256},{129,1},{257,129},{385,257},{130,2},{2... | collective-permute-start | bytes 49160 | tf_op jit(solution)/shard_map/ppermute | solution.py:23
  46.3 1.4 collective-permute-done.7
  47.7 2.3 collective-permute-start.8
  50.0 1.3 collective-permute-start.9
  51.3 4.2 %collective-permute-done.9 = bf16[2,18,1,128]{3,2,1,0:T(2,128)(2,1)S(1)} collective-permute-done((bf16[2,18,1,128]{3,2,1,0:T(2,128)(2,1)S(1)}, bf16[2,18,1,128]{3,2,1,0:T(2,128)(2,1)S(1)}, u32[]{:S(2)}, u32[]{:S(2)}) %collective-permute-start.9) | collective-permute-done | bytes 9248 | tf_op jit(solution)/shard_map/ppermute | solution.py:23
  55.9 3.8 %collective-permute-start.10 = (bf16[2,18,34,1]{3,2,1,0:T(8,128)(2,1)S(1)}, bf16[2,18,34,1]{3,2,1,0:T(8,128)(2,1)S(1)}, u32[]{:S(2)}, u32[]{:S(2)}) collective-permute-start(bf16[2,18,34,1]{3,2,1,0:T(8,128)(2,1)S(1)} %get-tuple-element.411), channel_id=1, source_target_pairs={{0,1},{1,2},{2,3},{3,4},{4,5},{5,6},{6,7},{7,8},{8,9},{9,10},{10,1... | collective-permute-start | bytes 7352 | tf_op jit(solution)/shard_map/ppermute | solution.py:21
  59.7 1.3 collective-permute-start.11
  61.0 6.1 %collective-permute-done.10 = bf16[2,18,34,1]{3,2,1,0:T(8,128)(2,1)S(1)} collective-permute-done((bf16[2,18,34,1]{3,2,1,0:T(8,128)(2,1)S(1)}, bf16[2,18,34,1]{3,2,1,0:T(8,128)(2,1)S(1)}, u32[]{:S(2)}, u32[]{:S(2)}) %collective-permute-start.10) | collective-permute-done | bytes 2480 | tf_op jit(solution)/shard_map/ppermute | solution.py:21
  67.1 5.3 %collective-permute-done.11 = bf16[2,18,34,1]{3,2,1,0:T(8,128)(2,1)S(1)} collective-permute-done((bf16[2,18,34,1]{3,2,1,0:T(8,128)(2,1)S(1)}, bf16[2,18,34,1]{3,2,1,0:T(8,128)(2,1)S(1)}, u32[]{:S(2)}, u32[]{:S(2)}) %collective-permute-start.11) | collective-permute-done | bytes 2480 | tf_op jit(solution)/shard_map/ppermute | solution.py:23
  74.2 1.3 collective-permute-start.12
  75.5 4.8 %collective-permute-start.13 = (bf16[2,1,32,128]{3,2,1,0:T(8,128)(2,1)S(1)}, bf16[2,1,32,128]{3,2,1,0:T(8,128)(2,1)S(1)}, u32[]{:S(2)}, u32[]{:S(2)}) collective-permute-start(bf16[2,1,32,128]{3,2,1,0:T(8,128)(2,1)S(1)} %get-tuple-element.422), channel_id=1, source_target_pairs={{128,0},{256,128},{384,256},{129,1},{257,129},{385,257},{130,2},{2... | collective-permute-start | bytes 49160 | tf_op jit(solution)/shard_map/ppermute | solution.py:23
  80.3 1.4 collective-permute-done.13
  81.8 2.4 collective-permute-start.14
  84.2 1.3 collective-permute-start.15
  85.5 3.8 %collective-permute-done.15 = bf16[2,18,1,128]{3,2,1,0:T(2,128)(2,1)S(1)} collective-permute-done((bf16[2,18,1,128]{3,2,1,0:T(2,128)(2,1)S(1)}, bf16[2,18,1,128]{3,2,1,0:T(2,128)(2,1)S(1)}, u32[]{:S(2)}, u32[]{:S(2)}) %collective-permute-start.15) | collective-permute-done | bytes 9248 | tf_op jit(solution)/shard_map/ppermute | solution.py:23
  89.7 5.4 %collective-permute-start.16 = (bf16[2,18,34,1]{3,2,1,0:T(8,128)(2,1)S(1)}, bf16[2,18,34,1]{3,2,1,0:T(8,128)(2,1)S(1)}, u32[]{:S(2)}, u32[]{:S(2)}) collective-permute-start(bf16[2,18,34,1]{3,2,1,0:T(8,128)(2,1)S(1)} %get-tuple-element.409), channel_id=1, source_target_pairs={{0,1},{1,2},{2,3},{3,4},{4,5},{5,6},{6,7},{7,8},{8,9},{9,10},{10,1... | collective-permute-start | bytes 7352 | tf_op jit(solution)/shard_map/ppermute | solution.py:21
  95.2 1.3 collective-permute-start.17
  96.5 6.1 %collective-permute-done.16 = bf16[2,18,34,1]{3,2,1,0:T(8,128)(2,1)S(1)} collective-permute-done((bf16[2,18,34,1]{3,2,1,0:T(8,128)(2,1)S(1)}, bf16[2,18,34,1]{3,2,1,0:T(8,128)(2,1)S(1)}, u32[]{:S(2)}, u32[]{:S(2)}) %collective-permute-start.16) | collective-permute-done | bytes 2480 | tf_op jit(solution)/shard_map/ppermute | solution.py:21
  102.6 4.7 %collective-permute-done.17 = bf16[2,18,34,1]{3,2,1,0:T(8,128)(2,1)S(1)} collective-permute-done((bf16[2,18,34,1]{3,2,1,0:T(8,128)(2,1)S(1)}, bf16[2,18,34,1]{3,2,1,0:T(8,128)(2,1)S(1)}, u32[]{:S(2)}, u32[]{:S(2)}) %collective-permute-start.17) | collective-permute-done | bytes 2480 | tf_op jit(solution)/shard_map/ppermute | solution.py:23
  110.0 4.3 %collective-permute-start.18 = (f32[2,16,32,3]{3,2,1,0:T(8,128)}, f32[2,16,32,3]{3,2,1,0:T(8,128)S(1)}, u32[]{:S(2)}, u32[]{:S(2)}) collective-permute-start(f32[2,16,32,3]{3,2,1,0:T(8,128)} %get-tuple-element.407), channel_id=1, source_target_pairs={{0,1},{1,2},{2,3},{3,4},{4,5},{5,6},{6,7},{7,8},{8,9},{9,10},{10,1... | collective-permute-start | bytes 36872 | tf_op jit(solution)/shard_map/ppermute | solution.py:21
  114.4 1.5 collective-permute-start.19
  116.0 10.9 %collective-permute-done.18 = f32[2,16,32,3]{3,2,1,0:T(8,128)S(1)} collective-permute-done((f32[2,16,32,3]{3,2,1,0:T(8,128)}, f32[2,16,32,3]{3,2,1,0:T(8,128)S(1)}, u32[]{:S(2)}, u32[]{:S(2)}) %collective-permute-start.18) | collective-permute-done | bytes 12320 | tf_op jit(solution)/shard_map/ppermute | solution.py:21
  127.7 3.3 collective-permute-done.19
  131.0 1.7 pad_maximum_fusion
  132.7 108.8 %while.18 = (s32[]{:T(128)}, f32[16,32,3,128]{3,2,1,0:T(4,128)S(1)}, f32[16,32,128]{2,1,0:T(8,128)S(1)}, f32[16,4,2]{0,1,2:T(4,128)S(1)}, s32[16]{0:T(128)S(1)},...) while((s32[]{:T(128)}, ...), condition=%wide.region_5.6_spmd.clone.clone, body=%wide.region_4.5_spmd.clone.clone.sunk | while | flops 215089280 | bytes 12881818 | solution.py:129
  143.1 1.2 convolution_bitcast_fusion.3
  149.9 1.2 convolution_bitcast_fusion.3
  156.7 1.2 convolution_bitcast_fusion.3
  163.5 1.2 convolution_bitcast_fusion.3
  177.1 1.2 convolution_bitcast_fusion.3
  190.7 1.2 convolution_bitcast_fusion.3
  204.3 1.2 convolution_bitcast_fusion.3
  243.5 54.3 %all-gather.3.cloned.1.call-done = f32[64,32,4,128]{3,1,2,0:T(8,128)} async-done(((f32[16,32,4,128]{3,1,2,0:T(8,128)}), f32[64,32,4,128]{3,1,2,0:T(8,128)}) %all-gather.3.cloned.1.call-update) | async-done | bytes 4194320 | tf_op jit(solution)/shard_map/all_gather | solution.py:135
  297.7 1.7 multiply_reduce_fusion
  300.7 12.5 %all-to-all-start = ((bf16[4,16,4,4,128]{4,3,2,0,1:T(4,128)(2,1)}), bf16[4,16,4,4,128]{4,3,2,0,1:T(4,128)(2,1)S(1)}, u32[]{:S(2)}, u32[]{:S(2)}) async-start(bf16[4,16,4,4,128]{4,3,2,0,1:T(4,128)(2,1)} %copy.51), calls=%async_computation | async-start | bytes 524288 | tf_op jit(solution)/shard_map/all_to_all | solution.py:163
  313.2 36.9 %all_gather.6 = s32[4,16,32,1]{2,3,1,0:T(1,128)S(1)} all-gather(s32[4,1,32,1]{2,3,1,0:T(1,128)S(1)} %copy-done.8), channel_id=1, replica_groups=mesh['depth'=4,'row'=8,'col'=16] {'col'}, dimensions={1}, use_global_device_ids=true | all-gather | bytes 8704 | tf_op jit(solution)/shard_map/all_gather | solution.py:165
  350.2 3.1 select_reduce_fusion
  (338 shorter events, 70.1 us)
Async XLA Ops:
  7.2 346.3 %copy-start = (bf16[16,128,128]{2,1,0:T(8,128)(2,1)S(1)}, bf16[16,128,128]{2,1,0:T(8,128)(2,1)}, u32[]{:S(2)}) copy-start(bf16[16,128,128]{2,1,0:T(8,128)(2,1)} %param.21) | copy-start | bytes 1572868
  7.2 290.5 %all-gather.3.cloned.1.call-start = ((), (), s32[]{:S(2)}) async-start(), calls=%async_computation.1 | async-start | bytes 5242880 | tf_op jit(solution)/shard_map/all_gather | solution.py:135
  8.4 5.9 %collective-permute-start = (bf16[2,1,32,128]{3,2,1,0:T(8,128)(2,1)S(1)}, bf16[2,1,32,128]{3,2,1,0:T(8,128)(2,1)S(1)}, u32[]{:S(2)}, u32[]{:S(2)}) collective-permute-start(bf16[2,1,32,128]{3,2,1,0:T(8,128)(2,1)S(1)} %get-tuple-element.425), channel_id=1, source_target_pairs={{0,128},{128,256},{256,384},{1,129},{129,257},{257,385},{2,130},{1... | collective-permute-start | bytes 49160 | tf_op jit(solution)/shard_map/ppermute | solution.py:21
  9.7 6.0 %collective-permute-start.1 = (bf16[2,1,32,128]{3,2,1,0:T(8,128)(2,1)S(1)}, bf16[2,1,32,128]{3,2,1,0:T(8,128)(2,1)S(1)}, u32[]{:S(2)}, u32[]{:S(2)}) collective-permute-start(bf16[2,1,32,128]{3,2,1,0:T(8,128)(2,1)S(1)} %get-tuple-element.426), channel_id=1, source_target_pairs={{128,0},{256,128},{384,256},{129,1},{257,129},{385,257},{130,2},{2... | collective-permute-start | bytes 49160 | tf_op jit(solution)/shard_map/ppermute | solution.py:23
  15.7 2.6 collective-permute-start.2
  17.0 4.9 %collective-permute-start.3 = (bf16[2,18,1,128]{3,2,1,0:T(2,128)(2,1)S(1)}, bf16[2,18,1,128]{3,2,1,0:T(2,128)(2,1)S(1)}, u32[]{:S(2)}, u32[]{:S(2)}) collective-permute-start(bf16[2,18,1,128]{3,2,1,0:T(2,128)(2,1)S(1)} %get-tuple-element.420), channel_id=1, source_target_pairs={{16,0},{32,16},{48,32},{64,48},{80,64},{96,80},{112,96},{17,1},{33... | collective-permute-start | bytes 27656 | tf_op jit(solution)/shard_map/ppermute | solution.py:23
  22.2 16.7 %copy-start.3 = (f32[16,32,128]{2,1,0:T(8,128)S(1)}, f32[16,32,128]{2,1,0:T(8,128)}, u32[]{:S(2)}) copy-start(f32[16,32,128]{2,1,0:T(8,128)} %param.14) | copy-start | bytes 786436
  22.3 11.4 %collective-permute-start.4 = (bf16[2,18,34,1]{3,2,1,0:T(8,128)(2,1)S(1)}, bf16[2,18,34,1]{3,2,1,0:T(8,128)(2,1)S(1)}, u32[]{:S(2)}, u32[]{:S(2)}) collective-permute-start(bf16[2,18,34,1]{3,2,1,0:T(8,128)(2,1)S(1)} %get-tuple-element.413), channel_id=1, source_target_pairs={{0,1},{1,2},{2,3},{3,4},{4,5},{5,6},{6,7},{7,8},{8,9},{9,10},{10,1... | collective-permute-start | bytes 7352 | tf_op jit(solution)/shard_map/ppermute | solution.py:21
  26.2 12.9 %copy-start.2 = (f32[2,16,32,128]{3,2,1,0:T(8,128)S(1)}, f32[2,16,32,128]{3,2,1,0:T(8,128)}, u32[]{:S(2)}) copy-start(f32[2,16,32,128]{3,2,1,0:T(8,128)} %param.12) | copy-start | bytes 1572868
  26.3 12.9 %copy-start.4 = (f32[16,32,128]{2,1,0:T(8,128)S(1)}, f32[16,32,128]{2,1,0:T(8,128)}, u32[]{:S(2)}) copy-start(f32[16,32,128]{2,1,0:T(8,128)} %param.13) | copy-start | bytes 786436
  26.3 12.1 %collective-permute-start.5 = (bf16[2,18,34,1]{3,2,1,0:T(8,128)(2,1)S(1)}, bf16[2,18,34,1]{3,2,1,0:T(8,128)(2,1)S(1)}, u32[]{:S(2)}, u32[]{:S(2)}) collective-permute-start(bf16[2,18,34,1]{3,2,1,0:T(8,128)(2,1)S(1)} %get-tuple-element.414), channel_id=1, source_target_pairs={{1,0},{2,1},{3,2},{4,3},{5,4},{6,5},{7,6},{8,7},{9,8},{10,9},{11,1... | collective-permute-start | bytes 7352 | tf_op jit(solution)/shard_map/ppermute | solution.py:23
  40.1 6.1 %collective-permute-start.6 = (bf16[2,1,32,128]{3,2,1,0:T(8,128)(2,1)S(1)}, bf16[2,1,32,128]{3,2,1,0:T(8,128)(2,1)S(1)}, u32[]{:S(2)}, u32[]{:S(2)}) collective-permute-start(bf16[2,1,32,128]{3,2,1,0:T(8,128)(2,1)S(1)} %get-tuple-element.423), channel_id=1, source_target_pairs={{0,128},{128,256},{256,384},{1,129},{129,257},{257,385},{2,130},{1... | collective-permute-start | bytes 49160 | tf_op jit(solution)/shard_map/ppermute | solution.py:21
  41.4 6.3 %collective-permute-start.7 = (bf16[2,1,32,128]{3,2,1,0:T(8,128)(2,1)S(1)}, bf16[2,1,32,128]{3,2,1,0:T(8,128)(2,1)S(1)}, u32[]{:S(2)}, u32[]{:S(2)}) collective-permute-start(bf16[2,1,32,128]{3,2,1,0:T(8,128)(2,1)S(1)} %get-tuple-element.424), channel_id=1, source_target_pairs={{128,0},{256,128},{384,256},{129,1},{257,129},{385,257},{130,2},{2... | collective-permute-start | bytes 49160 | tf_op jit(solution)/shard_map/ppermute | solution.py:23
  47.7 3.6 collective-permute-start.8
  50.0 5.6 %collective-permute-start.9 = (bf16[2,18,1,128]{3,2,1,0:T(2,128)(2,1)S(1)}, bf16[2,18,1,128]{3,2,1,0:T(2,128)(2,1)S(1)}, u32[]{:S(2)}, u32[]{:S(2)}) collective-permute-start(bf16[2,18,1,128]{3,2,1,0:T(2,128)(2,1)S(1)} %get-tuple-element.418), channel_id=1, source_target_pairs={{16,0},{32,16},{48,32},{64,48},{80,64},{96,80},{112,96},{17,1},{33... | collective-permute-start | bytes 27656 | tf_op jit(solution)/shard_map/ppermute | solution.py:23
  55.9 11.2 %collective-permute-start.10 = (bf16[2,18,34,1]{3,2,1,0:T(8,128)(2,1)S(1)}, bf16[2,18,34,1]{3,2,1,0:T(8,128)(2,1)S(1)}, u32[]{:S(2)}, u32[]{:S(2)}) collective-permute-start(bf16[2,18,34,1]{3,2,1,0:T(8,128)(2,1)S(1)} %get-tuple-element.411), channel_id=1, source_target_pairs={{0,1},{1,2},{2,3},{3,4},{4,5},{5,6},{6,7},{7,8},{8,9},{9,10},{10,1... | collective-permute-start | bytes 7352 | tf_op jit(solution)/shard_map/ppermute | solution.py:21
  59.7 12.7 %collective-permute-start.11 = (bf16[2,18,34,1]{3,2,1,0:T(8,128)(2,1)S(1)}, bf16[2,18,34,1]{3,2,1,0:T(8,128)(2,1)S(1)}, u32[]{:S(2)}, u32[]{:S(2)}) collective-permute-start(bf16[2,18,34,1]{3,2,1,0:T(8,128)(2,1)S(1)} %get-tuple-element.412), channel_id=1, source_target_pairs={{1,0},{2,1},{3,2},{4,3},{5,4},{6,5},{7,6},{8,7},{9,8},{10,9},{11,1... | collective-permute-start | bytes 7352 | tf_op jit(solution)/shard_map/ppermute | solution.py:23
  74.2 6.1 %collective-permute-start.12 = (bf16[2,1,32,128]{3,2,1,0:T(8,128)(2,1)S(1)}, bf16[2,1,32,128]{3,2,1,0:T(8,128)(2,1)S(1)}, u32[]{:S(2)}, u32[]{:S(2)}) collective-permute-start(bf16[2,1,32,128]{3,2,1,0:T(8,128)(2,1)S(1)} %get-tuple-element.421), channel_id=1, source_target_pairs={{0,128},{128,256},{256,384},{1,129},{129,257},{257,385},{2,130},{1... | collective-permute-start | bytes 49160 | tf_op jit(solution)/shard_map/ppermute | solution.py:21
  75.5 6.3 %collective-permute-start.13 = (bf16[2,1,32,128]{3,2,1,0:T(8,128)(2,1)S(1)}, bf16[2,1,32,128]{3,2,1,0:T(8,128)(2,1)S(1)}, u32[]{:S(2)}, u32[]{:S(2)}) collective-permute-start(bf16[2,1,32,128]{3,2,1,0:T(8,128)(2,1)S(1)} %get-tuple-element.422), channel_id=1, source_target_pairs={{128,0},{256,128},{384,256},{129,1},{257,129},{385,257},{130,2},{2... | collective-permute-start | bytes 49160 | tf_op jit(solution)/shard_map/ppermute | solution.py:23
  81.8 3.7 %collective-permute-start.14 = (bf16[2,18,1,128]{3,2,1,0:T(2,128)(2,1)S(1)}, bf16[2,18,1,128]{3,2,1,0:T(2,128)(2,1)S(1)}, u32[]{:S(2)}, u32[]{:S(2)}) collective-permute-start(bf16[2,18,1,128]{3,2,1,0:T(2,128)(2,1)S(1)} %get-tuple-element.415), channel_id=1, source_target_pairs={{0,16},{16,32},{32,48},{48,64},{64,80},{80,96},{96,112},{1,17},{17... | collective-permute-start | bytes 27656 | tf_op jit(solution)/shard_map/ppermute | solution.py:21
  84.2 5.1 %collective-permute-start.15 = (bf16[2,18,1,128]{3,2,1,0:T(2,128)(2,1)S(1)}, bf16[2,18,1,128]{3,2,1,0:T(2,128)(2,1)S(1)}, u32[]{:S(2)}, u32[]{:S(2)}) collective-permute-start(bf16[2,18,1,128]{3,2,1,0:T(2,128)(2,1)S(1)} %get-tuple-element.416), channel_id=1, source_target_pairs={{16,0},{32,16},{48,32},{64,48},{80,64},{96,80},{112,96},{17,1},{33... | collective-permute-start | bytes 27656 | tf_op jit(solution)/shard_map/ppermute | solution.py:23
  89.7 12.8 %collective-permute-start.16 = (bf16[2,18,34,1]{3,2,1,0:T(8,128)(2,1)S(1)}, bf16[2,18,34,1]{3,2,1,0:T(8,128)(2,1)S(1)}, u32[]{:S(2)}, u32[]{:S(2)}) collective-permute-start(bf16[2,18,34,1]{3,2,1,0:T(8,128)(2,1)S(1)} %get-tuple-element.409), channel_id=1, source_target_pairs={{0,1},{1,2},{2,3},{3,4},{4,5},{5,6},{6,7},{7,8},{8,9},{9,10},{10,1... | collective-permute-start | bytes 7352 | tf_op jit(solution)/shard_map/ppermute | solution.py:21
  95.2 12.1 %collective-permute-start.17 = (bf16[2,18,34,1]{3,2,1,0:T(8,128)(2,1)S(1)}, bf16[2,18,34,1]{3,2,1,0:T(8,128)(2,1)S(1)}, u32[]{:S(2)}, u32[]{:S(2)}) collective-permute-start(bf16[2,18,34,1]{3,2,1,0:T(8,128)(2,1)S(1)} %get-tuple-element.410), channel_id=1, source_target_pairs={{1,0},{2,1},{3,2},{4,3},{5,4},{6,5},{7,6},{8,7},{9,8},{10,9},{11,1... | collective-permute-start | bytes 7352 | tf_op jit(solution)/shard_map/ppermute | solution.py:23
  109.0 23.7 %copy-start.1 = (f32[2,16,32,128]{3,2,1,0:T(8,128)}, f32[2,16,32,128]{3,2,1,0:T(8,128)S(1)}, u32[]{:S(2)}) copy-start(f32[2,16,32,128]{3,2,1,0:T(8,128)S(1)} %fusion.34) | copy-start | bytes 1572868
  109.0 6.9 %copy-start.11 = (f32[16,4]{0,1:T(4,128)S(1)}, f32[16,4]{0,1:T(4,128)}, u32[]{:S(2)}) copy-start(f32[16,4]{0,1:T(4,128)} %param.17) | copy-start | bytes 772
  109.0 7.0 %copy-start.10 = (f32[16,4,2]{0,2,1:T(2,128)S(1)}, f32[16,4,2]{0,2,1:T(2,128)}, u32[]{:S(2)}) copy-start(f32[16,4,2]{0,2,1:T(2,128)} %param.16) | copy-start | bytes 1540
  110.0 22.7 %copy-start.9 = (f32[16]{0:T(128)S(1)}, f32[16]{0:T(128)}, u32[]{:S(2)}) copy-start(f32[16]{0:T(128)} %param.15) | copy-start | bytes 196
  110.0 16.8 %collective-permute-start.18 = (f32[2,16,32,3]{3,2,1,0:T(8,128)}, f32[2,16,32,3]{3,2,1,0:T(8,128)S(1)}, u32[]{:S(2)}, u32[]{:S(2)}) collective-permute-start(f32[2,16,32,3]{3,2,1,0:T(8,128)} %get-tuple-element.407), channel_id=1, source_target_pairs={{0,1},{1,2},{2,3},{3,4},{4,5},{5,6},{6,7},{7,8},{8,9},{9,10},{10,1... | collective-permute-start | bytes 36872 | tf_op jit(solution)/shard_map/ppermute | solution.py:21
  114.4 16.6 %collective-permute-start.19 = (f32[2,16,32,3]{3,2,1,0:T(8,128)S(1)}, f32[2,16,32,3]{3,2,1,0:T(8,128)}, u32[]{:S(2)}, u32[]{:S(2)}) collective-permute-start(f32[2,16,32,3]{3,2,1,0:T(8,128)S(1)} %get-tuple-element.408), channel_id=1, source_target_pairs={{1,0},{2,1},{3,2},{4,3},{5,4},{6,5},{7,6},{8,7},{9,8},{10,9},{11,1... | collective-permute-start | bytes 36872 | tf_op jit(solution)/shard_map/ppermute | solution.py:23
  132.8 4.8 %copy-start.5 = (f32[2,16,32,134]{3,2,1,0:T(8,128)}, f32[2,16,32,134]{3,2,1,0:T(8,128)S(1)}, u32[]{:S(2)}) copy-start(f32[2,16,32,134]{3,2,1,0:T(8,128)S(1)} %get-tuple-element.543) | copy-start | bytes 1646596 | tf_op jit(solution)/shard_map/while
  139.6 4.7 %copy-start.5 = (f32[2,16,32,134]{3,2,1,0:T(8,128)}, f32[2,16,32,134]{3,2,1,0:T(8,128)S(1)}, u32[]{:S(2)}) copy-start(f32[2,16,32,134]{3,2,1,0:T(8,128)S(1)} %get-tuple-element.543) | copy-start | bytes 1646596 | tf_op jit(solution)/shard_map/while
  146.4 4.7 %copy-start.5 = (f32[2,16,32,134]{3,2,1,0:T(8,128)}, f32[2,16,32,134]{3,2,1,0:T(8,128)S(1)}, u32[]{:S(2)}) copy-start(f32[2,16,32,134]{3,2,1,0:T(8,128)S(1)} %get-tuple-element.543) | copy-start | bytes 1646596 | tf_op jit(solution)/shard_map/while
  153.2 4.7 %copy-start.5 = (f32[2,16,32,134]{3,2,1,0:T(8,128)}, f32[2,16,32,134]{3,2,1,0:T(8,128)S(1)}, u32[]{:S(2)}) copy-start(f32[2,16,32,134]{3,2,1,0:T(8,128)S(1)} %get-tuple-element.543) | copy-start | bytes 1646596 | tf_op jit(solution)/shard_map/while
  160.0 4.7 %copy-start.5 = (f32[2,16,32,134]{3,2,1,0:T(8,128)}, f32[2,16,32,134]{3,2,1,0:T(8,128)S(1)}, u32[]{:S(2)}) copy-start(f32[2,16,32,134]{3,2,1,0:T(8,128)S(1)} %get-tuple-element.543) | copy-start | bytes 1646596 | tf_op jit(solution)/shard_map/while
  166.8 4.7 %copy-start.5 = (f32[2,16,32,134]{3,2,1,0:T(8,128)}, f32[2,16,32,134]{3,2,1,0:T(8,128)S(1)}, u32[]{:S(2)}) copy-start(f32[2,16,32,134]{3,2,1,0:T(8,128)S(1)} %get-tuple-element.543) | copy-start | bytes 1646596 | tf_op jit(solution)/shard_map/while
  173.6 4.7 %copy-start.5 = (f32[2,16,32,134]{3,2,1,0:T(8,128)}, f32[2,16,32,134]{3,2,1,0:T(8,128)S(1)}, u32[]{:S(2)}) copy-start(f32[2,16,32,134]{3,2,1,0:T(8,128)S(1)} %get-tuple-element.543) | copy-start | bytes 1646596 | tf_op jit(solution)/shard_map/while
  180.3 4.7 %copy-start.5 = (f32[2,16,32,134]{3,2,1,0:T(8,128)}, f32[2,16,32,134]{3,2,1,0:T(8,128)S(1)}, u32[]{:S(2)}) copy-start(f32[2,16,32,134]{3,2,1,0:T(8,128)S(1)} %get-tuple-element.543) | copy-start | bytes 1646596 | tf_op jit(solution)/shard_map/while
  187.1 4.7 %copy-start.5 = (f32[2,16,32,134]{3,2,1,0:T(8,128)}, f32[2,16,32,134]{3,2,1,0:T(8,128)S(1)}, u32[]{:S(2)}) copy-start(f32[2,16,32,134]{3,2,1,0:T(8,128)S(1)} %get-tuple-element.543) | copy-start | bytes 1646596 | tf_op jit(solution)/shard_map/while
  193.9 4.7 %copy-start.5 = (f32[2,16,32,134]{3,2,1,0:T(8,128)}, f32[2,16,32,134]{3,2,1,0:T(8,128)S(1)}, u32[]{:S(2)}) copy-start(f32[2,16,32,134]{3,2,1,0:T(8,128)S(1)} %get-tuple-element.543) | copy-start | bytes 1646596 | tf_op jit(solution)/shard_map/while
  200.7 4.7 %copy-start.5 = (f32[2,16,32,134]{3,2,1,0:T(8,128)}, f32[2,16,32,134]{3,2,1,0:T(8,128)S(1)}, u32[]{:S(2)}) copy-start(f32[2,16,32,134]{3,2,1,0:T(8,128)S(1)} %get-tuple-element.543) | copy-start | bytes 1646596 | tf_op jit(solution)/shard_map/while
  207.5 4.7 %copy-start.5 = (f32[2,16,32,134]{3,2,1,0:T(8,128)}, f32[2,16,32,134]{3,2,1,0:T(8,128)S(1)}, u32[]{:S(2)}) copy-start(f32[2,16,32,134]{3,2,1,0:T(8,128)S(1)} %get-tuple-element.543) | copy-start | bytes 1646596 | tf_op jit(solution)/shard_map/while
  214.3 4.7 %copy-start.5 = (f32[2,16,32,134]{3,2,1,0:T(8,128)}, f32[2,16,32,134]{3,2,1,0:T(8,128)S(1)}, u32[]{:S(2)}) copy-start(f32[2,16,32,134]{3,2,1,0:T(8,128)S(1)} %get-tuple-element.543) | copy-start | bytes 1646596 | tf_op jit(solution)/shard_map/while
  221.1 4.7 %copy-start.5 = (f32[2,16,32,134]{3,2,1,0:T(8,128)}, f32[2,16,32,134]{3,2,1,0:T(8,128)S(1)}, u32[]{:S(2)}) copy-start(f32[2,16,32,134]{3,2,1,0:T(8,128)S(1)} %get-tuple-element.543) | copy-start | bytes 1646596 | tf_op jit(solution)/shard_map/while
  227.9 4.7 %copy-start.5 = (f32[2,16,32,134]{3,2,1,0:T(8,128)}, f32[2,16,32,134]{3,2,1,0:T(8,128)S(1)}, u32[]{:S(2)}) copy-start(f32[2,16,32,134]{3,2,1,0:T(8,128)S(1)} %get-tuple-element.543) | copy-start | bytes 1646596 | tf_op jit(solution)/shard_map/while
  234.7 4.7 %copy-start.5 = (f32[2,16,32,134]{3,2,1,0:T(8,128)}, f32[2,16,32,134]{3,2,1,0:T(8,128)S(1)}, u32[]{:S(2)}) copy-start(f32[2,16,32,134]{3,2,1,0:T(8,128)S(1)} %get-tuple-element.543) | copy-start | bytes 1646596 | tf_op jit(solution)/shard_map/while
  241.6 1.3 copy-start.13
  241.7 1.7 copy-start.12
  300.7 52.8 %all-to-all-start = ((bf16[4,16,4,4,128]{4,3,2,0,1:T(4,128)(2,1)}), bf16[4,16,4,4,128]{4,3,2,0,1:T(4,128)(2,1)S(1)}, u32[]{:S(2)}, u32[]{:S(2)}) async-start(bf16[4,16,4,4,128]{4,3,2,0,1:T(4,128)(2,1)} %copy.51), calls=%async_computation | async-start | bytes 524288 | tf_op jit(solution)/shard_map/all_to_all | solution.py:163
  (18 other events, 21.6 us)
Sparse Core Ops, SparseCore 0:
  242.9 54.7 all-gather.2
where the time goes:
time: 365 us; the launch traced here: 362 us
  waiting for transfers between devices  117 us (32%)
  starting transfers between devices  63.5 us (17%)
  loops' own time  44.6 us (12%)
  local copies, waits for them, and re-layouts  37.4 us (10%)
  blocking collectives  36.9 us (10%)
  other arithmetic  28 us (8%)
  matrix products  19.4 us (5%)
  between operations  14.7 us (4%)
    all_gather x1, waiting for transfers between devices, body(): everything = lax.all_gather(slab[None], 'depth', axis=0, tiled=True)  54.3 us
    another operation x1, loops' own time, body(): lax.scan(march, start_state, jnp.arange(depth_cells, dtype=jnp.int32))  44.6 us
    all_gather x1, blocking collectives, body(): owner_map = lax.all_gather(owners, 'col', axis=1, tiled=True)[:, :, :, 0]  36.9 us
    ppermute x10, waiting for transfers between devices, with_halo(): lax.ppermute(head, axis, [((i + 1) % count, i) for i in range(ends)])  33.9 us
    ppermute x10, waiting for transfers between devices, with_halo(): lax.ppermute(tail, axis, [(i, (i + 1) % count) for i in range(ends)])  29.1 us
    ppermute x10, starting transfers between devices, with_halo(): lax.ppermute(tail, axis, [(i, (i + 1) % count) for i in range(ends)])  27.4 us
    ppermute x10, starting transfers between devices, with_halo(): lax.ppermute(head, axis, [((i + 1) % count, i) for i in range(ends)])  23.6 us
    while x96, local copies, waits for them, and re-layouts  20.6 us
  transfers between devices with their start and end apart: 22, of which 15 were waited for; matrix products, arithmetic and copies ran while one was open for 1% of the time, Pallas kernels for 0%

commit v1 on v0

v1 whole, which is shorter than its diff:
```python
import functools

import jax
import jax.numpy as jnp
from jax import lax
from jax.experimental import pallas as pl
from jax.experimental.pallas import tpu as pltpu
from jax.sharding import PartitionSpec as P

TIME_STEP = 0.1
RAY_STEP = 0.02
VEL_DEPTH = 0.3
VEL_ROW = 0.2
VEL_COL = 0.4

HALO = 3
RIM = 3
EDGE = 8
PLANES = 24
ROWS = 40
SHIFTS = 2 * RIM + 1
CAPACITY = 4

F32 = jnp.float32
BF16 = jnp.bfloat16
VMEM_SPEC = pl.BlockSpec(memory_space=pltpu.VMEM)
SMEM_SPEC = pl.BlockSpec(memory_space=pltpu.SMEM)
NT = (((1,), (1,)), ((), ()))
TN = (((0,), (0,)), ((), ()))


def call(kernel, out_shape, in_specs, scratch=(), limit=24):
    return pl.pallas_call(
        kernel,
        out_shape=out_shape,
        in_specs=in_specs,
        out_specs=jax.tree.map(lambda unused: VMEM_SPEC, out_shape),
        scratch_shapes=list(scratch),
        compiler_params=pltpu.CompilerParams(vmem_limit_bytes=limit << 20),
    )


def shift_up(x, axis):
    n = lax.axis_size(axis)
    return lax.ppermute(x, axis, [(i, i + 1) for i in range(n - 1)])


def shift_down(x, axis):
    n = lax.axis_size(axis)
    return lax.ppermute(x, axis, [(i + 1, i) for i in range(n - 1)])


def pack_depth(species, diff, rate, low, high):
    for f in range(2):
        low[f] = species[f, :HALO].astype(BF16)
        high[f] = species[f, -HALO:].astype(BF16)
    for f, ref in ((2, diff), (3, rate)):
        low[f] = ref[:HALO].astype(BF16)
        high[f] = ref[-HALO:].astype(BF16)


def pack_rows(species, diff, rate, before, after, low, high, wide):
    n = 32
    for f in range(4):
        base = f * PLANES * n
        own = species.at[f] if f < 2 else (diff if f == 2 else rate)
        wide[pl.ds(base, HALO * n), :] = before[f].astype(F32).reshape(HALO * n, 128)
        wide[pl.ds(base + HALO * n, 16 * n), :] = own[...].reshape(16 * n, 128)
        wide[pl.ds(base + 19 * n, HALO * n), :] = after[f].astype(F32).reshape(HALO * n, 128)
        wide[pl.ds(base + 22 * n, 2 * n), :] = jnp.zeros((2 * n, 128), F32)
    for r in range(HALO):
        low[r] = wide[pl.ds(r, 4 * PLANES, stride=n), :].astype(BF16)
        high[r] = wide[pl.ds(n - HALO + r, 4 * PLANES, stride=n), :].astype(BF16)


def column_picker():
    j = lax.broadcasted_iota(jnp.int32, (2 * EDGE, 128), 0)
    lane = lax.broadcasted_iota(jnp.int32, (2 * EDGE, 128), 1)
    return (lane == jnp.where(j < EDGE, j, 128 - 2 * EDGE + j)).astype(BF16)


def pack_columns(species, diff, rate, before, after, above, below, low, high):
    pick = column_picker()
    at = 0

    def put(rows):
        nonlocal at
        edge = lax.dot_general(pick, rows, NT, preferred_element_type=F32).astype(BF16)
        count = rows.shape[0]
        low[:, at : at + count] = edge[:EDGE]
        high[:, at : at + count] = edge[EDGE:]
        at += count

    for f in range(2):
        put(species[f].astype(BF16).reshape(512, 128))
    put(diff[...].astype(BF16).reshape(512, 128))
    put(rate[...].astype(BF16).reshape(512, 128))
    put(before[...].reshape(384, 128))
    put(after[...].reshape(384, 128))
    put(above[...].reshape(288, 128))
    put(below[...].reshape(288, 128))


EDGE_LENGTH = 4 * 512 + 2 * 384 + 2 * 288


def stencil(
    place,
    species,
    diff,
    rate,
    before,
    after,
    above,
    below,
    left,
    right,
    out,
    shifted,
    main,
    rim,
    first_main,
    first_rim,
    second_main,
    second_rim,
):
    n = ROWS
    for f in range(4):
        own = species.at[f] if f < 2 else (diff if f == 2 else rate)
        main[f, HALO : HALO + 16, 0:32, :] = own[...]
        main[f, 0:HALO, 0:32, :] = before[f].astype(F32)
        main[f, HALO + 16 : 22, 0:32, :] = after[f].astype(F32)
        main[f, :, 32:40, :] = jnp.zeros((PLANES, 8, 128), F32)
        rim[f, :, 32:40, :] = jnp.zeros((PLANES, 8, 128), F32)
    j = lax.broadcasted_iota(jnp.int32, (EDGE, 128), 0)
    lane8 = lax.broadcasted_iota(jnp.int32, (EDGE, 128), 1)
    reach = HALO + RIM
    put_left = ((lane8 == 128 - EDGE + j) & (j >= EDGE - reach)).astype(BF16)
    put_right = ((lane8 == j) & (j < reach)).astype(BF16)

    def spread(at, count):
        return lax.dot_general(
            left[:, at : at + count], put_left, TN, preferred_element_type=F32
        ) + lax.dot_general(right[:, at : at + count], put_right, TN, preferred_element_type=F32)

    for f in range(4):
        rim[f, HALO : HALO + 16, 0:32, :] = spread(512 * f, 512).reshape(16, 32, 128)
    side = spread(2048, 384).reshape(4, HALO, 32, 128)
    for f in range(4):
        rim[f, 0:HALO, 0:32, :] = side[f]
    side = spread(2432, 384).reshape(4, HALO, 32, 128)
    for f in range(4):
        rim[f, HALO + 16 : 22, 0:32, :] = side[f]
    up = spread(2816, 288).reshape(HALO, 96, 128)
    down = spread(3104, 288).reshape(HALO, 96, 128)
    for r in range(HALO):
        for f in range(4):
            own = pl.ds(f * PLANES, PLANES)
            part = slice(f * PLANES, (f + 1) * PLANES)
            main[f, :, n - HALO + r, :] = above[r, part, :].astype(F32)
            main[f, :, 32 + r, :] = below[r, part, :].astype(F32)
            rim[f, :, n - HALO + r, :] = up[r, part, :]
            rim[f, :, 32 + r, :] = down[r, part, :]

    depth_at, row_at, col_at = place[0], place[1], place[2]
    depth_last, row_last, col_last = place[3], place[4], place[5]
    row = lax.broadcasted_iota(jnp.int32, (n, 128), 0)
    lane = lax.broadcasted_iota(jnp.int32, (n, 128), 1)
    rows_in = (
        (row < 32)
        | ((row < 32 + HALO) & (row_at < row_last))
        | ((row >= n - HALO) & (row_at > 0))
    )
    lanes_in = ((lane < reach) & (col_at < col_last)) | ((lane >= 128 - reach) & (col_at > 0))
    step_main = jnp.where(rows_in, TIME_STEP, 0.0).astype(F32)
    step_rim = jnp.where(rows_in & lanes_in, TIME_STEP, 0.0).astype(F32)
    first_lane = lane == 0
    last_lane = lane == 127

    def tendency(m, r, p):
        results = []
        for part in range(2):
            here, there = (m, r) if part == 0 else (r, m)
            coefs = main if part == 0 else rim
            diffusivity = coefs[2, p]
            reaction = coefs[3, p]
            fuel, heat = here[0, p], here[1, p]
            square = heat * heat
            burned = reaction * fuel * square / (1.0 + square)
            both = []
            for f in range(2):
                centre = fuel if f == 0 else heat
                other = there[f, p]
                below_depth = here[f, p - 1]
                above_depth = here[f, p + 1]
                below_row = pltpu.roll(centre, 1, 0)
                above_row = pltpu.roll(centre, n - 1, 0)
                below_col = jnp.where(
                    first_lane, pltpu.roll(other, 1, 1), pltpu.roll(centre, 1, 1)
                )
                above_col = jnp.where(
                    last_lane, pltpu.roll(other, 127, 1), pltpu.roll(centre, 127, 1)
                )
                laplace = (
                    below_depth
                    + above_depth
                    + below_row
                    + above_row
                    + below_col
                    + above_col
                    - 6.0 * centre
                )
                advect = (
                    VEL_DEPTH * (centre - below_depth)
                    + VEL_ROW * (centre - below_row)
                    + VEL_COL * (centre - below_col)
                )
                gain = -burned if f == 0 else burned
                both.append(diffusivity * laplace - advect + gain)
            results.append(both)
        return results

    def inside(p):
        ok = ((p >= HALO) | (depth_at > 0)) & ((p < HALO + 16) | (depth_at < depth_last))
        return jnp.where(ok, 1.0, 0.0).astype(F32)

    @pl.loop(1, 21)
    def _(p):
        slope = tendency(main, rim, p)
        scale = inside(p)
        for f in range(2):
            first_main[f, p] = main[f, p] + (step_main * scale) * slope[0][f]
            first_rim[f, p] = rim[f, p] + (step_rim * scale) * slope[1][f]

    @pl.loop(2, 20)
    def _(p):
        slope = tendency(first_main, first_rim, p)
        scale = inside(p)
        for f in range(2):
            second_main[f, p] = 0.75 * main[f, p] + 0.25 * (
                first_main[f, p] + (step_main * scale) * slope[0][f]
            )
            second_rim[f, p] = 0.75 * rim[f, p] + 0.25 * (
                first_rim[f, p] + (step_rim * scale) * slope[1][f]
            )

    lane32 = lax.broadcasted_iota(jnp.int32, (32, 128), 1)

    @pl.loop(3, 19)
    def _(p):
        slope = tendency(second_main, second_rim, p)
        k = p - HALO
        for f in range(2):
            new_main = (
                main[f, p] / 3.0 + (2.0 / 3.0) * (second_main[f, p] + step_main * slope[0][f])
            )[:32]
            new_rim = (
                rim[f, p] / 3.0 + (2.0 / 3.0) * (second_rim[f, p] + step_rim * slope[1][f])
            )[:32]
            out[f, k] = new_main
            for shift in range(-RIM, RIM + 1):
                if shift == 0:
                    shifted[RIM, f, k] = new_main
                    continue
                turn = -shift % 128
                outside = lane32 >= 128 - shift if shift > 0 else lane32 < -shift
                shifted[shift + RIM, f, k] = jnp.where(
                    outside, pltpu.roll(new_rim, turn, 1), pltpu.roll(new_main, turn, 1)
                )


def render(start_ref, fraction_ref, weights, view_first, shifted, image):
    count = image.shape[0]
    depth_cells = shifted.shape[2]
    first = view_first[0]

    @pl.loop(0, count)
    def _(j):
        v = first + j

        def march(k, state):
            c0, c1, c2, total, through = state
            i = start_ref[v, k]
            t = fraction_ref[v, k]
            s0 = (1.0 - t) * shifted[i, 0, k] + t * shifted[i + 1, 0, k]
            s1 = (1.0 - t) * shifted[i, 1, k] + t * shifted[i + 1, 1, k]
            logits = [
                weights[v, 3 * c] * s0 + weights[v, 3 * c + 1] * s1 + weights[v, 3 * c + 2]
                for c in range(4)
            ]
            dense = logits[3]
            total = total + (jnp.maximum(dense, 0.0) + jnp.log(1.0 + jnp.exp(-jnp.abs(dense))))
            after = jnp.exp(-RAY_STEP * total)
            part = through - after
            c0 = c0 + part * jnp.tanh(logits[0])
            c1 = c1 + part * jnp.tanh(logits[1])
            c2 = c2 + part * jnp.tanh(logits[2])
            return c0, c1, c2, total, after

        zero = jnp.zeros((32, 128), F32)
        c0, c1, c2, total, through = lax.fori_loop(
            0, depth_cells, march, (zero, zero, zero, zero, zero + 1.0), unroll=2
        )
        opacity = 1.0 - through
        image[j, 0] = 0.5 * (c0 + opacity)
        image[j, 1] = 0.5 * (c1 + opacity)
        image[j, 2] = 0.5 * (c2 + opacity)
        image[j, 3] = opacity


def composite(order, codes, lengths, slab0, slab1, slab2, slab3, outgoing, pieces):
    lane = lax.broadcasted_iota(jnp.int32, (32, 128), 1)
    slabs = (slab0, slab1, slab2, slab3)

    def fetch(which, v, c):
        value = slabs[3][v, c]
        for offset in (2, 1, 0):
            value = jnp.where(which == offset, slabs[offset][v, c], value)
        return value

    for v in range(4):
        keep = lane < lengths[32 * v : 32 * (v + 1), :]
        channels = [fetch(order[v, 0], v, c) for c in range(4)]
        for position in range(1, 4):
            clear = 1.0 - channels[3]
            channels = [channels[c] + clear * fetch(order[v, position], v, c) for c in range(4)]
        for c in range(4):
            pieces[32 * v : 32 * (v + 1), 128 * c : 128 * (c + 1)] = jnp.where(
                keep, channels[c], 0.0
            ).astype(BF16)
    row_id = lax.broadcasted_iota(jnp.int32, (128, 128), 0) + 1
    pieces[:, 512:640] = row_id.astype(F32).astype(BF16)
    slot = lax.broadcasted_iota(jnp.int32, (256, 128), 0)
    select = (slot == codes[...]).astype(F32).astype(BF16)
    outgoing[...] = jnp.dot(select, pieces[...], preferred_element_type=F32).astype(BF16)


def resample(incoming, warp, frame):
    names = incoming[:, 512:640].astype(F32)
    lane = lax.broadcasted_iota(jnp.int32, (256, 128), 1) + 1
    place = (names == lane.astype(F32)).astype(F32).astype(BF16)
    total = lax.dot_general(place, incoming[:, 0:512], TN, preferred_element_type=F32)
    for v in range(4):
        matrix = warp[v].astype(F32)
        for c in range(4):
            rows = total[32 * v : 32 * (v + 1), 128 * c : 128 * (c + 1)]
            frame[pl.ds(128 * v + c, 32, stride=4), :] = jnp.dot(
                rows, matrix, preferred_element_type=F32, precision=lax.Precision.HIGHEST
            )


def body(
    species,
    diffusivity,
    reaction_rate,
    shear_rate,
    colour_weight,
    colour_bias,
    slab_order,
    lengths,
    owners,
    warp_matrix,
):
    depth_at, row_at, col_at = (lax.axis_index(a) for a in ("depth", "row", "col"))
    depth_devices, row_devices, col_devices = (lax.axis_size(a) for a in ("depth", "row", "col"))
    depth_cells = species.shape[1]
    depth_total = depth_cells * depth_devices
    views = shear_rate.shape[0]
    view_count = views // depth_devices

    face = jax.ShapeDtypeStruct((4, HALO, 32, 128), BF16)
    low, high = call(pack_depth, (face, face), [VMEM_SPEC] * 3)(species, diffusivity, reaction_rate)
    before, after = shift_up(high, "depth"), shift_down(low, "depth")
    face = jax.ShapeDtypeStruct((HALO, 4 * PLANES, 128), BF16)
    low, high = call(
        pack_rows, (face, face), [VMEM_SPEC] * 5, [pltpu.VMEM((4 * PLANES * 32, 128), F32)]
    )(species, diffusivity, reaction_rate, before, after)
    above, below = shift_up(high, "row"), shift_down(low, "row")
    face = jax.ShapeDtypeStruct((EDGE, EDGE_LENGTH), BF16)
    low, high = call(pack_columns, (face, face), [VMEM_SPEC] * 7)(
        species, diffusivity, reaction_rate, before, after, above, below
    )
    left, right = shift_up(high, "col"), shift_down(low, "col")
    place = jnp.stack(
        [
            depth_at,
            row_at,
            col_at,
            jnp.int32(depth_devices - 1),
            jnp.int32(row_devices - 1),
            jnp.int32(col_devices - 1),
        ]
    ).astype(jnp.int32)
    wide = pltpu.VMEM((2, PLANES, ROWS, 128), F32)
    species_out, shifted = call(
        stencil,
        (
            jax.ShapeDtypeStruct(species.shape, F32),
            jax.ShapeDtypeStruct((SHIFTS,) + species.shape, F32),
        ),
        [SMEM_SPEC] + [VMEM_SPEC] * 9,
        [pltpu.VMEM((4, PLANES, ROWS, 128), F32)] * 2 + [wide] * 4,
        limit=40,
    )(
        place,
        species,
        diffusivity,
        reaction_rate,
        before,
        after,
        above,
        below,
        left,
        right,
    )

    depth_index = depth_at * depth_cells + jnp.arange(depth_cells, dtype=jnp.int32)
    offset = shear_rate[:, None] * (depth_index.astype(F32) + 0.5 - 0.5 * depth_total)[None, :]
    floor_part = jnp.floor(offset)
    fraction = offset - floor_part
    start = jnp.clip(floor_part.astype(jnp.int32) + RIM, 0, SHIFTS - 2)
    weights = jnp.concatenate([colour_weight, colour_bias[:, :, None]], axis=2)
    weights = (weights * jnp.array([0.5, 0.5, 0.5, 1.0], F32)[None, :, None]).reshape(views, 12)

    image = jax.ShapeDtypeStruct((view_count, 4, 32, 128), F32)
    render_call = call(render, image, [SMEM_SPEC] * 4 + [VMEM_SPEC])
    slabs = [None] * 4
    for away in (2, 1, 3, 0):
        group = (depth_at + away) % depth_devices
        drawn = render_call(
            start, fraction, weights, (group * view_count).reshape(1).astype(jnp.int32), shifted
        )
        if away:
            drawn = lax.ppermute(
                drawn, "depth", [(i, (i + away) % depth_devices) for i in range(depth_devices)]
            )
        slabs[away] = drawn
    own_order = lax.dynamic_slice_in_dim(slab_order, depth_at * view_count, view_count, 0)
    order = (depth_at - own_order) % depth_devices

    mine = owners[:, 0, :, 0]
    line = jnp.arange(mine.shape[1], dtype=jnp.int32)
    same = (mine[:, :, None] == mine[:, None, :]) & (line[None, :] < line[:, None])[None]
    rank = jnp.sum(same.astype(jnp.int32), axis=2)
    view = jnp.arange(view_count, dtype=jnp.int32)[:, None]
    codes = (mine * (view_count * CAPACITY) + view * CAPACITY + rank).reshape(1, -1)
    lengths_wide = jnp.broadcast_to(lengths[:, 0, :].reshape(-1, 1), (128, 128))

    slots = col_devices * view_count * CAPACITY
    outgoing = call(
        composite,
        jax.ShapeDtypeStruct((slots, 640), BF16),
        [SMEM_SPEC] + [VMEM_SPEC] * 6,
        [pltpu.VMEM((128, 640), BF16)],
    )(order, codes, lengths_wide, *slabs)
    incoming = lax.all_to_all(
        outgoing.reshape(col_devices, slots // col_devices, 640),
        "col",
        split_axis=0,
        concat_axis=0,
        tiled=True,
    ).reshape(slots, 640)
    warp_own = lax.dynamic_slice_in_dim(warp_matrix, depth_at * view_count, view_count, 0)
    frame = call(
        resample, jax.ShapeDtypeStruct((512, 128), F32), [VMEM_SPEC] * 2
    )(incoming, warp_own)
    return species_out, frame.reshape(view_count, 32, 4, 128)


def solution(mesh):
    in_specs = (
        P(None, "depth", "row", "col"),
        P("depth", "row", "col"),
        P("depth", "row", "col"),
        P(),
        P(),
        P(),
        P(),
        P("depth", "col", "row"),
        P("depth", "col", "row", None),
        P(),
    )
    out_specs = (P(None, "depth", "row", "col"), P("depth", "row", None, "col"))
    return jax.shard_map(body, mesh=mesh, in_specs=in_specs, out_specs=out_specs, check_vma=False)
```

time: 365 us -> 117 us (0.32)
  waiting for transfers between devices: 117 us -> 32.4 us
  loops' own time: 44.6 us -> 0 us
  blocking collectives: 36.9 us -> 0 us
  Pallas kernels: 0 us -> 27.8 us
  starting transfers between devices: 63.5 us -> 37.6 us
  local copies, waits for them, and re-layouts: 37.4 us -> 13.1 us
  other arithmetic: 28 us -> 4.54 us
  matrix products: 19.4 us -> 0 us
  between operations: 14.7 us -> 0.95 us
    all_gather x1 -> x0, waiting for transfers between devices: 54.3 us -> none  [body(): everything = lax.all_gather(slab[None], 'depth', axis=0, tiled=True)]
    ppermute x20 -> x9, waiting for transfers between devices: 63 us -> 11.1 us  [the longest x3 7.14 us: shift_down(): return lax.ppermute(x, axis, [(i + 1, i) for i in range(n - 1)])]
    another operation x1 -> x0, loops' own time: 44.6 us -> none  [body(): lax.scan(march, start_state, jnp.arange(depth_cells, dtype=jnp.int32))]
    all_gather x1 -> x0, blocking collectives: 36.9 us -> none  [body(): owner_map = lax.all_gather(owners, 'col', axis=1, tiled=True)[:, :, :, 0]]
    ppermute x20 -> x9, starting transfers between devices: 51 us -> 22.3 us  [the longest x3 8.63 us: body(): lax.ppermute(drawn, 'depth', [(i, (i + away) % depth_devices) for i in ra...]
    pallas_call x0 -> x10, Pallas kernels: none -> 27.8 us  [the longest x4 12 us: body(): render_call(start, fraction, weights, (group * view_count).reshape(1).ast...]
    all_to_all x1, waiting for transfers between devices: 0.01 us -> 21.3 us  [body(): lax.all_to_all(outgoing.reshape(col_devices, slots // col_devices, 640),...]
    while x97 -> x0, local copies, waits for them, and re-layouts: 20.7 us -> none
  transfers between devices with their start and end apart: 22 -> 10, of which waited for: 15 -> 5; matrix products, arithmetic and copies ran while one was open for 1% -> 6% of each run, Pallas kernels for 0% -> 8%
where the time goes in v1:
time: 117 us; the launch traced here: 116 us
  starting transfers between devices  37.6 us (32%)
  waiting for transfers between devices  32.4 us (28%)
  Pallas kernels  27.8 us (24%)
  local copies, waits for them, and re-layouts  13.1 us (11%)
  other arithmetic  4.54 us (4%)
    all_to_all x1, waiting for transfers between devices, body(): lax.all_to_all(outgoing.reshape(col_devices, slots // col_devices, 640),...  21.3 us
    all_to_all x1, starting transfers between devices, body(): lax.all_to_all(outgoing.reshape(col_devices, slots // col_devices, 640),...  15.2 us
    pallas_call x4, Pallas kernels, body(): render_call(start, fraction, weights, (group * view_count).reshape(1).ast...  12 us
    unnamed x36, local copies, waits for them, and re-layouts  11.6 us
    pallas_call x1, Pallas kernels, body(): call(stencil, (jax.ShapeDtypeStruct(species.shape, F32), jax.ShapeDtypeSt...  11.5 us
    ppermute x3, starting transfers between devices, body(): lax.ppermute(drawn, 'depth', [(i, (i + away) % depth_devices) for i in ra...  8.63 us
    ppermute x3, waiting for transfers between devices, shift_down(): return lax.ppermute(x, axis, [(i + 1, i) for i in range(n - 1)])  7.14 us
    ppermute x3, starting transfers between devices, shift_down(): return lax.ppermute(x, axis, [(i + 1, i) for i in range(n - 1)])  7.14 us
  transfers between devices with their start and end apart: 10, of which 5 were waited for; matrix products, arithmetic and copies ran while one was open for 6% of the time, Pallas kernels for 8%

profile of v1, /device:TPU:6, one launch (start us, length us, event | category | flops | bytes accessed | tf_op | source)
XLA Modules:
  0.0 116.4 jit_solution(2805175499691718083)
XLA Ops:
  0.7 1.1 copy-done.3
  1.7 0.9 copy-done.7
  2.7 0.9 copy-done.11
  3.7 1.4 %collective-permute-start = (bf16[4,3,32,128]{3,2,1,0:T(8,128)(2,1)S(1)}, bf16[4,3,32,128]{3,2,1,0:T(8,128)(2,1)S(1)}, u32[]{:S(2)}, u32[]{:S(2)}) collective-permute-start(bf16[4,3,32,128]{3,2,1,0:T(8,128)(2,1)S(1)} %get-tuple-element.10), channel_id=1, source_target_pairs={{0,128},{128,256},{256,384},{1,129},{129,257},{257,385},{2,130},{1... | collective-permute-start | bytes 294920 | tf_op jit(solution)/shard_map/ppermute | solution.py:45
  5.1 4.6 %collective-permute-start.1 = (bf16[4,3,32,128]{3,2,1,0:T(8,128)(2,1)S(1)}, bf16[4,3,32,128]{3,2,1,0:T(8,128)(2,1)S(1)}, u32[]{:S(2)}, u32[]{:S(2)}) collective-permute-start(bf16[4,3,32,128]{3,2,1,0:T(8,128)(2,1)S(1)} %get-tuple-element.11), channel_id=1, source_target_pairs={{128,0},{256,128},{384,256},{129,1},{257,129},{385,257},{130,2},{2... | collective-permute-start | bytes 294920 | tf_op jit(solution)/shard_map/ppermute | solution.py:50
  9.7 0.7 floor_subtract_fusion.fraction_ref
  10.4 0.7 fusion.1.start_ref
  11.2 0.7 pad_maximum_fusion
  12.0 0.7 mul.78
  12.7 0.1 mul.79
  12.8 1.0 convert_reduce_fusion
  13.9 0.1 add.87
  14.0 1.0 copy-done.4
  15.1 0.9 copy-done.8
  16.0 0.9 copy-done.12
  17.0 0.3 shard_map.123
  17.2 1.3 %collective-permute-start.2 = (bf16[3,96,128]{2,1,0:T(8,128)(2,1)S(1)}, bf16[3,96,128]{2,1,0:T(8,128)(2,1)S(1)}, u32[]{:S(2)}, u32[]{:S(2)}) collective-permute-start(bf16[3,96,128]{2,1,0:T(8,128)(2,1)S(1)} %get-tuple-element.12), channel_id=1, source_target_pairs={{0,16},{16,32},{32,48},{48,64},{64,80},{80,96},{96,112},{1,17},{17... | collective-permute-start | bytes 221192 | tf_op jit(solution)/shard_map/ppermute | solution.py:45
  18.5 1.3 %collective-permute-start.3 = (bf16[3,96,128]{2,1,0:T(8,128)(2,1)S(1)}, bf16[3,96,128]{2,1,0:T(8,128)(2,1)S(1)}, u32[]{:S(2)}, u32[]{:S(2)}) collective-permute-start(bf16[3,96,128]{2,1,0:T(8,128)(2,1)S(1)} %get-tuple-element.13), channel_id=1, source_target_pairs={{16,0},{32,16},{48,32},{64,48},{80,64},{96,80},{112,96},{17,1},{33... | collective-permute-start | bytes 221192 | tf_op jit(solution)/shard_map/ppermute | solution.py:50
  19.8 0.7 multiply_reduce_fusion
  20.5 0.1 mul.72
  20.6 2.9 %collective-permute-done.3.below = bf16[3,96,128]{2,1,0:T(8,128)(2,1)S(1)} collective-permute-done((bf16[3,96,128]{2,1,0:T(8,128)(2,1)S(1)}, bf16[3,96,128]{2,1,0:T(8,128)(2,1)S(1)}, u32[]{:S(2)}, u32[]{:S(2)}) %collective-permute-start.3) | collective-permute-done | bytes 73760 | tf_op jit(solution)/shard_map/ppermute | solution.py:50
  23.5 1.0 copy-done.5
  24.6 0.9 copy-done.9
  25.5 0.9 copy-done.13
  26.5 0.4 shard_map.124
  26.9 3.8 %collective-permute-start.4 = (bf16[8,3392]{1,0:T(8,128)(2,1)S(1)}, bf16[8,3392]{1,0:T(8,128)(2,1)S(1)}, u32[]{:S(2)}, u32[]{:S(2)}) collective-permute-start(bf16[8,3392]{1,0:T(8,128)(2,1)S(1)} %get-tuple-element.14), channel_id=1, source_target_pairs={{0,1},{1,2},{2,3},{3,4},{4,5},{5,6},{6,7},{7,8},{8,9},{9,10},{10,1... | collective-permute-start | bytes 162824 | tf_op jit(solution)/shard_map/ppermute | solution.py:45
  30.7 1.3 %collective-permute-start.5 = (bf16[8,3392]{1,0:T(8,128)(2,1)S(1)}, bf16[8,3392]{1,0:T(8,128)(2,1)S(1)}, u32[]{:S(2)}, u32[]{:S(2)}) collective-permute-start(bf16[8,3392]{1,0:T(8,128)(2,1)S(1)} %get-tuple-element.15), channel_id=1, source_target_pairs={{1,0},{2,1},{3,2},{4,3},{5,4},{6,5},{7,6},{8,7},{9,8},{10,9},{11,1... | collective-permute-start | bytes 162824 | tf_op jit(solution)/shard_map/ppermute | solution.py:50
  32.1 0.1 stack.15.place
  32.1 0.4 collective-permute-done.4.left
  32.5 4.3 %collective-permute-done.5.right = bf16[8,3392]{1,0:T(8,128)(2,1)S(1)} collective-permute-done((bf16[8,3392]{1,0:T(8,128)(2,1)S(1)}, bf16[8,3392]{1,0:T(8,128)(2,1)S(1)}, u32[]{:S(2)}, u32[]{:S(2)}) %collective-permute-start.5) | collective-permute-done | bytes 54304 | tf_op jit(solution)/shard_map/ppermute | solution.py:50
  36.8 11.5 %shard_map.125 = (f32[2,16,32,128]{3,2,1,0:T(8,128)}, f32[7,2,16,32,128]{4,3,2,1,0:T(8,128)S(1)}) custom-call(s32[6]{0:T(128)S(1)} %stack.15.place, f32[2,16,32,128]{3,2,1,0:T(8,128)S(1)} %copy-done.6, f32[16,32,128]{2,1,0:T(8,128)S(1)} %copy-done.10, f32[16,32,128]{2,1,0:T(8,128)S(1)} %copy-done.14, ...), custom_call_target="tpu_custom_call" | custom-call | tf_op jit(solution)/shard_map/pallas_call | solution.py:395
  48.3 3.0 %shard_map.127 = f32[4,4,32,128]{3,2,1,0:T(8,128)S(1)} custom-call(s32[16,16]{1,0:T(8,128)S(1)} %fusion.1.start_ref, f32[16,16]{1,0:T(8,128)S(1)} %floor_subtract_fusion.fraction_ref, f32[16,12]{1,0:T(8,128)S(1)} %broadcast_multiply_fusion.weights, s32[1]{0:T(128)} %bitcast.7.view_first, f32[7,2,16,32,128]{4,3,2,1,0:T(8,128)S(1)} %get-tuple-element.17.shifted), custom_call_target="tpu_custom_call" | custom-call | tf_op jit(solution)/shard_map/pallas_call | solution.py:430
  51.3 2.1 %collective-permute-start.6 = (f32[4,4,32,128]{3,2,1,0:T(8,128)S(1)}, f32[4,4,32,128]{3,2,1,0:T(8,128)S(1)}, u32[]{:S(2)}, u32[]{:S(2)}) collective-permute-start(f32[4,4,32,128]{3,2,1,0:T(8,128)S(1)} %shard_map.127), channel_id=1, source_target_pairs={{0,128},{128,256},{256,384},{384,0},{1,129},{129,257},{257,385},{3... | collective-permute-start | bytes 786440 | tf_op jit(solution)/shard_map/ppermute | solution.py:434
  53.4 3.0 %shard_map.128 = f32[4,4,32,128]{3,2,1,0:T(8,128)S(1)} custom-call(s32[16,16]{1,0:T(8,128)S(1)} %fusion.1.start_ref, f32[16,16]{1,0:T(8,128)S(1)} %floor_subtract_fusion.fraction_ref, f32[16,12]{1,0:T(8,128)S(1)} %broadcast_multiply_fusion.weights, s32[1]{0:T(128)} %bitcast.8.view_first, f32[7,2,16,32,128]{4,3,2,1,0:T(8,128)S(1)} %get-tuple-element.17.shifted), custom_call_target="tpu_custom_call" | custom-call | tf_op jit(solution)/shard_map/pallas_call | solution.py:430
  56.5 4.6 %collective-permute-start.7 = (f32[4,4,32,128]{3,2,1,0:T(8,128)S(1)}, f32[4,4,32,128]{3,2,1,0:T(8,128)S(1)}, u32[]{:S(2)}, u32[]{:S(2)}) collective-permute-start(f32[4,4,32,128]{3,2,1,0:T(8,128)S(1)} %shard_map.128), channel_id=1, source_target_pairs={{0,256},{128,384},{256,0},{384,128},{1,257},{129,385},{257,1},{385... | collective-permute-start | bytes 786440 | tf_op jit(solution)/shard_map/ppermute | solution.py:434
  61.1 3.0 %shard_map.129 = f32[4,4,32,128]{3,2,1,0:T(8,128)S(1)} custom-call(s32[16,16]{1,0:T(8,128)S(1)} %fusion.1.start_ref, f32[16,16]{1,0:T(8,128)S(1)} %floor_subtract_fusion.fraction_ref, f32[16,12]{1,0:T(8,128)S(1)} %broadcast_multiply_fusion.weights, s32[1]{0:T(128)} %bitcast.9.view_first, f32[7,2,16,32,128]{4,3,2,1,0:T(8,128)S(1)} %get-tuple-element.17.shifted), custom_call_target="tpu_custom_call" | custom-call | tf_op jit(solution)/shard_map/pallas_call | solution.py:430
  64.1 1.9 %collective-permute-start.8 = (f32[4,4,32,128]{3,2,1,0:T(8,128)S(1)}, f32[4,4,32,128]{3,2,1,0:T(8,128)S(1)}, u32[]{:S(2)}, u32[]{:S(2)}) collective-permute-start(f32[4,4,32,128]{3,2,1,0:T(8,128)S(1)} %shard_map.129), channel_id=1, source_target_pairs={{0,384},{128,0},{256,128},{384,256},{1,385},{129,1},{257,129},{385... | collective-permute-start | bytes 786440 | tf_op jit(solution)/shard_map/ppermute | solution.py:434
  66.1 0.1 copy.22
  66.2 0.5 broadcast.61
  66.8 0.7 reduce.7
  67.4 0.1 broadcast_in_dim.6
  67.5 2.0 %copy-done.2 = f32[7,2,16,32,128]{4,3,2,1,0:T(8,128)S(1)} copy-done((f32[7,2,16,32,128]{4,3,2,1,0:T(8,128)S(1)}, f32[7,2,16,32,128]{4,3,2,1,0:T(8,128)}, u32[]{:S(2)}) %copy-start.2) | copy-done | bytes 3670040
  69.6 3.0 %shard_map.126.slab0 = f32[4,4,32,128]{3,2,1,0:T(8,128)S(1)} custom-call(s32[16,16]{1,0:T(8,128)S(1)} %fusion.1.start_ref, f32[16,16]{1,0:T(8,128)S(1)} %floor_subtract_fusion.fraction_ref, f32[16,12]{1,0:T(8,128)S(1)} %broadcast_multiply_fusion.weights, s32[1]{0:T(128)} %bitcast.6.view_first, f32[7,2,16,32,128]{4,3,2,1,0:T(8,128)S(1)} %copy-done.2), custom_call_target="tpu_custom_call" | custom-call | tf_op jit(solution)/shard_map/pallas_call | solution.py:430
  72.6 3.6 %collective-permute-done.8.slab3 = f32[4,4,32,128]{3,2,1,0:T(8,128)S(1)} collective-permute-done((f32[4,4,32,128]{3,2,1,0:T(8,128)S(1)}, f32[4,4,32,128]{3,2,1,0:T(8,128)S(1)}, u32[]{:S(2)}, u32[]{:S(2)}) %collective-permute-start.8) | collective-permute-done | bytes 262176 | tf_op jit(solution)/shard_map/ppermute | solution.py:434
  76.2 1.8 %shard_map.130 = bf16[256,640]{1,0:T(8,128)(2,1)} custom-call(s32[4,4]{1,0:T(4,128)S(1)} %add_select_fusion.order, s32[1,128]{1,0:T(1,128)S(1)} %add_add_fusion.codes, s32[128,128]{1,0:T(8,128)S(1)} %broadcast_in_dim.7.lengths, f32[4,4,32,128]{3,2,1,0:T(8,128)S(1)} %shard_map.126.slab0, f32[4,4,32,128]{3,2,1,0:T(8,128)S(1)} %collective-permute-done.6.slab1, ...), custom_call_target="tpu_custom_call" | custom-call | tf_op jit(solution)/shard_map/pallas_call | solution.py:450
  78.0 15.2 %all-to-all-start = ((bf16[16,16,640]{2,1,0:T(8,128)(2,1)}), bf16[16,16,640]{2,1,0:T(8,128)(2,1)S(1)}, u32[]{:S(2)}, u32[]{:S(2)}) async-start(bf16[16,16,640]{2,1,0:T(8,128)(2,1)} %bitcast.10), calls=%async_computation | async-start | bytes 655360 | tf_op jit(solution)/shard_map/all_to_all | solution.py:456
  93.3 21.3 %all-to-all-done = bf16[16,16,640]{2,1,0:T(8,128)(2,1)S(1)} async-done(((bf16[16,16,640]{2,1,0:T(8,128)(2,1)}), bf16[16,16,640]{2,1,0:T(8,128)(2,1)S(1)}, u32[]{:S(2)}, u32[]{:S(2)}) %all-to-all-start) | async-done | bytes 327712 | tf_op jit(solution)/shard_map/all_to_all | solution.py:456
  114.6 1.8 %shard_map.131 = f32[512,128]{1,0:T(8,128)} custom-call(bf16[256,640]{1,0:T(8,128)(2,1)S(1)} %bitcast.16, bf16[4,128,128]{2,1,0:T(8,128)(2,1)S(1)} %constant_dynamic-slice_fusion.warp), custom_call_target="tpu_custom_call" | custom-call | tf_op jit(solution)/shard_map/pallas_call | solution.py:464
  (43 shorter events, 0.5 us)
Async XLA Ops:
  0.6 92.6 %copy-start = (bf16[16,128,128]{2,1,0:T(8,128)(2,1)S(1)}, bf16[16,128,128]{2,1,0:T(8,128)(2,1)}, u32[]{:S(2)}) copy-start(bf16[16,128,128]{2,1,0:T(8,128)(2,1)} %param.20) | copy-start | bytes 1572868
  0.6 1.1 copy-start.3
  1.7 0.9 copy-start.7
  2.7 0.9 copy-start.11
  3.6 33.1 %copy-start.6 = (f32[2,16,32,128]{3,2,1,0:T(8,128)S(1)}, f32[2,16,32,128]{3,2,1,0:T(8,128)}, u32[]{:S(2)}) copy-start(f32[2,16,32,128]{3,2,1,0:T(8,128)} %species.7) | copy-start | bytes 1572868
  3.6 33.1 %copy-start.10 = (f32[16,32,128]{2,1,0:T(8,128)S(1)}, f32[16,32,128]{2,1,0:T(8,128)}, u32[]{:S(2)}) copy-start(f32[16,32,128]{2,1,0:T(8,128)} %diff.7) | copy-start | bytes 786436
  3.7 33.1 %copy-start.14 = (f32[16,32,128]{2,1,0:T(8,128)S(1)}, f32[16,32,128]{2,1,0:T(8,128)}, u32[]{:S(2)}) copy-start(f32[16,32,128]{2,1,0:T(8,128)} %rate.7) | copy-start | bytes 786436
  3.7 10.3 %collective-permute-start = (bf16[4,3,32,128]{3,2,1,0:T(8,128)(2,1)S(1)}, bf16[4,3,32,128]{3,2,1,0:T(8,128)(2,1)S(1)}, u32[]{:S(2)}, u32[]{:S(2)}) collective-permute-start(bf16[4,3,32,128]{3,2,1,0:T(8,128)(2,1)S(1)} %get-tuple-element.10), channel_id=1, source_target_pairs={{0,128},{128,256},{256,384},{1,129},{129,257},{257,385},{2,130},{1... | collective-permute-start | bytes 294920 | tf_op jit(solution)/shard_map/ppermute | solution.py:45
  5.1 8.9 %collective-permute-start.1 = (bf16[4,3,32,128]{3,2,1,0:T(8,128)(2,1)S(1)}, bf16[4,3,32,128]{3,2,1,0:T(8,128)(2,1)S(1)}, u32[]{:S(2)}, u32[]{:S(2)}) collective-permute-start(bf16[4,3,32,128]{3,2,1,0:T(8,128)(2,1)S(1)} %get-tuple-element.11), channel_id=1, source_target_pairs={{128,0},{256,128},{384,256},{129,1},{257,129},{385,257},{130,2},{2... | collective-permute-start | bytes 294920 | tf_op jit(solution)/shard_map/ppermute | solution.py:50
  14.0 1.0 copy-start.4
  15.1 0.9 copy-start.8
  16.0 0.9 copy-start.12
  17.2 3.4 %collective-permute-start.2 = (bf16[3,96,128]{2,1,0:T(8,128)(2,1)S(1)}, bf16[3,96,128]{2,1,0:T(8,128)(2,1)S(1)}, u32[]{:S(2)}, u32[]{:S(2)}) collective-permute-start(bf16[3,96,128]{2,1,0:T(8,128)(2,1)S(1)} %get-tuple-element.12), channel_id=1, source_target_pairs={{0,16},{16,32},{32,48},{48,64},{64,80},{80,96},{96,112},{1,17},{17... | collective-permute-start | bytes 221192 | tf_op jit(solution)/shard_map/ppermute | solution.py:45
  18.5 5.0 %collective-permute-start.3 = (bf16[3,96,128]{2,1,0:T(8,128)(2,1)S(1)}, bf16[3,96,128]{2,1,0:T(8,128)(2,1)S(1)}, u32[]{:S(2)}, u32[]{:S(2)}) collective-permute-start(bf16[3,96,128]{2,1,0:T(8,128)(2,1)S(1)} %get-tuple-element.13), channel_id=1, source_target_pairs={{16,0},{32,16},{48,32},{64,48},{80,64},{96,80},{112,96},{17,1},{33... | collective-permute-start | bytes 221192 | tf_op jit(solution)/shard_map/ppermute | solution.py:50
  23.5 1.0 copy-start.5
  24.6 0.9 copy-start.9
  25.5 0.9 copy-start.13
  26.9 5.6 %collective-permute-start.4 = (bf16[8,3392]{1,0:T(8,128)(2,1)S(1)}, bf16[8,3392]{1,0:T(8,128)(2,1)S(1)}, u32[]{:S(2)}, u32[]{:S(2)}) collective-permute-start(bf16[8,3392]{1,0:T(8,128)(2,1)S(1)} %get-tuple-element.14), channel_id=1, source_target_pairs={{0,1},{1,2},{2,3},{3,4},{4,5},{5,6},{6,7},{7,8},{8,9},{9,10},{10,1... | collective-permute-start | bytes 162824 | tf_op jit(solution)/shard_map/ppermute | solution.py:45
  30.7 6.0 %collective-permute-start.5 = (bf16[8,3392]{1,0:T(8,128)(2,1)S(1)}, bf16[8,3392]{1,0:T(8,128)(2,1)S(1)}, u32[]{:S(2)}, u32[]{:S(2)}) collective-permute-start(bf16[8,3392]{1,0:T(8,128)(2,1)S(1)} %get-tuple-element.15), channel_id=1, source_target_pairs={{1,0},{2,1},{3,2},{4,3},{5,4},{6,5},{7,6},{8,7},{9,8},{10,9},{11,1... | collective-permute-start | bytes 162824 | tf_op jit(solution)/shard_map/ppermute | solution.py:50
  48.3 12.8 %copy-start.1 = (f32[7,2,16,32,128]{4,3,2,1,0:T(8,128)}, f32[7,2,16,32,128]{4,3,2,1,0:T(8,128)S(1)}, u32[]{:S(2)}) copy-start(f32[7,2,16,32,128]{4,3,2,1,0:T(8,128)S(1)} %get-tuple-element.17.shifted) | copy-start | bytes 11010052
  51.3 21.2 %collective-permute-start.6 = (f32[4,4,32,128]{3,2,1,0:T(8,128)S(1)}, f32[4,4,32,128]{3,2,1,0:T(8,128)S(1)}, u32[]{:S(2)}, u32[]{:S(2)}) collective-permute-start(f32[4,4,32,128]{3,2,1,0:T(8,128)S(1)} %shard_map.127), channel_id=1, source_target_pairs={{0,128},{128,256},{256,384},{384,0},{1,129},{129,257},{257,385},{3... | collective-permute-start | bytes 786440 | tf_op jit(solution)/shard_map/ppermute | solution.py:434
  53.4 12.6 %copy-start.15 = (s32[16,4]{0,1:T(4,128)S(1)}, s32[16,4]{0,1:T(4,128)}, u32[]{:S(2)}) copy-start(s32[16,4]{0,1:T(4,128)} %param.17) | copy-start | bytes 772
  53.4 13.3 %copy-start.16 = (s32[4,1,32]{2,1,0:T(1,128)S(1)}, s32[4,1,32]{2,1,0:T(1,128)}, u32[]{:S(2)}) copy-start(s32[4,1,32]{2,1,0:T(1,128)} %param.18) | copy-start | bytes 1540
  56.5 16.1 %collective-permute-start.7 = (f32[4,4,32,128]{3,2,1,0:T(8,128)S(1)}, f32[4,4,32,128]{3,2,1,0:T(8,128)S(1)}, u32[]{:S(2)}, u32[]{:S(2)}) collective-permute-start(f32[4,4,32,128]{3,2,1,0:T(8,128)S(1)} %shard_map.128), channel_id=1, source_target_pairs={{0,256},{128,384},{256,0},{384,128},{1,257},{129,385},{257,1},{385... | collective-permute-start | bytes 786440 | tf_op jit(solution)/shard_map/ppermute | solution.py:434
  64.1 12.0 %collective-permute-start.8 = (f32[4,4,32,128]{3,2,1,0:T(8,128)S(1)}, f32[4,4,32,128]{3,2,1,0:T(8,128)S(1)}, u32[]{:S(2)}, u32[]{:S(2)}) collective-permute-start(f32[4,4,32,128]{3,2,1,0:T(8,128)S(1)} %shard_map.129), channel_id=1, source_target_pairs={{0,384},{128,0},{256,128},{384,256},{1,385},{129,1},{257,129},{385... | collective-permute-start | bytes 786440 | tf_op jit(solution)/shard_map/ppermute | solution.py:434
  67.5 2.0 %copy-start.2 = (f32[7,2,16,32,128]{4,3,2,1,0:T(8,128)S(1)}, f32[7,2,16,32,128]{4,3,2,1,0:T(8,128)}, u32[]{:S(2)}) copy-start(f32[7,2,16,32,128]{4,3,2,1,0:T(8,128)} %copy-done.1) | copy-start | bytes 11010052
  78.0 36.6 %all-to-all-start = ((bf16[16,16,640]{2,1,0:T(8,128)(2,1)}), bf16[16,16,640]{2,1,0:T(8,128)(2,1)S(1)}, u32[]{:S(2)}, u32[]{:S(2)}) async-start(bf16[16,16,640]{2,1,0:T(8,128)(2,1)} %bitcast.10), calls=%async_computation | async-start | bytes 655360 | tf_op jit(solution)/shard_map/all_to_all | solution.py:456

commit v2 on v1

v2 whole, which is shorter than its diff:
```python
import functools

import jax
import jax.numpy as jnp
from jax import lax
from jax.experimental import pallas as pl
from jax.experimental.pallas import tpu as pltpu
from jax.sharding import PartitionSpec as P

TIME_STEP = 0.1
RAY_STEP = 0.02
LOG2E = 1.4426950408889634
VEL_DEPTH = 0.3
VEL_ROW = 0.2
VEL_COL = 0.4

HALO = 3
RIM = 3
EDGE = 8
PLANES = 24
ROWS = 40
SHIFTS = 2 * RIM + 1
CAPACITY = 4

F32 = jnp.float32
BF16 = jnp.bfloat16
VMEM_SPEC = pl.BlockSpec(memory_space=pltpu.VMEM)
SMEM_SPEC = pl.BlockSpec(memory_space=pltpu.SMEM)
HBM_SPEC = pl.BlockSpec(memory_space=pltpu.HBM)
NT = (((1,), (1,)), ((), ()))
TN = (((0,), (0,)), ((), ()))


def call(kernel, out_shape, in_specs, scratch=(), limit=8, aliases=None):
    return pl.pallas_call(
        kernel,
        out_shape=out_shape,
        in_specs=in_specs,
        out_specs=jax.tree.map(lambda unused: VMEM_SPEC, out_shape),
        scratch_shapes=list(scratch),
        input_output_aliases=aliases or {},
        compiler_params=pltpu.CompilerParams(vmem_limit_bytes=limit << 20),
    )


def in_hbm(x):
    return pltpu.with_memory_space_constraint(x, pltpu.HBM)


def shift_up(x, axis):
    n = lax.axis_size(axis)
    return lax.ppermute(x, axis, [(i, i + 1) for i in range(n - 1)])


def shift_down(x, axis):
    n = lax.axis_size(axis)
    return lax.ppermute(x, axis, [(i + 1, i) for i in range(n - 1)])


def pack_depth(species, diff, rate, low, high, held, sems):
    copies = []
    for side, first in ((0, 0), (1, 16 - HALO)):
        cut = pl.ds(first, HALO)
        for source, at in (
            (species.at[0, cut], 0),
            (species.at[1, cut], 1),
            (diff.at[cut], 2),
            (rate.at[cut], 3),
        ):
            copies.append(
                pltpu.make_async_copy(source, held.at[side, at], sems.at[4 * side + at])
            )
    for copy in copies:
        copy.start()
    for copy in copies:
        copy.wait()
    low[...] = held[0].astype(BF16)
    high[...] = held[1].astype(BF16)


def load_brick(species, diff, rate, brick, sems):
    copies = [
        pltpu.make_async_copy(
            source, brick.at[f, pl.ds(HALO, 16), pl.ds(0, 32), :], sems.at[f]
        )
        for f, source in enumerate((species.at[0], species.at[1], diff, rate))
    ]
    for copy in copies:
        copy.start()
    for f in range(4):
        brick[f, :, 32:ROWS, :] = jnp.zeros((PLANES, ROWS - 32, 128), F32)
        brick[f, HALO + 16 + HALO :, 0:32, :] = jnp.zeros((PLANES - 22, 32, 128), F32)
    for copy in copies:
        copy.wait()


def pack_rows(unused, before, after, brick, low, high):
    for f in range(4):
        brick[f, 0:HALO, 0:32, :] = before[f].astype(F32)
        brick[f, HALO + 16 : 22, 0:32, :] = after[f].astype(F32)
    lines = brick.reshape(4 * PLANES * ROWS, 128)
    for r in range(HALO):
        low[r] = lines[pl.ds(r, 4 * PLANES, stride=ROWS), :].astype(BF16)
        high[r] = lines[pl.ds(32 - HALO + r, 4 * PLANES, stride=ROWS), :].astype(BF16)


def column_picker():
    j = lax.broadcasted_iota(jnp.int32, (2 * EDGE, 128), 0)
    lane = lax.broadcasted_iota(jnp.int32, (2 * EDGE, 128), 1)
    return (lane == jnp.where(j < EDGE, j, 128 - 2 * EDGE + j)).astype(BF16)


def pack_columns(unused, above, below, brick, low, high):
    lines = brick.reshape(4 * PLANES * ROWS, 128)
    for r in range(HALO):
        lines[pl.ds(ROWS - HALO + r, 4 * PLANES, stride=ROWS), :] = above[r].astype(F32)
        lines[pl.ds(32 + r, 4 * PLANES, stride=ROWS), :] = below[r].astype(F32)
    pick = column_picker()
    count = PLANES * ROWS
    for f in range(4):
        rows = brick[f].reshape(count, 128).astype(BF16)
        edge = lax.dot_general(pick, rows, NT, preferred_element_type=F32).astype(BF16)
        low[:, f * count : (f + 1) * count] = edge[:EDGE]
        high[:, f * count : (f + 1) * count] = edge[EDGE:]


def stencil(
    place,
    main,
    left,
    right,
    out,
    shifted,
    rim,
    first_main,
    first_rim,
    second_main,
    second_rim,
):
    n = ROWS
    j = lax.broadcasted_iota(jnp.int32, (EDGE, 128), 0)
    lane8 = lax.broadcasted_iota(jnp.int32, (EDGE, 128), 1)
    reach = HALO + RIM
    put_left = ((lane8 == 128 - EDGE + j) & (j >= EDGE - reach)).astype(BF16)
    put_right = ((lane8 == j) & (j < reach)).astype(BF16)
    count = PLANES * ROWS
    for f in range(4):
        cut = slice(f * count, (f + 1) * count)
        spread = lax.dot_general(
            left[:, cut], put_left, TN, preferred_element_type=F32
        ) + lax.dot_general(right[:, cut], put_right, TN, preferred_element_type=F32)
        rim[f] = spread.reshape(PLANES, ROWS, 128)

    depth_at, row_at, col_at = place[0], place[1], place[2]
    depth_last, row_last, col_last = place[3], place[4], place[5]
    row = lax.broadcasted_iota(jnp.int32, (n, 128), 0)
    lane = lax.broadcasted_iota(jnp.int32, (n, 128), 1)
    rows_in = (
        (row < 32)
        | ((row < 32 + HALO) & (row_at < row_last))
        | ((row >= n - HALO) & (row_at > 0))
    )
    lanes_in = ((lane < reach) & (col_at < col_last)) | ((lane >= 128 - reach) & (col_at > 0))
    step_main = jnp.where(rows_in, TIME_STEP, 0.0).astype(F32)
    step_rim = jnp.where(rows_in & lanes_in, TIME_STEP, 0.0).astype(F32)
    first_lane = lane == 0
    last_lane = lane == 127

    def tendency(m, r, p):
        results = []
        for part in range(2):
            here, there = (m, r) if part == 0 else (r, m)
            coefs = main if part == 0 else rim
            diffusivity = coefs[2, p]
            reaction = coefs[3, p]
            fuel, heat = here[0, p], here[1, p]
            square = heat * heat
            burned = reaction * fuel * square / (1.0 + square)
            both = []
            for f in range(2):
                centre = fuel if f == 0 else heat
                other = there[f, p]
                below_depth = here[f, p - 1]
                above_depth = here[f, p + 1]
                below_row = pltpu.roll(centre, 1, 0)
                above_row = pltpu.roll(centre, n - 1, 0)
                below_col = jnp.where(
                    first_lane, pltpu.roll(other, 1, 1), pltpu.roll(centre, 1, 1)
                )
                above_col = jnp.where(
                    last_lane, pltpu.roll(other, 127, 1), pltpu.roll(centre, 127, 1)
                )
                laplace = (
                    below_depth
                    + above_depth
                    + below_row
                    + above_row
                    + below_col
                    + above_col
                    - 6.0 * centre
                )
                advect = (
                    VEL_DEPTH * (centre - below_depth)
                    + VEL_ROW * (centre - below_row)
                    + VEL_COL * (centre - below_col)
                )
                gain = -burned if f == 0 else burned
                both.append(diffusivity * laplace - advect + gain)
            results.append(both)
        return results

    def inside(p):
        ok = ((p >= HALO) | (depth_at > 0)) & ((p < HALO + 16) | (depth_at < depth_last))
        return jnp.where(ok, 1.0, 0.0).astype(F32)

    @pl.loop(1, 21)
    def _(p):
        slope = tendency(main, rim, p)
        scale = inside(p)
        for f in range(2):
            first_main[f, p] = main[f, p] + (step_main * scale) * slope[0][f]
            first_rim[f, p] = rim[f, p] + (step_rim * scale) * slope[1][f]

    @pl.loop(2, 20)
    def _(p):
        slope = tendency(first_main, first_rim, p)
        scale = inside(p)
        for f in range(2):
            second_main[f, p] = 0.75 * main[f, p] + 0.25 * (
                first_main[f, p] + (step_main * scale) * slope[0][f]
            )
            second_rim[f, p] = 0.75 * rim[f, p] + 0.25 * (
                first_rim[f, p] + (step_rim * scale) * slope[1][f]
            )

    lane32 = lax.broadcasted_iota(jnp.int32, (32, 128), 1)

    @pl.loop(3, 19)
    def _(p):
        slope = tendency(second_main, second_rim, p)
        k = p - HALO
        for f in range(2):
            new_main = (
                main[f, p] / 3.0 + (2.0 / 3.0) * (second_main[f, p] + step_main * slope[0][f])
            )[:32]
            new_rim = (
                rim[f, p] / 3.0 + (2.0 / 3.0) * (second_rim[f, p] + step_rim * slope[1][f])
            )[:32]
            out[f, k] = new_main
            for shift in range(-RIM, RIM + 1):
                if shift == 0:
                    shifted[RIM, f, k] = new_main
                    continue
                turn = -shift % 128
                outside = lane32 >= 128 - shift if shift > 0 else lane32 < -shift
                shifted[shift + RIM, f, k] = jnp.where(
                    outside, pltpu.roll(new_rim, turn, 1), pltpu.roll(new_main, turn, 1)
                )


def render(away, place, shear, weight, bias, shifted, image):
    count = image.shape[0]
    depth_cells = shifted.shape[2]
    depth_at, depth_last = place[0], place[3]
    first = lax.rem(depth_at + away, depth_last + 1) * count
    middle = 0.5 * depth_cells * (depth_last + 1).astype(F32)

    @pl.loop(0, count)
    def _(j):
        v = first + j
        table = [
            tuple(
                (0.5 if c < 3 else 1.0) * value
                for value in (weight[c, 0, v], weight[c, 1, v], bias[c, v])
            )
            for c in range(4)
        ]
        slope = shear[v]

        def march(k, state):
            c0, c1, c2, total, through = state
            place_in_depth = (depth_at * depth_cells + k).astype(F32) + 0.5
            offset = slope * (place_in_depth - middle)
            whole = offset.astype(jnp.int32)
            whole = jnp.where(whole.astype(F32) > offset, whole - 1, whole)
            t = offset - whole.astype(F32)
            i = jnp.clip(whole + RIM, 0, SHIFTS - 2)
            s0 = (1.0 - t) * shifted[i, 0, k] + t * shifted[i + 1, 0, k]
            s1 = (1.0 - t) * shifted[i, 1, k] + t * shifted[i + 1, 1, k]
            logits = [table[c][0] * s0 + table[c][1] * s1 + table[c][2] for c in range(4)]
            dense = logits[3]
            total = total + (jnp.maximum(dense, 0.0) + jnp.log(1.0 + jnp.exp(-jnp.abs(dense))))
            after = jnp.exp2((-RAY_STEP * LOG2E) * total)
            part = through - after
            c0 = c0 + part * jnp.tanh(logits[0])
            c1 = c1 + part * jnp.tanh(logits[1])
            c2 = c2 + part * jnp.tanh(logits[2])
            return c0, c1, c2, total, after

        zero = jnp.zeros((32, 128), F32)
        c0, c1, c2, total, through = lax.fori_loop(
            0, depth_cells, march, (zero, zero, zero, zero, zero + 1.0), unroll=4
        )
        opacity = 1.0 - through
        image[j, 0] = 0.5 * (c0 + opacity)
        image[j, 1] = 0.5 * (c1 + opacity)
        image[j, 2] = 0.5 * (c2 + opacity)
        image[j, 3] = opacity


def deal(place, owners, lengths, warp, select, lengths_wide, warp_own, sem):
    views = warp_own.shape[0]
    copy = pltpu.make_async_copy(warp.at[pl.ds(place[0] * views, views)], warp_own, sem.at[0])
    copy.start()
    row = lax.broadcasted_iota(jnp.int32, (128, 128), 0)
    lane = lax.broadcasted_iota(jnp.int32, (128, 128), 1)
    name = jnp.concatenate([owners[v : v + 1, :] for v in range(views)], axis=1)
    length = jnp.concatenate([lengths[v : v + 1, :] for v in range(views)], axis=1)
    along = jnp.broadcast_to(name, (128, 128))
    across = along.T
    earlier = (along == across) & (row < lane) & (row // 32 == lane // 32)
    rank = jnp.sum(earlier.astype(F32), axis=0, keepdims=True).astype(jnp.int32)
    view = lane[0:1] // 32
    codes = name * (views * CAPACITY) + view * CAPACITY + rank
    slot = lax.broadcasted_iota(jnp.int32, select.shape, 0)
    select[...] = (slot == codes).astype(F32).astype(BF16)
    lengths_wide[...] = jnp.broadcast_to(length, (128, 128)).T
    copy.wait()


def composite(place, order, select, lengths, slab0, slab1, slab2, slab3, outgoing, pieces):
    lane = lax.broadcasted_iota(jnp.int32, (32, 128), 1)
    slabs = (slab0, slab1, slab2, slab3)
    depth_at, devices = place[0], place[3] + 1

    def fetch(which, v, c):
        value = slabs[3][v, c]
        for offset in (2, 1, 0):
            value = jnp.where(which == offset, slabs[offset][v, c], value)
        return value

    for v in range(4):
        keep = lane < lengths[32 * v : 32 * (v + 1), :]
        turn = [
            lax.rem(depth_at - order[position, depth_at * 4 + v] + devices, devices)
            for position in range(4)
        ]
        channels = [fetch(turn[0], v, c) for c in range(4)]
        for position in range(1, 4):
            clear = 1.0 - channels[3]
            channels = [channels[c] + clear * fetch(turn[position], v, c) for c in range(4)]
        for c in range(4):
            pieces[32 * v : 32 * (v + 1), 128 * c : 128 * (c + 1)] = jnp.where(
                keep, channels[c], 0.0
            ).astype(BF16)
    row_id = lax.broadcasted_iota(jnp.int32, (128, 128), 0) + 1
    pieces[:, 512:640] = row_id.astype(F32).astype(BF16)
    outgoing[...] = jnp.dot(select[...], pieces[...], preferred_element_type=F32).astype(BF16)


def resample(incoming, warp, frame):
    names = incoming[:, 512:640].astype(F32)
    lane = lax.broadcasted_iota(jnp.int32, (256, 128), 1) + 1
    place = (names == lane.astype(F32)).astype(F32).astype(BF16)
    total = lax.dot_general(place, incoming[:, 0:512], TN, preferred_element_type=F32)
    for v in range(4):
        matrix = warp[v].astype(F32)
        for c in range(4):
            rows = total[32 * v : 32 * (v + 1), 128 * c : 128 * (c + 1)]
            frame[pl.ds(128 * v + c, 32, stride=4), :] = jnp.dot(
                rows, matrix, preferred_element_type=F32, precision=lax.Precision.HIGHEST
            )


def body(
    species,
    diffusivity,
    reaction_rate,
    shear_rate,
    colour_weight,
    colour_bias,
    slab_order,
    lengths,
    owners,
    warp_matrix,
):
    depth_at, row_at, col_at = (lax.axis_index(a) for a in ("depth", "row", "col"))
    depth_devices, row_devices, col_devices = (lax.axis_size(a) for a in ("depth", "row", "col"))
    view_count = shear_rate.shape[0] // depth_devices

    place = jnp.stack(
        [
            depth_at,
            row_at,
            col_at,
            jnp.int32(depth_devices - 1),
            jnp.int32(row_devices - 1),
            jnp.int32(col_devices - 1),
        ]
    ).astype(jnp.int32)
    fields = tuple(in_hbm(x) for x in (species, diffusivity, reaction_rate))

    face = jax.ShapeDtypeStruct((4, HALO, 32, 128), BF16)
    low, high = call(
        pack_depth,
        (face, face),
        [HBM_SPEC] * 3,
        [pltpu.VMEM((2, 4, HALO, 32, 128), F32), pltpu.SemaphoreType.DMA((8,))],
    )(*fields)
    before, after = shift_up(high, "depth"), shift_down(low, "depth")
    brick_type = jax.ShapeDtypeStruct((4, PLANES, ROWS, 128), F32)
    brick = call(load_brick, brick_type, [HBM_SPEC] * 3, [pltpu.SemaphoreType.DMA((4,))])(*fields)
    face = jax.ShapeDtypeStruct((HALO, 4 * PLANES, 128), BF16)
    brick, low, high = call(
        pack_rows, (brick_type, face, face), [VMEM_SPEC] * 3, aliases={0: 0}
    )(brick, before, after)
    above, below = shift_up(high, "row"), shift_down(low, "row")
    slots = col_devices * view_count * CAPACITY
    lines = view_count * 32
    select, lengths_wide, warp_own = call(
        deal,
        (
            jax.ShapeDtypeStruct((slots, lines), BF16),
            jax.ShapeDtypeStruct((lines, 128), jnp.int32),
            jax.ShapeDtypeStruct((view_count, 128, 128), BF16),
        ),
        [SMEM_SPEC, VMEM_SPEC, VMEM_SPEC, HBM_SPEC],
        [pltpu.SemaphoreType.DMA((1,))],
    )(place, owners.reshape(view_count, 32), lengths.reshape(view_count, 32), in_hbm(warp_matrix))

    brick, select, lengths_wide, warp_own = lax.optimization_barrier(
        (brick, select, lengths_wide, warp_own)
    )
    face = jax.ShapeDtypeStruct((EDGE, 4 * PLANES * ROWS), BF16)
    brick, low, high = call(
        pack_columns, (brick_type, face, face), [VMEM_SPEC] * 3, aliases={0: 0}
    )(brick, above, below)
    left, right = shift_up(high, "col"), shift_down(low, "col")
    wide = pltpu.VMEM((2, PLANES, ROWS, 128), F32)
    species_out, shifted = call(
        stencil,
        (
            jax.ShapeDtypeStruct(species.shape, F32),
            jax.ShapeDtypeStruct((SHIFTS,) + species.shape, F32),
        ),
        [SMEM_SPEC] + [VMEM_SPEC] * 3,
        [pltpu.VMEM((4, PLANES, ROWS, 128), F32)] + [wide] * 4,
        limit=16,
    )(place, brick, left, right)

    image = jax.ShapeDtypeStruct((view_count, 4, 32, 128), F32)
    weight, bias = jnp.transpose(colour_weight, (1, 2, 0)), colour_bias.T
    slabs = [None] * 4
    for away in (2, 1, 3, 0):
        drawn = call(
            functools.partial(render, away), image, [SMEM_SPEC] * 4 + [VMEM_SPEC]
        )(place, shear_rate, weight, bias, shifted)
        if away:
            drawn = lax.ppermute(
                drawn, "depth", [(i, (i + away) % depth_devices) for i in range(depth_devices)]
            )
        slabs[away] = drawn
    outgoing = call(
        composite,
        jax.ShapeDtypeStruct((slots, 640), BF16),
        [SMEM_SPEC] * 2 + [VMEM_SPEC] * 6,
        [pltpu.VMEM((lines, 640), BF16)],
    )(place, slab_order.T, select, lengths_wide, *slabs)
    incoming = lax.all_to_all(
        outgoing.reshape(col_devices, slots // col_devices, 640),
        "col",
        split_axis=0,
        concat_axis=0,
        tiled=True,
    ).reshape(slots, 640)
    frame = call(resample, jax.ShapeDtypeStruct((4 * lines, 128), F32), [VMEM_SPEC] * 2)(
        incoming, warp_own
    )
    return species_out, frame.reshape(view_count, 32, 4, 128)


def solution(mesh):
    in_specs = (
        P(None, "depth", "row", "col"),
        P("depth", "row", "col"),
        P("depth", "row", "col"),
        P(),
        P(),
        P(),
        P(),
        P("depth", "col", "row"),
        P("depth", "col", "row", None),
        P(),
    )
    out_specs = (P(None, "depth", "row", "col"), P("depth", "row", None, "col"))
    return jax.shard_map(body, mesh=mesh, in_specs=in_specs, out_specs=out_specs, check_vma=False)
```

time: 117 us -> 109 us (0.932)
  blocking collectives: 0 us -> 36.2 us
  waiting for transfers between devices: 32.4 us -> 17.2 us
  starting transfers between devices: 37.6 us -> 24 us
  local copies, waits for them, and re-layouts: 13.1 us -> 0.12 us
  other arithmetic: 4.54 us -> 0 us
  Pallas kernels: 27.8 us -> 29.1 us
    all_to_all x0 -> x1, blocking collectives: none -> 36.2 us  [body(): lax.all_to_all(outgoing.reshape(col_devices, slots // col_devices, 640),...]
    all_to_all x1 -> x0, waiting for transfers between devices: 21.3 us -> none  [body(): lax.all_to_all(outgoing.reshape(col_devices, slots // col_devices, 640),...]
    all_to_all x1 -> x0, starting transfers between devices: 15.2 us -> none  [body(): lax.all_to_all(outgoing.reshape(col_devices, slots // col_devices, 640),...]
    unnamed x36 -> x12, local copies, waits for them, and re-layouts: 11.6 us -> 0.04 us
    ppermute x3, waiting for transfers between devices: 3.58 us -> 9.37 us  [body(): lax.ppermute(drawn, 'depth', [(i, (i + away) % depth_devices) for i in ra...]
    ppermute x3, starting transfers between devices: 8.63 us -> 10.4 us  [body(): lax.ppermute(drawn, 'depth', [(i, (i + away) % depth_devices) for i in ra...]
    pallas_call x9 -> x11, Pallas kernels: 16.3 us -> 17.6 us  [the longest x4 10.4 us: body(): call(functools.partial(render, away), image, [SMEM_SPEC] * 4 + [VMEM_SPEC])]
  transfers between devices with their start and end apart: 10 -> 9, of which waited for: 5 -> 6; matrix products, arithmetic and copies ran while one was open for 6% -> 0% of each run, Pallas kernels for 8% -> 5%
where the time goes in v2:
time: 109 us; the launch traced here: 107 us
  blocking collectives  36.2 us (33%)
  Pallas kernels  29.1 us (27%)
  starting transfers between devices  24 us (22%)
  waiting for transfers between devices  17.2 us (16%)
    all_to_all x1, blocking collectives, body(): lax.all_to_all(outgoing.reshape(col_devices, slots // col_devices, 640),...  36.2 us
    pallas_call x1, Pallas kernels, body(): call(stencil, (jax.ShapeDtypeStruct(species.shape, F32), jax.ShapeDtypeSt...  11.5 us
    pallas_call x4, Pallas kernels, body(): call(functools.partial(render, away), image, [SMEM_SPEC] * 4 + [VMEM_SPEC])  10.4 us
    ppermute x3, starting transfers between devices, body(): lax.ppermute(drawn, 'depth', [(i, (i + away) % depth_devices) for i in ra...  10.4 us
    ppermute x3, waiting for transfers between devices, body(): lax.ppermute(drawn, 'depth', [(i, (i + away) % depth_devices) for i in ra...  9.37 us
    ppermute x3, waiting for transfers between devices, shift_down(): return lax.ppermute(x, axis, [(i + 1, i) for i in range(n - 1)])  7.27 us
    ppermute x3, starting transfers between devices, shift_down(): return lax.ppermute(x, axis, [(i + 1, i) for i in range(n - 1)])  7.14 us
    ppermute x3, starting transfers between devices, shift_up(): return lax.ppermute(x, axis, [(i, i + 1) for i in range(n - 1)])  6.42 us
  transfers between devices with their start and end apart: 9, of which 6 were waited for; matrix products, arithmetic and copies ran while one was open for 0% of the time, Pallas kernels for 5%

profile of v2, /device:TPU:6, one launch (start us, length us, event | category | flops | bytes accessed | tf_op | source)
XLA Modules:
  0.0 107.4 jit_solution(2539827630536523726)
XLA Ops:
  0.6 1.1 shard_map.114
  1.7 1.3 %collective-permute-start = (bf16[4,3,32,128]{3,2,1,0:T(8,128)(2,1)S(1)}, bf16[4,3,32,128]{3,2,1,0:T(8,128)(2,1)S(1)}, u32[]{:S(2)}, u32[]{:S(2)}) collective-permute-start(bf16[4,3,32,128]{3,2,1,0:T(8,128)(2,1)S(1)} %get-tuple-element.19), channel_id=1, source_target_pairs={{0,128},{128,256},{256,384},{1,129},{129,257},{257,385},{2,130},{1... | collective-permute-start | bytes 294920 | tf_op jit(solution)/shard_map/ppermute | solution.py:52
  3.0 0.0 copy-start.3
  3.0 0.0 copy-start.4
  3.0 4.6 %collective-permute-start.1 = (bf16[4,3,32,128]{3,2,1,0:T(8,128)(2,1)S(1)}, bf16[4,3,32,128]{3,2,1,0:T(8,128)(2,1)S(1)}, u32[]{:S(2)}, u32[]{:S(2)}) collective-permute-start(bf16[4,3,32,128]{3,2,1,0:T(8,128)(2,1)S(1)} %get-tuple-element.20), channel_id=1, source_target_pairs={{128,0},{256,128},{384,256},{129,1},{257,129},{385,257},{130,2},{2... | collective-permute-start | bytes 294920 | tf_op jit(solution)/shard_map/ppermute | solution.py:57
  7.6 1.2 %shard_map.113.unused = f32[4,24,40,128]{3,2,1,0:T(8,128)S(1)} custom-call(f32[2,16,32,128]{3,2,1,0:T(8,128)} %species.3, f32[16,32,128]{2,1,0:T(8,128)} %diff.3, f32[16,32,128]{2,1,0:T(8,128)} %rate.3), custom_call_target="tpu_custom_call" | custom-call | tf_op jit(solution)/shard_map/pallas_call | solution.py:412
  8.8 0.0 collective-permute-done.before
  8.8 0.9 collective-permute-done.1.after
  9.8 0.1 shard_map.115
  9.8 1.3 %collective-permute-start.2 = (bf16[3,96,128]{2,1,0:T(8,128)(2,1)S(1)}, bf16[3,96,128]{2,1,0:T(8,128)(2,1)S(1)}, u32[]{:S(2)}, u32[]{:S(2)}) collective-permute-start(bf16[3,96,128]{2,1,0:T(8,128)(2,1)S(1)} %get-tuple-element.26), channel_id=1, source_target_pairs={{0,16},{16,32},{32,48},{48,64},{64,80},{80,96},{96,112},{1,17},{17... | collective-permute-start | bytes 221192 | tf_op jit(solution)/shard_map/ppermute | solution.py:52
  11.1 1.3 %collective-permute-start.3 = (bf16[3,96,128]{2,1,0:T(8,128)(2,1)S(1)}, bf16[3,96,128]{2,1,0:T(8,128)(2,1)S(1)}, u32[]{:S(2)}, u32[]{:S(2)}) collective-permute-start(bf16[3,96,128]{2,1,0:T(8,128)(2,1)S(1)} %get-tuple-element.27), channel_id=1, source_target_pairs={{16,0},{32,16},{48,32},{64,48},{80,64},{96,80},{112,96},{17,1},{33... | collective-permute-start | bytes 221192 | tf_op jit(solution)/shard_map/ppermute | solution.py:57
  12.5 0.1 stack.15.place
  12.5 0.0 copy-done.3
  12.5 0.0 copy-done.4
  12.5 1.5 %shard_map.116 = (bf16[256,128]{1,0:T(8,128)(2,1)S(1)}, s32[128,128]{1,0:T(8,128)S(1)}, bf16[4,128,128]{2,1,0:T(8,128)(2,1)S(1)}) custom-call(s32[6]{0:T(128)S(1)} %stack.15.place, s32[4,32]{1,0:T(4,128)S(1)} %bitcast.21, s32[4,32]{1,0:T(4,128)S(1)} %bitcast.22, bf16[16,128,128]{2,1,0:T(8,128)(2,1)} %warp.1), custom_call_target="tpu_custom_call" | custom-call | tf_op jit(solution)/shard_map/pallas_call | solution.py:420
  14.0 0.0 copy-start
  14.0 0.0 copy-start.1
  14.0 0.0 copy-start.2
  14.0 0.0 collective-permute-done.2.above
  14.1 2.1 %collective-permute-done.3.below = bf16[3,96,128]{2,1,0:T(8,128)(2,1)S(1)} collective-permute-done((bf16[3,96,128]{2,1,0:T(8,128)(2,1)S(1)}, bf16[3,96,128]{2,1,0:T(8,128)(2,1)S(1)}, u32[]{:S(2)}, u32[]{:S(2)}) %collective-permute-start.3) | collective-permute-done | bytes 73760 | tf_op jit(solution)/shard_map/ppermute | solution.py:57
  16.1 0.5 shard_map.117
  16.6 3.8 %collective-permute-start.4 = (bf16[8,3840]{1,0:T(8,128)(2,1)S(1)}, bf16[8,3840]{1,0:T(8,128)(2,1)S(1)}, u32[]{:S(2)}, u32[]{:S(2)}) collective-permute-start(bf16[8,3840]{1,0:T(8,128)(2,1)S(1)} %get-tuple-element.29), channel_id=1, source_target_pairs={{0,1},{1,2},{2,3},{3,4},{4,5},{5,6},{6,7},{7,8},{8,9},{9,10},{10,1... | collective-permute-start | bytes 184328 | tf_op jit(solution)/shard_map/ppermute | solution.py:52
  20.5 1.3 %collective-permute-start.5 = (bf16[8,3840]{1,0:T(8,128)(2,1)S(1)}, bf16[8,3840]{1,0:T(8,128)(2,1)S(1)}, u32[]{:S(2)}, u32[]{:S(2)}) collective-permute-start(bf16[8,3840]{1,0:T(8,128)(2,1)S(1)} %get-tuple-element.30), channel_id=1, source_target_pairs={{1,0},{2,1},{3,2},{4,3},{5,4},{6,5},{7,6},{8,7},{9,8},{10,9},{11,1... | collective-permute-start | bytes 184328 | tf_op jit(solution)/shard_map/ppermute | solution.py:57
  21.8 0.5 collective-permute-done.4.left
  22.3 4.3 %collective-permute-done.5.right = bf16[8,3840]{1,0:T(8,128)(2,1)S(1)} collective-permute-done((bf16[8,3840]{1,0:T(8,128)(2,1)S(1)}, bf16[8,3840]{1,0:T(8,128)(2,1)S(1)}, u32[]{:S(2)}, u32[]{:S(2)}) %collective-permute-start.5) | collective-permute-done | bytes 61472 | tf_op jit(solution)/shard_map/ppermute | solution.py:57
  26.6 11.5 %shard_map.118 = (f32[2,16,32,128]{3,2,1,0:T(8,128)}, f32[7,2,16,32,128]{4,3,2,1,0:T(8,128)S(1)}) custom-call(s32[6]{0:T(128)S(1)} %stack.15.place, f32[4,24,40,128]{3,2,1,0:T(8,128)S(1)} %get-tuple-element.28.main, bf16[8,3840]{1,0:T(8,128)(2,1)S(1)} %collective-permute-done.4.left, bf16[8,3840]{1,0:T(8,128)(2,1)S(1)} %collective-permute-done.5.right), custom_call_target="tpu_custom_call" | custom-call | tf_op jit(solution)/shard_map/pallas_call | solution.py:440
  38.1 0.0 copy-done
  38.1 0.0 copy-done.1
  38.1 0.0 copy-done.2
  38.1 2.6 %shard_map.122 = f32[4,4,32,128]{3,2,1,0:T(8,128)S(1)} custom-call(s32[6]{0:T(128)S(1)} %stack.15.place, f32[16]{0:T(128)S(1)} %copy-done.2, f32[4,2,16]{2,1,0:T(2,128)S(1)} %bitcast.13, f32[4,16]{1,0:T(4,128)S(1)} %bitcast.17, f32[7,2,16,32,128]{4,3,2,1,0:T(8,128)S(1)} %get-tuple-element.34.shifted), custom_call_target="tpu_custom_call" | custom-call | tf_op jit(solution)/shard_map/pallas_call | solution.py:455
  40.7 2.6 %shard_map.121 = f32[4,4,32,128]{3,2,1,0:T(8,128)S(1)} custom-call(s32[6]{0:T(128)S(1)} %stack.15.place, f32[16]{0:T(128)S(1)} %copy-done.2, f32[4,2,16]{2,1,0:T(2,128)S(1)} %bitcast.14, f32[4,16]{1,0:T(4,128)S(1)} %bitcast.18, f32[7,2,16,32,128]{4,3,2,1,0:T(8,128)S(1)} %get-tuple-element.34.shifted), custom_call_target="tpu_custom_call" | custom-call | tf_op jit(solution)/shard_map/pallas_call | solution.py:455
  43.3 2.6 %shard_map.120 = f32[4,4,32,128]{3,2,1,0:T(8,128)S(1)} custom-call(s32[6]{0:T(128)S(1)} %stack.15.place, f32[16]{0:T(128)S(1)} %copy-done.2, f32[4,2,16]{2,1,0:T(2,128)S(1)} %bitcast.15, f32[4,16]{1,0:T(4,128)S(1)} %bitcast.19, f32[7,2,16,32,128]{4,3,2,1,0:T(8,128)S(1)} %get-tuple-element.34.shifted), custom_call_target="tpu_custom_call" | custom-call | tf_op jit(solution)/shard_map/pallas_call | solution.py:455
  45.9 0.0 copy-start.5
  45.9 4.3 %collective-permute-start.6 = (f32[4,4,32,128]{3,2,1,0:T(8,128)S(1)}, f32[4,4,32,128]{3,2,1,0:T(8,128)S(1)}, u32[]{:S(2)}, u32[]{:S(2)}) collective-permute-start(f32[4,4,32,128]{3,2,1,0:T(8,128)S(1)} %shard_map.120), channel_id=1, source_target_pairs={{0,128},{128,256},{256,384},{384,0},{1,129},{129,257},{257,385},{3... | collective-permute-start | bytes 786440 | tf_op jit(solution)/shard_map/ppermute | solution.py:459
  50.2 4.0 %collective-permute-start.7 = (f32[4,4,32,128]{3,2,1,0:T(8,128)S(1)}, f32[4,4,32,128]{3,2,1,0:T(8,128)S(1)}, u32[]{:S(2)}, u32[]{:S(2)}) collective-permute-start(f32[4,4,32,128]{3,2,1,0:T(8,128)S(1)} %shard_map.121), channel_id=1, source_target_pairs={{0,256},{128,384},{256,0},{384,128},{1,257},{129,385},{257,1},{385... | collective-permute-start | bytes 786440 | tf_op jit(solution)/shard_map/ppermute | solution.py:459
  54.2 2.1 %collective-permute-start.8 = (f32[4,4,32,128]{3,2,1,0:T(8,128)S(1)}, f32[4,4,32,128]{3,2,1,0:T(8,128)S(1)}, u32[]{:S(2)}, u32[]{:S(2)}) collective-permute-start(f32[4,4,32,128]{3,2,1,0:T(8,128)S(1)} %shard_map.122), channel_id=1, source_target_pairs={{0,384},{128,0},{256,128},{384,256},{1,385},{129,1},{257,129},{385... | collective-permute-start | bytes 786440 | tf_op jit(solution)/shard_map/ppermute | solution.py:459
  56.4 2.6 %shard_map.119.slab0 = f32[4,4,32,128]{3,2,1,0:T(8,128)S(1)} custom-call(s32[6]{0:T(128)S(1)} %stack.15.place, f32[16]{0:T(128)S(1)} %copy-done.2, f32[4,2,16]{2,1,0:T(2,128)S(1)} %bitcast.16, f32[4,16]{1,0:T(4,128)S(1)} %bitcast.20, f32[7,2,16,32,128]{4,3,2,1,0:T(8,128)S(1)} %get-tuple-element.34.shifted), custom_call_target="tpu_custom_call" | custom-call | tf_op jit(solution)/shard_map/pallas_call | solution.py:455
  59.0 0.0 collective-permute-done.6.slab1
  59.0 3.4 %collective-permute-done.7.slab2 = f32[4,4,32,128]{3,2,1,0:T(8,128)S(1)} collective-permute-done((f32[4,4,32,128]{3,2,1,0:T(8,128)S(1)}, f32[4,4,32,128]{3,2,1,0:T(8,128)S(1)}, u32[]{:S(2)}, u32[]{:S(2)}) %collective-permute-start.7) | collective-permute-done | bytes 262176 | tf_op jit(solution)/shard_map/ppermute | solution.py:459
  62.3 6.0 %collective-permute-done.8.slab3 = f32[4,4,32,128]{3,2,1,0:T(8,128)S(1)} collective-permute-done((f32[4,4,32,128]{3,2,1,0:T(8,128)S(1)}, f32[4,4,32,128]{3,2,1,0:T(8,128)S(1)}, u32[]{:S(2)}, u32[]{:S(2)}) %collective-permute-start.8) | collective-permute-done | bytes 262176 | tf_op jit(solution)/shard_map/ppermute | solution.py:459
  68.4 0.0 copy-done.5
  68.4 1.1 shard_map.123
  69.4 36.2 %all_to_all.5 = bf16[16,16,640]{2,1,0:T(8,128)(2,1)S(1)} all-to-all(bf16[16,16,640]{2,1,0:T(8,128)(2,1)S(1)} %bitcast.12), channel_id=1, replica_groups=mesh['depth'=4,'row'=8,'col'=16] {'col'}, dimensions={0} | all-to-all | bytes 655360 | tf_op jit(solution)/shard_map/all_to_all | solution.py:469
  105.6 1.8 %shard_map.124 = f32[512,128]{1,0:T(8,128)} custom-call(bf16[256,640]{1,0:T(8,128)(2,1)S(1)} %bitcast.11, bf16[4,128,128]{2,1,0:T(8,128)(2,1)S(1)} %get-tuple-element.35.warp), custom_call_target="tpu_custom_call" | custom-call | tf_op jit(solution)/shard_map/pallas_call | solution.py:476
Async XLA Ops:
  1.7 7.1 %collective-permute-start = (bf16[4,3,32,128]{3,2,1,0:T(8,128)(2,1)S(1)}, bf16[4,3,32,128]{3,2,1,0:T(8,128)(2,1)S(1)}, u32[]{:S(2)}, u32[]{:S(2)}) collective-permute-start(bf16[4,3,32,128]{3,2,1,0:T(8,128)(2,1)S(1)} %get-tuple-element.19), channel_id=1, source_target_pairs={{0,128},{128,256},{256,384},{1,129},{129,257},{257,385},{2,130},{1... | collective-permute-start | bytes 294920 | tf_op jit(solution)/shard_map/ppermute | solution.py:52
  3.0 9.5 %copy-start.3 = (s32[4,1,32,1]{2,3,1,0:T(1,128)S(1)}, s32[4,1,32,1]{2,3,1,0:T(1,128)}, u32[]{:S(2)}) copy-start(s32[4,1,32,1]{2,3,1,0:T(1,128)} %param.18) | copy-start | bytes 1540
  3.0 9.5 %copy-start.4 = (s32[4,1,32]{2,1,0:T(1,128)S(1)}, s32[4,1,32]{2,1,0:T(1,128)}, u32[]{:S(2)}) copy-start(s32[4,1,32]{2,1,0:T(1,128)} %param.17) | copy-start | bytes 1540
  3.0 6.8 %collective-permute-start.1 = (bf16[4,3,32,128]{3,2,1,0:T(8,128)(2,1)S(1)}, bf16[4,3,32,128]{3,2,1,0:T(8,128)(2,1)S(1)}, u32[]{:S(2)}, u32[]{:S(2)}) collective-permute-start(bf16[4,3,32,128]{3,2,1,0:T(8,128)(2,1)S(1)} %get-tuple-element.20), channel_id=1, source_target_pairs={{128,0},{256,128},{384,256},{129,1},{257,129},{385,257},{130,2},{2... | collective-permute-start | bytes 294920 | tf_op jit(solution)/shard_map/ppermute | solution.py:57
  9.8 4.2 %collective-permute-start.2 = (bf16[3,96,128]{2,1,0:T(8,128)(2,1)S(1)}, bf16[3,96,128]{2,1,0:T(8,128)(2,1)S(1)}, u32[]{:S(2)}, u32[]{:S(2)}) collective-permute-start(bf16[3,96,128]{2,1,0:T(8,128)(2,1)S(1)} %get-tuple-element.26), channel_id=1, source_target_pairs={{0,16},{16,32},{32,48},{48,64},{64,80},{80,96},{96,112},{1,17},{17... | collective-permute-start | bytes 221192 | tf_op jit(solution)/shard_map/ppermute | solution.py:52
  11.1 5.0 %collective-permute-start.3 = (bf16[3,96,128]{2,1,0:T(8,128)(2,1)S(1)}, bf16[3,96,128]{2,1,0:T(8,128)(2,1)S(1)}, u32[]{:S(2)}, u32[]{:S(2)}) collective-permute-start(bf16[3,96,128]{2,1,0:T(8,128)(2,1)S(1)} %get-tuple-element.27), channel_id=1, source_target_pairs={{16,0},{32,16},{48,32},{64,48},{80,64},{96,80},{112,96},{17,1},{33... | collective-permute-start | bytes 221192 | tf_op jit(solution)/shard_map/ppermute | solution.py:57
  14.0 24.0 %copy-start = (f32[16,4,2]{0,2,1:T(2,128)S(1)}, f32[16,4,2]{0,2,1:T(2,128)}, u32[]{:S(2)}) copy-start(f32[16,4,2]{0,2,1:T(2,128)} %param.14) | copy-start | bytes 1540
  14.0 24.0 %copy-start.1 = (f32[16,4]{0,1:T(4,128)S(1)}, f32[16,4]{0,1:T(4,128)}, u32[]{:S(2)}) copy-start(f32[16,4]{0,1:T(4,128)} %param.15) | copy-start | bytes 772
  14.0 24.0 %copy-start.2 = (f32[16]{0:T(128)S(1)}, f32[16]{0:T(128)}, u32[]{:S(2)}) copy-start(f32[16]{0:T(128)} %shear.7) | copy-start | bytes 196
  16.6 5.7 %collective-permute-start.4 = (bf16[8,3840]{1,0:T(8,128)(2,1)S(1)}, bf16[8,3840]{1,0:T(8,128)(2,1)S(1)}, u32[]{:S(2)}, u32[]{:S(2)}) collective-permute-start(bf16[8,3840]{1,0:T(8,128)(2,1)S(1)} %get-tuple-element.29), channel_id=1, source_target_pairs={{0,1},{1,2},{2,3},{3,4},{4,5},{5,6},{6,7},{7,8},{8,9},{9,10},{10,1... | collective-permute-start | bytes 184328 | tf_op jit(solution)/shard_map/ppermute | solution.py:52
  20.5 6.1 %collective-permute-start.5 = (bf16[8,3840]{1,0:T(8,128)(2,1)S(1)}, bf16[8,3840]{1,0:T(8,128)(2,1)S(1)}, u32[]{:S(2)}, u32[]{:S(2)}) collective-permute-start(bf16[8,3840]{1,0:T(8,128)(2,1)S(1)} %get-tuple-element.30), channel_id=1, source_target_pairs={{1,0},{2,1},{3,2},{4,3},{5,4},{6,5},{7,6},{8,7},{9,8},{10,9},{11,1... | collective-permute-start | bytes 184328 | tf_op jit(solution)/shard_map/ppermute | solution.py:57
  45.9 22.5 %copy-start.5 = (s32[16,4]{0,1:T(4,128)S(1)}, s32[16,4]{0,1:T(4,128)}, u32[]{:S(2)}) copy-start(s32[16,4]{0,1:T(4,128)} %param.16) | copy-start | bytes 772
  45.9 13.1 %collective-permute-start.6 = (f32[4,4,32,128]{3,2,1,0:T(8,128)S(1)}, f32[4,4,32,128]{3,2,1,0:T(8,128)S(1)}, u32[]{:S(2)}, u32[]{:S(2)}) collective-permute-start(f32[4,4,32,128]{3,2,1,0:T(8,128)S(1)} %shard_map.120), channel_id=1, source_target_pairs={{0,128},{128,256},{256,384},{384,0},{1,129},{129,257},{257,385},{3... | collective-permute-start | bytes 786440 | tf_op jit(solution)/shard_map/ppermute | solution.py:459
  50.2 12.2 %collective-permute-start.7 = (f32[4,4,32,128]{3,2,1,0:T(8,128)S(1)}, f32[4,4,32,128]{3,2,1,0:T(8,128)S(1)}, u32[]{:S(2)}, u32[]{:S(2)}) collective-permute-start(f32[4,4,32,128]{3,2,1,0:T(8,128)S(1)} %shard_map.121), channel_id=1, source_target_pairs={{0,256},{128,384},{256,0},{384,128},{1,257},{129,385},{257,1},{385... | collective-permute-start | bytes 786440 | tf_op jit(solution)/shard_map/ppermute | solution.py:459
  54.2 14.1 %collective-permute-start.8 = (f32[4,4,32,128]{3,2,1,0:T(8,128)S(1)}, f32[4,4,32,128]{3,2,1,0:T(8,128)S(1)}, u32[]{:S(2)}, u32[]{:S(2)}) collective-permute-start(f32[4,4,32,128]{3,2,1,0:T(8,128)S(1)} %shard_map.122), channel_id=1, source_target_pairs={{0,384},{128,0},{256,128},{384,256},{1,385},{129,1},{257,129},{385... | collective-permute-start | bytes 786440 | tf_op jit(solution)/shard_map/ppermute | solution.py:459

commit v3 on v2

--- a/solution.py
+++ b/solution.py
@@ -45,6 +45,11 @@
 
 def in_hbm(x):
     return pltpu.with_memory_space_constraint(x, pltpu.HBM)
+
+
+def turn_by(x, axis, steps):
+    n = lax.axis_size(axis)
+    return lax.ppermute(x, axis, [(i, (i + steps) % n) for i in range(n)])
 
 
 def shift_up(x, axis):
@@ -110,11 +115,13 @@
     return (lane == jnp.where(j < EDGE, j, 128 - 2 * EDGE + j)).astype(BF16)
 
 
-def pack_columns(unused, above, below, brick, low, high):
+def pack_columns(place, unused, above, below, brick, low, high):
+    has_above = jnp.where(place[1] > 0, 1.0, 0.0).astype(F32)
+    has_below = jnp.where(place[1] < place[4], 1.0, 0.0).astype(F32)
     lines = brick.reshape(4 * PLANES * ROWS, 128)
     for r in range(HALO):
-        lines[pl.ds(ROWS - HALO + r, 4 * PLANES, stride=ROWS), :] = above[r].astype(F32)
-        lines[pl.ds(32 + r, 4 * PLANES, stride=ROWS), :] = below[r].astype(F32)
+        lines[pl.ds(ROWS - HALO + r, 4 * PLANES, stride=ROWS), :] = has_above * above[r].astype(F32)
+        lines[pl.ds(32 + r, 4 * PLANES, stride=ROWS), :] = has_below * below[r].astype(F32)
     pick = column_picker()
     count = PLANES * ROWS
     for f in range(4):
@@ -277,35 +284,38 @@
         ]
         slope = shear[v]
 
-        def march(k, state):
-            c0, c1, c2, total, through = state
-            place_in_depth = (depth_at * depth_cells + k).astype(F32) + 0.5
-            offset = slope * (place_in_depth - middle)
-            whole = offset.astype(jnp.int32)
-            whole = jnp.where(whole.astype(F32) > offset, whole - 1, whole)
-            t = offset - whole.astype(F32)
-            i = jnp.clip(whole + RIM, 0, SHIFTS - 2)
-            s0 = (1.0 - t) * shifted[i, 0, k] + t * shifted[i + 1, 0, k]
-            s1 = (1.0 - t) * shifted[i, 1, k] + t * shifted[i + 1, 1, k]
-            logits = [table[c][0] * s0 + table[c][1] * s1 + table[c][2] for c in range(4)]
-            dense = logits[3]
-            total = total + (jnp.maximum(dense, 0.0) + jnp.log(1.0 + jnp.exp(-jnp.abs(dense))))
-            after = jnp.exp2((-RAY_STEP * LOG2E) * total)
-            part = through - after
-            c0 = c0 + part * jnp.tanh(logits[0])
-            c1 = c1 + part * jnp.tanh(logits[1])
-            c2 = c2 + part * jnp.tanh(logits[2])
-            return c0, c1, c2, total, after
-
-        zero = jnp.zeros((32, 128), F32)
-        c0, c1, c2, total, through = lax.fori_loop(
-            0, depth_cells, march, (zero, zero, zero, zero, zero + 1.0), unroll=4
-        )
-        opacity = 1.0 - through
-        image[j, 0] = 0.5 * (c0 + opacity)
-        image[j, 1] = 0.5 * (c1 + opacity)
-        image[j, 2] = 0.5 * (c2 + opacity)
-        image[j, 3] = opacity
+        for part in range(4):
+            strip = slice(part * 8, (part + 1) * 8)
+
+            def march(k, state):
+                c0, c1, c2, total, through = state
+                place_in_depth = (depth_at * depth_cells + k).astype(F32) + 0.5
+                offset = slope * (place_in_depth - middle)
+                whole = offset.astype(jnp.int32)
+                whole = jnp.where(whole.astype(F32) > offset, whole - 1, whole)
+                t = offset - whole.astype(F32)
+                i = jnp.clip(whole + RIM, 0, SHIFTS - 2)
+                s0 = (1.0 - t) * shifted[i, 0, k, strip] + t * shifted[i + 1, 0, k, strip]
+                s1 = (1.0 - t) * shifted[i, 1, k, strip] + t * shifted[i + 1, 1, k, strip]
+                logits = [table[c][0] * s0 + table[c][1] * s1 + table[c][2] for c in range(4)]
+                dense = logits[3]
+                total = total + (jnp.maximum(dense, 0.0) + jnp.log(1.0 + jnp.exp(-jnp.abs(dense))))
+                after = jnp.exp2((-RAY_STEP * LOG2E) * total)
+                part = through - after
+                c0 = c0 + part * jnp.tanh(logits[0])
+                c1 = c1 + part * jnp.tanh(logits[1])
+                c2 = c2 + part * jnp.tanh(logits[2])
+                return c0, c1, c2, total, after
+
+            zero = jnp.zeros((8, 128), F32)
+            c0, c1, c2, _, through = lax.fori_loop(
+                0, depth_cells, march, (zero, zero, zero, zero, zero + 1.0), unroll=16
+            )
+            opacity = 1.0 - through
+            image[j, 0, strip] = 0.5 * (c0 + opacity)
+            image[j, 1, strip] = 0.5 * (c1 + opacity)
+            image[j, 2, strip] = 0.5 * (c2 + opacity)
+            image[j, 3, strip] = opacity
 
 
 def deal(place, owners, lengths, warp, select, lengths_wide, warp_own, sem):
@@ -321,7 +331,9 @@
     earlier = (along == across) & (row < lane) & (row // 32 == lane // 32)
     rank = jnp.sum(earlier.astype(F32), axis=0, keepdims=True).astype(jnp.int32)
     view = lane[0:1] // 32
-    codes = name * (views * CAPACITY) + view * CAPACITY + rank
+    half = select.shape[0] // 2
+    codes = name * (views * CAPACITY // 2) + view * (CAPACITY // 2) + rank // 2
+    codes = codes + (rank % 2) * half
     slot = lax.broadcasted_iota(jnp.int32, select.shape, 0)
     select[...] = (slot == codes).astype(F32).astype(BF16)
     lengths_wide[...] = jnp.broadcast_to(length, (128, 128)).T
@@ -355,14 +367,26 @@
             ).astype(BF16)
     row_id = lax.broadcasted_iota(jnp.int32, (128, 128), 0) + 1
     pieces[:, 512:640] = row_id.astype(F32).astype(BF16)
-    outgoing[...] = jnp.dot(select[...], pieces[...], preferred_element_type=F32).astype(BF16)
+    dealt = jnp.dot(select[...], pieces[...], preferred_element_type=F32).astype(BF16)
+    half = outgoing.shape[0]
+    outgoing[:, 0:512] = dealt[:half, 0:512]
+    outgoing[:, 512:1024] = dealt[half:, 0:512]
+    outgoing[:, 1024:1088] = dealt[:half, 512:576]
+    outgoing[:, 1088:1152] = dealt[half:, 576:640]
 
 
 def resample(incoming, warp, frame):
-    names = incoming[:, 512:640].astype(F32)
-    lane = lax.broadcasted_iota(jnp.int32, (256, 128), 1) + 1
-    place = (names == lane.astype(F32)).astype(F32).astype(BF16)
-    total = lax.dot_general(place, incoming[:, 0:512], TN, preferred_element_type=F32)
+    rows = incoming.shape[0]
+    ids = incoming[:, 1024:1152].astype(F32)
+    lane = lax.broadcasted_iota(jnp.int32, (rows, 128), 1)
+    swapped = pltpu.roll(ids, 64, 1)
+    line = (lane + 1).astype(F32)
+    total = jnp.zeros((128, 512), F32)
+    for odd in range(2):
+        names = jnp.where((lane < 64) == (odd == 0), ids, swapped)
+        place = (names == line).astype(F32).astype(BF16)
+        part = incoming[:, 512 * odd : 512 * (odd + 1)]
+        total = total + lax.dot_general(place, part, TN, preferred_element_type=F32)
     for v in range(4):
         matrix = warp[v].astype(F32)
         for c in range(4):
@@ -414,7 +438,7 @@
     brick, low, high = call(
         pack_rows, (brick_type, face, face), [VMEM_SPEC] * 3, aliases={0: 0}
     )(brick, before, after)
-    above, below = shift_up(high, "row"), shift_down(low, "row")
+    above, below = turn_by(high, "row", 1), turn_by(low, "row", -1)
     slots = col_devices * view_count * CAPACITY
     lines = view_count * 32
     select, lengths_wide, warp_own = call(
@@ -433,8 +457,8 @@
     )
     face = jax.ShapeDtypeStruct((EDGE, 4 * PLANES * ROWS), BF16)
     brick, low, high = call(
-        pack_columns, (brick_type, face, face), [VMEM_SPEC] * 3, aliases={0: 0}
-    )(brick, above, below)
+        pack_columns, (brick_type, face, face), [SMEM_SPEC] + [VMEM_SPEC] * 3, aliases={1: 0}
+    )(place, brick, above, below)
     left, right = shift_up(high, "col"), shift_down(low, "col")
     wide = pltpu.VMEM((2, PLANES, ROWS, 128), F32)
     species_out, shifted = call(
@@ -456,23 +480,21 @@
             functools.partial(render, away), image, [SMEM_SPEC] * 4 + [VMEM_SPEC]
         )(place, shear_rate, weight, bias, shifted)
         if away:
-            drawn = lax.ppermute(
-                drawn, "depth", [(i, (i + away) % depth_devices) for i in range(depth_devices)]
-            )
+            drawn = turn_by(drawn, "depth", away)
         slabs[away] = drawn
     outgoing = call(
         composite,
-        jax.ShapeDtypeStruct((slots, 640), BF16),
+        jax.ShapeDtypeStruct((slots // 2, 1152), BF16),
         [SMEM_SPEC] * 2 + [VMEM_SPEC] * 6,
         [pltpu.VMEM((lines, 640), BF16)],
     )(place, slab_order.T, select, lengths_wide, *slabs)
     incoming = lax.all_to_all(
-        outgoing.reshape(col_devices, slots // col_devices, 640),
+        outgoing.reshape(col_devices, -1, 1152),
         "col",
         split_axis=0,
         concat_axis=0,
         tiled=True,
-    ).reshape(slots, 640)
+    ).reshape(slots // 2, 1152)
     frame = call(resample, jax.ShapeDtypeStruct((4 * lines, 128), F32), [VMEM_SPEC] * 2)(
         incoming, warp_own
     )

time: 109 us -> 104 us (0.954)
  the two profiles are of different devices: /device:TPU:6 before, /device:TPU:18 now
where the time goes in v3:
time: 104 us
  blocking collectives  34.8 us (33%)
  Pallas kernels  28.9 us (28%)
  starting transfers between devices  21.7 us (21%)
  waiting for transfers between devices  17.2 us (17%)
    all_to_all x1, blocking collectives, body(): lax.all_to_all(outgoing.reshape(col_devices, -1, 1152), 'col', split_axis...  34.8 us
    pallas_call x1, Pallas kernels, body(): call(stencil, (jax.ShapeDtypeStruct(species.shape, F32), jax.ShapeDtypeSt...  11.5 us
    ppermute x5, starting transfers between devices, turn_by(): return lax.ppermute(x, axis, [(i, (i + steps) % n) for i in range(n)])  10.8 us
    pallas_call x4, Pallas kernels, body(): call(functools.partial(render, away), image, [SMEM_SPEC] * 4 + [VMEM_SPEC])  9.6 us
    ppermute x5, waiting for transfers between devices, turn_by(): return lax.ppermute(x, axis, [(i, (i + steps) % n) for i in range(n)])  9.22 us
    ppermute x2, waiting for transfers between devices, shift_down(): return lax.ppermute(x, axis, [(i + 1, i) for i in range(n - 1)])  7.31 us
    ppermute x2, starting transfers between devices, shift_up(): return lax.ppermute(x, axis, [(i, i + 1) for i in range(n - 1)])  7.23 us
    ppermute x2, starting transfers between devices, shift_down(): return lax.ppermute(x, axis, [(i + 1, i) for i in range(n - 1)])  3.74 us
  transfers between devices with their start and end apart: 9, of which 6 were waited for; matrix products, arithmetic and copies ran while one was open for 0% of the time, Pallas kernels for 5%

profile of v3, /device:TPU:18, one launch (start us, length us, event | category | flops | bytes accessed | tf_op | source)
XLA Modules:
  0.0 103.5 jit_solution(15429381670972936526)
XLA Ops:
  0.6 1.1 %shard_map.114 = (bf16[4,3,32,128]{3,2,1,0:T(8,128)(2,1)S(1)}, bf16[4,3,32,128]{3,2,1,0:T(8,128)(2,1)S(1)}) custom-call(f32[2,16,32,128]{3,2,1,0:T(8,128)} %species.3, f32[16,32,128]{2,1,0:T(8,128)} %diff.3, f32[16,32,128]{2,1,0:T(8,128)} %rate.3), custom_call_target="tpu_custom_call" | custom-call | tf_op jit(solution)/shard_map/pallas_call | solution.py:428
  1.7 3.4 %collective-permute-start = (bf16[4,3,32,128]{3,2,1,0:T(8,128)(2,1)S(1)}, bf16[4,3,32,128]{3,2,1,0:T(8,128)(2,1)S(1)}, u32[]{:S(2)}, u32[]{:S(2)}) collective-permute-start(bf16[4,3,32,128]{3,2,1,0:T(8,128)(2,1)S(1)} %get-tuple-element.19), channel_id=1, source_target_pairs={{0,128},{128,256},{256,384},{1,129},{129,257},{257,385},{2,130},{1... | collective-permute-start | bytes 294920 | tf_op jit(solution)/shard_map/ppermute | solution.py:57
  5.1 0.0 copy-start.3
  5.1 0.0 copy-start.4
  5.1 2.4 %collective-permute-start.1 = (bf16[4,3,32,128]{3,2,1,0:T(8,128)(2,1)S(1)}, bf16[4,3,32,128]{3,2,1,0:T(8,128)(2,1)S(1)}, u32[]{:S(2)}, u32[]{:S(2)}) collective-permute-start(bf16[4,3,32,128]{3,2,1,0:T(8,128)(2,1)S(1)} %get-tuple-element.20), channel_id=1, source_target_pairs={{128,0},{256,128},{384,256},{129,1},{257,129},{385,257},{130,2},{2... | collective-permute-start | bytes 294920 | tf_op jit(solution)/shard_map/ppermute | solution.py:62
  7.6 1.2 %shard_map.113.unused = f32[4,24,40,128]{3,2,1,0:T(8,128)S(1)} custom-call(f32[2,16,32,128]{3,2,1,0:T(8,128)} %species.3, f32[16,32,128]{2,1,0:T(8,128)} %diff.3, f32[16,32,128]{2,1,0:T(8,128)} %rate.3), custom_call_target="tpu_custom_call" | custom-call | tf_op jit(solution)/shard_map/pallas_call | solution.py:436
  8.8 0.0 collective-permute-done.before
  8.8 2.8 %collective-permute-done.1.after = bf16[4,3,32,128]{3,2,1,0:T(8,128)(2,1)S(1)} collective-permute-done((bf16[4,3,32,128]{3,2,1,0:T(8,128)(2,1)S(1)}, bf16[4,3,32,128]{3,2,1,0:T(8,128)(2,1)S(1)}, u32[]{:S(2)}, u32[]{:S(2)}) %collective-permute-start.1) | collective-permute-done | bytes 98336 | tf_op jit(solution)/shard_map/ppermute | solution.py:62
  11.6 0.1 shard_map.115
  11.7 0.0 collective-permute-start.2
  11.7 1.7 %collective-permute-start.3 = (bf16[3,96,128]{2,1,0:T(8,128)(2,1)S(1)}, bf16[3,96,128]{2,1,0:T(8,128)(2,1)S(1)}, u32[]{:S(2)}, u32[]{:S(2)}) collective-permute-start(bf16[3,96,128]{2,1,0:T(8,128)(2,1)S(1)} %get-tuple-element.27), channel_id=1, source_target_pairs={{0,112},{16,0},{32,16},{48,32},{64,48},{80,64},{96,80},{112,96},{1... | collective-permute-start | bytes 221192 | tf_op jit(solution)/shard_map/ppermute | solution.py:52
  13.5 0.1 stack.15.place
  13.6 0.0 copy-done.3
  13.6 0.0 copy-done.4
  13.6 1.5 %shard_map.116 = (bf16[256,128]{1,0:T(8,128)(2,1)S(1)}, s32[128,128]{1,0:T(8,128)S(1)}, bf16[4,128,128]{2,1,0:T(8,128)(2,1)S(1)}) custom-call(s32[6]{0:T(128)S(1)} %stack.15.place, s32[4,32]{1,0:T(4,128)S(1)} %bitcast.21, s32[4,32]{1,0:T(4,128)S(1)} %bitcast.22, bf16[16,128,128]{2,1,0:T(8,128)(2,1)} %warp.1), custom_call_target="tpu_custom_call" | custom-call | tf_op jit(solution)/shard_map/pallas_call | solution.py:444
  15.0 0.0 copy-start
  15.0 0.0 copy-start.1
  15.1 0.0 copy-start.2
  15.1 0.4 collective-permute-done.2.above
  15.5 0.0 collective-permute-done.3.below
  15.5 1.1 %shard_map.117 = (f32[4,24,40,128]{3,2,1,0:T(8,128)S(1)}, bf16[8,3840]{1,0:T(8,128)(2,1)S(1)}, bf16[8,3840]{1,0:T(8,128)(2,1)S(1)}) custom-call(s32[6]{0:T(128)S(1)} %stack.15.place, f32[4,24,40,128]{3,2,1,0:T(8,128)S(1)} %get-tuple-element.25.unused, bf16[3,96,128]{2,1,0:T(8,128)(2,1)S(1)} %collective-permute-done.2.above, ...), custom_call_target="tpu_custom_call", output_to_operand_aliasing={{0}: (1, {})} | custom-call | tf_op jit(solution)/shard_map/pallas_call | solution.py:459
  16.6 3.8 %collective-permute-start.4 = (bf16[8,3840]{1,0:T(8,128)(2,1)S(1)}, bf16[8,3840]{1,0:T(8,128)(2,1)S(1)}, u32[]{:S(2)}, u32[]{:S(2)}) collective-permute-start(bf16[8,3840]{1,0:T(8,128)(2,1)S(1)} %get-tuple-element.29), channel_id=1, source_target_pairs={{0,1},{1,2},{2,3},{3,4},{4,5},{5,6},{6,7},{7,8},{8,9},{9,10},{10,1... | collective-permute-start | bytes 184328 | tf_op jit(solution)/shard_map/ppermute | solution.py:57
  20.4 1.3 %collective-permute-start.5 = (bf16[8,3840]{1,0:T(8,128)(2,1)S(1)}, bf16[8,3840]{1,0:T(8,128)(2,1)S(1)}, u32[]{:S(2)}, u32[]{:S(2)}) collective-permute-start(bf16[8,3840]{1,0:T(8,128)(2,1)S(1)} %get-tuple-element.30), channel_id=1, source_target_pairs={{1,0},{2,1},{3,2},{4,3},{5,4},{6,5},{7,6},{8,7},{9,8},{10,9},{11,1... | collective-permute-start | bytes 184328 | tf_op jit(solution)/shard_map/ppermute | solution.py:62
  21.7 0.6 collective-permute-done.4.left
  22.4 4.5 %collective-permute-done.5.right = bf16[8,3840]{1,0:T(8,128)(2,1)S(1)} collective-permute-done((bf16[8,3840]{1,0:T(8,128)(2,1)S(1)}, bf16[8,3840]{1,0:T(8,128)(2,1)S(1)}, u32[]{:S(2)}, u32[]{:S(2)}) %collective-permute-start.5) | collective-permute-done | bytes 61472 | tf_op jit(solution)/shard_map/ppermute | solution.py:62
  26.8 11.5 %shard_map.118 = (f32[2,16,32,128]{3,2,1,0:T(8,128)}, f32[7,2,16,32,128]{4,3,2,1,0:T(8,128)S(1)}) custom-call(s32[6]{0:T(128)S(1)} %stack.15.place, f32[4,24,40,128]{3,2,1,0:T(8,128)S(1)} %get-tuple-element.28.main, bf16[8,3840]{1,0:T(8,128)(2,1)S(1)} %collective-permute-done.4.left, bf16[8,3840]{1,0:T(8,128)(2,1)S(1)} %collective-permute-done.5.right), custom_call_target="tpu_custom_call" | custom-call | tf_op jit(solution)/shard_map/pallas_call | solution.py:464
  38.3 0.0 copy-done
  38.3 0.0 copy-done.1
  38.3 0.0 copy-done.2
  38.3 2.4 %shard_map.122 = f32[4,4,32,128]{3,2,1,0:T(8,128)S(1)} custom-call(s32[6]{0:T(128)S(1)} %stack.15.place, f32[16]{0:T(128)S(1)} %copy-done.2, f32[4,2,16]{2,1,0:T(2,128)S(1)} %bitcast.13, f32[4,16]{1,0:T(4,128)S(1)} %bitcast.17, f32[7,2,16,32,128]{4,3,2,1,0:T(8,128)S(1)} %get-tuple-element.34.shifted), custom_call_target="tpu_custom_call" | custom-call | tf_op jit(solution)/shard_map/pallas_call | solution.py:479
  40.7 2.4 %shard_map.121 = f32[4,4,32,128]{3,2,1,0:T(8,128)S(1)} custom-call(s32[6]{0:T(128)S(1)} %stack.15.place, f32[16]{0:T(128)S(1)} %copy-done.2, f32[4,2,16]{2,1,0:T(2,128)S(1)} %bitcast.14, f32[4,16]{1,0:T(4,128)S(1)} %bitcast.18, f32[7,2,16,32,128]{4,3,2,1,0:T(8,128)S(1)} %get-tuple-element.34.shifted), custom_call_target="tpu_custom_call" | custom-call | tf_op jit(solution)/shard_map/pallas_call | solution.py:479
  43.1 2.4 %shard_map.120 = f32[4,4,32,128]{3,2,1,0:T(8,128)S(1)} custom-call(s32[6]{0:T(128)S(1)} %stack.15.place, f32[16]{0:T(128)S(1)} %copy-done.2, f32[4,2,16]{2,1,0:T(2,128)S(1)} %bitcast.15, f32[4,16]{1,0:T(4,128)S(1)} %bitcast.19, f32[7,2,16,32,128]{4,3,2,1,0:T(8,128)S(1)} %get-tuple-element.34.shifted), custom_call_target="tpu_custom_call" | custom-call | tf_op jit(solution)/shard_map/pallas_call | solution.py:479
  45.5 0.0 copy-start.5
  45.6 3.1 %collective-permute-start.6 = (f32[4,4,32,128]{3,2,1,0:T(8,128)S(1)}, f32[4,4,32,128]{3,2,1,0:T(8,128)S(1)}, u32[]{:S(2)}, u32[]{:S(2)}) collective-permute-start(f32[4,4,32,128]{3,2,1,0:T(8,128)S(1)} %shard_map.120), channel_id=1, source_target_pairs={{0,128},{128,256},{256,384},{384,0},{1,129},{129,257},{257,385},{3... | collective-permute-start | bytes 786440 | tf_op jit(solution)/shard_map/ppermute | solution.py:52
  48.7 3.3 %collective-permute-start.7 = (f32[4,4,32,128]{3,2,1,0:T(8,128)S(1)}, f32[4,4,32,128]{3,2,1,0:T(8,128)S(1)}, u32[]{:S(2)}, u32[]{:S(2)}) collective-permute-start(f32[4,4,32,128]{3,2,1,0:T(8,128)S(1)} %shard_map.121), channel_id=1, source_target_pairs={{0,256},{128,384},{256,0},{384,128},{1,257},{129,385},{257,1},{385... | collective-permute-start | bytes 786440 | tf_op jit(solution)/shard_map/ppermute | solution.py:52
  52.0 2.6 %collective-permute-start.8 = (f32[4,4,32,128]{3,2,1,0:T(8,128)S(1)}, f32[4,4,32,128]{3,2,1,0:T(8,128)S(1)}, u32[]{:S(2)}, u32[]{:S(2)}) collective-permute-start(f32[4,4,32,128]{3,2,1,0:T(8,128)S(1)} %shard_map.122), channel_id=1, source_target_pairs={{0,384},{128,0},{256,128},{384,256},{1,385},{129,1},{257,129},{385... | collective-permute-start | bytes 786440 | tf_op jit(solution)/shard_map/ppermute | solution.py:52
  54.6 2.4 %shard_map.119.slab0 = f32[4,4,32,128]{3,2,1,0:T(8,128)S(1)} custom-call(s32[6]{0:T(128)S(1)} %stack.15.place, f32[16]{0:T(128)S(1)} %copy-done.2, f32[4,2,16]{2,1,0:T(2,128)S(1)} %bitcast.16, f32[4,16]{1,0:T(4,128)S(1)} %bitcast.20, f32[7,2,16,32,128]{4,3,2,1,0:T(8,128)S(1)} %get-tuple-element.34.shifted), custom_call_target="tpu_custom_call" | custom-call | tf_op jit(solution)/shard_map/pallas_call | solution.py:479
  57.0 0.0 collective-permute-done.6.slab1
  57.0 4.3 %collective-permute-done.7.slab2 = f32[4,4,32,128]{3,2,1,0:T(8,128)S(1)} collective-permute-done((f32[4,4,32,128]{3,2,1,0:T(8,128)S(1)}, f32[4,4,32,128]{3,2,1,0:T(8,128)S(1)}, u32[]{:S(2)}, u32[]{:S(2)}) %collective-permute-start.7) | collective-permute-done | bytes 262176 | tf_op jit(solution)/shard_map/ppermute | solution.py:52
  61.3 4.5 %collective-permute-done.8.slab3 = f32[4,4,32,128]{3,2,1,0:T(8,128)S(1)} collective-permute-done((f32[4,4,32,128]{3,2,1,0:T(8,128)S(1)}, f32[4,4,32,128]{3,2,1,0:T(8,128)S(1)}, u32[]{:S(2)}, u32[]{:S(2)}) %collective-permute-start.8) | collective-permute-done | bytes 262176 | tf_op jit(solution)/shard_map/ppermute | solution.py:52
  65.8 0.0 copy-done.5
  65.8 1.1 %shard_map.123 = bf16[128,1152]{1,0:T(8,128)(2,1)S(1)} custom-call(s32[6]{0:T(128)S(1)} %stack.15.place, s32[4,16]{1,0:T(4,128)S(1)} %bitcast.23, bf16[256,128]{1,0:T(8,128)(2,1)S(1)} %get-tuple-element.32.select, s32[128,128]{1,0:T(8,128)S(1)} %get-tuple-element.33.lengths, f32[4,4,32,128]{3,2,1,0:T(8,128)S(1)} %shard_map.119.slab0, ...), custom_call_target="tpu_custom_call" | custom-call | tf_op jit(solution)/shard_map/pallas_call | solution.py:485
  66.8 34.8 %all_to_all.5 = bf16[16,8,1152]{2,1,0:T(8,128)(2,1)S(1)} all-to-all(bf16[16,8,1152]{2,1,0:T(8,128)(2,1)S(1)} %bitcast.11), channel_id=1, replica_groups=mesh['depth'=4,'row'=8,'col'=16] {'col'}, dimensions={0} | all-to-all | bytes 589824 | tf_op jit(solution)/shard_map/all_to_all | solution.py:491
  101.6 1.9 %shard_map.124 = f32[512,128]{1,0:T(8,128)} custom-call(bf16[128,1152]{1,0:T(8,128)(2,1)S(1)} %bitcast.12, bf16[4,128,128]{2,1,0:T(8,128)(2,1)S(1)} %get-tuple-element.35.warp), custom_call_target="tpu_custom_call" | custom-call | tf_op jit(solution)/shard_map/pallas_call | solution.py:498
Async XLA Ops:
  1.7 7.1 %collective-permute-start = (bf16[4,3,32,128]{3,2,1,0:T(8,128)(2,1)S(1)}, bf16[4,3,32,128]{3,2,1,0:T(8,128)(2,1)S(1)}, u32[]{:S(2)}, u32[]{:S(2)}) collective-permute-start(bf16[4,3,32,128]{3,2,1,0:T(8,128)(2,1)S(1)} %get-tuple-element.19), channel_id=1, source_target_pairs={{0,128},{128,256},{256,384},{1,129},{129,257},{257,385},{2,130},{1... | collective-permute-start | bytes 294920 | tf_op jit(solution)/shard_map/ppermute | solution.py:57
  5.1 8.5 %copy-start.3 = (s32[4,1,32,1]{2,3,1,0:T(1,128)S(1)}, s32[4,1,32,1]{2,3,1,0:T(1,128)}, u32[]{:S(2)}) copy-start(s32[4,1,32,1]{2,3,1,0:T(1,128)} %param.18) | copy-start | bytes 1540
  5.1 8.4 %copy-start.4 = (s32[4,1,32]{2,1,0:T(1,128)S(1)}, s32[4,1,32]{2,1,0:T(1,128)}, u32[]{:S(2)}) copy-start(s32[4,1,32]{2,1,0:T(1,128)} %param.17) | copy-start | bytes 1540
  5.1 6.5 %collective-permute-start.1 = (bf16[4,3,32,128]{3,2,1,0:T(8,128)(2,1)S(1)}, bf16[4,3,32,128]{3,2,1,0:T(8,128)(2,1)S(1)}, u32[]{:S(2)}, u32[]{:S(2)}) collective-permute-start(bf16[4,3,32,128]{3,2,1,0:T(8,128)(2,1)S(1)} %get-tuple-element.20), channel_id=1, source_target_pairs={{128,0},{256,128},{384,256},{129,1},{257,129},{385,257},{130,2},{2... | collective-permute-start | bytes 294920 | tf_op jit(solution)/shard_map/ppermute | solution.py:62
  11.7 3.8 %collective-permute-start.2 = (bf16[3,96,128]{2,1,0:T(8,128)(2,1)S(1)}, bf16[3,96,128]{2,1,0:T(8,128)(2,1)S(1)}, u32[]{:S(2)}, u32[]{:S(2)}) collective-permute-start(bf16[3,96,128]{2,1,0:T(8,128)(2,1)S(1)} %get-tuple-element.26), channel_id=1, source_target_pairs={{0,16},{16,32},{32,48},{48,64},{64,80},{80,96},{96,112},{112,0},{1... | collective-permute-start | bytes 221192 | tf_op jit(solution)/shard_map/ppermute | solution.py:52
  11.7 3.8 %collective-permute-start.3 = (bf16[3,96,128]{2,1,0:T(8,128)(2,1)S(1)}, bf16[3,96,128]{2,1,0:T(8,128)(2,1)S(1)}, u32[]{:S(2)}, u32[]{:S(2)}) collective-permute-start(bf16[3,96,128]{2,1,0:T(8,128)(2,1)S(1)} %get-tuple-element.27), channel_id=1, source_target_pairs={{0,112},{16,0},{32,16},{48,32},{64,48},{80,64},{96,80},{112,96},{1... | collective-permute-start | bytes 221192 | tf_op jit(solution)/shard_map/ppermute | solution.py:52
  15.0 23.3 %copy-start = (f32[16,4,2]{0,2,1:T(2,128)S(1)}, f32[16,4,2]{0,2,1:T(2,128)}, u32[]{:S(2)}) copy-start(f32[16,4,2]{0,2,1:T(2,128)} %param.14) | copy-start | bytes 1540
  15.0 23.3 %copy-start.1 = (f32[16,4]{0,1:T(4,128)S(1)}, f32[16,4]{0,1:T(4,128)}, u32[]{:S(2)}) copy-start(f32[16,4]{0,1:T(4,128)} %param.15) | copy-start | bytes 772
  15.1 23.3 %copy-start.2 = (f32[16]{0:T(128)S(1)}, f32[16]{0:T(128)}, u32[]{:S(2)}) copy-start(f32[16]{0:T(128)} %shear.7) | copy-start | bytes 196
  16.6 5.8 %collective-permute-start.4 = (bf16[8,3840]{1,0:T(8,128)(2,1)S(1)}, bf16[8,3840]{1,0:T(8,128)(2,1)S(1)}, u32[]{:S(2)}, u32[]{:S(2)}) collective-permute-start(bf16[8,3840]{1,0:T(8,128)(2,1)S(1)} %get-tuple-element.29), channel_id=1, source_target_pairs={{0,1},{1,2},{2,3},{3,4},{4,5},{5,6},{6,7},{7,8},{8,9},{9,10},{10,1... | collective-permute-start | bytes 184328 | tf_op jit(solution)/shard_map/ppermute | solution.py:57
  20.4 6.4 %collective-permute-start.5 = (bf16[8,3840]{1,0:T(8,128)(2,1)S(1)}, bf16[8,3840]{1,0:T(8,128)(2,1)S(1)}, u32[]{:S(2)}, u32[]{:S(2)}) collective-permute-start(bf16[8,3840]{1,0:T(8,128)(2,1)S(1)} %get-tuple-element.30), channel_id=1, source_target_pairs={{1,0},{2,1},{3,2},{4,3},{5,4},{6,5},{7,6},{8,7},{9,8},{10,9},{11,1... | collective-permute-start | bytes 184328 | tf_op jit(solution)/shard_map/ppermute | solution.py:62
  45.5 20.2 %copy-start.5 = (s32[16,4]{0,1:T(4,128)S(1)}, s32[16,4]{0,1:T(4,128)}, u32[]{:S(2)}) copy-start(s32[16,4]{0,1:T(4,128)} %param.16) | copy-start | bytes 772
  45.6 11.4 %collective-permute-start.6 = (f32[4,4,32,128]{3,2,1,0:T(8,128)S(1)}, f32[4,4,32,128]{3,2,1,0:T(8,128)S(1)}, u32[]{:S(2)}, u32[]{:S(2)}) collective-permute-start(f32[4,4,32,128]{3,2,1,0:T(8,128)S(1)} %shard_map.120), channel_id=1, source_target_pairs={{0,128},{128,256},{256,384},{384,0},{1,129},{129,257},{257,385},{3... | collective-permute-start | bytes 786440 | tf_op jit(solution)/shard_map/ppermute | solution.py:52
  48.7 12.6 %collective-permute-start.7 = (f32[4,4,32,128]{3,2,1,0:T(8,128)S(1)}, f32[4,4,32,128]{3,2,1,0:T(8,128)S(1)}, u32[]{:S(2)}, u32[]{:S(2)}) collective-permute-start(f32[4,4,32,128]{3,2,1,0:T(8,128)S(1)} %shard_map.121), channel_id=1, source_target_pairs={{0,256},{128,384},{256,0},{384,128},{1,257},{129,385},{257,1},{385... | collective-permute-start | bytes 786440 | tf_op jit(solution)/shard_map/ppermute | solution.py:52
  52.0 13.8 %collective-permute-start.8 = (f32[4,4,32,128]{3,2,1,0:T(8,128)S(1)}, f32[4,4,32,128]{3,2,1,0:T(8,128)S(1)}, u32[]{:S(2)}, u32[]{:S(2)}) collective-permute-start(f32[4,4,32,128]{3,2,1,0:T(8,128)S(1)} %shard_map.122), channel_id=1, source_target_pairs={{0,384},{128,0},{256,128},{384,256},{1,385},{129,1},{257,129},{385... | collective-permute-start | bytes 786440 | tf_op jit(solution)/shard_map/ppermute | solution.py:52

commit v4 on v3

--- a/solution.py
+++ b/solution.py
@@ -19,6 +19,7 @@
 EDGE = 8
 PLANES = 24
 ROWS = 40
+LINES = 1024
 SHIFTS = 2 * RIM + 1
 CAPACITY = 4
 
@@ -112,7 +113,7 @@
 def column_picker():
     j = lax.broadcasted_iota(jnp.int32, (2 * EDGE, 128), 0)
     lane = lax.broadcasted_iota(jnp.int32, (2 * EDGE, 128), 1)
-    return (lane == jnp.where(j < EDGE, j, 128 - 2 * EDGE + j)).astype(BF16)
+    return (lane == jnp.where(j < EDGE, j, 128 - 2 * EDGE + j)).astype(F32)
 
 
 def pack_columns(place, unused, above, below, brick, low, high):
@@ -122,99 +123,64 @@
     for r in range(HALO):
         lines[pl.ds(ROWS - HALO + r, 4 * PLANES, stride=ROWS), :] = has_above * above[r].astype(F32)
         lines[pl.ds(32 + r, 4 * PLANES, stride=ROWS), :] = has_below * below[r].astype(F32)
-    pick = column_picker()
+    pick = column_picker().astype(BF16)
     count = PLANES * ROWS
     for f in range(4):
         rows = brick[f].reshape(count, 128).astype(BF16)
         edge = lax.dot_general(pick, rows, NT, preferred_element_type=F32).astype(BF16)
-        low[:, f * count : (f + 1) * count] = edge[:EDGE]
-        high[:, f * count : (f + 1) * count] = edge[EDGE:]
-
-
-def stencil(
-    place,
-    main,
-    left,
-    right,
-    out,
-    shifted,
-    rim,
-    first_main,
-    first_rim,
-    second_main,
-    second_rim,
-):
+        at = f * LINES
+        low[:, at : at + count] = edge[:EDGE]
+        high[:, at : at + count] = edge[EDGE:]
+        low[:, at + count : at + LINES] = jnp.zeros((EDGE, LINES - count), BF16)
+        high[:, at + count : at + LINES] = jnp.zeros((EDGE, LINES - count), BF16)
+
+
+def slope_of(fields, diffusivity, reaction, neighbours):
+    fuel, heat = fields
+    square = heat * heat
+    burned = reaction * fuel * square / (1.0 + square)
+    slopes = []
+    for f in range(2):
+        centre = fields[f]
+        below_depth, above_depth, below_row, above_row, below_col, above_col = neighbours(f)
+        laplace = (
+            below_depth + above_depth + below_row + above_row + below_col + above_col - 6.0 * centre
+        )
+        advect = (
+            VEL_DEPTH * (centre - below_depth)
+            + VEL_ROW * (centre - below_row)
+            + VEL_COL * (centre - below_col)
+        )
+        gain = -burned if f == 0 else burned
+        slopes.append(diffusivity * laplace - advect + gain)
+    return slopes
+
+
+def advance_own(place, brick, shifted, edges, first, second):
     n = ROWS
-    j = lax.broadcasted_iota(jnp.int32, (EDGE, 128), 0)
-    lane8 = lax.broadcasted_iota(jnp.int32, (EDGE, 128), 1)
-    reach = HALO + RIM
-    put_left = ((lane8 == 128 - EDGE + j) & (j >= EDGE - reach)).astype(BF16)
-    put_right = ((lane8 == j) & (j < reach)).astype(BF16)
-    count = PLANES * ROWS
-    for f in range(4):
-        cut = slice(f * count, (f + 1) * count)
-        spread = lax.dot_general(
-            left[:, cut], put_left, TN, preferred_element_type=F32
-        ) + lax.dot_general(right[:, cut], put_right, TN, preferred_element_type=F32)
-        rim[f] = spread.reshape(PLANES, ROWS, 128)
-
-    depth_at, row_at, col_at = place[0], place[1], place[2]
-    depth_last, row_last, col_last = place[3], place[4], place[5]
+    depth_at, row_at = place[0], place[1]
+    depth_last, row_last = place[3], place[4]
     row = lax.broadcasted_iota(jnp.int32, (n, 128), 0)
-    lane = lax.broadcasted_iota(jnp.int32, (n, 128), 1)
     rows_in = (
         (row < 32)
         | ((row < 32 + HALO) & (row_at < row_last))
         | ((row >= n - HALO) & (row_at > 0))
     )
-    lanes_in = ((lane < reach) & (col_at < col_last)) | ((lane >= 128 - reach) & (col_at > 0))
-    step_main = jnp.where(rows_in, TIME_STEP, 0.0).astype(F32)
-    step_rim = jnp.where(rows_in & lanes_in, TIME_STEP, 0.0).astype(F32)
-    first_lane = lane == 0
-    last_lane = lane == 127
-
-    def tendency(m, r, p):
-        results = []
-        for part in range(2):
-            here, there = (m, r) if part == 0 else (r, m)
-            coefs = main if part == 0 else rim
-            diffusivity = coefs[2, p]
-            reaction = coefs[3, p]
-            fuel, heat = here[0, p], here[1, p]
-            square = heat * heat
-            burned = reaction * fuel * square / (1.0 + square)
-            both = []
-            for f in range(2):
-                centre = fuel if f == 0 else heat
-                other = there[f, p]
-                below_depth = here[f, p - 1]
-                above_depth = here[f, p + 1]
-                below_row = pltpu.roll(centre, 1, 0)
-                above_row = pltpu.roll(centre, n - 1, 0)
-                below_col = jnp.where(
-                    first_lane, pltpu.roll(other, 1, 1), pltpu.roll(centre, 1, 1)
-                )
-                above_col = jnp.where(
-                    last_lane, pltpu.roll(other, 127, 1), pltpu.roll(centre, 127, 1)
-                )
-                laplace = (
-                    below_depth
-                    + above_depth
-                    + below_row
-                    + above_row
-                    + below_col
-                    + above_col
-                    - 6.0 * centre
-                )
-                advect = (
-                    VEL_DEPTH * (centre - below_depth)
-                    + VEL_ROW * (centre - below_row)
-                    + VEL_COL * (centre - below_col)
-                )
-                gain = -burned if f == 0 else burned
-                both.append(diffusivity * laplace - advect + gain)
-            results.append(both)
-        return results
+    step = jnp.where(rows_in, TIME_STEP, 0.0).astype(F32)
+
+    def tendency(source, p):
+        def neighbours(f):
+            centre = source[f, p]
+            return (
+                source[f, p - 1],
+                source[f, p + 1],
+                pltpu.roll(centre, 1, 0),
+                pltpu.roll(centre, n - 1, 0),
+                pltpu.roll(centre, 1, 1),
+                pltpu.roll(centre, 127, 1),
+            )
+
+        return slope_of((source[0, p], source[1, p]), brick[2, p], brick[3, p], neighbours)
 
     def inside(p):
         ok = ((p >= HALO) | (depth_at > 0)) & ((p < HALO + 16) | (depth_at < depth_last))
@@ -222,47 +188,116 @@
 
     @pl.loop(1, 21)
     def _(p):
-        slope = tendency(main, rim, p)
+        slope = tendency(brick, p)
         scale = inside(p)
         for f in range(2):
-            first_main[f, p] = main[f, p] + (step_main * scale) * slope[0][f]
-            first_rim[f, p] = rim[f, p] + (step_rim * scale) * slope[1][f]
+            first[f, p] = brick[f, p] + (step * scale) * slope[f]
 
     @pl.loop(2, 20)
     def _(p):
-        slope = tendency(first_main, first_rim, p)
+        slope = tendency(first, p)
         scale = inside(p)
         for f in range(2):
-            second_main[f, p] = 0.75 * main[f, p] + 0.25 * (
-                first_main[f, p] + (step_main * scale) * slope[0][f]
-            )
-            second_rim[f, p] = 0.75 * rim[f, p] + 0.25 * (
-                first_rim[f, p] + (step_rim * scale) * slope[1][f]
-            )
-
-    lane32 = lax.broadcasted_iota(jnp.int32, (32, 128), 1)
+            second[f, p] = 0.75 * brick[f, p] + 0.25 * (first[f, p] + (step * scale) * slope[f])
 
     @pl.loop(3, 19)
     def _(p):
-        slope = tendency(second_main, second_rim, p)
+        slope = tendency(second, p)
         k = p - HALO
         for f in range(2):
-            new_main = (
-                main[f, p] / 3.0 + (2.0 / 3.0) * (second_main[f, p] + step_main * slope[0][f])
-            )[:32]
-            new_rim = (
-                rim[f, p] / 3.0 + (2.0 / 3.0) * (second_rim[f, p] + step_rim * slope[1][f])
-            )[:32]
-            out[f, k] = new_main
+            new = (brick[f, p] / 3.0 + (2.0 / 3.0) * (second[f, p] + step * slope[f]))[:32]
             for shift in range(-RIM, RIM + 1):
+                shifted[shift + RIM, f, k] = pltpu.roll(new, -shift % 128, 1) if shift else new
+
+    pick = column_picker()
+    count = PLANES * ROWS
+    for f in range(2):
+        edges[:, f * LINES : f * LINES + count] = lax.dot_general(
+            pick,
+            brick[f].reshape(count, 128),
+            NT,
+            preferred_element_type=F32,
+            precision=lax.Precision.HIGHEST,
+        )
+        edges[:, f * LINES + count : (f + 1) * LINES] = jnp.zeros((2 * EDGE, LINES - count), F32)
+
+
+def advance_edges(place, unused, edges, low, high, left, right, shifted, out, turned):
+    row_at, col_at, depth_at = place[1], place[2], place[0]
+    depth_last, row_last, col_last = place[3], place[4], place[5]
+    shape = (4 * EDGE, LINES)
+    col = lax.broadcasted_iota(jnp.int32, shape, 0)
+    lane = lax.broadcasted_iota(jnp.int32, shape, 1)
+    plane = jnp.floor((lane.astype(F32) + 0.5) * (1.0 / ROWS)).astype(jnp.int32)
+    row = lane - plane * ROWS
+    rows_in = (
+        (row < 32)
+        | ((row < 32 + HALO) & (row_at < row_last))
+        | ((row >= ROWS - HALO) & (row_at > 0))
+    )
+    cols_in = ((col >= EDGE) | (col_at > 0)) & ((col < 3 * EDGE) | (col_at < col_last))
+    planes_in = ((plane >= HALO) | (depth_at > 0)) & (
+        (plane < HALO + 16) | ((plane < 22) & (depth_at < depth_last))
+    )
+    step = jnp.where(rows_in & cols_in & planes_in, TIME_STEP, 0.0).astype(F32)
+    first_row, last_row = row == 0, row == ROWS - 1
+
+    def gather(f):
+        cut = slice(f * LINES, (f + 1) * LINES)
+        if f < 2:
+            own = (edges[0:EDGE, cut], edges[EDGE : 2 * EDGE, cut])
+        else:
+            own = (low[:, cut].astype(F32), high[:, cut].astype(F32))
+        return jnp.concatenate(
+            [left[:, cut].astype(F32), own[0], own[1], right[:, cut].astype(F32)], axis=0
+        )
+
+    start = (gather(0), gather(1))
+    diffusivity, reaction = gather(2), gather(3)
+
+    def tendency(fields):
+        def neighbours(f):
+            x = fields[f]
+            return (
+                pltpu.roll(x, ROWS, 1),
+                pltpu.roll(x, LINES - ROWS, 1),
+                jnp.where(first_row, pltpu.roll(x, LINES - ROWS + 1, 1), pltpu.roll(x, 1, 1)),
+                jnp.where(last_row, pltpu.roll(x, ROWS - 1, 1), pltpu.roll(x, LINES - 1, 1)),
+                pltpu.roll(x, 1, 0),
+                pltpu.roll(x, 4 * EDGE - 1, 0),
+            )
+
+        return slope_of(fields, diffusivity, reaction, neighbours)
+
+    slope = tendency(start)
+    first = tuple(start[f] + step * slope[f] for f in range(2))
+    slope = tendency(first)
+    second = tuple(0.75 * start[f] + 0.25 * (first[f] + step * slope[f]) for f in range(2))
+    slope = tendency(second)
+    blank = jnp.zeros((128 - 4 * EDGE, 128), F32)
+    for f in range(2):
+        new = start[f] / 3.0 + (2.0 / 3.0) * (second[f] + step * slope[f])
+        for block in range(LINES // 128):
+            cut = slice(128 * block, 128 * (block + 1))
+            turned[f, cut, :] = jnp.concatenate([new[:, cut], blank], axis=0).T
+
+    lane = lax.broadcasted_iota(jnp.int32, (32, 128), 1)
+
+    @pl.loop(0, 16)
+    def _(k):
+        for f in range(2):
+            lines = turned[f, pl.ds(pl.multiple_of((k + HALO) * ROWS, 8), 32), :]
+            near = pltpu.roll(lines, 128 - EDGE, 1)
+            far = pltpu.roll(lines, 128 - 3 * EDGE, 1)
+            for shift in range(-RIM, RIM + 1):
+                from_far = (lane >= 64) & (lane < 128 + min(shift, 0)) | (lane < shift)
+                patch = jnp.where(from_far, far, near)
+                patch = pltpu.roll(patch, -shift % 128, 1) if shift else patch
+                wrong = (lane <= RIM - 1 - shift) | (lane >= 128 - RIM - shift)
+                value = jnp.where(wrong, patch, shifted[shift + RIM, f, k])
+                shifted[shift + RIM, f, k] = value
                 if shift == 0:
-                    shifted[RIM, f, k] = new_main
-                    continue
-                turn = -shift % 128
-                outside = lane32 >= 128 - shift if shift > 0 else lane32 < -shift
-                shifted[shift + RIM, f, k] = jnp.where(
-                    outside, pltpu.roll(new_rim, turn, 1), pltpu.roll(new_main, turn, 1)
-                )
+                    out[f, k] = value
 
 
 def render(away, place, shear, weight, bias, shifted, image):
@@ -455,22 +490,27 @@
     brick, select, lengths_wide, warp_own = lax.optimization_barrier(
         (brick, select, lengths_wide, warp_own)
     )
-    face = jax.ShapeDtypeStruct((EDGE, 4 * PLANES * ROWS), BF16)
+    face = jax.ShapeDtypeStruct((EDGE, 4 * LINES), BF16)
     brick, low, high = call(
         pack_columns, (brick_type, face, face), [SMEM_SPEC] + [VMEM_SPEC] * 3, aliases={1: 0}
     )(place, brick, above, below)
-    left, right = shift_up(high, "col"), shift_down(low, "col")
+    left = shift_up(high, "col")
+    right = shift_down(low, "col")
     wide = pltpu.VMEM((2, PLANES, ROWS, 128), F32)
-    species_out, shifted = call(
-        stencil,
-        (
-            jax.ShapeDtypeStruct(species.shape, F32),
-            jax.ShapeDtypeStruct((SHIFTS,) + species.shape, F32),
-        ),
-        [SMEM_SPEC] + [VMEM_SPEC] * 3,
-        [pltpu.VMEM((4, PLANES, ROWS, 128), F32)] + [wide] * 4,
-        limit=16,
-    )(place, brick, left, right)
+    shifted_type = jax.ShapeDtypeStruct((SHIFTS,) + species.shape, F32)
+    shifted, edges = call(
+        advance_own,
+        (shifted_type, jax.ShapeDtypeStruct((2 * EDGE, 2 * LINES), F32)),
+        [SMEM_SPEC, VMEM_SPEC],
+        [wide, wide],
+    )(place, brick)
+    shifted, species_out = call(
+        advance_edges,
+        (shifted_type, jax.ShapeDtypeStruct(species.shape, F32)),
+        [SMEM_SPEC] + [VMEM_SPEC] * 6,
+        [pltpu.VMEM((2, LINES, 128), F32)],
+        aliases={1: 0},
+    )(place, shifted, edges, low, high, left, right)
 
     image = jax.ShapeDtypeStruct((view_count, 4, 32, 128), F32)
     weight, bias = jnp.transpose(colour_weight, (1, 2, 0)), colour_bias.T

time: 104 us -> 104 us (level)
  the two profiles are of different devices: /device:TPU:18 before, /device:TPU:6 now
where the time goes in v4:
time: 104 us; the launch traced here: 102 us
  blocking collectives  33.6 us (32%)
  Pallas kernels  32.3 us (31%)
  starting transfers between devices  26.8 us (26%)
  waiting for transfers between devices  8.78 us (8%)
    all_to_all x1, blocking collectives, body(): lax.all_to_all(outgoing.reshape(col_devices, -1, 1152), 'col', split_axis...  33.6 us
    ppermute x5, starting transfers between devices, turn_by(): return lax.ppermute(x, axis, [(i, (i + steps) % n) for i in range(n)])  15.1 us
    pallas_call x4, Pallas kernels, body(): call(functools.partial(render, away), image, [SMEM_SPEC] * 4 + [VMEM_SPEC])  9.66 us
    pallas_call x1, Pallas kernels, body(): call(advance_own, (shifted_type, jax.ShapeDtypeStruct((2 * EDGE, 2 * LINE...  8.55 us
    ppermute x5, waiting for transfers between devices, turn_by(): return lax.ppermute(x, axis, [(i, (i + steps) % n) for i in range(n)])  7.82 us
    pallas_call x1, Pallas kernels, body(): call(advance_edges, (shifted_type, jax.ShapeDtypeStruct(species.shape, F3...  6.27 us
    ppermute x2, starting transfers between devices, shift_down(): return lax.ppermute(x, axis, [(i + 1, i) for i in range(n - 1)])  5.85 us
    ppermute x2, starting transfers between devices, shift_up(): return lax.ppermute(x, axis, [(i, i + 1) for i in range(n - 1)])  5.84 us
  transfers between devices with their start and end apart: 9, of which 5 were waited for; matrix products, arithmetic and copies ran while one was open for 0% of the time, Pallas kernels for 13%

profile of v4, /device:TPU:6, one launch (start us, length us, event | category | flops | bytes accessed | tf_op | source)
XLA Modules:
  0.0 102.4 jit_solution(8295470346839333201)
XLA Ops:
  0.6 1.1 %shard_map.114 = (bf16[4,3,32,128]{3,2,1,0:T(8,128)(2,1)S(1)}, bf16[4,3,32,128]{3,2,1,0:T(8,128)(2,1)S(1)}) custom-call(f32[2,16,32,128]{3,2,1,0:T(8,128)} %species.3, f32[16,32,128]{2,1,0:T(8,128)} %diff.3, f32[16,32,128]{2,1,0:T(8,128)} %rate.3), custom_call_target="tpu_custom_call" | custom-call | tf_op jit(solution)/shard_map/pallas_call | solution.py:463
  1.7 1.3 %collective-permute-start = (bf16[4,3,32,128]{3,2,1,0:T(8,128)(2,1)S(1)}, bf16[4,3,32,128]{3,2,1,0:T(8,128)(2,1)S(1)}, u32[]{:S(2)}, u32[]{:S(2)}) collective-permute-start(bf16[4,3,32,128]{3,2,1,0:T(8,128)(2,1)S(1)} %get-tuple-element.21), channel_id=1, source_target_pairs={{0,128},{128,256},{256,384},{1,129},{129,257},{257,385},{2,130},{1... | collective-permute-start | bytes 294920 | tf_op jit(solution)/shard_map/ppermute | solution.py:58
  3.0 0.0 copy-start.3
  3.0 0.0 copy-start.4
  3.0 4.6 %collective-permute-start.1 = (bf16[4,3,32,128]{3,2,1,0:T(8,128)(2,1)S(1)}, bf16[4,3,32,128]{3,2,1,0:T(8,128)(2,1)S(1)}, u32[]{:S(2)}, u32[]{:S(2)}) collective-permute-start(bf16[4,3,32,128]{3,2,1,0:T(8,128)(2,1)S(1)} %get-tuple-element.22), channel_id=1, source_target_pairs={{128,0},{256,128},{384,256},{129,1},{257,129},{385,257},{130,2},{2... | collective-permute-start | bytes 294920 | tf_op jit(solution)/shard_map/ppermute | solution.py:63
  7.6 1.2 %shard_map.113.unused = f32[4,24,40,128]{3,2,1,0:T(8,128)S(1)} custom-call(f32[2,16,32,128]{3,2,1,0:T(8,128)} %species.3, f32[16,32,128]{2,1,0:T(8,128)} %diff.3, f32[16,32,128]{2,1,0:T(8,128)} %rate.3), custom_call_target="tpu_custom_call" | custom-call | tf_op jit(solution)/shard_map/pallas_call | solution.py:471
  8.8 0.0 collective-permute-done.before
  8.8 0.9 collective-permute-done.1.after
  9.8 0.1 shard_map.115
  9.8 0.0 collective-permute-start.2
  9.9 2.9 %collective-permute-start.3 = (bf16[3,96,128]{2,1,0:T(8,128)(2,1)S(1)}, bf16[3,96,128]{2,1,0:T(8,128)(2,1)S(1)}, u32[]{:S(2)}, u32[]{:S(2)}) collective-permute-start(bf16[3,96,128]{2,1,0:T(8,128)(2,1)S(1)} %get-tuple-element.29), channel_id=1, source_target_pairs={{0,112},{16,0},{32,16},{48,32},{64,48},{80,64},{96,80},{112,96},{1... | collective-permute-start | bytes 221192 | tf_op jit(solution)/shard_map/ppermute | solution.py:53
  12.8 0.1 stack.15.place
  12.9 0.0 copy-done.3
  12.9 0.0 copy-done.4
  12.9 1.5 %shard_map.116 = (bf16[256,128]{1,0:T(8,128)(2,1)S(1)}, s32[128,128]{1,0:T(8,128)S(1)}, bf16[4,128,128]{2,1,0:T(8,128)(2,1)S(1)}) custom-call(s32[6]{0:T(128)S(1)} %stack.15.place, s32[4,32]{1,0:T(4,128)S(1)} %bitcast.21, s32[4,32]{1,0:T(4,128)S(1)} %bitcast.22, bf16[16,128,128]{2,1,0:T(8,128)(2,1)} %warp.1), custom_call_target="tpu_custom_call" | custom-call | tf_op jit(solution)/shard_map/pallas_call | solution.py:479
  14.4 0.5 collective-permute-done.2.above
  14.8 0.0 collective-permute-done.3.below
  14.8 1.0 shard_map.117
  15.8 1.3 %collective-permute-start.5 = (bf16[8,4096]{1,0:T(8,128)(2,1)S(1)}, bf16[8,4096]{1,0:T(8,128)(2,1)S(1)}, u32[]{:S(2)}, u32[]{:S(2)}) collective-permute-start(bf16[8,4096]{1,0:T(8,128)(2,1)S(1)} %get-tuple-element.33.low), channel_id=1, source_target_pairs={{1,0},{2,1},{3,2},{4,3},{5,4},{6,5},{7,6},{8,7},{9,8},{10,9},{11,1... | collective-permute-start | bytes 196616 | tf_op jit(solution)/shard_map/ppermute | solution.py:63
  17.1 4.5 %collective-permute-start.4 = (bf16[8,4096]{1,0:T(8,128)(2,1)S(1)}, bf16[8,4096]{1,0:T(8,128)(2,1)S(1)}, u32[]{:S(2)}, u32[]{:S(2)}) collective-permute-start(bf16[8,4096]{1,0:T(8,128)(2,1)S(1)} %get-tuple-element.34.high), channel_id=1, source_target_pairs={{0,1},{1,2},{2,3},{3,4},{4,5},{5,6},{6,7},{7,8},{8,9},{9,10},{10,1... | collective-permute-start | bytes 196616 | tf_op jit(solution)/shard_map/ppermute | solution.py:58
  21.7 8.5 %shard_map.118 = (f32[7,2,16,32,128]{4,3,2,1,0:T(8,128)S(1)}, f32[16,2048]{1,0:T(8,128)S(1)}) custom-call(s32[6]{0:T(128)S(1)} %stack.15.place, f32[4,24,40,128]{3,2,1,0:T(8,128)S(1)} %get-tuple-element.30.brick), custom_call_target="tpu_custom_call" | custom-call | tf_op jit(solution)/shard_map/pallas_call | solution.py:501
  30.2 0.0 collective-permute-done.5.right
  30.3 0.0 collective-permute-done.4.left
  30.3 0.0 copy-start
  30.3 0.0 copy-start.1
  30.3 0.0 copy-start.2
  30.3 6.3 %shard_map.119 = (f32[7,2,16,32,128]{4,3,2,1,0:T(8,128)S(1)}, f32[2,16,32,128]{3,2,1,0:T(8,128)}) custom-call(s32[6]{0:T(128)S(1)} %stack.15.place, f32[7,2,16,32,128]{4,3,2,1,0:T(8,128)S(1)} %get-tuple-element.31.unused, f32[16,2048]{1,0:T(8,128)S(1)} %get-tuple-element.32.edges, ...), custom_call_target="tpu_custom_call", output_to_operand_aliasing={{0}: (1, {})} | custom-call | tf_op jit(solution)/shard_map/pallas_call | solution.py:507
  36.6 0.0 copy-done
  36.6 0.0 copy-done.1
  36.6 0.0 copy-done.2
  36.6 2.4 %shard_map.123 = f32[4,4,32,128]{3,2,1,0:T(8,128)S(1)} custom-call(s32[6]{0:T(128)S(1)} %stack.15.place, f32[16]{0:T(128)S(1)} %copy-done.2, f32[4,2,16]{2,1,0:T(2,128)S(1)} %bitcast.13, f32[4,16]{1,0:T(4,128)S(1)} %bitcast.17, f32[7,2,16,32,128]{4,3,2,1,0:T(8,128)S(1)} %get-tuple-element.38.shifted), custom_call_target="tpu_custom_call" | custom-call | tf_op jit(solution)/shard_map/pallas_call | solution.py:519
  39.0 2.4 %shard_map.122 = f32[4,4,32,128]{3,2,1,0:T(8,128)S(1)} custom-call(s32[6]{0:T(128)S(1)} %stack.15.place, f32[16]{0:T(128)S(1)} %copy-done.2, f32[4,2,16]{2,1,0:T(2,128)S(1)} %bitcast.14, f32[4,16]{1,0:T(4,128)S(1)} %bitcast.18, f32[7,2,16,32,128]{4,3,2,1,0:T(8,128)S(1)} %get-tuple-element.38.shifted), custom_call_target="tpu_custom_call" | custom-call | tf_op jit(solution)/shard_map/pallas_call | solution.py:519
  41.4 2.4 %shard_map.121 = f32[4,4,32,128]{3,2,1,0:T(8,128)S(1)} custom-call(s32[6]{0:T(128)S(1)} %stack.15.place, f32[16]{0:T(128)S(1)} %copy-done.2, f32[4,2,16]{2,1,0:T(2,128)S(1)} %bitcast.15, f32[4,16]{1,0:T(4,128)S(1)} %bitcast.19, f32[7,2,16,32,128]{4,3,2,1,0:T(8,128)S(1)} %get-tuple-element.38.shifted), custom_call_target="tpu_custom_call" | custom-call | tf_op jit(solution)/shard_map/pallas_call | solution.py:519
  43.8 0.0 copy-start.5
  43.9 7.5 %collective-permute-start.6 = (f32[4,4,32,128]{3,2,1,0:T(8,128)S(1)}, f32[4,4,32,128]{3,2,1,0:T(8,128)S(1)}, u32[]{:S(2)}, u32[]{:S(2)}) collective-permute-start(f32[4,4,32,128]{3,2,1,0:T(8,128)S(1)} %shard_map.121), channel_id=1, source_target_pairs={{0,128},{128,256},{256,384},{384,0},{1,129},{129,257},{257,385},{3... | collective-permute-start | bytes 786440 | tf_op jit(solution)/shard_map/ppermute | solution.py:53
  51.4 1.9 %collective-permute-start.7 = (f32[4,4,32,128]{3,2,1,0:T(8,128)S(1)}, f32[4,4,32,128]{3,2,1,0:T(8,128)S(1)}, u32[]{:S(2)}, u32[]{:S(2)}) collective-permute-start(f32[4,4,32,128]{3,2,1,0:T(8,128)S(1)} %shard_map.122), channel_id=1, source_target_pairs={{0,256},{128,384},{256,0},{384,128},{1,257},{129,385},{257,1},{385... | collective-permute-start | bytes 786440 | tf_op jit(solution)/shard_map/ppermute | solution.py:53
  53.3 2.8 %collective-permute-start.8 = (f32[4,4,32,128]{3,2,1,0:T(8,128)S(1)}, f32[4,4,32,128]{3,2,1,0:T(8,128)S(1)}, u32[]{:S(2)}, u32[]{:S(2)}) collective-permute-start(f32[4,4,32,128]{3,2,1,0:T(8,128)S(1)} %shard_map.123), channel_id=1, source_target_pairs={{0,384},{128,0},{256,128},{384,256},{1,385},{129,1},{257,129},{385... | collective-permute-start | bytes 786440 | tf_op jit(solution)/shard_map/ppermute | solution.py:53
  56.1 2.4 %shard_map.120.slab0 = f32[4,4,32,128]{3,2,1,0:T(8,128)S(1)} custom-call(s32[6]{0:T(128)S(1)} %stack.15.place, f32[16]{0:T(128)S(1)} %copy-done.2, f32[4,2,16]{2,1,0:T(2,128)S(1)} %bitcast.16, f32[4,16]{1,0:T(4,128)S(1)} %bitcast.20, f32[7,2,16,32,128]{4,3,2,1,0:T(8,128)S(1)} %get-tuple-element.38.shifted), custom_call_target="tpu_custom_call" | custom-call | tf_op jit(solution)/shard_map/pallas_call | solution.py:519
  58.5 2.4 %collective-permute-done.6.slab1 = f32[4,4,32,128]{3,2,1,0:T(8,128)S(1)} collective-permute-done((f32[4,4,32,128]{3,2,1,0:T(8,128)S(1)}, f32[4,4,32,128]{3,2,1,0:T(8,128)S(1)}, u32[]{:S(2)}, u32[]{:S(2)}) %collective-permute-start.6) | collective-permute-done | bytes 262176 | tf_op jit(solution)/shard_map/ppermute | solution.py:53
  60.9 1.6 %collective-permute-done.7.slab2 = f32[4,4,32,128]{3,2,1,0:T(8,128)S(1)} collective-permute-done((f32[4,4,32,128]{3,2,1,0:T(8,128)S(1)}, f32[4,4,32,128]{3,2,1,0:T(8,128)S(1)}, u32[]{:S(2)}, u32[]{:S(2)}) %collective-permute-start.7) | collective-permute-done | bytes 262176 | tf_op jit(solution)/shard_map/ppermute | solution.py:53
  62.5 3.4 %collective-permute-done.8.slab3 = f32[4,4,32,128]{3,2,1,0:T(8,128)S(1)} collective-permute-done((f32[4,4,32,128]{3,2,1,0:T(8,128)S(1)}, f32[4,4,32,128]{3,2,1,0:T(8,128)S(1)}, u32[]{:S(2)}, u32[]{:S(2)}) %collective-permute-start.8) | collective-permute-done | bytes 262176 | tf_op jit(solution)/shard_map/ppermute | solution.py:53
  65.8 0.0 copy-done.5
  65.8 1.1 %shard_map.124 = bf16[128,1152]{1,0:T(8,128)(2,1)S(1)} custom-call(s32[6]{0:T(128)S(1)} %stack.15.place, s32[4,16]{1,0:T(4,128)S(1)} %bitcast.23, bf16[256,128]{1,0:T(8,128)(2,1)S(1)} %get-tuple-element.36.select, s32[128,128]{1,0:T(8,128)S(1)} %get-tuple-element.37.lengths, f32[4,4,32,128]{3,2,1,0:T(8,128)S(1)} %shard_map.120.slab0, ...), custom_call_target="tpu_custom_call" | custom-call | tf_op jit(solution)/shard_map/pallas_call | solution.py:525
  66.9 33.6 %all_to_all.5 = bf16[16,8,1152]{2,1,0:T(8,128)(2,1)S(1)} all-to-all(bf16[16,8,1152]{2,1,0:T(8,128)(2,1)S(1)} %bitcast.11), channel_id=1, replica_groups=mesh['depth'=4,'row'=8,'col'=16] {'col'}, dimensions={0} | all-to-all | bytes 589824 | tf_op jit(solution)/shard_map/all_to_all | solution.py:531
  100.5 1.9 %shard_map.125 = f32[512,128]{1,0:T(8,128)} custom-call(bf16[128,1152]{1,0:T(8,128)(2,1)S(1)} %bitcast.12, bf16[4,128,128]{2,1,0:T(8,128)(2,1)S(1)} %get-tuple-element.39.warp), custom_call_target="tpu_custom_call" | custom-call | tf_op jit(solution)/shard_map/pallas_call | solution.py:538
Async XLA Ops:
  1.7 7.1 %collective-permute-start = (bf16[4,3,32,128]{3,2,1,0:T(8,128)(2,1)S(1)}, bf16[4,3,32,128]{3,2,1,0:T(8,128)(2,1)S(1)}, u32[]{:S(2)}, u32[]{:S(2)}) collective-permute-start(bf16[4,3,32,128]{3,2,1,0:T(8,128)(2,1)S(1)} %get-tuple-element.21), channel_id=1, source_target_pairs={{0,128},{128,256},{256,384},{1,129},{129,257},{257,385},{2,130},{1... | collective-permute-start | bytes 294920 | tf_op jit(solution)/shard_map/ppermute | solution.py:58
  3.0 9.9 %copy-start.3 = (s32[4,1,32,1]{2,3,1,0:T(1,128)S(1)}, s32[4,1,32,1]{2,3,1,0:T(1,128)}, u32[]{:S(2)}) copy-start(s32[4,1,32,1]{2,3,1,0:T(1,128)} %param.18) | copy-start | bytes 1540
  3.0 9.9 %copy-start.4 = (s32[4,1,32]{2,1,0:T(1,128)S(1)}, s32[4,1,32]{2,1,0:T(1,128)}, u32[]{:S(2)}) copy-start(s32[4,1,32]{2,1,0:T(1,128)} %param.17) | copy-start | bytes 1540
  3.0 6.8 %collective-permute-start.1 = (bf16[4,3,32,128]{3,2,1,0:T(8,128)(2,1)S(1)}, bf16[4,3,32,128]{3,2,1,0:T(8,128)(2,1)S(1)}, u32[]{:S(2)}, u32[]{:S(2)}) collective-permute-start(bf16[4,3,32,128]{3,2,1,0:T(8,128)(2,1)S(1)} %get-tuple-element.22), channel_id=1, source_target_pairs={{128,0},{256,128},{384,256},{129,1},{257,129},{385,257},{130,2},{2... | collective-permute-start | bytes 294920 | tf_op jit(solution)/shard_map/ppermute | solution.py:63
  9.8 5.0 %collective-permute-start.2 = (bf16[3,96,128]{2,1,0:T(8,128)(2,1)S(1)}, bf16[3,96,128]{2,1,0:T(8,128)(2,1)S(1)}, u32[]{:S(2)}, u32[]{:S(2)}) collective-permute-start(bf16[3,96,128]{2,1,0:T(8,128)(2,1)S(1)} %get-tuple-element.28), channel_id=1, source_target_pairs={{0,16},{16,32},{32,48},{48,64},{64,80},{80,96},{96,112},{112,0},{1... | collective-permute-start | bytes 221192 | tf_op jit(solution)/shard_map/ppermute | solution.py:53
  9.9 5.0 %collective-permute-start.3 = (bf16[3,96,128]{2,1,0:T(8,128)(2,1)S(1)}, bf16[3,96,128]{2,1,0:T(8,128)(2,1)S(1)}, u32[]{:S(2)}, u32[]{:S(2)}) collective-permute-start(bf16[3,96,128]{2,1,0:T(8,128)(2,1)S(1)} %get-tuple-element.29), channel_id=1, source_target_pairs={{0,112},{16,0},{32,16},{48,32},{64,48},{80,64},{96,80},{112,96},{1... | collective-permute-start | bytes 221192 | tf_op jit(solution)/shard_map/ppermute | solution.py:53
  15.8 14.4 %collective-permute-start.5 = (bf16[8,4096]{1,0:T(8,128)(2,1)S(1)}, bf16[8,4096]{1,0:T(8,128)(2,1)S(1)}, u32[]{:S(2)}, u32[]{:S(2)}) collective-permute-start(bf16[8,4096]{1,0:T(8,128)(2,1)S(1)} %get-tuple-element.33.low), channel_id=1, source_target_pairs={{1,0},{2,1},{3,2},{4,3},{5,4},{6,5},{7,6},{8,7},{9,8},{10,9},{11,1... | collective-permute-start | bytes 196616 | tf_op jit(solution)/shard_map/ppermute | solution.py:63
  17.1 13.1 %collective-permute-start.4 = (bf16[8,4096]{1,0:T(8,128)(2,1)S(1)}, bf16[8,4096]{1,0:T(8,128)(2,1)S(1)}, u32[]{:S(2)}, u32[]{:S(2)}) collective-permute-start(bf16[8,4096]{1,0:T(8,128)(2,1)S(1)} %get-tuple-element.34.high), channel_id=1, source_target_pairs={{0,1},{1,2},{2,3},{3,4},{4,5},{5,6},{6,7},{7,8},{8,9},{9,10},{10,1... | collective-permute-start | bytes 196616 | tf_op jit(solution)/shard_map/ppermute | solution.py:58
  30.3 6.3 %copy-start = (f32[16,4,2]{0,2,1:T(2,128)S(1)}, f32[16,4,2]{0,2,1:T(2,128)}, u32[]{:S(2)}) copy-start(f32[16,4,2]{0,2,1:T(2,128)} %param.14) | copy-start | bytes 1540
  30.3 6.3 %copy-start.1 = (f32[16,4]{0,1:T(4,128)S(1)}, f32[16,4]{0,1:T(4,128)}, u32[]{:S(2)}) copy-start(f32[16,4]{0,1:T(4,128)} %param.15) | copy-start | bytes 772
  30.3 6.3 %copy-start.2 = (f32[16]{0:T(128)S(1)}, f32[16]{0:T(128)}, u32[]{:S(2)}) copy-start(f32[16]{0:T(128)} %shear.7) | copy-start | bytes 196
  43.8 22.0 %copy-start.5 = (s32[16,4]{0,1:T(4,128)S(1)}, s32[16,4]{0,1:T(4,128)}, u32[]{:S(2)}) copy-start(s32[16,4]{0,1:T(4,128)} %param.16) | copy-start | bytes 772
  43.9 17.0 %collective-permute-start.6 = (f32[4,4,32,128]{3,2,1,0:T(8,128)S(1)}, f32[4,4,32,128]{3,2,1,0:T(8,128)S(1)}, u32[]{:S(2)}, u32[]{:S(2)}) collective-permute-start(f32[4,4,32,128]{3,2,1,0:T(8,128)S(1)} %shard_map.121), channel_id=1, source_target_pairs={{0,128},{128,256},{256,384},{384,0},{1,129},{129,257},{257,385},{3... | collective-permute-start | bytes 786440 | tf_op jit(solution)/shard_map/ppermute | solution.py:53
  51.4 11.1 %collective-permute-start.7 = (f32[4,4,32,128]{3,2,1,0:T(8,128)S(1)}, f32[4,4,32,128]{3,2,1,0:T(8,128)S(1)}, u32[]{:S(2)}, u32[]{:S(2)}) collective-permute-start(f32[4,4,32,128]{3,2,1,0:T(8,128)S(1)} %shard_map.122), channel_id=1, source_target_pairs={{0,256},{128,384},{256,0},{384,128},{1,257},{129,385},{257,1},{385... | collective-permute-start | bytes 786440 | tf_op jit(solution)/shard_map/ppermute | solution.py:53
  53.3 12.5 %collective-permute-start.8 = (f32[4,4,32,128]{3,2,1,0:T(8,128)S(1)}, f32[4,4,32,128]{3,2,1,0:T(8,128)S(1)}, u32[]{:S(2)}, u32[]{:S(2)}) collective-permute-start(f32[4,4,32,128]{3,2,1,0:T(8,128)S(1)} %shard_map.123), channel_id=1, source_target_pairs={{0,384},{128,0},{256,128},{384,256},{1,385},{129,1},{257,129},{385... | collective-permute-start | bytes 786440 | tf_op jit(solution)/shard_map/ppermute | solution.py:53

commit v5 on v4

--- a/solution.py
+++ b/solution.py
@@ -16,10 +16,11 @@
 
 HALO = 3
 RIM = 3
-EDGE = 8
-PLANES = 24
+EDGE = 6
+PLANES = 22
 ROWS = 40
-LINES = 1024
+LINES = 896
+BLOCKS = LINES // 128
 SHIFTS = 2 * RIM + 1
 CAPACITY = 4
 
@@ -95,7 +96,6 @@
         copy.start()
     for f in range(4):
         brick[f, :, 32:ROWS, :] = jnp.zeros((PLANES, ROWS - 32, 128), F32)
-        brick[f, HALO + 16 + HALO :, 0:32, :] = jnp.zeros((PLANES - 22, 32, 128), F32)
     for copy in copies:
         copy.wait()
 
@@ -110,10 +110,11 @@
         high[r] = lines[pl.ds(32 - HALO + r, 4 * PLANES, stride=ROWS), :].astype(BF16)
 
 
-def column_picker():
-    j = lax.broadcasted_iota(jnp.int32, (2 * EDGE, 128), 0)
-    lane = lax.broadcasted_iota(jnp.int32, (2 * EDGE, 128), 1)
-    return (lane == jnp.where(j < EDGE, j, 128 - 2 * EDGE + j)).astype(F32)
+def column_picker(first_low, first_high):
+    j = lax.broadcasted_iota(jnp.int32, (16, 128), 0)
+    lane = lax.broadcasted_iota(jnp.int32, (16, 128), 1)
+    at = jnp.where(j < 8, first_low + j, first_high + j - 8)
+    return ((lane == at) & (j % 8 < EDGE)).astype(F32).astype(BF16)
 
 
 def pack_columns(place, unused, above, below, brick, low, high):
@@ -123,16 +124,16 @@
     for r in range(HALO):
         lines[pl.ds(ROWS - HALO + r, 4 * PLANES, stride=ROWS), :] = has_above * above[r].astype(F32)
         lines[pl.ds(32 + r, 4 * PLANES, stride=ROWS), :] = has_below * below[r].astype(F32)
-    pick = column_picker().astype(BF16)
+    pick = column_picker(0, 128 - EDGE)
     count = PLANES * ROWS
+    blank = jnp.zeros((8, LINES - count), BF16)
     for f in range(4):
         rows = brick[f].reshape(count, 128).astype(BF16)
         edge = lax.dot_general(pick, rows, NT, preferred_element_type=F32).astype(BF16)
         at = f * LINES
-        low[:, at : at + count] = edge[:EDGE]
-        high[:, at : at + count] = edge[EDGE:]
-        low[:, at + count : at + LINES] = jnp.zeros((EDGE, LINES - count), BF16)
-        high[:, at + count : at + LINES] = jnp.zeros((EDGE, LINES - count), BF16)
+        for side, part in ((low, edge[:8]), (high, edge[8:])):
+            side[:, at : at + count] = part
+            side[:, at + count : at + LINES] = blank
 
 
 def slope_of(fields, diffusivity, reaction, neighbours):
@@ -186,21 +187,21 @@
         ok = ((p >= HALO) | (depth_at > 0)) & ((p < HALO + 16) | (depth_at < depth_last))
         return jnp.where(ok, 1.0, 0.0).astype(F32)
 
-    @pl.loop(1, 21)
+    @pl.loop(1, 21, unroll=2)
     def _(p):
         slope = tendency(brick, p)
         scale = inside(p)
         for f in range(2):
             first[f, p] = brick[f, p] + (step * scale) * slope[f]
 
-    @pl.loop(2, 20)
+    @pl.loop(2, 20, unroll=2)
     def _(p):
         slope = tendency(first, p)
         scale = inside(p)
         for f in range(2):
             second[f, p] = 0.75 * brick[f, p] + 0.25 * (first[f, p] + (step * scale) * slope[f])
 
-    @pl.loop(3, 19)
+    @pl.loop(3, 19, unroll=2)
     def _(p):
         slope = tendency(second, p)
         k = p - HALO
@@ -209,95 +210,130 @@
             for shift in range(-RIM, RIM + 1):
                 shifted[shift + RIM, f, k] = pltpu.roll(new, -shift % 128, 1) if shift else new
 
-    pick = column_picker()
+    pick = column_picker(0, 128 - EDGE)
     count = PLANES * ROWS
     for f in range(2):
+        rows = brick[f].reshape(count, 128)
+        rest = (rows - rows.astype(BF16).astype(F32)).astype(BF16)
         edges[:, f * LINES : f * LINES + count] = lax.dot_general(
-            pick,
-            brick[f].reshape(count, 128),
-            NT,
-            preferred_element_type=F32,
-            precision=lax.Precision.HIGHEST,
+            pick, rest, NT, preferred_element_type=F32
         )
-        edges[:, f * LINES + count : (f + 1) * LINES] = jnp.zeros((2 * EDGE, LINES - count), F32)
-
-
-def advance_edges(place, unused, edges, low, high, left, right, shifted, out, turned):
+        edges[:, f * LINES + count : (f + 1) * LINES] = jnp.zeros((16, LINES - count), F32)
+
+
+def advance_edges(
+    place, unused, edges, low, high, left, right, shifted, out, start, coefs, first, second, turned
+):
     row_at, col_at, depth_at = place[1], place[2], place[0]
     depth_last, row_last, col_last = place[3], place[4], place[5]
-    shape = (4 * EDGE, LINES)
+    shape = (4 * EDGE, 128)
     col = lax.broadcasted_iota(jnp.int32, shape, 0)
     lane = lax.broadcasted_iota(jnp.int32, shape, 1)
-    plane = jnp.floor((lane.astype(F32) + 0.5) * (1.0 / ROWS)).astype(jnp.int32)
-    row = lane - plane * ROWS
-    rows_in = (
-        (row < 32)
-        | ((row < 32 + HALO) & (row_at < row_last))
-        | ((row >= ROWS - HALO) & (row_at > 0))
-    )
     cols_in = ((col >= EDGE) | (col_at > 0)) & ((col < 3 * EDGE) | (col_at < col_last))
-    planes_in = ((plane >= HALO) | (depth_at > 0)) & (
-        (plane < HALO + 16) | ((plane < 22) & (depth_at < depth_last))
-    )
-    step = jnp.where(rows_in & cols_in & planes_in, TIME_STEP, 0.0).astype(F32)
-    first_row, last_row = row == 0, row == ROWS - 1
-
-    def gather(f):
-        cut = slice(f * LINES, (f + 1) * LINES)
-        if f < 2:
-            own = (edges[0:EDGE, cut], edges[EDGE : 2 * EDGE, cut])
-        else:
-            own = (low[:, cut].astype(F32), high[:, cut].astype(F32))
-        return jnp.concatenate(
-            [left[:, cut].astype(F32), own[0], own[1], right[:, cut].astype(F32)], axis=0
+
+    def table(b):
+        line = lane + 128 * b
+        plane = jnp.floor((line.astype(F32) + 0.5) * (1.0 / ROWS)).astype(jnp.int32)
+        row = line - plane * ROWS
+        rows_in = (
+            (row < 32)
+            | ((row < 32 + HALO) & (row_at < row_last))
+            | ((row >= ROWS - HALO) & (row_at > 0))
         )
-
-    start = (gather(0), gather(1))
-    diffusivity, reaction = gather(2), gather(3)
-
-    def tendency(fields):
-        def neighbours(f):
-            x = fields[f]
-            return (
-                pltpu.roll(x, ROWS, 1),
-                pltpu.roll(x, LINES - ROWS, 1),
-                jnp.where(first_row, pltpu.roll(x, LINES - ROWS + 1, 1), pltpu.roll(x, 1, 1)),
-                jnp.where(last_row, pltpu.roll(x, ROWS - 1, 1), pltpu.roll(x, LINES - 1, 1)),
-                pltpu.roll(x, 1, 0),
-                pltpu.roll(x, 4 * EDGE - 1, 0),
+        planes_in = ((plane >= HALO) | (depth_at > 0)) & (
+            (plane < HALO + 16) | ((plane < PLANES) & (depth_at < depth_last))
+        )
+        step = jnp.where(rows_in & cols_in & planes_in, TIME_STEP, 0.0).astype(F32)
+        return step, row == 0, row == ROWS - 1
+
+    for f in range(4):
+        for b in range(BLOCKS):
+            cut = slice(f * LINES + 128 * b, f * LINES + 128 * (b + 1))
+            own_low, own_high = low[:, cut].astype(F32), high[:, cut].astype(F32)
+            if f < 2:
+                own_low = own_low + edges[0:8, cut]
+                own_high = own_high + edges[8:16, cut]
+            gathered = jnp.concatenate(
+                [
+                    left[:, cut].astype(F32)[:EDGE],
+                    own_low[:EDGE],
+                    own_high[:EDGE],
+                    right[:, cut].astype(F32)[:EDGE],
+                ],
+                axis=0,
             )
-
-        return slope_of(fields, diffusivity, reaction, neighbours)
-
-    slope = tendency(start)
-    first = tuple(start[f] + step * slope[f] for f in range(2))
-    slope = tendency(first)
-    second = tuple(0.75 * start[f] + 0.25 * (first[f] + step * slope[f]) for f in range(2))
-    slope = tendency(second)
+            if f < 2:
+                start[f, b] = gathered
+            else:
+                coefs[f - 2, b] = gathered
+
+    def stage(source, finish):
+        held = {}
+
+        def turn(f, b, by):
+            b = b % BLOCKS
+            if (f, b, by) not in held:
+                held[f, b, by] = pltpu.roll(source[f, b], by, 1)
+            return held[f, b, by]
+
+        def from_before(f, b, by):
+            return jnp.where(lane < by, turn(f, b - 1, by), turn(f, b, by))
+
+        def from_after(f, b, by):
+            return jnp.where(lane >= 128 - by, turn(f, b + 1, 128 - by), turn(f, b, 128 - by))
+
+        for b in range(BLOCKS):
+            step, first_row, last_row = table(b)
+
+            def neighbours(f):
+                x = source[f, b]
+                return (
+                    from_before(f, b, ROWS),
+                    from_after(f, b, ROWS),
+                    jnp.where(first_row, from_after(f, b, ROWS - 1), from_before(f, b, 1)),
+                    jnp.where(last_row, from_before(f, b, ROWS - 1), from_after(f, b, 1)),
+                    pltpu.roll(x, 1, 0),
+                    pltpu.roll(x, 4 * EDGE - 1, 0),
+                )
+
+            slope = slope_of((source[0, b], source[1, b]), coefs[0, b], coefs[1, b], neighbours)
+            for f in range(2):
+                finish(f, b, step * slope[f])
+
+    def finish_first(f, b, change):
+        first[f, b] = start[f, b] + change
+
+    def finish_second(f, b, change):
+        second[f, b] = 0.75 * start[f, b] + 0.25 * (first[f, b] + change)
+
     blank = jnp.zeros((128 - 4 * EDGE, 128), F32)
-    for f in range(2):
-        new = start[f] / 3.0 + (2.0 / 3.0) * (second[f] + step * slope[f])
-        for block in range(LINES // 128):
-            cut = slice(128 * block, 128 * (block + 1))
-            turned[f, cut, :] = jnp.concatenate([new[:, cut], blank], axis=0).T
-
-    lane = lax.broadcasted_iota(jnp.int32, (32, 128), 1)
-
-    @pl.loop(0, 16)
+
+    def finish_third(f, b, change):
+        new = start[f, b] / 3.0 + (2.0 / 3.0) * (second[f, b] + change)
+        turned[f, 128 * b : 128 * (b + 1), :] = jnp.concatenate([new, blank], axis=0).T
+
+    stage(start, finish_first)
+    stage(first, finish_second)
+    stage(second, finish_third)
+    lane32 = lax.broadcasted_iota(jnp.int32, (32, 128), 1)
+
+    @pl.loop(0, 16, unroll=2)
     def _(k):
         for f in range(2):
             lines = turned[f, pl.ds(pl.multiple_of((k + HALO) * ROWS, 8), 32), :]
             near = pltpu.roll(lines, 128 - EDGE, 1)
             far = pltpu.roll(lines, 128 - 3 * EDGE, 1)
             for shift in range(-RIM, RIM + 1):
-                from_far = (lane >= 64) & (lane < 128 + min(shift, 0)) | (lane < shift)
+                from_far = (lane32 >= 64) & (lane32 < 128 + min(shift, 0)) | (lane32 < shift)
                 patch = jnp.where(from_far, far, near)
                 patch = pltpu.roll(patch, -shift % 128, 1) if shift else patch
-                wrong = (lane <= RIM - 1 - shift) | (lane >= 128 - RIM - shift)
-                value = jnp.where(wrong, patch, shifted[shift + RIM, f, k])
-                shifted[shift + RIM, f, k] = value
+                wrong = (lane32 <= RIM - 1 - shift) | (lane32 >= 128 - RIM - shift)
                 if shift == 0:
-                    out[f, k] = value
+                    patch = jnp.where(wrong, patch, shifted[RIM, f, k])
+                    shifted[RIM, f, k] = patch
+                    out[f, k] = patch
+                else:
+                    pltpu.store(shifted.at[shift + RIM, f, k], patch, mask=wrong)
 
 
 def render(away, place, shear, weight, bias, shifted, image):
@@ -490,7 +526,7 @@
     brick, select, lengths_wide, warp_own = lax.optimization_barrier(
         (brick, select, lengths_wide, warp_own)
     )
-    face = jax.ShapeDtypeStruct((EDGE, 4 * LINES), BF16)
+    face = jax.ShapeDtypeStruct((8, 4 * LINES), BF16)
     brick, low, high = call(
         pack_columns, (brick_type, face, face), [SMEM_SPEC] + [VMEM_SPEC] * 3, aliases={1: 0}
     )(place, brick, above, below)
@@ -500,7 +536,7 @@
     shifted_type = jax.ShapeDtypeStruct((SHIFTS,) + species.shape, F32)
     shifted, edges = call(
         advance_own,
-        (shifted_type, jax.ShapeDtypeStruct((2 * EDGE, 2 * LINES), F32)),
+        (shifted_type, jax.ShapeDtypeStruct((16, 2 * LINES), F32)),
         [SMEM_SPEC, VMEM_SPEC],
         [wide, wide],
     )(place, brick)
@@ -508,7 +544,7 @@
         advance_edges,
         (shifted_type, jax.ShapeDtypeStruct(species.shape, F32)),
         [SMEM_SPEC] + [VMEM_SPEC] * 6,
-        [pltpu.VMEM((2, LINES, 128), F32)],
+        [pltpu.VMEM((2, BLOCKS, 4 * EDGE, 128), F32)] * 4 + [pltpu.VMEM((2, LINES, 128), F32)],
         aliases={1: 0},
     )(place, shifted, edges, low, high, left, right)
 

time: 104 us -> 99.2 us (0.954)
  Pallas kernels: 32.3 us -> 27.6 us
    pallas_call x1, Pallas kernels: 8.55 us -> 5.2 us  [body(): call(advance_own, (shifted_type, jax.ShapeDtypeStruct((16, 2 * LINES), F3...]
    pallas_call x1, Pallas kernels: 6.27 us -> 5.02 us  [body(): call(advance_edges, (shifted_type, jax.ShapeDtypeStruct(species.shape, F3...]
  transfers between devices with their start and end apart: 9 -> 9, of which waited for: 5 -> 5; matrix products, arithmetic and copies ran while one was open for 0% -> 0% of each run, Pallas kernels for 13% -> 11%
where the time goes in v5:
time: 99.2 us; the launch traced here: 97.6 us
  blocking collectives  33.6 us (34%)
  Pallas kernels  27.6 us (28%)
  starting transfers between devices  26.8 us (27%)
  waiting for transfers between devices  8.72 us (9%)
    all_to_all x1, blocking collectives, body(): lax.all_to_all(outgoing.reshape(col_devices, -1, 1152), 'col', split_axis...  33.6 us
    ppermute x5, starting transfers between devices, turn_by(): return lax.ppermute(x, axis, [(i, (i + steps) % n) for i in range(n)])  15.1 us
    pallas_call x4, Pallas kernels, body(): call(functools.partial(render, away), image, [SMEM_SPEC] * 4 + [VMEM_SPEC])  9.66 us
    ppermute x5, waiting for transfers between devices, turn_by(): return lax.ppermute(x, axis, [(i, (i + steps) % n) for i in range(n)])  7.76 us
    ppermute x2, starting transfers between devices, shift_down(): return lax.ppermute(x, axis, [(i + 1, i) for i in range(n - 1)])  5.85 us
    ppermute x2, starting transfers between devices, shift_up(): return lax.ppermute(x, axis, [(i, i + 1) for i in range(n - 1)])  5.84 us
    pallas_call x1, Pallas kernels, body(): call(advance_own, (shifted_type, jax.ShapeDtypeStruct((16, 2 * LINES), F3...  5.2 us
    pallas_call x1, Pallas kernels, body(): call(advance_edges, (shifted_type, jax.ShapeDtypeStruct(species.shape, F3...  5.02 us
  transfers between devices with their start and end apart: 9, of which 5 were waited for; matrix products, arithmetic and copies ran while one was open for 0% of the time, Pallas kernels for 11%

profile of v5, /device:TPU:6, one launch (start us, length us, event | category | flops | bytes accessed | tf_op | source)
XLA Modules:
  0.0 97.6 jit_solution(4080395484345876042)
XLA Ops:
  0.6 1.1 %shard_map.114 = (bf16[4,3,32,128]{3,2,1,0:T(8,128)(2,1)S(1)}, bf16[4,3,32,128]{3,2,1,0:T(8,128)(2,1)S(1)}) custom-call(f32[2,16,32,128]{3,2,1,0:T(8,128)} %species.3, f32[16,32,128]{2,1,0:T(8,128)} %diff.3, f32[16,32,128]{2,1,0:T(8,128)} %rate.3), custom_call_target="tpu_custom_call" | custom-call | tf_op jit(solution)/shard_map/pallas_call | solution.py:499
  1.7 1.3 %collective-permute-start = (bf16[4,3,32,128]{3,2,1,0:T(8,128)(2,1)S(1)}, bf16[4,3,32,128]{3,2,1,0:T(8,128)(2,1)S(1)}, u32[]{:S(2)}, u32[]{:S(2)}) collective-permute-start(bf16[4,3,32,128]{3,2,1,0:T(8,128)(2,1)S(1)} %get-tuple-element.21), channel_id=1, source_target_pairs={{0,128},{128,256},{256,384},{1,129},{129,257},{257,385},{2,130},{1... | collective-permute-start | bytes 294920 | tf_op jit(solution)/shard_map/ppermute | solution.py:59
  3.0 0.0 copy-start.3
  3.0 0.0 copy-start.4
  3.0 4.6 %collective-permute-start.1 = (bf16[4,3,32,128]{3,2,1,0:T(8,128)(2,1)S(1)}, bf16[4,3,32,128]{3,2,1,0:T(8,128)(2,1)S(1)}, u32[]{:S(2)}, u32[]{:S(2)}) collective-permute-start(bf16[4,3,32,128]{3,2,1,0:T(8,128)(2,1)S(1)} %get-tuple-element.22), channel_id=1, source_target_pairs={{128,0},{256,128},{384,256},{129,1},{257,129},{385,257},{130,2},{2... | collective-permute-start | bytes 294920 | tf_op jit(solution)/shard_map/ppermute | solution.py:64
  7.6 1.2 %shard_map.113.unused = f32[4,22,40,128]{3,2,1,0:T(8,128)S(1)} custom-call(f32[2,16,32,128]{3,2,1,0:T(8,128)} %species.3, f32[16,32,128]{2,1,0:T(8,128)} %diff.3, f32[16,32,128]{2,1,0:T(8,128)} %rate.3), custom_call_target="tpu_custom_call" | custom-call | tf_op jit(solution)/shard_map/pallas_call | solution.py:507
  8.8 0.0 collective-permute-done.before
  8.8 0.9 collective-permute-done.1.after
  9.8 0.1 shard_map.115
  9.8 0.0 collective-permute-start.2
  9.9 2.9 %collective-permute-start.3 = (bf16[3,88,128]{2,1,0:T(8,128)(2,1)S(1)}, bf16[3,88,128]{2,1,0:T(8,128)(2,1)S(1)}, u32[]{:S(2)}, u32[]{:S(2)}) collective-permute-start(bf16[3,88,128]{2,1,0:T(8,128)(2,1)S(1)} %get-tuple-element.29), channel_id=1, source_target_pairs={{0,112},{16,0},{32,16},{48,32},{64,48},{80,64},{96,80},{112,96},{1... | collective-permute-start | bytes 202760 | tf_op jit(solution)/shard_map/ppermute | solution.py:54
  12.8 0.1 stack.15.place
  12.9 0.0 copy-done.3
  12.9 0.0 copy-done.4
  12.9 1.5 %shard_map.116 = (bf16[256,128]{1,0:T(8,128)(2,1)S(1)}, s32[128,128]{1,0:T(8,128)S(1)}, bf16[4,128,128]{2,1,0:T(8,128)(2,1)S(1)}) custom-call(s32[6]{0:T(128)S(1)} %stack.15.place, s32[4,32]{1,0:T(4,128)S(1)} %bitcast.21, s32[4,32]{1,0:T(4,128)S(1)} %bitcast.22, bf16[16,128,128]{2,1,0:T(8,128)(2,1)} %warp.1), custom_call_target="tpu_custom_call" | custom-call | tf_op jit(solution)/shard_map/pallas_call | solution.py:515
  14.4 0.4 collective-permute-done.2.above
  14.8 0.0 collective-permute-done.3.below
  14.8 0.9 shard_map.117
  15.7 1.3 %collective-permute-start.5 = (bf16[8,3584]{1,0:T(8,128)(2,1)S(1)}, bf16[8,3584]{1,0:T(8,128)(2,1)S(1)}, u32[]{:S(2)}, u32[]{:S(2)}) collective-permute-start(bf16[8,3584]{1,0:T(8,128)(2,1)S(1)} %get-tuple-element.33.low), channel_id=1, source_target_pairs={{1,0},{2,1},{3,2},{4,3},{5,4},{6,5},{7,6},{8,7},{9,8},{10,9},{11,1... | collective-permute-start | bytes 172040 | tf_op jit(solution)/shard_map/ppermute | solution.py:64
  17.0 4.5 %collective-permute-start.4 = (bf16[8,3584]{1,0:T(8,128)(2,1)S(1)}, bf16[8,3584]{1,0:T(8,128)(2,1)S(1)}, u32[]{:S(2)}, u32[]{:S(2)}) collective-permute-start(bf16[8,3584]{1,0:T(8,128)(2,1)S(1)} %get-tuple-element.34.high), channel_id=1, source_target_pairs={{0,1},{1,2},{2,3},{3,4},{4,5},{5,6},{6,7},{7,8},{8,9},{9,10},{10,1... | collective-permute-start | bytes 172040 | tf_op jit(solution)/shard_map/ppermute | solution.py:59
  21.6 5.2 %shard_map.118 = (f32[7,2,16,32,128]{4,3,2,1,0:T(8,128)S(1)}, f32[16,1792]{1,0:T(8,128)S(1)}) custom-call(s32[6]{0:T(128)S(1)} %stack.15.place, f32[4,22,40,128]{3,2,1,0:T(8,128)S(1)} %get-tuple-element.30.brick), custom_call_target="tpu_custom_call" | custom-call | tf_op jit(solution)/shard_map/pallas_call | solution.py:537
  26.8 0.0 collective-permute-done.5.right
  26.8 0.0 collective-permute-done.4.left
  26.8 0.0 copy-start
  26.8 0.0 copy-start.1
  26.8 0.0 copy-start.2
  26.8 5.0 %shard_map.119 = (f32[7,2,16,32,128]{4,3,2,1,0:T(8,128)S(1)}, f32[2,16,32,128]{3,2,1,0:T(8,128)}) custom-call(s32[6]{0:T(128)S(1)} %stack.15.place, f32[7,2,16,32,128]{4,3,2,1,0:T(8,128)S(1)} %get-tuple-element.31.unused, f32[16,1792]{1,0:T(8,128)S(1)} %get-tuple-element.32.edges, ...), custom_call_target="tpu_custom_call", output_to_operand_aliasing={{0}: (1, {})} | custom-call | tf_op jit(solution)/shard_map/pallas_call | solution.py:543
  31.9 0.0 copy-done
  31.9 0.0 copy-done.1
  31.9 0.0 copy-done.2
  31.9 2.4 %shard_map.123 = f32[4,4,32,128]{3,2,1,0:T(8,128)S(1)} custom-call(s32[6]{0:T(128)S(1)} %stack.15.place, f32[16]{0:T(128)S(1)} %copy-done.2, f32[4,2,16]{2,1,0:T(2,128)S(1)} %bitcast.13, f32[4,16]{1,0:T(4,128)S(1)} %bitcast.17, f32[7,2,16,32,128]{4,3,2,1,0:T(8,128)S(1)} %get-tuple-element.38.shifted), custom_call_target="tpu_custom_call" | custom-call | tf_op jit(solution)/shard_map/pallas_call | solution.py:555
  34.3 2.4 %shard_map.122 = f32[4,4,32,128]{3,2,1,0:T(8,128)S(1)} custom-call(s32[6]{0:T(128)S(1)} %stack.15.place, f32[16]{0:T(128)S(1)} %copy-done.2, f32[4,2,16]{2,1,0:T(2,128)S(1)} %bitcast.14, f32[4,16]{1,0:T(4,128)S(1)} %bitcast.18, f32[7,2,16,32,128]{4,3,2,1,0:T(8,128)S(1)} %get-tuple-element.38.shifted), custom_call_target="tpu_custom_call" | custom-call | tf_op jit(solution)/shard_map/pallas_call | solution.py:555
  36.7 2.4 %shard_map.121 = f32[4,4,32,128]{3,2,1,0:T(8,128)S(1)} custom-call(s32[6]{0:T(128)S(1)} %stack.15.place, f32[16]{0:T(128)S(1)} %copy-done.2, f32[4,2,16]{2,1,0:T(2,128)S(1)} %bitcast.15, f32[4,16]{1,0:T(4,128)S(1)} %bitcast.19, f32[7,2,16,32,128]{4,3,2,1,0:T(8,128)S(1)} %get-tuple-element.38.shifted), custom_call_target="tpu_custom_call" | custom-call | tf_op jit(solution)/shard_map/pallas_call | solution.py:555
  39.1 0.0 copy-start.5
  39.1 7.5 %collective-permute-start.6 = (f32[4,4,32,128]{3,2,1,0:T(8,128)S(1)}, f32[4,4,32,128]{3,2,1,0:T(8,128)S(1)}, u32[]{:S(2)}, u32[]{:S(2)}) collective-permute-start(f32[4,4,32,128]{3,2,1,0:T(8,128)S(1)} %shard_map.121), channel_id=1, source_target_pairs={{0,128},{128,256},{256,384},{384,0},{1,129},{129,257},{257,385},{3... | collective-permute-start | bytes 786440 | tf_op jit(solution)/shard_map/ppermute | solution.py:54
  46.6 1.9 %collective-permute-start.7 = (f32[4,4,32,128]{3,2,1,0:T(8,128)S(1)}, f32[4,4,32,128]{3,2,1,0:T(8,128)S(1)}, u32[]{:S(2)}, u32[]{:S(2)}) collective-permute-start(f32[4,4,32,128]{3,2,1,0:T(8,128)S(1)} %shard_map.122), channel_id=1, source_target_pairs={{0,256},{128,384},{256,0},{384,128},{1,257},{129,385},{257,1},{385... | collective-permute-start | bytes 786440 | tf_op jit(solution)/shard_map/ppermute | solution.py:54
  48.6 2.8 %collective-permute-start.8 = (f32[4,4,32,128]{3,2,1,0:T(8,128)S(1)}, f32[4,4,32,128]{3,2,1,0:T(8,128)S(1)}, u32[]{:S(2)}, u32[]{:S(2)}) collective-permute-start(f32[4,4,32,128]{3,2,1,0:T(8,128)S(1)} %shard_map.123), channel_id=1, source_target_pairs={{0,384},{128,0},{256,128},{384,256},{1,385},{129,1},{257,129},{385... | collective-permute-start | bytes 786440 | tf_op jit(solution)/shard_map/ppermute | solution.py:54
  51.3 2.4 %shard_map.120.slab0 = f32[4,4,32,128]{3,2,1,0:T(8,128)S(1)} custom-call(s32[6]{0:T(128)S(1)} %stack.15.place, f32[16]{0:T(128)S(1)} %copy-done.2, f32[4,2,16]{2,1,0:T(2,128)S(1)} %bitcast.16, f32[4,16]{1,0:T(4,128)S(1)} %bitcast.20, f32[7,2,16,32,128]{4,3,2,1,0:T(8,128)S(1)} %get-tuple-element.38.shifted), custom_call_target="tpu_custom_call" | custom-call | tf_op jit(solution)/shard_map/pallas_call | solution.py:555
  53.8 2.4 %collective-permute-done.6.slab1 = f32[4,4,32,128]{3,2,1,0:T(8,128)S(1)} collective-permute-done((f32[4,4,32,128]{3,2,1,0:T(8,128)S(1)}, f32[4,4,32,128]{3,2,1,0:T(8,128)S(1)}, u32[]{:S(2)}, u32[]{:S(2)}) %collective-permute-start.6) | collective-permute-done | bytes 262176 | tf_op jit(solution)/shard_map/ppermute | solution.py:54
  56.1 1.6 %collective-permute-done.7.slab2 = f32[4,4,32,128]{3,2,1,0:T(8,128)S(1)} collective-permute-done((f32[4,4,32,128]{3,2,1,0:T(8,128)S(1)}, f32[4,4,32,128]{3,2,1,0:T(8,128)S(1)}, u32[]{:S(2)}, u32[]{:S(2)}) %collective-permute-start.7) | collective-permute-done | bytes 262176 | tf_op jit(solution)/shard_map/ppermute | solution.py:54
  57.7 3.4 %collective-permute-done.8.slab3 = f32[4,4,32,128]{3,2,1,0:T(8,128)S(1)} collective-permute-done((f32[4,4,32,128]{3,2,1,0:T(8,128)S(1)}, f32[4,4,32,128]{3,2,1,0:T(8,128)S(1)}, u32[]{:S(2)}, u32[]{:S(2)}) %collective-permute-start.8) | collective-permute-done | bytes 262176 | tf_op jit(solution)/shard_map/ppermute | solution.py:54
  61.1 0.0 copy-done.5
  61.1 1.1 %shard_map.124 = bf16[128,1152]{1,0:T(8,128)(2,1)S(1)} custom-call(s32[6]{0:T(128)S(1)} %stack.15.place, s32[4,16]{1,0:T(4,128)S(1)} %bitcast.23, bf16[256,128]{1,0:T(8,128)(2,1)S(1)} %get-tuple-element.36.select, s32[128,128]{1,0:T(8,128)S(1)} %get-tuple-element.37.lengths, f32[4,4,32,128]{3,2,1,0:T(8,128)S(1)} %shard_map.120.slab0, ...), custom_call_target="tpu_custom_call" | custom-call | tf_op jit(solution)/shard_map/pallas_call | solution.py:561
  62.2 33.6 %all_to_all.5 = bf16[16,8,1152]{2,1,0:T(8,128)(2,1)S(1)} all-to-all(bf16[16,8,1152]{2,1,0:T(8,128)(2,1)S(1)} %bitcast.11), channel_id=1, replica_groups=mesh['depth'=4,'row'=8,'col'=16] {'col'}, dimensions={0} | all-to-all | bytes 589824 | tf_op jit(solution)/shard_map/all_to_all | solution.py:567
  95.7 1.9 %shard_map.125 = f32[512,128]{1,0:T(8,128)} custom-call(bf16[128,1152]{1,0:T(8,128)(2,1)S(1)} %bitcast.12, bf16[4,128,128]{2,1,0:T(8,128)(2,1)S(1)} %get-tuple-element.39.warp), custom_call_target="tpu_custom_call" | custom-call | tf_op jit(solution)/shard_map/pallas_call | solution.py:574
Async XLA Ops:
  1.7 7.1 %collective-permute-start = (bf16[4,3,32,128]{3,2,1,0:T(8,128)(2,1)S(1)}, bf16[4,3,32,128]{3,2,1,0:T(8,128)(2,1)S(1)}, u32[]{:S(2)}, u32[]{:S(2)}) collective-permute-start(bf16[4,3,32,128]{3,2,1,0:T(8,128)(2,1)S(1)} %get-tuple-element.21), channel_id=1, source_target_pairs={{0,128},{128,256},{256,384},{1,129},{129,257},{257,385},{2,130},{1... | collective-permute-start | bytes 294920 | tf_op jit(solution)/shard_map/ppermute | solution.py:59
  3.0 9.9 %copy-start.3 = (s32[4,1,32,1]{2,3,1,0:T(1,128)S(1)}, s32[4,1,32,1]{2,3,1,0:T(1,128)}, u32[]{:S(2)}) copy-start(s32[4,1,32,1]{2,3,1,0:T(1,128)} %param.18) | copy-start | bytes 1540
  3.0 9.9 %copy-start.4 = (s32[4,1,32]{2,1,0:T(1,128)S(1)}, s32[4,1,32]{2,1,0:T(1,128)}, u32[]{:S(2)}) copy-start(s32[4,1,32]{2,1,0:T(1,128)} %param.17) | copy-start | bytes 1540
  3.0 6.8 %collective-permute-start.1 = (bf16[4,3,32,128]{3,2,1,0:T(8,128)(2,1)S(1)}, bf16[4,3,32,128]{3,2,1,0:T(8,128)(2,1)S(1)}, u32[]{:S(2)}, u32[]{:S(2)}) collective-permute-start(bf16[4,3,32,128]{3,2,1,0:T(8,128)(2,1)S(1)} %get-tuple-element.22), channel_id=1, source_target_pairs={{128,0},{256,128},{384,256},{129,1},{257,129},{385,257},{130,2},{2... | collective-permute-start | bytes 294920 | tf_op jit(solution)/shard_map/ppermute | solution.py:64
  9.8 4.9 %collective-permute-start.2 = (bf16[3,88,128]{2,1,0:T(8,128)(2,1)S(1)}, bf16[3,88,128]{2,1,0:T(8,128)(2,1)S(1)}, u32[]{:S(2)}, u32[]{:S(2)}) collective-permute-start(bf16[3,88,128]{2,1,0:T(8,128)(2,1)S(1)} %get-tuple-element.28), channel_id=1, source_target_pairs={{0,16},{16,32},{32,48},{48,64},{64,80},{80,96},{96,112},{112,0},{1... | collective-permute-start | bytes 202760 | tf_op jit(solution)/shard_map/ppermute | solution.py:54
  9.9 4.9 %collective-permute-start.3 = (bf16[3,88,128]{2,1,0:T(8,128)(2,1)S(1)}, bf16[3,88,128]{2,1,0:T(8,128)(2,1)S(1)}, u32[]{:S(2)}, u32[]{:S(2)}) collective-permute-start(bf16[3,88,128]{2,1,0:T(8,128)(2,1)S(1)} %get-tuple-element.29), channel_id=1, source_target_pairs={{0,112},{16,0},{32,16},{48,32},{64,48},{80,64},{96,80},{112,96},{1... | collective-permute-start | bytes 202760 | tf_op jit(solution)/shard_map/ppermute | solution.py:54
  15.7 11.1 %collective-permute-start.5 = (bf16[8,3584]{1,0:T(8,128)(2,1)S(1)}, bf16[8,3584]{1,0:T(8,128)(2,1)S(1)}, u32[]{:S(2)}, u32[]{:S(2)}) collective-permute-start(bf16[8,3584]{1,0:T(8,128)(2,1)S(1)} %get-tuple-element.33.low), channel_id=1, source_target_pairs={{1,0},{2,1},{3,2},{4,3},{5,4},{6,5},{7,6},{8,7},{9,8},{10,9},{11,1... | collective-permute-start | bytes 172040 | tf_op jit(solution)/shard_map/ppermute | solution.py:64
  17.0 9.8 %collective-permute-start.4 = (bf16[8,3584]{1,0:T(8,128)(2,1)S(1)}, bf16[8,3584]{1,0:T(8,128)(2,1)S(1)}, u32[]{:S(2)}, u32[]{:S(2)}) collective-permute-start(bf16[8,3584]{1,0:T(8,128)(2,1)S(1)} %get-tuple-element.34.high), channel_id=1, source_target_pairs={{0,1},{1,2},{2,3},{3,4},{4,5},{5,6},{6,7},{7,8},{8,9},{9,10},{10,1... | collective-permute-start | bytes 172040 | tf_op jit(solution)/shard_map/ppermute | solution.py:59
  26.8 5.1 %copy-start = (f32[16,4,2]{0,2,1:T(2,128)S(1)}, f32[16,4,2]{0,2,1:T(2,128)}, u32[]{:S(2)}) copy-start(f32[16,4,2]{0,2,1:T(2,128)} %param.14) | copy-start | bytes 1540
  26.8 5.1 %copy-start.1 = (f32[16,4]{0,1:T(4,128)S(1)}, f32[16,4]{0,1:T(4,128)}, u32[]{:S(2)}) copy-start(f32[16,4]{0,1:T(4,128)} %param.15) | copy-start | bytes 772
  26.8 5.0 %copy-start.2 = (f32[16]{0:T(128)S(1)}, f32[16]{0:T(128)}, u32[]{:S(2)}) copy-start(f32[16]{0:T(128)} %shear.7) | copy-start | bytes 196
  39.1 22.0 %copy-start.5 = (s32[16,4]{0,1:T(4,128)S(1)}, s32[16,4]{0,1:T(4,128)}, u32[]{:S(2)}) copy-start(s32[16,4]{0,1:T(4,128)} %param.16) | copy-start | bytes 772
  39.1 17.0 %collective-permute-start.6 = (f32[4,4,32,128]{3,2,1,0:T(8,128)S(1)}, f32[4,4,32,128]{3,2,1,0:T(8,128)S(1)}, u32[]{:S(2)}, u32[]{:S(2)}) collective-permute-start(f32[4,4,32,128]{3,2,1,0:T(8,128)S(1)} %shard_map.121), channel_id=1, source_target_pairs={{0,128},{128,256},{256,384},{384,0},{1,129},{129,257},{257,385},{3... | collective-permute-start | bytes 786440 | tf_op jit(solution)/shard_map/ppermute | solution.py:54
  46.6 11.1 %collective-permute-start.7 = (f32[4,4,32,128]{3,2,1,0:T(8,128)S(1)}, f32[4,4,32,128]{3,2,1,0:T(8,128)S(1)}, u32[]{:S(2)}, u32[]{:S(2)}) collective-permute-start(f32[4,4,32,128]{3,2,1,0:T(8,128)S(1)} %shard_map.122), channel_id=1, source_target_pairs={{0,256},{128,384},{256,0},{384,128},{1,257},{129,385},{257,1},{385... | collective-permute-start | bytes 786440 | tf_op jit(solution)/shard_map/ppermute | solution.py:54
  48.6 12.5 %collective-permute-start.8 = (f32[4,4,32,128]{3,2,1,0:T(8,128)S(1)}, f32[4,4,32,128]{3,2,1,0:T(8,128)S(1)}, u32[]{:S(2)}, u32[]{:S(2)}) collective-permute-start(f32[4,4,32,128]{3,2,1,0:T(8,128)S(1)} %shard_map.123), channel_id=1, source_target_pairs={{0,384},{128,0},{256,128},{384,256},{1,385},{129,1},{257,129},{385... | collective-permute-start | bytes 786440 | tf_op jit(solution)/shard_map/ppermute | solution.py:54

commit v6 on v5

--- a/solution.py
+++ b/solution.py
@@ -23,6 +23,7 @@
 BLOCKS = LINES // 128
 SHIFTS = 2 * RIM + 1
 CAPACITY = 4
+SAVER = 1
 
 F32 = jnp.float32
 BF16 = jnp.bfloat16
@@ -33,12 +34,12 @@
 TN = (((0,), (0,)), ((), ()))
 
 
-def call(kernel, out_shape, in_specs, scratch=(), limit=8, aliases=None):
+def call(kernel, out_shape, in_specs, scratch=(), limit=8, aliases=None, out_specs=None):
     return pl.pallas_call(
         kernel,
         out_shape=out_shape,
         in_specs=in_specs,
-        out_specs=jax.tree.map(lambda unused: VMEM_SPEC, out_shape),
+        out_specs=out_specs or jax.tree.map(lambda unused: VMEM_SPEC, out_shape),
         scratch_shapes=list(scratch),
         input_output_aliases=aliases or {},
         compiler_params=pltpu.CompilerParams(vmem_limit_bytes=limit << 20),
@@ -222,7 +223,7 @@
 
 
 def advance_edges(
-    place, unused, edges, low, high, left, right, shifted, out, start, coefs, first, second, turned
+    place, unused, edges, low, high, left, right, shifted, start, coefs, first, second, turned
 ):
     row_at, col_at, depth_at = place[1], place[2], place[0]
     depth_last, row_last, col_last = place[3], place[4], place[5]
@@ -328,12 +329,14 @@
                 patch = jnp.where(from_far, far, near)
                 patch = pltpu.roll(patch, -shift % 128, 1) if shift else patch
                 wrong = (lane32 <= RIM - 1 - shift) | (lane32 >= 128 - RIM - shift)
-                if shift == 0:
-                    patch = jnp.where(wrong, patch, shifted[RIM, f, k])
-                    shifted[RIM, f, k] = patch
-                    out[f, k] = patch
-                else:
-                    pltpu.store(shifted.at[shift + RIM, f, k], patch, mask=wrong)
+                pltpu.store(shifted.at[shift + RIM, f, k], patch, mask=wrong)
+
+
+def render_and_save(away, place, shear, weight, bias, shifted, image, out, sem):
+    copy = pltpu.make_async_copy(shifted.at[RIM], out, sem.at[0])
+    copy.start()
+    render(away, place, shear, weight, bias, shifted, image)
+    copy.wait()
 
 
 def render(away, place, shear, weight, bias, shifted, image):
@@ -459,12 +462,16 @@
         part = incoming[:, 512 * odd : 512 * (odd + 1)]
         total = total + lax.dot_general(place, part, TN, preferred_element_type=F32)
     for v in range(4):
-        matrix = warp[v].astype(F32)
+        rows = jnp.concatenate(
+            [total[32 * v : 32 * (v + 1), 128 * c : 128 * (c + 1)] for c in range(4)], axis=0
+        )
+        warped = jnp.zeros((128, 128), F32)
+        for _ in range(3):
+            part = rows.astype(BF16)
+            warped = warped + jnp.dot(part, warp[v], preferred_element_type=F32)
+            rows = rows - part.astype(F32)
         for c in range(4):
-            rows = total[32 * v : 32 * (v + 1), 128 * c : 128 * (c + 1)]
-            frame[pl.ds(128 * v + c, 32, stride=4), :] = jnp.dot(
-                rows, matrix, preferred_element_type=F32, precision=lax.Precision.HIGHEST
-            )
+            frame[pl.ds(128 * v + c, 32, stride=4), :] = warped[32 * c : 32 * (c + 1)]
 
 
 def body(
@@ -540,9 +547,9 @@
         [SMEM_SPEC, VMEM_SPEC],
         [wide, wide],
     )(place, brick)
-    shifted, species_out = call(
+    shifted = call(
         advance_edges,
-        (shifted_type, jax.ShapeDtypeStruct(species.shape, F32)),
+        shifted_type,
         [SMEM_SPEC] + [VMEM_SPEC] * 6,
         [pltpu.VMEM((2, BLOCKS, 4 * EDGE, 128), F32)] * 4 + [pltpu.VMEM((2, LINES, 128), F32)],
         aliases={1: 0},
@@ -552,9 +559,18 @@
     weight, bias = jnp.transpose(colour_weight, (1, 2, 0)), colour_bias.T
     slabs = [None] * 4
     for away in (2, 1, 3, 0):
-        drawn = call(
-            functools.partial(render, away), image, [SMEM_SPEC] * 4 + [VMEM_SPEC]
-        )(place, shear_rate, weight, bias, shifted)
+        if away == SAVER:
+            drawn, species_out = call(
+                functools.partial(render_and_save, away),
+                (image, jax.ShapeDtypeStruct(species.shape, F32)),
+                [SMEM_SPEC] * 4 + [VMEM_SPEC],
+                [pltpu.SemaphoreType.DMA((1,))],
+                out_specs=(VMEM_SPEC, HBM_SPEC),
+            )(place, shear_rate, weight, bias, shifted)
+        else:
+            drawn = call(
+                functools.partial(render, away), image, [SMEM_SPEC] * 4 + [VMEM_SPEC]
+            )(place, shear_rate, weight, bias, shifted)
         if away:
             drawn = turn_by(drawn, "depth", away)
         slabs[away] = drawn

time: 99.2 us -> 97.9 us (0.987)
  Pallas kernels: 27.6 us -> 26.3 us
    pallas_call x4 -> x3, Pallas kernels: 9.66 us -> 7.25 us  [body(): call(functools.partial(render, away), image, [SMEM_SPEC] * 4 + [VMEM_SPEC])]
    pallas_call x1 -> x2, Pallas kernels: 5.02 us -> 6.76 us  [the longest x1 4.33 us: body(): call(advance_edges, shifted_type, [SMEM_SPEC] + [VMEM_SPEC] * 6, [pltpu.V...]
where the time goes in v6:
time: 97.9 us; the launch traced here: 96.3 us
  blocking collectives  33.6 us (34%)
  starting transfers between devices  26.8 us (27%)
  Pallas kernels  26.3 us (27%)
  waiting for transfers between devices  8.72 us (9%)
    all_to_all x1, blocking collectives, body(): lax.all_to_all(outgoing.reshape(col_devices, -1, 1152), 'col', split_axis...  33.6 us
    ppermute x5, starting transfers between devices, turn_by(): return lax.ppermute(x, axis, [(i, (i + steps) % n) for i in range(n)])  15.1 us
    ppermute x5, waiting for transfers between devices, turn_by(): return lax.ppermute(x, axis, [(i, (i + steps) % n) for i in range(n)])  7.76 us
    pallas_call x3, Pallas kernels, body(): call(functools.partial(render, away), image, [SMEM_SPEC] * 4 + [VMEM_SPEC])  7.25 us
    ppermute x2, starting transfers between devices, shift_down(): return lax.ppermute(x, axis, [(i + 1, i) for i in range(n - 1)])  5.85 us
    ppermute x2, starting transfers between devices, shift_up(): return lax.ppermute(x, axis, [(i, i + 1) for i in range(n - 1)])  5.84 us
    pallas_call x1, Pallas kernels, body(): call(advance_own, (shifted_type, jax.ShapeDtypeStruct((16, 2 * LINES), F3...  5.2 us
    pallas_call x1, Pallas kernels, body(): call(advance_edges, shifted_type, [SMEM_SPEC] + [VMEM_SPEC] * 6, [pltpu.V...  4.33 us
  transfers between devices with their start and end apart: 9, of which 5 were waited for; matrix products, arithmetic and copies ran while one was open for 0% of the time, Pallas kernels for 11%

profile of v6, /device:TPU:6, one launch (start us, length us, event | category | flops | bytes accessed | tf_op | source)
XLA Modules:
  0.0 96.3 jit_solution(14630829749964373113)
XLA Ops:
  0.6 1.1 %shard_map.114 = (bf16[4,3,32,128]{3,2,1,0:T(8,128)(2,1)S(1)}, bf16[4,3,32,128]{3,2,1,0:T(8,128)(2,1)S(1)}) custom-call(f32[2,16,32,128]{3,2,1,0:T(8,128)} %species.3, f32[16,32,128]{2,1,0:T(8,128)} %diff.3, f32[16,32,128]{2,1,0:T(8,128)} %rate.3), custom_call_target="tpu_custom_call" | custom-call | tf_op jit(solution)/shard_map/pallas_call | solution.py:506
  1.7 1.3 %collective-permute-start = (bf16[4,3,32,128]{3,2,1,0:T(8,128)(2,1)S(1)}, bf16[4,3,32,128]{3,2,1,0:T(8,128)(2,1)S(1)}, u32[]{:S(2)}, u32[]{:S(2)}) collective-permute-start(bf16[4,3,32,128]{3,2,1,0:T(8,128)(2,1)S(1)} %get-tuple-element.21), channel_id=1, source_target_pairs={{0,128},{128,256},{256,384},{1,129},{129,257},{257,385},{2,130},{1... | collective-permute-start | bytes 294920 | tf_op jit(solution)/shard_map/ppermute | solution.py:60
  3.0 0.0 copy-start.3
  3.0 0.0 copy-start.4
  3.0 4.6 %collective-permute-start.1 = (bf16[4,3,32,128]{3,2,1,0:T(8,128)(2,1)S(1)}, bf16[4,3,32,128]{3,2,1,0:T(8,128)(2,1)S(1)}, u32[]{:S(2)}, u32[]{:S(2)}) collective-permute-start(bf16[4,3,32,128]{3,2,1,0:T(8,128)(2,1)S(1)} %get-tuple-element.22), channel_id=1, source_target_pairs={{128,0},{256,128},{384,256},{129,1},{257,129},{385,257},{130,2},{2... | collective-permute-start | bytes 294920 | tf_op jit(solution)/shard_map/ppermute | solution.py:65
  7.6 1.2 %shard_map.113.unused = f32[4,22,40,128]{3,2,1,0:T(8,128)S(1)} custom-call(f32[2,16,32,128]{3,2,1,0:T(8,128)} %species.3, f32[16,32,128]{2,1,0:T(8,128)} %diff.3, f32[16,32,128]{2,1,0:T(8,128)} %rate.3), custom_call_target="tpu_custom_call" | custom-call | tf_op jit(solution)/shard_map/pallas_call | solution.py:514
  8.8 0.0 collective-permute-done.before
  8.8 0.9 collective-permute-done.1.after
  9.8 0.1 shard_map.115
  9.8 0.0 collective-permute-start.2
  9.9 2.9 %collective-permute-start.3 = (bf16[3,88,128]{2,1,0:T(8,128)(2,1)S(1)}, bf16[3,88,128]{2,1,0:T(8,128)(2,1)S(1)}, u32[]{:S(2)}, u32[]{:S(2)}) collective-permute-start(bf16[3,88,128]{2,1,0:T(8,128)(2,1)S(1)} %get-tuple-element.29), channel_id=1, source_target_pairs={{0,112},{16,0},{32,16},{48,32},{64,48},{80,64},{96,80},{112,96},{1... | collective-permute-start | bytes 202760 | tf_op jit(solution)/shard_map/ppermute | solution.py:55
  12.8 0.1 stack.15.place
  12.9 0.0 copy-done.3
  12.9 0.0 copy-done.4
  12.9 1.5 %shard_map.116 = (bf16[256,128]{1,0:T(8,128)(2,1)S(1)}, s32[128,128]{1,0:T(8,128)S(1)}, bf16[4,128,128]{2,1,0:T(8,128)(2,1)S(1)}) custom-call(s32[6]{0:T(128)S(1)} %stack.15.place, s32[4,32]{1,0:T(4,128)S(1)} %bitcast.21, s32[4,32]{1,0:T(4,128)S(1)} %bitcast.22, bf16[16,128,128]{2,1,0:T(8,128)(2,1)} %warp.1), custom_call_target="tpu_custom_call" | custom-call | tf_op jit(solution)/shard_map/pallas_call | solution.py:522
  14.4 0.4 collective-permute-done.2.above
  14.8 0.0 collective-permute-done.3.below
  14.8 0.9 shard_map.117
  15.7 1.3 %collective-permute-start.5 = (bf16[8,3584]{1,0:T(8,128)(2,1)S(1)}, bf16[8,3584]{1,0:T(8,128)(2,1)S(1)}, u32[]{:S(2)}, u32[]{:S(2)}) collective-permute-start(bf16[8,3584]{1,0:T(8,128)(2,1)S(1)} %get-tuple-element.33.low), channel_id=1, source_target_pairs={{1,0},{2,1},{3,2},{4,3},{5,4},{6,5},{7,6},{8,7},{9,8},{10,9},{11,1... | collective-permute-start | bytes 172040 | tf_op jit(solution)/shard_map/ppermute | solution.py:65
  17.0 4.5 %collective-permute-start.4 = (bf16[8,3584]{1,0:T(8,128)(2,1)S(1)}, bf16[8,3584]{1,0:T(8,128)(2,1)S(1)}, u32[]{:S(2)}, u32[]{:S(2)}) collective-permute-start(bf16[8,3584]{1,0:T(8,128)(2,1)S(1)} %get-tuple-element.34.high), channel_id=1, source_target_pairs={{0,1},{1,2},{2,3},{3,4},{4,5},{5,6},{6,7},{7,8},{8,9},{9,10},{10,1... | collective-permute-start | bytes 172040 | tf_op jit(solution)/shard_map/ppermute | solution.py:60
  21.6 5.2 %shard_map.118 = (f32[7,2,16,32,128]{4,3,2,1,0:T(8,128)S(1)}, f32[16,1792]{1,0:T(8,128)S(1)}) custom-call(s32[6]{0:T(128)S(1)} %stack.15.place, f32[4,22,40,128]{3,2,1,0:T(8,128)S(1)} %get-tuple-element.30.brick), custom_call_target="tpu_custom_call" | custom-call | tf_op jit(solution)/shard_map/pallas_call | solution.py:544
  26.8 0.0 collective-permute-done.5.right
  26.8 0.0 collective-permute-done.4.left
  26.8 0.0 copy-start
  26.8 0.0 copy-start.1
  26.8 0.0 copy-start.2
  26.8 4.3 %shard_map.119.shifted = f32[7,2,16,32,128]{4,3,2,1,0:T(8,128)S(1)} custom-call(s32[6]{0:T(128)S(1)} %stack.15.place, f32[7,2,16,32,128]{4,3,2,1,0:T(8,128)S(1)} %get-tuple-element.31.unused, f32[16,1792]{1,0:T(8,128)S(1)} %get-tuple-element.32.edges, bf16[8,3584]{1,0:T(8,128)(2,1)S(1)} %get-tuple-element.33.low, ...), custom_call_target="tpu_custom_call", output_to_operand_aliasing={{}: (1, {})} | custom-call | tf_op jit(solution)/shard_map/pallas_call | solution.py:550
  31.2 0.0 copy-done
  31.2 0.0 copy-done.1
  31.2 0.0 copy-done.2
  31.2 2.4 %shard_map.123 = f32[4,4,32,128]{3,2,1,0:T(8,128)S(1)} custom-call(s32[6]{0:T(128)S(1)} %stack.15.place, f32[16]{0:T(128)S(1)} %copy-done.2, f32[4,2,16]{2,1,0:T(2,128)S(1)} %bitcast.13, f32[4,16]{1,0:T(4,128)S(1)} %bitcast.17, f32[7,2,16,32,128]{4,3,2,1,0:T(8,128)S(1)} %shard_map.119.shifted), custom_call_target="tpu_custom_call" | custom-call | tf_op jit(solution)/shard_map/pallas_call | solution.py:571
  33.6 2.4 %shard_map.122 = f32[4,4,32,128]{3,2,1,0:T(8,128)S(1)} custom-call(s32[6]{0:T(128)S(1)} %stack.15.place, f32[16]{0:T(128)S(1)} %copy-done.2, f32[4,2,16]{2,1,0:T(2,128)S(1)} %bitcast.14, f32[4,16]{1,0:T(4,128)S(1)} %bitcast.18, f32[7,2,16,32,128]{4,3,2,1,0:T(8,128)S(1)} %shard_map.119.shifted), custom_call_target="tpu_custom_call" | custom-call | tf_op jit(solution)/shard_map/pallas_call | solution.py:571
  36.0 2.4 %shard_map.120 = (f32[4,4,32,128]{3,2,1,0:T(8,128)S(1)}, f32[2,16,32,128]{3,2,1,0:T(8,128)}) custom-call(s32[6]{0:T(128)S(1)} %stack.15.place, f32[16]{0:T(128)S(1)} %copy-done.2, f32[4,2,16]{2,1,0:T(2,128)S(1)} %bitcast.15, f32[4,16]{1,0:T(4,128)S(1)} %bitcast.19, f32[7,2,16,32,128]{4,3,2,1,0:T(8,128)S(1)} %shard_map.119.shifted), custom_call_target="tpu_custom_call" | custom-call | tf_op jit(solution)/shard_map/pallas_call | solution.py:563
  38.5 0.0 copy-start.5
  38.5 7.5 %collective-permute-start.6 = (f32[4,4,32,128]{3,2,1,0:T(8,128)S(1)}, f32[4,4,32,128]{3,2,1,0:T(8,128)S(1)}, u32[]{:S(2)}, u32[]{:S(2)}) collective-permute-start(f32[4,4,32,128]{3,2,1,0:T(8,128)S(1)} %get-tuple-element.38), channel_id=1, source_target_pairs={{0,128},{128,256},{256,384},{384,0},{1,129},{129,257},{257,385},{3... | collective-permute-start | bytes 786440 | tf_op jit(solution)/shard_map/ppermute | solution.py:55
  46.0 1.9 %collective-permute-start.7 = (f32[4,4,32,128]{3,2,1,0:T(8,128)S(1)}, f32[4,4,32,128]{3,2,1,0:T(8,128)S(1)}, u32[]{:S(2)}, u32[]{:S(2)}) collective-permute-start(f32[4,4,32,128]{3,2,1,0:T(8,128)S(1)} %shard_map.122), channel_id=1, source_target_pairs={{0,256},{128,384},{256,0},{384,128},{1,257},{129,385},{257,1},{385... | collective-permute-start | bytes 786440 | tf_op jit(solution)/shard_map/ppermute | solution.py:55
  47.9 2.8 %collective-permute-start.8 = (f32[4,4,32,128]{3,2,1,0:T(8,128)S(1)}, f32[4,4,32,128]{3,2,1,0:T(8,128)S(1)}, u32[]{:S(2)}, u32[]{:S(2)}) collective-permute-start(f32[4,4,32,128]{3,2,1,0:T(8,128)S(1)} %shard_map.123), channel_id=1, source_target_pairs={{0,384},{128,0},{256,128},{384,256},{1,385},{129,1},{257,129},{385... | collective-permute-start | bytes 786440 | tf_op jit(solution)/shard_map/ppermute | solution.py:55
  50.7 2.4 %shard_map.121.slab0 = f32[4,4,32,128]{3,2,1,0:T(8,128)S(1)} custom-call(s32[6]{0:T(128)S(1)} %stack.15.place, f32[16]{0:T(128)S(1)} %copy-done.2, f32[4,2,16]{2,1,0:T(2,128)S(1)} %bitcast.16, f32[4,16]{1,0:T(4,128)S(1)} %bitcast.20, f32[7,2,16,32,128]{4,3,2,1,0:T(8,128)S(1)} %shard_map.119.shifted), custom_call_target="tpu_custom_call" | custom-call | tf_op jit(solution)/shard_map/pallas_call | solution.py:571
  53.1 2.4 %collective-permute-done.6.slab1 = f32[4,4,32,128]{3,2,1,0:T(8,128)S(1)} collective-permute-done((f32[4,4,32,128]{3,2,1,0:T(8,128)S(1)}, f32[4,4,32,128]{3,2,1,0:T(8,128)S(1)}, u32[]{:S(2)}, u32[]{:S(2)}) %collective-permute-start.6) | collective-permute-done | bytes 262176 | tf_op jit(solution)/shard_map/ppermute | solution.py:55
  55.5 1.6 %collective-permute-done.7.slab2 = f32[4,4,32,128]{3,2,1,0:T(8,128)S(1)} collective-permute-done((f32[4,4,32,128]{3,2,1,0:T(8,128)S(1)}, f32[4,4,32,128]{3,2,1,0:T(8,128)S(1)}, u32[]{:S(2)}, u32[]{:S(2)}) %collective-permute-start.7) | collective-permute-done | bytes 262176 | tf_op jit(solution)/shard_map/ppermute | solution.py:55
  57.1 3.4 %collective-permute-done.8.slab3 = f32[4,4,32,128]{3,2,1,0:T(8,128)S(1)} collective-permute-done((f32[4,4,32,128]{3,2,1,0:T(8,128)S(1)}, f32[4,4,32,128]{3,2,1,0:T(8,128)S(1)}, u32[]{:S(2)}, u32[]{:S(2)}) %collective-permute-start.8) | collective-permute-done | bytes 262176 | tf_op jit(solution)/shard_map/ppermute | solution.py:55
  60.4 0.0 copy-done.5
  60.4 1.1 %shard_map.124 = bf16[128,1152]{1,0:T(8,128)(2,1)S(1)} custom-call(s32[6]{0:T(128)S(1)} %stack.15.place, s32[4,16]{1,0:T(4,128)S(1)} %bitcast.23, bf16[256,128]{1,0:T(8,128)(2,1)S(1)} %get-tuple-element.36.select, s32[128,128]{1,0:T(8,128)S(1)} %get-tuple-element.37.lengths, f32[4,4,32,128]{3,2,1,0:T(8,128)S(1)} %shard_map.121.slab0, ...), custom_call_target="tpu_custom_call" | custom-call | tf_op jit(solution)/shard_map/pallas_call | solution.py:577
  61.5 33.6 %all_to_all.5 = bf16[16,8,1152]{2,1,0:T(8,128)(2,1)S(1)} all-to-all(bf16[16,8,1152]{2,1,0:T(8,128)(2,1)S(1)} %bitcast.11), channel_id=1, replica_groups=mesh['depth'=4,'row'=8,'col'=16] {'col'}, dimensions={0} | all-to-all | bytes 589824 | tf_op jit(solution)/shard_map/all_to_all | solution.py:583
  95.1 1.3 %shard_map.125 = f32[512,128]{1,0:T(8,128)} custom-call(bf16[128,1152]{1,0:T(8,128)(2,1)S(1)} %bitcast.12, bf16[4,128,128]{2,1,0:T(8,128)(2,1)S(1)} %get-tuple-element.39.warp), custom_call_target="tpu_custom_call" | custom-call | tf_op jit(solution)/shard_map/pallas_call | solution.py:590
Async XLA Ops:
  1.7 7.1 %collective-permute-start = (bf16[4,3,32,128]{3,2,1,0:T(8,128)(2,1)S(1)}, bf16[4,3,32,128]{3,2,1,0:T(8,128)(2,1)S(1)}, u32[]{:S(2)}, u32[]{:S(2)}) collective-permute-start(bf16[4,3,32,128]{3,2,1,0:T(8,128)(2,1)S(1)} %get-tuple-element.21), channel_id=1, source_target_pairs={{0,128},{128,256},{256,384},{1,129},{129,257},{257,385},{2,130},{1... | collective-permute-start | bytes 294920 | tf_op jit(solution)/shard_map/ppermute | solution.py:60
  3.0 9.9 %copy-start.3 = (s32[4,1,32,1]{2,3,1,0:T(1,128)S(1)}, s32[4,1,32,1]{2,3,1,0:T(1,128)}, u32[]{:S(2)}) copy-start(s32[4,1,32,1]{2,3,1,0:T(1,128)} %param.18) | copy-start | bytes 1540
  3.0 9.9 %copy-start.4 = (s32[4,1,32]{2,1,0:T(1,128)S(1)}, s32[4,1,32]{2,1,0:T(1,128)}, u32[]{:S(2)}) copy-start(s32[4,1,32]{2,1,0:T(1,128)} %param.17) | copy-start | bytes 1540
  3.0 6.8 %collective-permute-start.1 = (bf16[4,3,32,128]{3,2,1,0:T(8,128)(2,1)S(1)}, bf16[4,3,32,128]{3,2,1,0:T(8,128)(2,1)S(1)}, u32[]{:S(2)}, u32[]{:S(2)}) collective-permute-start(bf16[4,3,32,128]{3,2,1,0:T(8,128)(2,1)S(1)} %get-tuple-element.22), channel_id=1, source_target_pairs={{128,0},{256,128},{384,256},{129,1},{257,129},{385,257},{130,2},{2... | collective-permute-start | bytes 294920 | tf_op jit(solution)/shard_map/ppermute | solution.py:65
  9.8 4.9 %collective-permute-start.2 = (bf16[3,88,128]{2,1,0:T(8,128)(2,1)S(1)}, bf16[3,88,128]{2,1,0:T(8,128)(2,1)S(1)}, u32[]{:S(2)}, u32[]{:S(2)}) collective-permute-start(bf16[3,88,128]{2,1,0:T(8,128)(2,1)S(1)} %get-tuple-element.28), channel_id=1, source_target_pairs={{0,16},{16,32},{32,48},{48,64},{64,80},{80,96},{96,112},{112,0},{1... | collective-permute-start | bytes 202760 | tf_op jit(solution)/shard_map/ppermute | solution.py:55
  9.9 4.9 %collective-permute-start.3 = (bf16[3,88,128]{2,1,0:T(8,128)(2,1)S(1)}, bf16[3,88,128]{2,1,0:T(8,128)(2,1)S(1)}, u32[]{:S(2)}, u32[]{:S(2)}) collective-permute-start(bf16[3,88,128]{2,1,0:T(8,128)(2,1)S(1)} %get-tuple-element.29), channel_id=1, source_target_pairs={{0,112},{16,0},{32,16},{48,32},{64,48},{80,64},{96,80},{112,96},{1... | collective-permute-start | bytes 202760 | tf_op jit(solution)/shard_map/ppermute | solution.py:55
  15.7 11.1 %collective-permute-start.5 = (bf16[8,3584]{1,0:T(8,128)(2,1)S(1)}, bf16[8,3584]{1,0:T(8,128)(2,1)S(1)}, u32[]{:S(2)}, u32[]{:S(2)}) collective-permute-start(bf16[8,3584]{1,0:T(8,128)(2,1)S(1)} %get-tuple-element.33.low), channel_id=1, source_target_pairs={{1,0},{2,1},{3,2},{4,3},{5,4},{6,5},{7,6},{8,7},{9,8},{10,9},{11,1... | collective-permute-start | bytes 172040 | tf_op jit(solution)/shard_map/ppermute | solution.py:65
  17.0 9.8 %collective-permute-start.4 = (bf16[8,3584]{1,0:T(8,128)(2,1)S(1)}, bf16[8,3584]{1,0:T(8,128)(2,1)S(1)}, u32[]{:S(2)}, u32[]{:S(2)}) collective-permute-start(bf16[8,3584]{1,0:T(8,128)(2,1)S(1)} %get-tuple-element.34.high), channel_id=1, source_target_pairs={{0,1},{1,2},{2,3},{3,4},{4,5},{5,6},{6,7},{7,8},{8,9},{9,10},{10,1... | collective-permute-start | bytes 172040 | tf_op jit(solution)/shard_map/ppermute | solution.py:60
  26.8 4.4 %copy-start = (f32[16,4,2]{0,2,1:T(2,128)S(1)}, f32[16,4,2]{0,2,1:T(2,128)}, u32[]{:S(2)}) copy-start(f32[16,4,2]{0,2,1:T(2,128)} %param.14) | copy-start | bytes 1540
  26.8 4.4 %copy-start.1 = (f32[16,4]{0,1:T(4,128)S(1)}, f32[16,4]{0,1:T(4,128)}, u32[]{:S(2)}) copy-start(f32[16,4]{0,1:T(4,128)} %param.15) | copy-start | bytes 772
  26.8 4.4 %copy-start.2 = (f32[16]{0:T(128)S(1)}, f32[16]{0:T(128)}, u32[]{:S(2)}) copy-start(f32[16]{0:T(128)} %shear.7) | copy-start | bytes 196
  38.5 22.0 %copy-start.5 = (s32[16,4]{0,1:T(4,128)S(1)}, s32[16,4]{0,1:T(4,128)}, u32[]{:S(2)}) copy-start(s32[16,4]{0,1:T(4,128)} %param.16) | copy-start | bytes 772
  38.5 17.0 %collective-permute-start.6 = (f32[4,4,32,128]{3,2,1,0:T(8,128)S(1)}, f32[4,4,32,128]{3,2,1,0:T(8,128)S(1)}, u32[]{:S(2)}, u32[]{:S(2)}) collective-permute-start(f32[4,4,32,128]{3,2,1,0:T(8,128)S(1)} %get-tuple-element.38), channel_id=1, source_target_pairs={{0,128},{128,256},{256,384},{384,0},{1,129},{129,257},{257,385},{3... | collective-permute-start | bytes 786440 | tf_op jit(solution)/shard_map/ppermute | solution.py:55
  46.0 11.1 %collective-permute-start.7 = (f32[4,4,32,128]{3,2,1,0:T(8,128)S(1)}, f32[4,4,32,128]{3,2,1,0:T(8,128)S(1)}, u32[]{:S(2)}, u32[]{:S(2)}) collective-permute-start(f32[4,4,32,128]{3,2,1,0:T(8,128)S(1)} %shard_map.122), channel_id=1, source_target_pairs={{0,256},{128,384},{256,0},{384,128},{1,257},{129,385},{257,1},{385... | collective-permute-start | bytes 786440 | tf_op jit(solution)/shard_map/ppermute | solution.py:55
  47.9 12.5 %collective-permute-start.8 = (f32[4,4,32,128]{3,2,1,0:T(8,128)S(1)}, f32[4,4,32,128]{3,2,1,0:T(8,128)S(1)}, u32[]{:S(2)}, u32[]{:S(2)}) collective-permute-start(f32[4,4,32,128]{3,2,1,0:T(8,128)S(1)} %shard_map.123), channel_id=1, source_target_pairs={{0,384},{128,0},{256,128},{384,256},{1,385},{129,1},{257,129},{385... | collective-permute-start | bytes 786440 | tf_op jit(solution)/shard_map/ppermute | solution.py:55

commit v7 on v6

--- a/solution.py
+++ b/solution.py
@@ -137,28 +137,36 @@
             side[:, at + count : at + LINES] = blank
 
 
-def slope_of(fields, diffusivity, reaction, neighbours):
+def coefficients(step, diffusivity, reaction):
+    spread = step * diffusivity
+    return (
+        1.0 - (6.0 * spread + (VEL_DEPTH + VEL_ROW + VEL_COL) * step),
+        spread + VEL_DEPTH * step,
+        spread + VEL_ROW * step,
+        spread + VEL_COL * step,
+        spread,
+        step * reaction,
+    )
+
+
+def stepped(fields, coefs, neighbours):
     fuel, heat = fields
+    cell, from_depth, from_row, from_col, from_above, reaction = coefs
     square = heat * heat
-    burned = reaction * fuel * square / (1.0 + square)
-    slopes = []
+    burned = reaction * (fuel * (square / (1.0 + square)))
+    results = []
     for f in range(2):
-        centre = fields[f]
         below_depth, above_depth, below_row, above_row, below_col, above_col = neighbours(f)
-        laplace = (
-            below_depth + above_depth + below_row + above_row + below_col + above_col - 6.0 * centre
+        total = (
+            (cell * fields[f] + from_depth * below_depth)
+            + (from_row * below_row + from_col * below_col)
+            + from_above * (above_depth + above_row + above_col)
         )
-        advect = (
-            VEL_DEPTH * (centre - below_depth)
-            + VEL_ROW * (centre - below_row)
-            + VEL_COL * (centre - below_col)
-        )
-        gain = -burned if f == 0 else burned
-        slopes.append(diffusivity * laplace - advect + gain)
-    return slopes
-
-
-def advance_own(place, brick, shifted, edges, first, second):
+        results.append(total - burned if f == 0 else total + burned)
+    return results
+
+
+def advance_own(place, brick, shifted, edges, first, second, coefs):
     n = ROWS
     depth_at, row_at = place[0], place[1]
     depth_last, row_last = place[3], place[4]
@@ -170,7 +178,7 @@
     )
     step = jnp.where(rows_in, TIME_STEP, 0.0).astype(F32)
 
-    def tendency(source, p):
+    def advanced(source, table, p):
         def neighbours(f):
             centre = source[f, p]
             return (
@@ -182,34 +190,44 @@
                 pltpu.roll(centre, 127, 1),
             )
 
-        return slope_of((source[0, p], source[1, p]), brick[2, p], brick[3, p], neighbours)
-
-    def inside(p):
+        return stepped((source[0, p], source[1, p]), table, neighbours)
+
+    def table_at(p):
+        return tuple(coefs[i, p] for i in range(6))
+
+    @pl.loop(1, 21, unroll=4)
+    def _(p):
         ok = ((p >= HALO) | (depth_at > 0)) & ((p < HALO + 16) | (depth_at < depth_last))
-        return jnp.where(ok, 1.0, 0.0).astype(F32)
-
-    @pl.loop(1, 21, unroll=2)
+        scale = jnp.where(ok, 1.0, 0.0).astype(F32)
+        table = coefficients(step * scale, brick[2, p], brick[3, p])
+        for i in range(6):
+            coefs[i, p] = table[i]
+        moved = advanced(brick, table, p)
+        for f in range(2):
+            first[f, p] = moved[f]
+
+    @pl.loop(2, 20, unroll=3)
     def _(p):
-        slope = tendency(brick, p)
-        scale = inside(p)
+        moved = advanced(first, table_at(p), p)
         for f in range(2):
-            first[f, p] = brick[f, p] + (step * scale) * slope[f]
-
-    @pl.loop(2, 20, unroll=2)
-    def _(p):
-        slope = tendency(first, p)
-        scale = inside(p)
+            second[f, p] = 0.75 * brick[f, p] + 0.25 * moved[f]
+
+    def shift_plane(k):
         for f in range(2):
-            second[f, p] = 0.75 * brick[f, p] + 0.25 * (first[f, p] + (step * scale) * slope[f])
-
-    @pl.loop(3, 19, unroll=2)
-    def _(p):
-        slope = tendency(second, p)
-        k = p - HALO
+            new = shifted[RIM, f, k]
+            for shift in range(-RIM, RIM + 1):
+                if shift:
+                    shifted[shift + RIM, f, k] = pltpu.roll(new, -shift % 128, 1)
+
+    @pl.loop(0, 16, unroll=2)
+    def _(k):
+        p = k + HALO
+        shift_plane(jnp.maximum(k - 1, 0))
+        moved = advanced(second, table_at(p), p)
         for f in range(2):
-            new = (brick[f, p] / 3.0 + (2.0 / 3.0) * (second[f, p] + step * slope[f]))[:32]
-            for shift in range(-RIM, RIM + 1):
-                shifted[shift + RIM, f, k] = pltpu.roll(new, -shift % 128, 1) if shift else new
+            shifted[RIM, f, k] = (brick[f, p] * (1.0 / 3.0) + (2.0 / 3.0) * moved[f])[:32]
+
+    shift_plane(15)
 
     pick = column_picker(0, 128 - EDGE)
     count = PLANES * ROWS
@@ -266,7 +284,14 @@
             if f < 2:
                 start[f, b] = gathered
             else:
-                coefs[f - 2, b] = gathered
+                first[f - 2, b] = gathered
+    masks = []
+    for b in range(BLOCKS):
+        step, first_row, last_row = table(b)
+        masks.append((first_row, last_row))
+        made = coefficients(step, first[0, b], first[1, b])
+        for i in range(6):
+            coefs[i, b] = made[i]
 
     def stage(source, finish):
         held = {}
@@ -284,7 +309,7 @@
             return jnp.where(lane >= 128 - by, turn(f, b + 1, 128 - by), turn(f, b, 128 - by))
 
         for b in range(BLOCKS):
-            step, first_row, last_row = table(b)
+            first_row, last_row = masks[b]
 
             def neighbours(f):
                 x = source[f, b]
@@ -297,20 +322,22 @@
                     pltpu.roll(x, 4 * EDGE - 1, 0),
                 )
 
-            slope = slope_of((source[0, b], source[1, b]), coefs[0, b], coefs[1, b], neighbours)
+            moved = stepped(
+                (source[0, b], source[1, b]), tuple(coefs[i, b] for i in range(6)), neighbours
+            )
             for f in range(2):
-                finish(f, b, step * slope[f])
-
-    def finish_first(f, b, change):
-        first[f, b] = start[f, b] + change
-
-    def finish_second(f, b, change):
-        second[f, b] = 0.75 * start[f, b] + 0.25 * (first[f, b] + change)
+                finish(f, b, moved[f])
+
+    def finish_first(f, b, moved):
+        first[f, b] = moved
+
+    def finish_second(f, b, moved):
+        second[f, b] = 0.75 * start[f, b] + 0.25 * moved
 
     blank = jnp.zeros((128 - 4 * EDGE, 128), F32)
 
-    def finish_third(f, b, change):
-        new = start[f, b] / 3.0 + (2.0 / 3.0) * (second[f, b] + change)
+    def finish_third(f, b, moved):
+        new = start[f, b] * (1.0 / 3.0) + (2.0 / 3.0) * moved
         turned[f, 128 * b : 128 * (b + 1), :] = jnp.concatenate([new, blank], axis=0).T
 
     stage(start, finish_first)
@@ -318,7 +345,7 @@
     stage(second, finish_third)
     lane32 = lax.broadcasted_iota(jnp.int32, (32, 128), 1)
 
-    @pl.loop(0, 16, unroll=2)
+    @pl.loop(0, 16, unroll=4)
     def _(k):
         for f in range(2):
             lines = turned[f, pl.ds(pl.multiple_of((k + HALO) * ROWS, 8), 32), :]
@@ -545,13 +572,15 @@
         advance_own,
         (shifted_type, jax.ShapeDtypeStruct((16, 2 * LINES), F32)),
         [SMEM_SPEC, VMEM_SPEC],
-        [wide, wide],
+        [wide, wide, pltpu.VMEM((6, PLANES, ROWS, 128), F32)],
+        limit=12,
     )(place, brick)
     shifted = call(
         advance_edges,
         shifted_type,
         [SMEM_SPEC] + [VMEM_SPEC] * 6,
-        [pltpu.VMEM((2, BLOCKS, 4 * EDGE, 128), F32)] * 4 + [pltpu.VMEM((2, LINES, 128), F32)],
+        [pltpu.VMEM((n, BLOCKS, 4 * EDGE, 128), F32) for n in (2, 6, 2, 2)]
+        + [pltpu.VMEM((2, LINES, 128), F32)],
         aliases={1: 0},
     )(place, shifted, edges, low, high, left, right)
 

time: 97.9 us -> 97.7 us (level)
  transfers between devices with their start and end apart: 9 -> 9, of which waited for: 5 -> 5; matrix products, arithmetic and copies ran while one was open for 0% -> 0% of each run, Pallas kernels for 11% -> 10%
where the time goes in v7:
time: 97.7 us; the launch traced here: 96.1 us
  blocking collectives  33.6 us (34%)
  starting transfers between devices  26.8 us (27%)
  Pallas kernels  26.1 us (27%)
  waiting for transfers between devices  8.71 us (9%)
    all_to_all x1, blocking collectives, body(): lax.all_to_all(outgoing.reshape(col_devices, -1, 1152), 'col', split_axis...  33.6 us
    ppermute x5, starting transfers between devices, turn_by(): return lax.ppermute(x, axis, [(i, (i + steps) % n) for i in range(n)])  15.1 us
    ppermute x5, waiting for transfers between devices, turn_by(): return lax.ppermute(x, axis, [(i, (i + steps) % n) for i in range(n)])  7.76 us
    pallas_call x3, Pallas kernels, body(): call(functools.partial(render, away), image, [SMEM_SPEC] * 4 + [VMEM_SPEC])  7.25 us
    ppermute x2, starting transfers between devices, shift_down(): return lax.ppermute(x, axis, [(i + 1, i) for i in range(n - 1)])  5.85 us
    ppermute x2, starting transfers between devices, shift_up(): return lax.ppermute(x, axis, [(i, i + 1) for i in range(n - 1)])  5.84 us
    pallas_call x1, Pallas kernels, body(): call(advance_own, (shifted_type, jax.ShapeDtypeStruct((16, 2 * LINES), F3...  4.7 us
    pallas_call x1, Pallas kernels, body(): call(advance_edges, shifted_type, [SMEM_SPEC] + [VMEM_SPEC] * 6, [pltpu.V...  4.62 us
  transfers between devices with their start and end apart: 9, of which 5 were waited for; matrix products, arithmetic and copies ran while one was open for 0% of the time, Pallas kernels for 10%

profile of v7, /device:TPU:6, one launch (start us, length us, event | category | flops | bytes accessed | tf_op | source)
XLA Modules:
  0.0 96.1 jit_solution(3295734496230064506)
XLA Ops:
  0.6 1.1 %shard_map.114 = (bf16[4,3,32,128]{3,2,1,0:T(8,128)(2,1)S(1)}, bf16[4,3,32,128]{3,2,1,0:T(8,128)(2,1)S(1)}) custom-call(f32[2,16,32,128]{3,2,1,0:T(8,128)} %species.3, f32[16,32,128]{2,1,0:T(8,128)} %diff.3, f32[16,32,128]{2,1,0:T(8,128)} %rate.3), custom_call_target="tpu_custom_call" | custom-call | tf_op jit(solution)/shard_map/pallas_call | solution.py:533
  1.7 1.3 %collective-permute-start = (bf16[4,3,32,128]{3,2,1,0:T(8,128)(2,1)S(1)}, bf16[4,3,32,128]{3,2,1,0:T(8,128)(2,1)S(1)}, u32[]{:S(2)}, u32[]{:S(2)}) collective-permute-start(bf16[4,3,32,128]{3,2,1,0:T(8,128)(2,1)S(1)} %get-tuple-element.21), channel_id=1, source_target_pairs={{0,128},{128,256},{256,384},{1,129},{129,257},{257,385},{2,130},{1... | collective-permute-start | bytes 294920 | tf_op jit(solution)/shard_map/ppermute | solution.py:60
  3.0 0.0 copy-start.3
  3.0 0.0 copy-start.4
  3.0 4.6 %collective-permute-start.1 = (bf16[4,3,32,128]{3,2,1,0:T(8,128)(2,1)S(1)}, bf16[4,3,32,128]{3,2,1,0:T(8,128)(2,1)S(1)}, u32[]{:S(2)}, u32[]{:S(2)}) collective-permute-start(bf16[4,3,32,128]{3,2,1,0:T(8,128)(2,1)S(1)} %get-tuple-element.22), channel_id=1, source_target_pairs={{128,0},{256,128},{384,256},{129,1},{257,129},{385,257},{130,2},{2... | collective-permute-start | bytes 294920 | tf_op jit(solution)/shard_map/ppermute | solution.py:65
  7.6 1.2 %shard_map.113.unused = f32[4,22,40,128]{3,2,1,0:T(8,128)S(1)} custom-call(f32[2,16,32,128]{3,2,1,0:T(8,128)} %species.3, f32[16,32,128]{2,1,0:T(8,128)} %diff.3, f32[16,32,128]{2,1,0:T(8,128)} %rate.3), custom_call_target="tpu_custom_call" | custom-call | tf_op jit(solution)/shard_map/pallas_call | solution.py:541
  8.8 0.0 collective-permute-done.before
  8.8 0.9 collective-permute-done.1.after
  9.8 0.1 shard_map.115
  9.8 0.0 collective-permute-start.2
  9.9 2.9 %collective-permute-start.3 = (bf16[3,88,128]{2,1,0:T(8,128)(2,1)S(1)}, bf16[3,88,128]{2,1,0:T(8,128)(2,1)S(1)}, u32[]{:S(2)}, u32[]{:S(2)}) collective-permute-start(bf16[3,88,128]{2,1,0:T(8,128)(2,1)S(1)} %get-tuple-element.29), channel_id=1, source_target_pairs={{0,112},{16,0},{32,16},{48,32},{64,48},{80,64},{96,80},{112,96},{1... | collective-permute-start | bytes 202760 | tf_op jit(solution)/shard_map/ppermute | solution.py:55
  12.8 0.1 stack.15.place
  12.9 0.0 copy-done.3
  12.9 0.0 copy-done.4
  12.9 1.5 %shard_map.116 = (bf16[256,128]{1,0:T(8,128)(2,1)S(1)}, s32[128,128]{1,0:T(8,128)S(1)}, bf16[4,128,128]{2,1,0:T(8,128)(2,1)S(1)}) custom-call(s32[6]{0:T(128)S(1)} %stack.15.place, s32[4,32]{1,0:T(4,128)S(1)} %bitcast.21, s32[4,32]{1,0:T(4,128)S(1)} %bitcast.22, bf16[16,128,128]{2,1,0:T(8,128)(2,1)} %warp.1), custom_call_target="tpu_custom_call" | custom-call | tf_op jit(solution)/shard_map/pallas_call | solution.py:549
  14.4 0.4 collective-permute-done.2.above
  14.8 0.0 collective-permute-done.3.below
  14.8 0.9 shard_map.117
  15.7 1.3 %collective-permute-start.5 = (bf16[8,3584]{1,0:T(8,128)(2,1)S(1)}, bf16[8,3584]{1,0:T(8,128)(2,1)S(1)}, u32[]{:S(2)}, u32[]{:S(2)}) collective-permute-start(bf16[8,3584]{1,0:T(8,128)(2,1)S(1)} %get-tuple-element.33.low), channel_id=1, source_target_pairs={{1,0},{2,1},{3,2},{4,3},{5,4},{6,5},{7,6},{8,7},{9,8},{10,9},{11,1... | collective-permute-start | bytes 172040 | tf_op jit(solution)/shard_map/ppermute | solution.py:65
  17.0 4.5 %collective-permute-start.4 = (bf16[8,3584]{1,0:T(8,128)(2,1)S(1)}, bf16[8,3584]{1,0:T(8,128)(2,1)S(1)}, u32[]{:S(2)}, u32[]{:S(2)}) collective-permute-start(bf16[8,3584]{1,0:T(8,128)(2,1)S(1)} %get-tuple-element.34.high), channel_id=1, source_target_pairs={{0,1},{1,2},{2,3},{3,4},{4,5},{5,6},{6,7},{7,8},{8,9},{9,10},{10,1... | collective-permute-start | bytes 172040 | tf_op jit(solution)/shard_map/ppermute | solution.py:60
  21.6 4.7 %shard_map.118 = (f32[7,2,16,32,128]{4,3,2,1,0:T(8,128)S(1)}, f32[16,1792]{1,0:T(8,128)S(1)}) custom-call(s32[6]{0:T(128)S(1)} %stack.15.place, f32[4,22,40,128]{3,2,1,0:T(8,128)S(1)} %get-tuple-element.30.brick), custom_call_target="tpu_custom_call" | custom-call | tf_op jit(solution)/shard_map/pallas_call | solution.py:571
  26.3 0.0 collective-permute-done.5.right
  26.3 0.0 collective-permute-done.4.left
  26.3 0.0 copy-start
  26.3 0.0 copy-start.1
  26.3 0.0 copy-start.2
  26.3 4.6 %shard_map.119.shifted = f32[7,2,16,32,128]{4,3,2,1,0:T(8,128)S(1)} custom-call(s32[6]{0:T(128)S(1)} %stack.15.place, f32[7,2,16,32,128]{4,3,2,1,0:T(8,128)S(1)} %get-tuple-element.31.unused, f32[16,1792]{1,0:T(8,128)S(1)} %get-tuple-element.32.edges, bf16[8,3584]{1,0:T(8,128)(2,1)S(1)} %get-tuple-element.33.low, ...), custom_call_target="tpu_custom_call", output_to_operand_aliasing={{}: (1, {})} | custom-call | tf_op jit(solution)/shard_map/pallas_call | solution.py:578
  31.0 0.0 copy-done
  31.0 0.0 copy-done.1
  31.0 0.0 copy-done.2
  31.0 2.4 %shard_map.123 = f32[4,4,32,128]{3,2,1,0:T(8,128)S(1)} custom-call(s32[6]{0:T(128)S(1)} %stack.15.place, f32[16]{0:T(128)S(1)} %copy-done.2, f32[4,2,16]{2,1,0:T(2,128)S(1)} %bitcast.13, f32[4,16]{1,0:T(4,128)S(1)} %bitcast.17, f32[7,2,16,32,128]{4,3,2,1,0:T(8,128)S(1)} %shard_map.119.shifted), custom_call_target="tpu_custom_call" | custom-call | tf_op jit(solution)/shard_map/pallas_call | solution.py:600
  33.4 2.4 %shard_map.122 = f32[4,4,32,128]{3,2,1,0:T(8,128)S(1)} custom-call(s32[6]{0:T(128)S(1)} %stack.15.place, f32[16]{0:T(128)S(1)} %copy-done.2, f32[4,2,16]{2,1,0:T(2,128)S(1)} %bitcast.14, f32[4,16]{1,0:T(4,128)S(1)} %bitcast.18, f32[7,2,16,32,128]{4,3,2,1,0:T(8,128)S(1)} %shard_map.119.shifted), custom_call_target="tpu_custom_call" | custom-call | tf_op jit(solution)/shard_map/pallas_call | solution.py:600
  35.8 2.4 %shard_map.120 = (f32[4,4,32,128]{3,2,1,0:T(8,128)S(1)}, f32[2,16,32,128]{3,2,1,0:T(8,128)}) custom-call(s32[6]{0:T(128)S(1)} %stack.15.place, f32[16]{0:T(128)S(1)} %copy-done.2, f32[4,2,16]{2,1,0:T(2,128)S(1)} %bitcast.15, f32[4,16]{1,0:T(4,128)S(1)} %bitcast.19, f32[7,2,16,32,128]{4,3,2,1,0:T(8,128)S(1)} %shard_map.119.shifted), custom_call_target="tpu_custom_call" | custom-call | tf_op jit(solution)/shard_map/pallas_call | solution.py:592
  38.3 0.0 copy-start.5
  38.3 7.5 %collective-permute-start.6 = (f32[4,4,32,128]{3,2,1,0:T(8,128)S(1)}, f32[4,4,32,128]{3,2,1,0:T(8,128)S(1)}, u32[]{:S(2)}, u32[]{:S(2)}) collective-permute-start(f32[4,4,32,128]{3,2,1,0:T(8,128)S(1)} %get-tuple-element.38), channel_id=1, source_target_pairs={{0,128},{128,256},{256,384},{384,0},{1,129},{129,257},{257,385},{3... | collective-permute-start | bytes 786440 | tf_op jit(solution)/shard_map/ppermute | solution.py:55
  45.8 1.9 %collective-permute-start.7 = (f32[4,4,32,128]{3,2,1,0:T(8,128)S(1)}, f32[4,4,32,128]{3,2,1,0:T(8,128)S(1)}, u32[]{:S(2)}, u32[]{:S(2)}) collective-permute-start(f32[4,4,32,128]{3,2,1,0:T(8,128)S(1)} %shard_map.122), channel_id=1, source_target_pairs={{0,256},{128,384},{256,0},{384,128},{1,257},{129,385},{257,1},{385... | collective-permute-start | bytes 786440 | tf_op jit(solution)/shard_map/ppermute | solution.py:55
  47.7 2.8 %collective-permute-start.8 = (f32[4,4,32,128]{3,2,1,0:T(8,128)S(1)}, f32[4,4,32,128]{3,2,1,0:T(8,128)S(1)}, u32[]{:S(2)}, u32[]{:S(2)}) collective-permute-start(f32[4,4,32,128]{3,2,1,0:T(8,128)S(1)} %shard_map.123), channel_id=1, source_target_pairs={{0,384},{128,0},{256,128},{384,256},{1,385},{129,1},{257,129},{385... | collective-permute-start | bytes 786440 | tf_op jit(solution)/shard_map/ppermute | solution.py:55
  50.5 2.4 %shard_map.121.slab0 = f32[4,4,32,128]{3,2,1,0:T(8,128)S(1)} custom-call(s32[6]{0:T(128)S(1)} %stack.15.place, f32[16]{0:T(128)S(1)} %copy-done.2, f32[4,2,16]{2,1,0:T(2,128)S(1)} %bitcast.16, f32[4,16]{1,0:T(4,128)S(1)} %bitcast.20, f32[7,2,16,32,128]{4,3,2,1,0:T(8,128)S(1)} %shard_map.119.shifted), custom_call_target="tpu_custom_call" | custom-call | tf_op jit(solution)/shard_map/pallas_call | solution.py:600
  52.9 2.4 %collective-permute-done.6.slab1 = f32[4,4,32,128]{3,2,1,0:T(8,128)S(1)} collective-permute-done((f32[4,4,32,128]{3,2,1,0:T(8,128)S(1)}, f32[4,4,32,128]{3,2,1,0:T(8,128)S(1)}, u32[]{:S(2)}, u32[]{:S(2)}) %collective-permute-start.6) | collective-permute-done | bytes 262176 | tf_op jit(solution)/shard_map/ppermute | solution.py:55
  55.3 1.6 %collective-permute-done.7.slab2 = f32[4,4,32,128]{3,2,1,0:T(8,128)S(1)} collective-permute-done((f32[4,4,32,128]{3,2,1,0:T(8,128)S(1)}, f32[4,4,32,128]{3,2,1,0:T(8,128)S(1)}, u32[]{:S(2)}, u32[]{:S(2)}) %collective-permute-start.7) | collective-permute-done | bytes 262176 | tf_op jit(solution)/shard_map/ppermute | solution.py:55
  56.9 3.4 %collective-permute-done.8.slab3 = f32[4,4,32,128]{3,2,1,0:T(8,128)S(1)} collective-permute-done((f32[4,4,32,128]{3,2,1,0:T(8,128)S(1)}, f32[4,4,32,128]{3,2,1,0:T(8,128)S(1)}, u32[]{:S(2)}, u32[]{:S(2)}) %collective-permute-start.8) | collective-permute-done | bytes 262176 | tf_op jit(solution)/shard_map/ppermute | solution.py:55
  60.2 0.0 copy-done.5
  60.2 1.1 %shard_map.124 = bf16[128,1152]{1,0:T(8,128)(2,1)S(1)} custom-call(s32[6]{0:T(128)S(1)} %stack.15.place, s32[4,16]{1,0:T(4,128)S(1)} %bitcast.23, bf16[256,128]{1,0:T(8,128)(2,1)S(1)} %get-tuple-element.36.select, s32[128,128]{1,0:T(8,128)S(1)} %get-tuple-element.37.lengths, f32[4,4,32,128]{3,2,1,0:T(8,128)S(1)} %shard_map.121.slab0, ...), custom_call_target="tpu_custom_call" | custom-call | tf_op jit(solution)/shard_map/pallas_call | solution.py:606
  61.3 33.6 %all_to_all.5 = bf16[16,8,1152]{2,1,0:T(8,128)(2,1)S(1)} all-to-all(bf16[16,8,1152]{2,1,0:T(8,128)(2,1)S(1)} %bitcast.11), channel_id=1, replica_groups=mesh['depth'=4,'row'=8,'col'=16] {'col'}, dimensions={0} | all-to-all | bytes 589824 | tf_op jit(solution)/shard_map/all_to_all | solution.py:612
  94.9 1.3 %shard_map.125 = f32[512,128]{1,0:T(8,128)} custom-call(bf16[128,1152]{1,0:T(8,128)(2,1)S(1)} %bitcast.12, bf16[4,128,128]{2,1,0:T(8,128)(2,1)S(1)} %get-tuple-element.39.warp), custom_call_target="tpu_custom_call" | custom-call | tf_op jit(solution)/shard_map/pallas_call | solution.py:619
Async XLA Ops:
  1.7 7.1 %collective-permute-start = (bf16[4,3,32,128]{3,2,1,0:T(8,128)(2,1)S(1)}, bf16[4,3,32,128]{3,2,1,0:T(8,128)(2,1)S(1)}, u32[]{:S(2)}, u32[]{:S(2)}) collective-permute-start(bf16[4,3,32,128]{3,2,1,0:T(8,128)(2,1)S(1)} %get-tuple-element.21), channel_id=1, source_target_pairs={{0,128},{128,256},{256,384},{1,129},{129,257},{257,385},{2,130},{1... | collective-permute-start | bytes 294920 | tf_op jit(solution)/shard_map/ppermute | solution.py:60
  3.0 9.9 %copy-start.3 = (s32[4,1,32,1]{2,3,1,0:T(1,128)S(1)}, s32[4,1,32,1]{2,3,1,0:T(1,128)}, u32[]{:S(2)}) copy-start(s32[4,1,32,1]{2,3,1,0:T(1,128)} %param.18) | copy-start | bytes 1540
  3.0 9.9 %copy-start.4 = (s32[4,1,32]{2,1,0:T(1,128)S(1)}, s32[4,1,32]{2,1,0:T(1,128)}, u32[]{:S(2)}) copy-start(s32[4,1,32]{2,1,0:T(1,128)} %param.17) | copy-start | bytes 1540
  3.0 6.8 %collective-permute-start.1 = (bf16[4,3,32,128]{3,2,1,0:T(8,128)(2,1)S(1)}, bf16[4,3,32,128]{3,2,1,0:T(8,128)(2,1)S(1)}, u32[]{:S(2)}, u32[]{:S(2)}) collective-permute-start(bf16[4,3,32,128]{3,2,1,0:T(8,128)(2,1)S(1)} %get-tuple-element.22), channel_id=1, source_target_pairs={{128,0},{256,128},{384,256},{129,1},{257,129},{385,257},{130,2},{2... | collective-permute-start | bytes 294920 | tf_op jit(solution)/shard_map/ppermute | solution.py:65
  9.8 4.9 %collective-permute-start.2 = (bf16[3,88,128]{2,1,0:T(8,128)(2,1)S(1)}, bf16[3,88,128]{2,1,0:T(8,128)(2,1)S(1)}, u32[]{:S(2)}, u32[]{:S(2)}) collective-permute-start(bf16[3,88,128]{2,1,0:T(8,128)(2,1)S(1)} %get-tuple-element.28), channel_id=1, source_target_pairs={{0,16},{16,32},{32,48},{48,64},{64,80},{80,96},{96,112},{112,0},{1... | collective-permute-start | bytes 202760 | tf_op jit(solution)/shard_map/ppermute | solution.py:55
  9.9 4.9 %collective-permute-start.3 = (bf16[3,88,128]{2,1,0:T(8,128)(2,1)S(1)}, bf16[3,88,128]{2,1,0:T(8,128)(2,1)S(1)}, u32[]{:S(2)}, u32[]{:S(2)}) collective-permute-start(bf16[3,88,128]{2,1,0:T(8,128)(2,1)S(1)} %get-tuple-element.29), channel_id=1, source_target_pairs={{0,112},{16,0},{32,16},{48,32},{64,48},{80,64},{96,80},{112,96},{1... | collective-permute-start | bytes 202760 | tf_op jit(solution)/shard_map/ppermute | solution.py:55
  15.7 10.6 %collective-permute-start.5 = (bf16[8,3584]{1,0:T(8,128)(2,1)S(1)}, bf16[8,3584]{1,0:T(8,128)(2,1)S(1)}, u32[]{:S(2)}, u32[]{:S(2)}) collective-permute-start(bf16[8,3584]{1,0:T(8,128)(2,1)S(1)} %get-tuple-element.33.low), channel_id=1, source_target_pairs={{1,0},{2,1},{3,2},{4,3},{5,4},{6,5},{7,6},{8,7},{9,8},{10,9},{11,1... | collective-permute-start | bytes 172040 | tf_op jit(solution)/shard_map/ppermute | solution.py:65
  17.0 9.3 %collective-permute-start.4 = (bf16[8,3584]{1,0:T(8,128)(2,1)S(1)}, bf16[8,3584]{1,0:T(8,128)(2,1)S(1)}, u32[]{:S(2)}, u32[]{:S(2)}) collective-permute-start(bf16[8,3584]{1,0:T(8,128)(2,1)S(1)} %get-tuple-element.34.high), channel_id=1, source_target_pairs={{0,1},{1,2},{2,3},{3,4},{4,5},{5,6},{6,7},{7,8},{8,9},{9,10},{10,1... | collective-permute-start | bytes 172040 | tf_op jit(solution)/shard_map/ppermute | solution.py:60
  26.3 4.7 %copy-start = (f32[16,4,2]{0,2,1:T(2,128)S(1)}, f32[16,4,2]{0,2,1:T(2,128)}, u32[]{:S(2)}) copy-start(f32[16,4,2]{0,2,1:T(2,128)} %param.14) | copy-start | bytes 1540
  26.3 4.7 %copy-start.1 = (f32[16,4]{0,1:T(4,128)S(1)}, f32[16,4]{0,1:T(4,128)}, u32[]{:S(2)}) copy-start(f32[16,4]{0,1:T(4,128)} %param.15) | copy-start | bytes 772
  26.3 4.7 %copy-start.2 = (f32[16]{0:T(128)S(1)}, f32[16]{0:T(128)}, u32[]{:S(2)}) copy-start(f32[16]{0:T(128)} %shear.7) | copy-start | bytes 196
  38.3 22.0 %copy-start.5 = (s32[16,4]{0,1:T(4,128)S(1)}, s32[16,4]{0,1:T(4,128)}, u32[]{:S(2)}) copy-start(s32[16,4]{0,1:T(4,128)} %param.16) | copy-start | bytes 772
  38.3 17.0 %collective-permute-start.6 = (f32[4,4,32,128]{3,2,1,0:T(8,128)S(1)}, f32[4,4,32,128]{3,2,1,0:T(8,128)S(1)}, u32[]{:S(2)}, u32[]{:S(2)}) collective-permute-start(f32[4,4,32,128]{3,2,1,0:T(8,128)S(1)} %get-tuple-element.38), channel_id=1, source_target_pairs={{0,128},{128,256},{256,384},{384,0},{1,129},{129,257},{257,385},{3... | collective-permute-start | bytes 786440 | tf_op jit(solution)/shard_map/ppermute | solution.py:55
  45.8 11.1 %collective-permute-start.7 = (f32[4,4,32,128]{3,2,1,0:T(8,128)S(1)}, f32[4,4,32,128]{3,2,1,0:T(8,128)S(1)}, u32[]{:S(2)}, u32[]{:S(2)}) collective-permute-start(f32[4,4,32,128]{3,2,1,0:T(8,128)S(1)} %shard_map.122), channel_id=1, source_target_pairs={{0,256},{128,384},{256,0},{384,128},{1,257},{129,385},{257,1},{385... | collective-permute-start | bytes 786440 | tf_op jit(solution)/shard_map/ppermute | solution.py:55
  47.7 12.5 %collective-permute-start.8 = (f32[4,4,32,128]{3,2,1,0:T(8,128)S(1)}, f32[4,4,32,128]{3,2,1,0:T(8,128)S(1)}, u32[]{:S(2)}, u32[]{:S(2)}) collective-permute-start(f32[4,4,32,128]{3,2,1,0:T(8,128)S(1)} %shard_map.123), channel_id=1, source_target_pairs={{0,384},{128,0},{256,128},{384,256},{1,385},{129,1},{257,129},{385... | collective-permute-start | bytes 786440 | tf_op jit(solution)/shard_map/ppermute | solution.py:55

commit v8 on v7

--- a/solution.py
+++ b/solution.py
@@ -241,7 +241,7 @@
 
 
 def advance_edges(
-    place, unused, edges, low, high, left, right, shifted, start, coefs, first, second, turned
+    place, unused, edges, low, high, left, right, shifted, start, coefs, first, second
 ):
     row_at, col_at, depth_at = place[1], place[2], place[0]
     depth_last, row_last, col_last = place[3], place[4], place[5]
@@ -334,29 +334,44 @@
     def finish_second(f, b, moved):
         second[f, b] = 0.75 * start[f, b] + 0.25 * moved
 
-    blank = jnp.zeros((128 - 4 * EDGE, 128), F32)
-
     def finish_third(f, b, moved):
-        new = start[f, b] * (1.0 / 3.0) + (2.0 / 3.0) * moved
-        turned[f, 128 * b : 128 * (b + 1), :] = jnp.concatenate([new, blank], axis=0).T
+        first[f, b] = start[f, b] * (1.0 / 3.0) + (2.0 / 3.0) * moved
 
     stage(start, finish_first)
     stage(first, finish_second)
     stage(second, finish_third)
-    lane32 = lax.broadcasted_iota(jnp.int32, (32, 128), 1)
-
-    @pl.loop(0, 16, unroll=4)
-    def _(k):
-        for f in range(2):
-            lines = turned[f, pl.ds(pl.multiple_of((k + HALO) * ROWS, 8), 32), :]
-            near = pltpu.roll(lines, 128 - EDGE, 1)
-            far = pltpu.roll(lines, 128 - 3 * EDGE, 1)
-            for shift in range(-RIM, RIM + 1):
-                from_far = (lane32 >= 64) & (lane32 < 128 + min(shift, 0)) | (lane32 < shift)
-                patch = jnp.where(from_far, far, near)
-                patch = pltpu.roll(patch, -shift % 128, 1) if shift else patch
-                wrong = (lane32 <= RIM - 1 - shift) | (lane32 >= 128 - RIM - shift)
-                pltpu.store(shifted.at[shift + RIM, f, k], patch, mask=wrong)
+
+    m = lax.broadcasted_iota(jnp.int32, (4 * EDGE, 128), 0)
+    column = jnp.where(m < 2 * EDGE, m - EDGE, m + 128 - 3 * EDGE)
+    used = ((column >= -RIM) & (column < RIM)) | ((column >= 128 - RIM) & (column < 128 + RIM))
+    placed = jnp.concatenate(
+        [(used & (column == lane + shift)).astype(F32) for shift in range(-RIM, RIM + 1)], axis=1
+    )
+    placed = jnp.concatenate([placed] * 3, axis=0).astype(BF16)
+    lane8 = lax.broadcasted_iota(jnp.int32, (8, 128), 1)
+    for f in range(2):
+        for b in range(BLOCKS):
+            rest = first[f, b]
+            parts = []
+            for _ in range(3):
+                part = rest.astype(BF16).astype(F32)
+                parts.append(part)
+                rest = rest - part
+            patch = lax.dot_general(
+                jnp.concatenate(parts, axis=0).astype(BF16), placed, TN, preferred_element_type=F32
+            )
+            for g in range(16):
+                plane, strip = divmod(16 * b + g, ROWS // 8)
+                if strip == 4 or not HALO <= plane < HALO + 16:
+                    continue
+                for i in range(SHIFTS):
+                    shift = i - RIM
+                    wrong = (lane8 < RIM - shift) | (lane8 >= 128 - RIM - shift)
+                    pltpu.store(
+                        shifted.at[i, f, plane - HALO, 8 * strip : 8 * strip + 8],
+                        patch[8 * g : 8 * g + 8, 128 * i : 128 * (i + 1)],
+                        mask=wrong,
+                    )
 
 
 def render_and_save(away, place, shear, weight, bias, shifted, image, out, sem):
@@ -579,8 +594,7 @@
         advance_edges,
         shifted_type,
         [SMEM_SPEC] + [VMEM_SPEC] * 6,
-        [pltpu.VMEM((n, BLOCKS, 4 * EDGE, 128), F32) for n in (2, 6, 2, 2)]
-        + [pltpu.VMEM((2, LINES, 128), F32)],
+        [pltpu.VMEM((n, BLOCKS, 4 * EDGE, 128), F32) for n in (2, 6, 2, 2)],
         aliases={1: 0},
     )(place, shifted, edges, low, high, left, right)
 

time: 97.7 us -> 95.6 us (0.979)
  Pallas kernels: 26.1 us -> 24 us
    pallas_call x1, Pallas kernels: 4.62 us -> 2.53 us  [body(): call(advance_edges, shifted_type, [SMEM_SPEC] + [VMEM_SPEC] * 6, [pltpu.V...]
where the time goes in v8:
time: 95.6 us; the launch traced here: 94 us
  blocking collectives  33.6 us (35%)
  starting transfers between devices  26.8 us (28%)
  Pallas kernels  24 us (25%)
  waiting for transfers between devices  8.71 us (9%)
    all_to_all x1, blocking collectives, body(): lax.all_to_all(outgoing.reshape(col_devices, -1, 1152), 'col', split_axis...  33.6 us
    ppermute x5, starting transfers between devices, turn_by(): return lax.ppermute(x, axis, [(i, (i + steps) % n) for i in range(n)])  15.1 us
    ppermute x5, waiting for transfers between devices, turn_by(): return lax.ppermute(x, axis, [(i, (i + steps) % n) for i in range(n)])  7.75 us
    pallas_call x3, Pallas kernels, body(): call(functools.partial(render, away), image, [SMEM_SPEC] * 4 + [VMEM_SPEC])  7.25 us
    ppermute x2, starting transfers between devices, shift_down(): return lax.ppermute(x, axis, [(i + 1, i) for i in range(n - 1)])  5.85 us
    ppermute x2, starting transfers between devices, shift_up(): return lax.ppermute(x, axis, [(i, i + 1) for i in range(n - 1)])  5.84 us
    pallas_call x1, Pallas kernels, body(): call(advance_own, (shifted_type, jax.ShapeDtypeStruct((16, 2 * LINES), F3...  4.7 us
    pallas_call x1, Pallas kernels, body(): call(advance_edges, shifted_type, [SMEM_SPEC] + [VMEM_SPEC] * 6, [pltpu.V...  2.53 us
  transfers between devices with their start and end apart: 9, of which 5 were waited for; matrix products, arithmetic and copies ran while one was open for 0% of the time, Pallas kernels for 10%

profile of v8, /device:TPU:6, one launch (start us, length us, event | category | flops | bytes accessed | tf_op | source)
XLA Modules:
  0.0 94.0 jit_solution(15026408888080588865)
XLA Ops:
  0.6 1.1 %shard_map.114 = (bf16[4,3,32,128]{3,2,1,0:T(8,128)(2,1)S(1)}, bf16[4,3,32,128]{3,2,1,0:T(8,128)(2,1)S(1)}) custom-call(f32[2,16,32,128]{3,2,1,0:T(8,128)} %species.3, f32[16,32,128]{2,1,0:T(8,128)} %diff.3, f32[16,32,128]{2,1,0:T(8,128)} %rate.3), custom_call_target="tpu_custom_call" | custom-call | tf_op jit(solution)/shard_map/pallas_call | solution.py:548
  1.7 1.3 %collective-permute-start = (bf16[4,3,32,128]{3,2,1,0:T(8,128)(2,1)S(1)}, bf16[4,3,32,128]{3,2,1,0:T(8,128)(2,1)S(1)}, u32[]{:S(2)}, u32[]{:S(2)}) collective-permute-start(bf16[4,3,32,128]{3,2,1,0:T(8,128)(2,1)S(1)} %get-tuple-element.21), channel_id=1, source_target_pairs={{0,128},{128,256},{256,384},{1,129},{129,257},{257,385},{2,130},{1... | collective-permute-start | bytes 294920 | tf_op jit(solution)/shard_map/ppermute | solution.py:60
  3.0 0.0 copy-start.3
  3.0 0.0 copy-start.4
  3.0 4.6 %collective-permute-start.1 = (bf16[4,3,32,128]{3,2,1,0:T(8,128)(2,1)S(1)}, bf16[4,3,32,128]{3,2,1,0:T(8,128)(2,1)S(1)}, u32[]{:S(2)}, u32[]{:S(2)}) collective-permute-start(bf16[4,3,32,128]{3,2,1,0:T(8,128)(2,1)S(1)} %get-tuple-element.22), channel_id=1, source_target_pairs={{128,0},{256,128},{384,256},{129,1},{257,129},{385,257},{130,2},{2... | collective-permute-start | bytes 294920 | tf_op jit(solution)/shard_map/ppermute | solution.py:65
  7.6 1.2 %shard_map.113.unused = f32[4,22,40,128]{3,2,1,0:T(8,128)S(1)} custom-call(f32[2,16,32,128]{3,2,1,0:T(8,128)} %species.3, f32[16,32,128]{2,1,0:T(8,128)} %diff.3, f32[16,32,128]{2,1,0:T(8,128)} %rate.3), custom_call_target="tpu_custom_call" | custom-call | tf_op jit(solution)/shard_map/pallas_call | solution.py:556
  8.8 0.0 collective-permute-done.before
  8.8 0.9 %collective-permute-done.1.after = bf16[4,3,32,128]{3,2,1,0:T(8,128)(2,1)S(1)} collective-permute-done((bf16[4,3,32,128]{3,2,1,0:T(8,128)(2,1)S(1)}, bf16[4,3,32,128]{3,2,1,0:T(8,128)(2,1)S(1)}, u32[]{:S(2)}, u32[]{:S(2)}) %collective-permute-start.1) | collective-permute-done | bytes 98336 | tf_op jit(solution)/shard_map/ppermute | solution.py:65
  9.8 0.1 shard_map.115
  9.8 0.0 collective-permute-start.2
  9.9 2.9 %collective-permute-start.3 = (bf16[3,88,128]{2,1,0:T(8,128)(2,1)S(1)}, bf16[3,88,128]{2,1,0:T(8,128)(2,1)S(1)}, u32[]{:S(2)}, u32[]{:S(2)}) collective-permute-start(bf16[3,88,128]{2,1,0:T(8,128)(2,1)S(1)} %get-tuple-element.29), channel_id=1, source_target_pairs={{0,112},{16,0},{32,16},{48,32},{64,48},{80,64},{96,80},{112,96},{1... | collective-permute-start | bytes 202760 | tf_op jit(solution)/shard_map/ppermute | solution.py:55
  12.8 0.1 stack.15.place
  12.9 0.0 copy-done.3
  12.9 0.0 copy-done.4
  12.9 1.5 %shard_map.116 = (bf16[256,128]{1,0:T(8,128)(2,1)S(1)}, s32[128,128]{1,0:T(8,128)S(1)}, bf16[4,128,128]{2,1,0:T(8,128)(2,1)S(1)}) custom-call(s32[6]{0:T(128)S(1)} %stack.15.place, s32[4,32]{1,0:T(4,128)S(1)} %bitcast.21, s32[4,32]{1,0:T(4,128)S(1)} %bitcast.22, bf16[16,128,128]{2,1,0:T(8,128)(2,1)} %warp.1), custom_call_target="tpu_custom_call" | custom-call | tf_op jit(solution)/shard_map/pallas_call | solution.py:564
  14.4 0.4 collective-permute-done.2.above
  14.8 0.0 collective-permute-done.3.below
  14.8 0.9 shard_map.117
  15.7 1.3 %collective-permute-start.5 = (bf16[8,3584]{1,0:T(8,128)(2,1)S(1)}, bf16[8,3584]{1,0:T(8,128)(2,1)S(1)}, u32[]{:S(2)}, u32[]{:S(2)}) collective-permute-start(bf16[8,3584]{1,0:T(8,128)(2,1)S(1)} %get-tuple-element.33.low), channel_id=1, source_target_pairs={{1,0},{2,1},{3,2},{4,3},{5,4},{6,5},{7,6},{8,7},{9,8},{10,9},{11,1... | collective-permute-start | bytes 172040 | tf_op jit(solution)/shard_map/ppermute | solution.py:65
  17.0 4.5 %collective-permute-start.4 = (bf16[8,3584]{1,0:T(8,128)(2,1)S(1)}, bf16[8,3584]{1,0:T(8,128)(2,1)S(1)}, u32[]{:S(2)}, u32[]{:S(2)}) collective-permute-start(bf16[8,3584]{1,0:T(8,128)(2,1)S(1)} %get-tuple-element.34.high), channel_id=1, source_target_pairs={{0,1},{1,2},{2,3},{3,4},{4,5},{5,6},{6,7},{7,8},{8,9},{9,10},{10,1... | collective-permute-start | bytes 172040 | tf_op jit(solution)/shard_map/ppermute | solution.py:60
  21.6 4.7 %shard_map.118 = (f32[7,2,16,32,128]{4,3,2,1,0:T(8,128)S(1)}, f32[16,1792]{1,0:T(8,128)S(1)}) custom-call(s32[6]{0:T(128)S(1)} %stack.15.place, f32[4,22,40,128]{3,2,1,0:T(8,128)S(1)} %get-tuple-element.30.brick), custom_call_target="tpu_custom_call" | custom-call | tf_op jit(solution)/shard_map/pallas_call | solution.py:586
  26.3 0.0 collective-permute-done.5.right
  26.3 0.0 collective-permute-done.4.left
  26.3 0.0 copy-start
  26.3 0.0 copy-start.1
  26.3 0.0 copy-start.2
  26.3 2.5 %shard_map.119.shifted = f32[7,2,16,32,128]{4,3,2,1,0:T(8,128)S(1)} custom-call(s32[6]{0:T(128)S(1)} %stack.15.place, f32[7,2,16,32,128]{4,3,2,1,0:T(8,128)S(1)} %get-tuple-element.31.unused, f32[16,1792]{1,0:T(8,128)S(1)} %get-tuple-element.32.edges, bf16[8,3584]{1,0:T(8,128)(2,1)S(1)} %get-tuple-element.33.low, ...), custom_call_target="tpu_custom_call", output_to_operand_aliasing={{}: (1, {})} | custom-call | tf_op jit(solution)/shard_map/pallas_call | solution.py:593
  28.9 0.0 copy-done
  28.9 0.0 copy-done.1
  28.9 0.0 copy-done.2
  28.9 2.4 %shard_map.123 = f32[4,4,32,128]{3,2,1,0:T(8,128)S(1)} custom-call(s32[6]{0:T(128)S(1)} %stack.15.place, f32[16]{0:T(128)S(1)} %copy-done.2, f32[4,2,16]{2,1,0:T(2,128)S(1)} %bitcast.13, f32[4,16]{1,0:T(4,128)S(1)} %bitcast.17, f32[7,2,16,32,128]{4,3,2,1,0:T(8,128)S(1)} %shard_map.119.shifted), custom_call_target="tpu_custom_call" | custom-call | tf_op jit(solution)/shard_map/pallas_call | solution.py:614
  31.3 2.4 %shard_map.122 = f32[4,4,32,128]{3,2,1,0:T(8,128)S(1)} custom-call(s32[6]{0:T(128)S(1)} %stack.15.place, f32[16]{0:T(128)S(1)} %copy-done.2, f32[4,2,16]{2,1,0:T(2,128)S(1)} %bitcast.14, f32[4,16]{1,0:T(4,128)S(1)} %bitcast.18, f32[7,2,16,32,128]{4,3,2,1,0:T(8,128)S(1)} %shard_map.119.shifted), custom_call_target="tpu_custom_call" | custom-call | tf_op jit(solution)/shard_map/pallas_call | solution.py:614
  33.7 2.4 %shard_map.120 = (f32[4,4,32,128]{3,2,1,0:T(8,128)S(1)}, f32[2,16,32,128]{3,2,1,0:T(8,128)}) custom-call(s32[6]{0:T(128)S(1)} %stack.15.place, f32[16]{0:T(128)S(1)} %copy-done.2, f32[4,2,16]{2,1,0:T(2,128)S(1)} %bitcast.15, f32[4,16]{1,0:T(4,128)S(1)} %bitcast.19, f32[7,2,16,32,128]{4,3,2,1,0:T(8,128)S(1)} %shard_map.119.shifted), custom_call_target="tpu_custom_call" | custom-call | tf_op jit(solution)/shard_map/pallas_call | solution.py:606
  36.2 0.0 copy-start.5
  36.2 7.5 %collective-permute-start.6 = (f32[4,4,32,128]{3,2,1,0:T(8,128)S(1)}, f32[4,4,32,128]{3,2,1,0:T(8,128)S(1)}, u32[]{:S(2)}, u32[]{:S(2)}) collective-permute-start(f32[4,4,32,128]{3,2,1,0:T(8,128)S(1)} %get-tuple-element.38), channel_id=1, source_target_pairs={{0,128},{128,256},{256,384},{384,0},{1,129},{129,257},{257,385},{3... | collective-permute-start | bytes 786440 | tf_op jit(solution)/shard_map/ppermute | solution.py:55
  43.7 1.9 %collective-permute-start.7 = (f32[4,4,32,128]{3,2,1,0:T(8,128)S(1)}, f32[4,4,32,128]{3,2,1,0:T(8,128)S(1)}, u32[]{:S(2)}, u32[]{:S(2)}) collective-permute-start(f32[4,4,32,128]{3,2,1,0:T(8,128)S(1)} %shard_map.122), channel_id=1, source_target_pairs={{0,256},{128,384},{256,0},{384,128},{1,257},{129,385},{257,1},{385... | collective-permute-start | bytes 786440 | tf_op jit(solution)/shard_map/ppermute | solution.py:55
  45.6 2.8 %collective-permute-start.8 = (f32[4,4,32,128]{3,2,1,0:T(8,128)S(1)}, f32[4,4,32,128]{3,2,1,0:T(8,128)S(1)}, u32[]{:S(2)}, u32[]{:S(2)}) collective-permute-start(f32[4,4,32,128]{3,2,1,0:T(8,128)S(1)} %shard_map.123), channel_id=1, source_target_pairs={{0,384},{128,0},{256,128},{384,256},{1,385},{129,1},{257,129},{385... | collective-permute-start | bytes 786440 | tf_op jit(solution)/shard_map/ppermute | solution.py:55
  48.4 2.4 %shard_map.121.slab0 = f32[4,4,32,128]{3,2,1,0:T(8,128)S(1)} custom-call(s32[6]{0:T(128)S(1)} %stack.15.place, f32[16]{0:T(128)S(1)} %copy-done.2, f32[4,2,16]{2,1,0:T(2,128)S(1)} %bitcast.16, f32[4,16]{1,0:T(4,128)S(1)} %bitcast.20, f32[7,2,16,32,128]{4,3,2,1,0:T(8,128)S(1)} %shard_map.119.shifted), custom_call_target="tpu_custom_call" | custom-call | tf_op jit(solution)/shard_map/pallas_call | solution.py:614
  50.8 2.4 %collective-permute-done.6.slab1 = f32[4,4,32,128]{3,2,1,0:T(8,128)S(1)} collective-permute-done((f32[4,4,32,128]{3,2,1,0:T(8,128)S(1)}, f32[4,4,32,128]{3,2,1,0:T(8,128)S(1)}, u32[]{:S(2)}, u32[]{:S(2)}) %collective-permute-start.6) | collective-permute-done | bytes 262176 | tf_op jit(solution)/shard_map/ppermute | solution.py:55
  53.2 1.6 %collective-permute-done.7.slab2 = f32[4,4,32,128]{3,2,1,0:T(8,128)S(1)} collective-permute-done((f32[4,4,32,128]{3,2,1,0:T(8,128)S(1)}, f32[4,4,32,128]{3,2,1,0:T(8,128)S(1)}, u32[]{:S(2)}, u32[]{:S(2)}) %collective-permute-start.7) | collective-permute-done | bytes 262176 | tf_op jit(solution)/shard_map/ppermute | solution.py:55
  54.8 3.4 %collective-permute-done.8.slab3 = f32[4,4,32,128]{3,2,1,0:T(8,128)S(1)} collective-permute-done((f32[4,4,32,128]{3,2,1,0:T(8,128)S(1)}, f32[4,4,32,128]{3,2,1,0:T(8,128)S(1)}, u32[]{:S(2)}, u32[]{:S(2)}) %collective-permute-start.8) | collective-permute-done | bytes 262176 | tf_op jit(solution)/shard_map/ppermute | solution.py:55
  58.1 0.0 copy-done.5
  58.1 1.1 %shard_map.124 = bf16[128,1152]{1,0:T(8,128)(2,1)S(1)} custom-call(s32[6]{0:T(128)S(1)} %stack.15.place, s32[4,16]{1,0:T(4,128)S(1)} %bitcast.23, bf16[256,128]{1,0:T(8,128)(2,1)S(1)} %get-tuple-element.36.select, s32[128,128]{1,0:T(8,128)S(1)} %get-tuple-element.37.lengths, f32[4,4,32,128]{3,2,1,0:T(8,128)S(1)} %shard_map.121.slab0, ...), custom_call_target="tpu_custom_call" | custom-call | tf_op jit(solution)/shard_map/pallas_call | solution.py:620
  59.2 33.6 %all_to_all.5 = bf16[16,8,1152]{2,1,0:T(8,128)(2,1)S(1)} all-to-all(bf16[16,8,1152]{2,1,0:T(8,128)(2,1)S(1)} %bitcast.11), channel_id=1, replica_groups=mesh['depth'=4,'row'=8,'col'=16] {'col'}, dimensions={0} | all-to-all | bytes 589824 | tf_op jit(solution)/shard_map/all_to_all | solution.py:626
  92.8 1.3 %shard_map.125 = f32[512,128]{1,0:T(8,128)} custom-call(bf16[128,1152]{1,0:T(8,128)(2,1)S(1)} %bitcast.12, bf16[4,128,128]{2,1,0:T(8,128)(2,1)S(1)} %get-tuple-element.39.warp), custom_call_target="tpu_custom_call" | custom-call | tf_op jit(solution)/shard_map/pallas_call | solution.py:633
Async XLA Ops:
  1.7 7.1 %collective-permute-start = (bf16[4,3,32,128]{3,2,1,0:T(8,128)(2,1)S(1)}, bf16[4,3,32,128]{3,2,1,0:T(8,128)(2,1)S(1)}, u32[]{:S(2)}, u32[]{:S(2)}) collective-permute-start(bf16[4,3,32,128]{3,2,1,0:T(8,128)(2,1)S(1)} %get-tuple-element.21), channel_id=1, source_target_pairs={{0,128},{128,256},{256,384},{1,129},{129,257},{257,385},{2,130},{1... | collective-permute-start | bytes 294920 | tf_op jit(solution)/shard_map/ppermute | solution.py:60
  3.0 9.9 %copy-start.3 = (s32[4,1,32,1]{2,3,1,0:T(1,128)S(1)}, s32[4,1,32,1]{2,3,1,0:T(1,128)}, u32[]{:S(2)}) copy-start(s32[4,1,32,1]{2,3,1,0:T(1,128)} %param.18) | copy-start | bytes 1540
  3.0 9.9 %copy-start.4 = (s32[4,1,32]{2,1,0:T(1,128)S(1)}, s32[4,1,32]{2,1,0:T(1,128)}, u32[]{:S(2)}) copy-start(s32[4,1,32]{2,1,0:T(1,128)} %param.17) | copy-start | bytes 1540
  3.0 6.8 %collective-permute-start.1 = (bf16[4,3,32,128]{3,2,1,0:T(8,128)(2,1)S(1)}, bf16[4,3,32,128]{3,2,1,0:T(8,128)(2,1)S(1)}, u32[]{:S(2)}, u32[]{:S(2)}) collective-permute-start(bf16[4,3,32,128]{3,2,1,0:T(8,128)(2,1)S(1)} %get-tuple-element.22), channel_id=1, source_target_pairs={{128,0},{256,128},{384,256},{129,1},{257,129},{385,257},{130,2},{2... | collective-permute-start | bytes 294920 | tf_op jit(solution)/shard_map/ppermute | solution.py:65
  9.8 4.9 %collective-permute-start.2 = (bf16[3,88,128]{2,1,0:T(8,128)(2,1)S(1)}, bf16[3,88,128]{2,1,0:T(8,128)(2,1)S(1)}, u32[]{:S(2)}, u32[]{:S(2)}) collective-permute-start(bf16[3,88,128]{2,1,0:T(8,128)(2,1)S(1)} %get-tuple-element.28), channel_id=1, source_target_pairs={{0,16},{16,32},{32,48},{48,64},{64,80},{80,96},{96,112},{112,0},{1... | collective-permute-start | bytes 202760 | tf_op jit(solution)/shard_map/ppermute | solution.py:55
  9.9 4.9 %collective-permute-start.3 = (bf16[3,88,128]{2,1,0:T(8,128)(2,1)S(1)}, bf16[3,88,128]{2,1,0:T(8,128)(2,1)S(1)}, u32[]{:S(2)}, u32[]{:S(2)}) collective-permute-start(bf16[3,88,128]{2,1,0:T(8,128)(2,1)S(1)} %get-tuple-element.29), channel_id=1, source_target_pairs={{0,112},{16,0},{32,16},{48,32},{64,48},{80,64},{96,80},{112,96},{1... | collective-permute-start | bytes 202760 | tf_op jit(solution)/shard_map/ppermute | solution.py:55
  15.7 10.6 %collective-permute-start.5 = (bf16[8,3584]{1,0:T(8,128)(2,1)S(1)}, bf16[8,3584]{1,0:T(8,128)(2,1)S(1)}, u32[]{:S(2)}, u32[]{:S(2)}) collective-permute-start(bf16[8,3584]{1,0:T(8,128)(2,1)S(1)} %get-tuple-element.33.low), channel_id=1, source_target_pairs={{1,0},{2,1},{3,2},{4,3},{5,4},{6,5},{7,6},{8,7},{9,8},{10,9},{11,1... | collective-permute-start | bytes 172040 | tf_op jit(solution)/shard_map/ppermute | solution.py:65
  17.0 9.3 %collective-permute-start.4 = (bf16[8,3584]{1,0:T(8,128)(2,1)S(1)}, bf16[8,3584]{1,0:T(8,128)(2,1)S(1)}, u32[]{:S(2)}, u32[]{:S(2)}) collective-permute-start(bf16[8,3584]{1,0:T(8,128)(2,1)S(1)} %get-tuple-element.34.high), channel_id=1, source_target_pairs={{0,1},{1,2},{2,3},{3,4},{4,5},{5,6},{6,7},{7,8},{8,9},{9,10},{10,1... | collective-permute-start | bytes 172040 | tf_op jit(solution)/shard_map/ppermute | solution.py:60
  26.3 2.6 %copy-start = (f32[16,4,2]{0,2,1:T(2,128)S(1)}, f32[16,4,2]{0,2,1:T(2,128)}, u32[]{:S(2)}) copy-start(f32[16,4,2]{0,2,1:T(2,128)} %param.14) | copy-start | bytes 1540
  26.3 2.6 %copy-start.1 = (f32[16,4]{0,1:T(4,128)S(1)}, f32[16,4]{0,1:T(4,128)}, u32[]{:S(2)}) copy-start(f32[16,4]{0,1:T(4,128)} %param.15) | copy-start | bytes 772
  26.3 2.6 %copy-start.2 = (f32[16]{0:T(128)S(1)}, f32[16]{0:T(128)}, u32[]{:S(2)}) copy-start(f32[16]{0:T(128)} %shear.7) | copy-start | bytes 196
  36.2 22.0 %copy-start.5 = (s32[16,4]{0,1:T(4,128)S(1)}, s32[16,4]{0,1:T(4,128)}, u32[]{:S(2)}) copy-start(s32[16,4]{0,1:T(4,128)} %param.16) | copy-start | bytes 772
  36.2 17.0 %collective-permute-start.6 = (f32[4,4,32,128]{3,2,1,0:T(8,128)S(1)}, f32[4,4,32,128]{3,2,1,0:T(8,128)S(1)}, u32[]{:S(2)}, u32[]{:S(2)}) collective-permute-start(f32[4,4,32,128]{3,2,1,0:T(8,128)S(1)} %get-tuple-element.38), channel_id=1, source_target_pairs={{0,128},{128,256},{256,384},{384,0},{1,129},{129,257},{257,385},{3... | collective-permute-start | bytes 786440 | tf_op jit(solution)/shard_map/ppermute | solution.py:55
  43.7 11.1 %collective-permute-start.7 = (f32[4,4,32,128]{3,2,1,0:T(8,128)S(1)}, f32[4,4,32,128]{3,2,1,0:T(8,128)S(1)}, u32[]{:S(2)}, u32[]{:S(2)}) collective-permute-start(f32[4,4,32,128]{3,2,1,0:T(8,128)S(1)} %shard_map.122), channel_id=1, source_target_pairs={{0,256},{128,384},{256,0},{384,128},{1,257},{129,385},{257,1},{385... | collective-permute-start | bytes 786440 | tf_op jit(solution)/shard_map/ppermute | solution.py:55
  45.6 12.5 %collective-permute-start.8 = (f32[4,4,32,128]{3,2,1,0:T(8,128)S(1)}, f32[4,4,32,128]{3,2,1,0:T(8,128)S(1)}, u32[]{:S(2)}, u32[]{:S(2)}) collective-permute-start(f32[4,4,32,128]{3,2,1,0:T(8,128)S(1)} %shard_map.123), channel_id=1, source_target_pairs={{0,384},{128,0},{256,128},{384,256},{1,385},{129,1},{257,129},{385... | collective-permute-start | bytes 786440 | tf_op jit(solution)/shard_map/ppermute | solution.py:55

commit v9 on v8

--- a/solution.py
+++ b/solution.py
@@ -393,7 +393,7 @@
         v = first + j
         table = [
             tuple(
-                (0.5 if c < 3 else 1.0) * value
+                (0.5 if c < 3 else LOG2E) * value
                 for value in (weight[c, 0, v], weight[c, 1, v], bias[c, v])
             )
             for c in range(4)
@@ -414,8 +414,7 @@
                 s0 = (1.0 - t) * shifted[i, 0, k, strip] + t * shifted[i + 1, 0, k, strip]
                 s1 = (1.0 - t) * shifted[i, 1, k, strip] + t * shifted[i + 1, 1, k, strip]
                 logits = [table[c][0] * s0 + table[c][1] * s1 + table[c][2] for c in range(4)]
-                dense = logits[3]
-                total = total + (jnp.maximum(dense, 0.0) + jnp.log(1.0 + jnp.exp(-jnp.abs(dense))))
+                total = total + jnp.log(1.0 + jnp.exp2(logits[3]))
                 after = jnp.exp2((-RAY_STEP * LOG2E) * total)
                 part = through - after
                 c0 = c0 + part * jnp.tanh(logits[0])
@@ -461,25 +460,24 @@
     slabs = (slab0, slab1, slab2, slab3)
     depth_at, devices = place[0], place[3] + 1
 
-    def fetch(which, v, c):
-        value = slabs[3][v, c]
-        for offset in (2, 1, 0):
-            value = jnp.where(which == offset, slabs[offset][v, c], value)
-        return value
-
     for v in range(4):
         keep = lane < lengths[32 * v : 32 * (v + 1), :]
-        turn = [
-            lax.rem(depth_at - order[position, depth_at * 4 + v] + devices, devices)
-            for position in range(4)
-        ]
-        channels = [fetch(turn[0], v, c) for c in range(4)]
-        for position in range(1, 4):
-            clear = 1.0 - channels[3]
-            channels = [channels[c] + clear * fetch(turn[position], v, c) for c in range(4)]
+        when = [jnp.int32(0)] * 4
+        for position in range(4):
+            turn = lax.rem(depth_at - order[position, depth_at * 4 + v] + devices, devices)
+            when = [jnp.where(turn == i, position, when[i]) for i in range(4)]
+        opacity = [slabs[i][v, 3] for i in range(4)]
+        weight = [None] * 4
+        for i in range(4):
+            for j in range(4):
+                if i != j:
+                    ahead = jnp.where(when[j] < when[i], 1.0, 0.0).astype(F32)
+                    clear = 1.0 - ahead * opacity[j]
+                    weight[i] = clear if weight[i] is None else weight[i] * clear
         for c in range(4):
+            value = sum(weight[i] * (slabs[i][v, c] if c < 3 else opacity[i]) for i in range(4))
             pieces[32 * v : 32 * (v + 1), 128 * c : 128 * (c + 1)] = jnp.where(
-                keep, channels[c], 0.0
+                keep, value, 0.0
             ).astype(BF16)
     row_id = lax.broadcasted_iota(jnp.int32, (128, 128), 0) + 1
     pieces[:, 512:640] = row_id.astype(F32).astype(BF16)

time: 95.6 us -> 95 us (level)
  no operation moved by 1% of the time
where the time goes in v9:
time: 95 us; the launch traced here: 93.4 us
  blocking collectives  33.6 us (35%)
  starting transfers between devices  26.8 us (28%)
  Pallas kernels  23.1 us (24%)
  waiting for transfers between devices  8.9 us (9%)
    all_to_all x1, blocking collectives, body(): lax.all_to_all(outgoing.reshape(col_devices, -1, 1152), 'col', split_axis...  33.6 us
    ppermute x5, starting transfers between devices, turn_by(): return lax.ppermute(x, axis, [(i, (i + steps) % n) for i in range(n)])  15.1 us
    ppermute x5, waiting for transfers between devices, turn_by(): return lax.ppermute(x, axis, [(i, (i + steps) % n) for i in range(n)])  7.95 us
    pallas_call x3, Pallas kernels, body(): call(functools.partial(render, away), image, [SMEM_SPEC] * 4 + [VMEM_SPEC])  6.67 us
    ppermute x2, starting transfers between devices, shift_down(): return lax.ppermute(x, axis, [(i + 1, i) for i in range(n - 1)])  5.85 us
    ppermute x2, starting transfers between devices, shift_up(): return lax.ppermute(x, axis, [(i, i + 1) for i in range(n - 1)])  5.84 us
    pallas_call x1, Pallas kernels, body(): call(advance_own, (shifted_type, jax.ShapeDtypeStruct((16, 2 * LINES), F3...  4.7 us
    pallas_call x1, Pallas kernels, body(): call(advance_edges, shifted_type, [SMEM_SPEC] + [VMEM_SPEC] * 6, [pltpu.V...  2.53 us
  transfers between devices with their start and end apart: 9, of which 5 were waited for; matrix products, arithmetic and copies ran while one was open for 0% of the time, Pallas kernels for 10%

profile of v9, /device:TPU:6, one launch (start us, length us, event | category | flops | bytes accessed | tf_op | source)
XLA Modules:
  0.0 93.4 jit_solution(17298882882337463429)
XLA Ops:
  0.6 1.1 %shard_map.114 = (bf16[4,3,32,128]{3,2,1,0:T(8,128)(2,1)S(1)}, bf16[4,3,32,128]{3,2,1,0:T(8,128)(2,1)S(1)}) custom-call(f32[2,16,32,128]{3,2,1,0:T(8,128)} %species.3, f32[16,32,128]{2,1,0:T(8,128)} %diff.3, f32[16,32,128]{2,1,0:T(8,128)} %rate.3), custom_call_target="tpu_custom_call" | custom-call | tf_op jit(solution)/shard_map/pallas_call | solution.py:546
  1.7 1.3 %collective-permute-start = (bf16[4,3,32,128]{3,2,1,0:T(8,128)(2,1)S(1)}, bf16[4,3,32,128]{3,2,1,0:T(8,128)(2,1)S(1)}, u32[]{:S(2)}, u32[]{:S(2)}) collective-permute-start(bf16[4,3,32,128]{3,2,1,0:T(8,128)(2,1)S(1)} %get-tuple-element.21), channel_id=1, source_target_pairs={{0,128},{128,256},{256,384},{1,129},{129,257},{257,385},{2,130},{1... | collective-permute-start | bytes 294920 | tf_op jit(solution)/shard_map/ppermute | solution.py:60
  3.0 0.0 copy-start.3
  3.0 0.0 copy-start.4
  3.0 4.6 %collective-permute-start.1 = (bf16[4,3,32,128]{3,2,1,0:T(8,128)(2,1)S(1)}, bf16[4,3,32,128]{3,2,1,0:T(8,128)(2,1)S(1)}, u32[]{:S(2)}, u32[]{:S(2)}) collective-permute-start(bf16[4,3,32,128]{3,2,1,0:T(8,128)(2,1)S(1)} %get-tuple-element.22), channel_id=1, source_target_pairs={{128,0},{256,128},{384,256},{129,1},{257,129},{385,257},{130,2},{2... | collective-permute-start | bytes 294920 | tf_op jit(solution)/shard_map/ppermute | solution.py:65
  7.6 1.2 %shard_map.113.unused = f32[4,22,40,128]{3,2,1,0:T(8,128)S(1)} custom-call(f32[2,16,32,128]{3,2,1,0:T(8,128)} %species.3, f32[16,32,128]{2,1,0:T(8,128)} %diff.3, f32[16,32,128]{2,1,0:T(8,128)} %rate.3), custom_call_target="tpu_custom_call" | custom-call | tf_op jit(solution)/shard_map/pallas_call | solution.py:554
  8.8 0.0 collective-permute-done.before
  8.8 0.9 %collective-permute-done.1.after = bf16[4,3,32,128]{3,2,1,0:T(8,128)(2,1)S(1)} collective-permute-done((bf16[4,3,32,128]{3,2,1,0:T(8,128)(2,1)S(1)}, bf16[4,3,32,128]{3,2,1,0:T(8,128)(2,1)S(1)}, u32[]{:S(2)}, u32[]{:S(2)}) %collective-permute-start.1) | collective-permute-done | bytes 98336 | tf_op jit(solution)/shard_map/ppermute | solution.py:65
  9.8 0.1 shard_map.115
  9.8 0.0 collective-permute-start.2
  9.9 2.9 %collective-permute-start.3 = (bf16[3,88,128]{2,1,0:T(8,128)(2,1)S(1)}, bf16[3,88,128]{2,1,0:T(8,128)(2,1)S(1)}, u32[]{:S(2)}, u32[]{:S(2)}) collective-permute-start(bf16[3,88,128]{2,1,0:T(8,128)(2,1)S(1)} %get-tuple-element.29), channel_id=1, source_target_pairs={{0,112},{16,0},{32,16},{48,32},{64,48},{80,64},{96,80},{112,96},{1... | collective-permute-start | bytes 202760 | tf_op jit(solution)/shard_map/ppermute | solution.py:55
  12.8 0.1 stack.15.place
  12.9 0.0 copy-done.3
  12.9 0.0 copy-done.4
  12.9 1.5 %shard_map.116 = (bf16[256,128]{1,0:T(8,128)(2,1)S(1)}, s32[128,128]{1,0:T(8,128)S(1)}, bf16[4,128,128]{2,1,0:T(8,128)(2,1)S(1)}) custom-call(s32[6]{0:T(128)S(1)} %stack.15.place, s32[4,32]{1,0:T(4,128)S(1)} %bitcast.21, s32[4,32]{1,0:T(4,128)S(1)} %bitcast.22, bf16[16,128,128]{2,1,0:T(8,128)(2,1)} %warp.1), custom_call_target="tpu_custom_call" | custom-call | tf_op jit(solution)/shard_map/pallas_call | solution.py:562
  14.4 0.4 collective-permute-done.2.above
  14.8 0.0 collective-permute-done.3.below
  14.8 0.9 shard_map.117
  15.7 1.3 %collective-permute-start.5 = (bf16[8,3584]{1,0:T(8,128)(2,1)S(1)}, bf16[8,3584]{1,0:T(8,128)(2,1)S(1)}, u32[]{:S(2)}, u32[]{:S(2)}) collective-permute-start(bf16[8,3584]{1,0:T(8,128)(2,1)S(1)} %get-tuple-element.33.low), channel_id=1, source_target_pairs={{1,0},{2,1},{3,2},{4,3},{5,4},{6,5},{7,6},{8,7},{9,8},{10,9},{11,1... | collective-permute-start | bytes 172040 | tf_op jit(solution)/shard_map/ppermute | solution.py:65
  17.0 4.5 %collective-permute-start.4 = (bf16[8,3584]{1,0:T(8,128)(2,1)S(1)}, bf16[8,3584]{1,0:T(8,128)(2,1)S(1)}, u32[]{:S(2)}, u32[]{:S(2)}) collective-permute-start(bf16[8,3584]{1,0:T(8,128)(2,1)S(1)} %get-tuple-element.34.high), channel_id=1, source_target_pairs={{0,1},{1,2},{2,3},{3,4},{4,5},{5,6},{6,7},{7,8},{8,9},{9,10},{10,1... | collective-permute-start | bytes 172040 | tf_op jit(solution)/shard_map/ppermute | solution.py:60
  21.6 4.7 %shard_map.118 = (f32[7,2,16,32,128]{4,3,2,1,0:T(8,128)S(1)}, f32[16,1792]{1,0:T(8,128)S(1)}) custom-call(s32[6]{0:T(128)S(1)} %stack.15.place, f32[4,22,40,128]{3,2,1,0:T(8,128)S(1)} %get-tuple-element.30.brick), custom_call_target="tpu_custom_call" | custom-call | tf_op jit(solution)/shard_map/pallas_call | solution.py:584
  26.3 0.0 collective-permute-done.5.right
  26.3 0.0 collective-permute-done.4.left
  26.3 0.0 copy-start
  26.3 0.0 copy-start.1
  26.3 0.0 copy-start.2
  26.3 2.5 %shard_map.119.shifted = f32[7,2,16,32,128]{4,3,2,1,0:T(8,128)S(1)} custom-call(s32[6]{0:T(128)S(1)} %stack.15.place, f32[7,2,16,32,128]{4,3,2,1,0:T(8,128)S(1)} %get-tuple-element.31.unused, f32[16,1792]{1,0:T(8,128)S(1)} %get-tuple-element.32.edges, bf16[8,3584]{1,0:T(8,128)(2,1)S(1)} %get-tuple-element.33.low, ...), custom_call_target="tpu_custom_call", output_to_operand_aliasing={{}: (1, {})} | custom-call | tf_op jit(solution)/shard_map/pallas_call | solution.py:591
  28.9 0.0 copy-done
  28.9 0.0 copy-done.1
  28.9 0.0 copy-done.2
  28.9 2.2 %shard_map.123 = f32[4,4,32,128]{3,2,1,0:T(8,128)S(1)} custom-call(s32[6]{0:T(128)S(1)} %stack.15.place, f32[16]{0:T(128)S(1)} %copy-done.2, f32[4,2,16]{2,1,0:T(2,128)S(1)} %bitcast.13, f32[4,16]{1,0:T(4,128)S(1)} %bitcast.17, f32[7,2,16,32,128]{4,3,2,1,0:T(8,128)S(1)} %shard_map.119.shifted), custom_call_target="tpu_custom_call" | custom-call | tf_op jit(solution)/shard_map/pallas_call | solution.py:612
  31.1 2.2 %shard_map.122 = f32[4,4,32,128]{3,2,1,0:T(8,128)S(1)} custom-call(s32[6]{0:T(128)S(1)} %stack.15.place, f32[16]{0:T(128)S(1)} %copy-done.2, f32[4,2,16]{2,1,0:T(2,128)S(1)} %bitcast.14, f32[4,16]{1,0:T(4,128)S(1)} %bitcast.18, f32[7,2,16,32,128]{4,3,2,1,0:T(8,128)S(1)} %shard_map.119.shifted), custom_call_target="tpu_custom_call" | custom-call | tf_op jit(solution)/shard_map/pallas_call | solution.py:612
  33.3 2.2 %shard_map.120 = (f32[4,4,32,128]{3,2,1,0:T(8,128)S(1)}, f32[2,16,32,128]{3,2,1,0:T(8,128)}) custom-call(s32[6]{0:T(128)S(1)} %stack.15.place, f32[16]{0:T(128)S(1)} %copy-done.2, f32[4,2,16]{2,1,0:T(2,128)S(1)} %bitcast.15, f32[4,16]{1,0:T(4,128)S(1)} %bitcast.19, f32[7,2,16,32,128]{4,3,2,1,0:T(8,128)S(1)} %shard_map.119.shifted), custom_call_target="tpu_custom_call" | custom-call | tf_op jit(solution)/shard_map/pallas_call | solution.py:604
  35.6 0.0 copy-start.5
  35.6 7.5 %collective-permute-start.6 = (f32[4,4,32,128]{3,2,1,0:T(8,128)S(1)}, f32[4,4,32,128]{3,2,1,0:T(8,128)S(1)}, u32[]{:S(2)}, u32[]{:S(2)}) collective-permute-start(f32[4,4,32,128]{3,2,1,0:T(8,128)S(1)} %get-tuple-element.38), channel_id=1, source_target_pairs={{0,128},{128,256},{256,384},{384,0},{1,129},{129,257},{257,385},{3... | collective-permute-start | bytes 786440 | tf_op jit(solution)/shard_map/ppermute | solution.py:55
  43.1 1.9 %collective-permute-start.7 = (f32[4,4,32,128]{3,2,1,0:T(8,128)S(1)}, f32[4,4,32,128]{3,2,1,0:T(8,128)S(1)}, u32[]{:S(2)}, u32[]{:S(2)}) collective-permute-start(f32[4,4,32,128]{3,2,1,0:T(8,128)S(1)} %shard_map.122), channel_id=1, source_target_pairs={{0,256},{128,384},{256,0},{384,128},{1,257},{129,385},{257,1},{385... | collective-permute-start | bytes 786440 | tf_op jit(solution)/shard_map/ppermute | solution.py:55
  45.0 2.8 %collective-permute-start.8 = (f32[4,4,32,128]{3,2,1,0:T(8,128)S(1)}, f32[4,4,32,128]{3,2,1,0:T(8,128)S(1)}, u32[]{:S(2)}, u32[]{:S(2)}) collective-permute-start(f32[4,4,32,128]{3,2,1,0:T(8,128)S(1)} %shard_map.123), channel_id=1, source_target_pairs={{0,384},{128,0},{256,128},{384,256},{1,385},{129,1},{257,129},{385... | collective-permute-start | bytes 786440 | tf_op jit(solution)/shard_map/ppermute | solution.py:55
  47.8 2.2 %shard_map.121.slab0 = f32[4,4,32,128]{3,2,1,0:T(8,128)S(1)} custom-call(s32[6]{0:T(128)S(1)} %stack.15.place, f32[16]{0:T(128)S(1)} %copy-done.2, f32[4,2,16]{2,1,0:T(2,128)S(1)} %bitcast.16, f32[4,16]{1,0:T(4,128)S(1)} %bitcast.20, f32[7,2,16,32,128]{4,3,2,1,0:T(8,128)S(1)} %shard_map.119.shifted), custom_call_target="tpu_custom_call" | custom-call | tf_op jit(solution)/shard_map/pallas_call | solution.py:612
  50.0 2.6 %collective-permute-done.6.slab1 = f32[4,4,32,128]{3,2,1,0:T(8,128)S(1)} collective-permute-done((f32[4,4,32,128]{3,2,1,0:T(8,128)S(1)}, f32[4,4,32,128]{3,2,1,0:T(8,128)S(1)}, u32[]{:S(2)}, u32[]{:S(2)}) %collective-permute-start.6) | collective-permute-done | bytes 262176 | tf_op jit(solution)/shard_map/ppermute | solution.py:55
  52.6 1.6 %collective-permute-done.7.slab2 = f32[4,4,32,128]{3,2,1,0:T(8,128)S(1)} collective-permute-done((f32[4,4,32,128]{3,2,1,0:T(8,128)S(1)}, f32[4,4,32,128]{3,2,1,0:T(8,128)S(1)}, u32[]{:S(2)}, u32[]{:S(2)}) %collective-permute-start.7) | collective-permute-done | bytes 262176 | tf_op jit(solution)/shard_map/ppermute | solution.py:55
  54.2 3.4 %collective-permute-done.8.slab3 = f32[4,4,32,128]{3,2,1,0:T(8,128)S(1)} collective-permute-done((f32[4,4,32,128]{3,2,1,0:T(8,128)S(1)}, f32[4,4,32,128]{3,2,1,0:T(8,128)S(1)}, u32[]{:S(2)}, u32[]{:S(2)}) %collective-permute-start.8) | collective-permute-done | bytes 262176 | tf_op jit(solution)/shard_map/ppermute | solution.py:55
  57.6 0.0 copy-done.5
  57.6 1.0 %shard_map.124 = bf16[128,1152]{1,0:T(8,128)(2,1)S(1)} custom-call(s32[6]{0:T(128)S(1)} %stack.15.place, s32[4,16]{1,0:T(4,128)S(1)} %bitcast.23, bf16[256,128]{1,0:T(8,128)(2,1)S(1)} %get-tuple-element.36.select, s32[128,128]{1,0:T(8,128)S(1)} %get-tuple-element.37.lengths, f32[4,4,32,128]{3,2,1,0:T(8,128)S(1)} %shard_map.121.slab0, ...), custom_call_target="tpu_custom_call" | custom-call | tf_op jit(solution)/shard_map/pallas_call | solution.py:618
  58.6 33.6 %all_to_all.5 = bf16[16,8,1152]{2,1,0:T(8,128)(2,1)S(1)} all-to-all(bf16[16,8,1152]{2,1,0:T(8,128)(2,1)S(1)} %bitcast.11), channel_id=1, replica_groups=mesh['depth'=4,'row'=8,'col'=16] {'col'}, dimensions={0} | all-to-all | bytes 589824 | tf_op jit(solution)/shard_map/all_to_all | solution.py:624
  92.1 1.3 %shard_map.125 = f32[512,128]{1,0:T(8,128)} custom-call(bf16[128,1152]{1,0:T(8,128)(2,1)S(1)} %bitcast.12, bf16[4,128,128]{2,1,0:T(8,128)(2,1)S(1)} %get-tuple-element.39.warp), custom_call_target="tpu_custom_call" | custom-call | tf_op jit(solution)/shard_map/pallas_call | solution.py:631
Async XLA Ops:
  1.7 7.1 %collective-permute-start = (bf16[4,3,32,128]{3,2,1,0:T(8,128)(2,1)S(1)}, bf16[4,3,32,128]{3,2,1,0:T(8,128)(2,1)S(1)}, u32[]{:S(2)}, u32[]{:S(2)}) collective-permute-start(bf16[4,3,32,128]{3,2,1,0:T(8,128)(2,1)S(1)} %get-tuple-element.21), channel_id=1, source_target_pairs={{0,128},{128,256},{256,384},{1,129},{129,257},{257,385},{2,130},{1... | collective-permute-start | bytes 294920 | tf_op jit(solution)/shard_map/ppermute | solution.py:60
  3.0 9.9 %copy-start.3 = (s32[4,1,32,1]{2,3,1,0:T(1,128)S(1)}, s32[4,1,32,1]{2,3,1,0:T(1,128)}, u32[]{:S(2)}) copy-start(s32[4,1,32,1]{2,3,1,0:T(1,128)} %param.18) | copy-start | bytes 1540
  3.0 9.9 %copy-start.4 = (s32[4,1,32]{2,1,0:T(1,128)S(1)}, s32[4,1,32]{2,1,0:T(1,128)}, u32[]{:S(2)}) copy-start(s32[4,1,32]{2,1,0:T(1,128)} %param.17) | copy-start | bytes 1540
  3.0 6.8 %collective-permute-start.1 = (bf16[4,3,32,128]{3,2,1,0:T(8,128)(2,1)S(1)}, bf16[4,3,32,128]{3,2,1,0:T(8,128)(2,1)S(1)}, u32[]{:S(2)}, u32[]{:S(2)}) collective-permute-start(bf16[4,3,32,128]{3,2,1,0:T(8,128)(2,1)S(1)} %get-tuple-element.22), channel_id=1, source_target_pairs={{128,0},{256,128},{384,256},{129,1},{257,129},{385,257},{130,2},{2... | collective-permute-start | bytes 294920 | tf_op jit(solution)/shard_map/ppermute | solution.py:65
  9.8 4.9 %collective-permute-start.2 = (bf16[3,88,128]{2,1,0:T(8,128)(2,1)S(1)}, bf16[3,88,128]{2,1,0:T(8,128)(2,1)S(1)}, u32[]{:S(2)}, u32[]{:S(2)}) collective-permute-start(bf16[3,88,128]{2,1,0:T(8,128)(2,1)S(1)} %get-tuple-element.28), channel_id=1, source_target_pairs={{0,16},{16,32},{32,48},{48,64},{64,80},{80,96},{96,112},{112,0},{1... | collective-permute-start | bytes 202760 | tf_op jit(solution)/shard_map/ppermute | solution.py:55
  9.9 4.9 %collective-permute-start.3 = (bf16[3,88,128]{2,1,0:T(8,128)(2,1)S(1)}, bf16[3,88,128]{2,1,0:T(8,128)(2,1)S(1)}, u32[]{:S(2)}, u32[]{:S(2)}) collective-permute-start(bf16[3,88,128]{2,1,0:T(8,128)(2,1)S(1)} %get-tuple-element.29), channel_id=1, source_target_pairs={{0,112},{16,0},{32,16},{48,32},{64,48},{80,64},{96,80},{112,96},{1... | collective-permute-start | bytes 202760 | tf_op jit(solution)/shard_map/ppermute | solution.py:55
  15.7 10.6 %collective-permute-start.5 = (bf16[8,3584]{1,0:T(8,128)(2,1)S(1)}, bf16[8,3584]{1,0:T(8,128)(2,1)S(1)}, u32[]{:S(2)}, u32[]{:S(2)}) collective-permute-start(bf16[8,3584]{1,0:T(8,128)(2,1)S(1)} %get-tuple-element.33.low), channel_id=1, source_target_pairs={{1,0},{2,1},{3,2},{4,3},{5,4},{6,5},{7,6},{8,7},{9,8},{10,9},{11,1... | collective-permute-start | bytes 172040 | tf_op jit(solution)/shard_map/ppermute | solution.py:65
  17.0 9.3 %collective-permute-start.4 = (bf16[8,3584]{1,0:T(8,128)(2,1)S(1)}, bf16[8,3584]{1,0:T(8,128)(2,1)S(1)}, u32[]{:S(2)}, u32[]{:S(2)}) collective-permute-start(bf16[8,3584]{1,0:T(8,128)(2,1)S(1)} %get-tuple-element.34.high), channel_id=1, source_target_pairs={{0,1},{1,2},{2,3},{3,4},{4,5},{5,6},{6,7},{7,8},{8,9},{9,10},{10,1... | collective-permute-start | bytes 172040 | tf_op jit(solution)/shard_map/ppermute | solution.py:60
  26.3 2.6 %copy-start = (f32[16,4,2]{0,2,1:T(2,128)S(1)}, f32[16,4,2]{0,2,1:T(2,128)}, u32[]{:S(2)}) copy-start(f32[16,4,2]{0,2,1:T(2,128)} %param.14) | copy-start | bytes 1540
  26.3 2.6 %copy-start.1 = (f32[16,4]{0,1:T(4,128)S(1)}, f32[16,4]{0,1:T(4,128)}, u32[]{:S(2)}) copy-start(f32[16,4]{0,1:T(4,128)} %param.15) | copy-start | bytes 772
  26.3 2.6 %copy-start.2 = (f32[16]{0:T(128)S(1)}, f32[16]{0:T(128)}, u32[]{:S(2)}) copy-start(f32[16]{0:T(128)} %shear.7) | copy-start | bytes 196
  35.6 22.0 %copy-start.5 = (s32[16,4]{0,1:T(4,128)S(1)}, s32[16,4]{0,1:T(4,128)}, u32[]{:S(2)}) copy-start(s32[16,4]{0,1:T(4,128)} %param.16) | copy-start | bytes 772
  35.6 17.0 %collective-permute-start.6 = (f32[4,4,32,128]{3,2,1,0:T(8,128)S(1)}, f32[4,4,32,128]{3,2,1,0:T(8,128)S(1)}, u32[]{:S(2)}, u32[]{:S(2)}) collective-permute-start(f32[4,4,32,128]{3,2,1,0:T(8,128)S(1)} %get-tuple-element.38), channel_id=1, source_target_pairs={{0,128},{128,256},{256,384},{384,0},{1,129},{129,257},{257,385},{3... | collective-permute-start | bytes 786440 | tf_op jit(solution)/shard_map/ppermute | solution.py:55
  43.1 11.1 %collective-permute-start.7 = (f32[4,4,32,128]{3,2,1,0:T(8,128)S(1)}, f32[4,4,32,128]{3,2,1,0:T(8,128)S(1)}, u32[]{:S(2)}, u32[]{:S(2)}) collective-permute-start(f32[4,4,32,128]{3,2,1,0:T(8,128)S(1)} %shard_map.122), channel_id=1, source_target_pairs={{0,256},{128,384},{256,0},{384,128},{1,257},{129,385},{257,1},{385... | collective-permute-start | bytes 786440 | tf_op jit(solution)/shard_map/ppermute | solution.py:55
  45.0 12.5 %collective-permute-start.8 = (f32[4,4,32,128]{3,2,1,0:T(8,128)S(1)}, f32[4,4,32,128]{3,2,1,0:T(8,128)S(1)}, u32[]{:S(2)}, u32[]{:S(2)}) collective-permute-start(f32[4,4,32,128]{3,2,1,0:T(8,128)S(1)} %shard_map.123), channel_id=1, source_target_pairs={{0,384},{128,0},{256,128},{384,256},{1,385},{129,1},{257,129},{385... | collective-permute-start | bytes 786440 | tf_op jit(solution)/shard_map/ppermute | solution.py:55

commit v10 on v9

--- a/solution.py
+++ b/solution.py
@@ -86,7 +86,7 @@
     high[...] = held[1].astype(BF16)
 
 
-def load_brick(species, diff, rate, brick, sems):
+def load_brick(species, diff, rate, brick, edges, sems):
     copies = [
         pltpu.make_async_copy(
             source, brick.at[f, pl.ds(HALO, 16), pl.ds(0, 32), :], sems.at[f]
@@ -97,8 +97,19 @@
         copy.start()
     for f in range(4):
         brick[f, :, 32:ROWS, :] = jnp.zeros((PLANES, ROWS - 32, 128), F32)
+        brick[f, 0:HALO, 0:32, :] = jnp.zeros((HALO, 32, 128), F32)
+        brick[f, HALO + 16 :, 0:32, :] = jnp.zeros((HALO, 32, 128), F32)
     for copy in copies:
         copy.wait()
+    pick = column_picker(0, 128 - EDGE)
+    count = PLANES * ROWS
+    for f in range(2):
+        rows = brick[f].reshape(count, 128)
+        rest = (rows - rows.astype(BF16).astype(F32)).astype(BF16)
+        edges[:, f * LINES : f * LINES + count] = lax.dot_general(
+            pick, rest, NT, preferred_element_type=F32
+        )
+        edges[:, f * LINES + count : (f + 1) * LINES] = jnp.zeros((16, LINES - count), F32)
 
 
 def pack_rows(unused, before, after, brick, low, high):
@@ -166,7 +177,7 @@
     return results
 
 
-def advance_own(place, brick, shifted, edges, first, second, coefs):
+def advance_own(place, brick, shifted, first, second, coefs):
     n = ROWS
     depth_at, row_at = place[0], place[1]
     depth_last, row_last = place[3], place[4]
@@ -228,16 +239,6 @@
             shifted[RIM, f, k] = (brick[f, p] * (1.0 / 3.0) + (2.0 / 3.0) * moved[f])[:32]
 
     shift_plane(15)
-
-    pick = column_picker(0, 128 - EDGE)
-    count = PLANES * ROWS
-    for f in range(2):
-        rows = brick[f].reshape(count, 128)
-        rest = (rows - rows.astype(BF16).astype(F32)).astype(BF16)
-        edges[:, f * LINES : f * LINES + count] = lax.dot_general(
-            pick, rest, NT, preferred_element_type=F32
-        )
-        edges[:, f * LINES + count : (f + 1) * LINES] = jnp.zeros((16, LINES - count), F32)
 
 
 def advance_edges(
@@ -489,7 +490,7 @@
     outgoing[:, 1088:1152] = dealt[half:, 576:640]
 
 
-def resample(incoming, warp, frame):
+def resample(incoming, warp, frame, done, sems):
     rows = incoming.shape[0]
     ids = incoming[:, 1024:1152].astype(F32)
     lane = lax.broadcasted_iota(jnp.int32, (rows, 128), 1)
@@ -501,6 +502,7 @@
         place = (names == line).astype(F32).astype(BF16)
         part = incoming[:, 512 * odd : 512 * (odd + 1)]
         total = total + lax.dot_general(place, part, TN, preferred_element_type=F32)
+    copies = []
     for v in range(4):
         rows = jnp.concatenate(
             [total[32 * v : 32 * (v + 1), 128 * c : 128 * (c + 1)] for c in range(4)], axis=0
@@ -511,7 +513,12 @@
             warped = warped + jnp.dot(part, warp[v], preferred_element_type=F32)
             rows = rows - part.astype(F32)
         for c in range(4):
-            frame[pl.ds(128 * v + c, 32, stride=4), :] = warped[32 * c : 32 * (c + 1)]
+            done[pl.ds(128 * v + c, 32, stride=4), :] = warped[32 * c : 32 * (c + 1)]
+        cut = pl.ds(128 * v, 128)
+        copies.append(pltpu.make_async_copy(done.at[cut], frame.at[cut], sems.at[v]))
+        copies[-1].start()
+    for copy in copies:
+        copy.wait()
 
 
 def body(
@@ -551,7 +558,12 @@
     )(*fields)
     before, after = shift_up(high, "depth"), shift_down(low, "depth")
     brick_type = jax.ShapeDtypeStruct((4, PLANES, ROWS, 128), F32)
-    brick = call(load_brick, brick_type, [HBM_SPEC] * 3, [pltpu.SemaphoreType.DMA((4,))])(*fields)
+    brick, edges = call(
+        load_brick,
+        (brick_type, jax.ShapeDtypeStruct((16, 2 * LINES), F32)),
+        [HBM_SPEC] * 3,
+        [pltpu.SemaphoreType.DMA((4,))],
+    )(*fields)
     face = jax.ShapeDtypeStruct((HALO, 4 * PLANES, 128), BF16)
     brick, low, high = call(
         pack_rows, (brick_type, face, face), [VMEM_SPEC] * 3, aliases={0: 0}
@@ -581,9 +593,9 @@
     right = shift_down(low, "col")
     wide = pltpu.VMEM((2, PLANES, ROWS, 128), F32)
     shifted_type = jax.ShapeDtypeStruct((SHIFTS,) + species.shape, F32)
-    shifted, edges = call(
+    shifted = call(
         advance_own,
-        (shifted_type, jax.ShapeDtypeStruct((16, 2 * LINES), F32)),
+        shifted_type,
         [SMEM_SPEC, VMEM_SPEC],
         [wide, wide, pltpu.VMEM((6, PLANES, ROWS, 128), F32)],
         limit=12,
@@ -628,9 +640,13 @@
         concat_axis=0,
         tiled=True,
     ).reshape(slots // 2, 1152)
-    frame = call(resample, jax.ShapeDtypeStruct((4 * lines, 128), F32), [VMEM_SPEC] * 2)(
-        incoming, warp_own
-    )
+    frame = call(
+        resample,
+        jax.ShapeDtypeStruct((4 * lines, 128), F32),
+        [VMEM_SPEC] * 2,
+        [pltpu.VMEM((4 * lines, 128), F32), pltpu.SemaphoreType.DMA((4,))],
+        out_specs=HBM_SPEC,
+    )(incoming, warp_own)
     return species_out, frame.reshape(view_count, 32, 4, 128)
 
 

time: 95 us -> 94.9 us (level)
  no operation moved by 1% of the time
where the time goes in v10:
time: 94.9 us; the launch traced here: 93.3 us
  blocking collectives  33.6 us (35%)
  starting transfers between devices  26.8 us (28%)
  Pallas kernels  23.2 us (24%)
  waiting for transfers between devices  8.66 us (9%)
    all_to_all x1, blocking collectives, body(): lax.all_to_all(outgoing.reshape(col_devices, -1, 1152), 'col', split_axis...  33.6 us
    ppermute x5, starting transfers between devices, turn_by(): return lax.ppermute(x, axis, [(i, (i + steps) % n) for i in range(n)])  15.1 us
    ppermute x5, waiting for transfers between devices, turn_by(): return lax.ppermute(x, axis, [(i, (i + steps) % n) for i in range(n)])  7.96 us
    pallas_call x3, Pallas kernels, body(): call(functools.partial(render, away), image, [SMEM_SPEC] * 4 + [VMEM_SPEC])  6.67 us
    ppermute x2, starting transfers between devices, shift_down(): return lax.ppermute(x, axis, [(i + 1, i) for i in range(n - 1)])  5.85 us
    ppermute x2, starting transfers between devices, shift_up(): return lax.ppermute(x, axis, [(i, i + 1) for i in range(n - 1)])  5.84 us
    pallas_call x1, Pallas kernels, body(): call(advance_own, shifted_type, [SMEM_SPEC, VMEM_SPEC], [wide, wide, pltp...  4.58 us
    pallas_call x1, Pallas kernels, body(): call(advance_edges, shifted_type, [SMEM_SPEC] + [VMEM_SPEC] * 6, [pltpu.V...  2.53 us
  transfers between devices with their start and end apart: 9, of which 5 were waited for; matrix products, arithmetic and copies ran while one was open for 0% of the time, Pallas kernels for 10%

profile of v10, /device:TPU:6, one launch (start us, length us, event | category | flops | bytes accessed | tf_op | source)
XLA Modules:
  0.0 93.3 jit_solution(1547777366862611367)
XLA Ops:
  0.6 1.1 %shard_map.114 = (bf16[4,3,32,128]{3,2,1,0:T(8,128)(2,1)S(1)}, bf16[4,3,32,128]{3,2,1,0:T(8,128)(2,1)S(1)}) custom-call(f32[2,16,32,128]{3,2,1,0:T(8,128)} %species.3, f32[16,32,128]{2,1,0:T(8,128)} %diff.3, f32[16,32,128]{2,1,0:T(8,128)} %rate.3), custom_call_target="tpu_custom_call" | custom-call | tf_op jit(solution)/shard_map/pallas_call | solution.py:553
  1.7 0.0 copy-start.3
  1.7 0.0 copy-start.4
  1.7 1.3 %collective-permute-start = (bf16[4,3,32,128]{3,2,1,0:T(8,128)(2,1)S(1)}, bf16[4,3,32,128]{3,2,1,0:T(8,128)(2,1)S(1)}, u32[]{:S(2)}, u32[]{:S(2)}) collective-permute-start(bf16[4,3,32,128]{3,2,1,0:T(8,128)(2,1)S(1)} %get-tuple-element.22), channel_id=1, source_target_pairs={{0,128},{128,256},{256,384},{1,129},{129,257},{257,385},{2,130},{1... | collective-permute-start | bytes 294920 | tf_op jit(solution)/shard_map/ppermute | solution.py:60
  3.0 4.6 %collective-permute-start.1 = (bf16[4,3,32,128]{3,2,1,0:T(8,128)(2,1)S(1)}, bf16[4,3,32,128]{3,2,1,0:T(8,128)(2,1)S(1)}, u32[]{:S(2)}, u32[]{:S(2)}) collective-permute-start(bf16[4,3,32,128]{3,2,1,0:T(8,128)(2,1)S(1)} %get-tuple-element.23), channel_id=1, source_target_pairs={{128,0},{256,128},{384,256},{129,1},{257,129},{385,257},{130,2},{2... | collective-permute-start | bytes 294920 | tf_op jit(solution)/shard_map/ppermute | solution.py:65
  7.6 1.5 %shard_map.113 = (f32[4,22,40,128]{3,2,1,0:T(8,128)S(1)}, f32[16,1792]{1,0:T(8,128)S(1)}) custom-call(f32[2,16,32,128]{3,2,1,0:T(8,128)} %species.3, f32[16,32,128]{2,1,0:T(8,128)} %diff.3, f32[16,32,128]{2,1,0:T(8,128)} %rate.3), custom_call_target="tpu_custom_call" | custom-call | tf_op jit(solution)/shard_map/pallas_call | solution.py:561
  9.1 0.0 collective-permute-done.before
  9.1 0.7 collective-permute-done.1.after
  9.8 0.1 shard_map.115
  9.8 0.0 collective-permute-start.2
  9.9 2.9 %collective-permute-start.3 = (bf16[3,88,128]{2,1,0:T(8,128)(2,1)S(1)}, bf16[3,88,128]{2,1,0:T(8,128)(2,1)S(1)}, u32[]{:S(2)}, u32[]{:S(2)}) collective-permute-start(bf16[3,88,128]{2,1,0:T(8,128)(2,1)S(1)} %get-tuple-element.30), channel_id=1, source_target_pairs={{0,112},{16,0},{32,16},{48,32},{64,48},{80,64},{96,80},{112,96},{1... | collective-permute-start | bytes 202760 | tf_op jit(solution)/shard_map/ppermute | solution.py:55
  12.8 0.1 stack.15.place
  12.9 0.0 copy-done.3
  12.9 0.0 copy-done.4
  12.9 1.5 %shard_map.116 = (bf16[256,128]{1,0:T(8,128)(2,1)S(1)}, s32[128,128]{1,0:T(8,128)S(1)}, bf16[4,128,128]{2,1,0:T(8,128)(2,1)S(1)}) custom-call(s32[6]{0:T(128)S(1)} %stack.15.place, s32[4,32]{1,0:T(4,128)S(1)} %bitcast.21, s32[4,32]{1,0:T(4,128)S(1)} %bitcast.22, bf16[16,128,128]{2,1,0:T(8,128)(2,1)} %warp.1), custom_call_target="tpu_custom_call" | custom-call | tf_op jit(solution)/shard_map/pallas_call | solution.py:574
  14.4 0.4 collective-permute-done.2.above
  14.8 0.0 collective-permute-done.3.below
  14.8 0.9 shard_map.117
  15.7 1.3 %collective-permute-start.5 = (bf16[8,3584]{1,0:T(8,128)(2,1)S(1)}, bf16[8,3584]{1,0:T(8,128)(2,1)S(1)}, u32[]{:S(2)}, u32[]{:S(2)}) collective-permute-start(bf16[8,3584]{1,0:T(8,128)(2,1)S(1)} %get-tuple-element.33.low), channel_id=1, source_target_pairs={{1,0},{2,1},{3,2},{4,3},{5,4},{6,5},{7,6},{8,7},{9,8},{10,9},{11,1... | collective-permute-start | bytes 172040 | tf_op jit(solution)/shard_map/ppermute | solution.py:65
  17.0 4.5 %collective-permute-start.4 = (bf16[8,3584]{1,0:T(8,128)(2,1)S(1)}, bf16[8,3584]{1,0:T(8,128)(2,1)S(1)}, u32[]{:S(2)}, u32[]{:S(2)}) collective-permute-start(bf16[8,3584]{1,0:T(8,128)(2,1)S(1)} %get-tuple-element.34.high), channel_id=1, source_target_pairs={{0,1},{1,2},{2,3},{3,4},{4,5},{5,6},{6,7},{7,8},{8,9},{9,10},{10,1... | collective-permute-start | bytes 172040 | tf_op jit(solution)/shard_map/ppermute | solution.py:60
  21.6 4.6 %shard_map.118.unused = f32[7,2,16,32,128]{4,3,2,1,0:T(8,128)S(1)} custom-call(s32[6]{0:T(128)S(1)} %stack.15.place, f32[4,22,40,128]{3,2,1,0:T(8,128)S(1)} %get-tuple-element.31.brick), custom_call_target="tpu_custom_call" | custom-call | tf_op jit(solution)/shard_map/pallas_call | solution.py:596
  26.2 0.0 collective-permute-done.5.right
  26.2 0.0 collective-permute-done.4.left
  26.2 0.0 copy-start
  26.2 0.0 copy-start.1
  26.2 0.0 copy-start.2
  26.2 2.5 %shard_map.119.shifted = f32[7,2,16,32,128]{4,3,2,1,0:T(8,128)S(1)} custom-call(s32[6]{0:T(128)S(1)} %stack.15.place, f32[7,2,16,32,128]{4,3,2,1,0:T(8,128)S(1)} %shard_map.118.unused, f32[16,1792]{1,0:T(8,128)S(1)} %get-tuple-element.32.edges, bf16[8,3584]{1,0:T(8,128)(2,1)S(1)} %get-tuple-element.33.low, ...), custom_call_target="tpu_custom_call", output_to_operand_aliasing={{}: (1, {})} | custom-call | tf_op jit(solution)/shard_map/pallas_call | solution.py:603
  28.8 0.0 copy-done
  28.8 0.0 copy-done.1
  28.8 0.0 copy-done.2
  28.8 2.2 %shard_map.123 = f32[4,4,32,128]{3,2,1,0:T(8,128)S(1)} custom-call(s32[6]{0:T(128)S(1)} %stack.15.place, f32[16]{0:T(128)S(1)} %copy-done.2, f32[4,2,16]{2,1,0:T(2,128)S(1)} %bitcast.13, f32[4,16]{1,0:T(4,128)S(1)} %bitcast.17, f32[7,2,16,32,128]{4,3,2,1,0:T(8,128)S(1)} %shard_map.119.shifted), custom_call_target="tpu_custom_call" | custom-call | tf_op jit(solution)/shard_map/pallas_call | solution.py:624
  31.0 2.2 %shard_map.122 = f32[4,4,32,128]{3,2,1,0:T(8,128)S(1)} custom-call(s32[6]{0:T(128)S(1)} %stack.15.place, f32[16]{0:T(128)S(1)} %copy-done.2, f32[4,2,16]{2,1,0:T(2,128)S(1)} %bitcast.14, f32[4,16]{1,0:T(4,128)S(1)} %bitcast.18, f32[7,2,16,32,128]{4,3,2,1,0:T(8,128)S(1)} %shard_map.119.shifted), custom_call_target="tpu_custom_call" | custom-call | tf_op jit(solution)/shard_map/pallas_call | solution.py:624
  33.2 2.2 %shard_map.120 = (f32[4,4,32,128]{3,2,1,0:T(8,128)S(1)}, f32[2,16,32,128]{3,2,1,0:T(8,128)}) custom-call(s32[6]{0:T(128)S(1)} %stack.15.place, f32[16]{0:T(128)S(1)} %copy-done.2, f32[4,2,16]{2,1,0:T(2,128)S(1)} %bitcast.15, f32[4,16]{1,0:T(4,128)S(1)} %bitcast.19, f32[7,2,16,32,128]{4,3,2,1,0:T(8,128)S(1)} %shard_map.119.shifted), custom_call_target="tpu_custom_call" | custom-call | tf_op jit(solution)/shard_map/pallas_call | solution.py:616
  35.5 0.0 copy-start.5
  35.5 7.5 %collective-permute-start.6 = (f32[4,4,32,128]{3,2,1,0:T(8,128)S(1)}, f32[4,4,32,128]{3,2,1,0:T(8,128)S(1)}, u32[]{:S(2)}, u32[]{:S(2)}) collective-permute-start(f32[4,4,32,128]{3,2,1,0:T(8,128)S(1)} %get-tuple-element.38), channel_id=1, source_target_pairs={{0,128},{128,256},{256,384},{384,0},{1,129},{129,257},{257,385},{3... | collective-permute-start | bytes 786440 | tf_op jit(solution)/shard_map/ppermute | solution.py:55
  43.0 1.9 %collective-permute-start.7 = (f32[4,4,32,128]{3,2,1,0:T(8,128)S(1)}, f32[4,4,32,128]{3,2,1,0:T(8,128)S(1)}, u32[]{:S(2)}, u32[]{:S(2)}) collective-permute-start(f32[4,4,32,128]{3,2,1,0:T(8,128)S(1)} %shard_map.122), channel_id=1, source_target_pairs={{0,256},{128,384},{256,0},{384,128},{1,257},{129,385},{257,1},{385... | collective-permute-start | bytes 786440 | tf_op jit(solution)/shard_map/ppermute | solution.py:55
  44.9 2.8 %collective-permute-start.8 = (f32[4,4,32,128]{3,2,1,0:T(8,128)S(1)}, f32[4,4,32,128]{3,2,1,0:T(8,128)S(1)}, u32[]{:S(2)}, u32[]{:S(2)}) collective-permute-start(f32[4,4,32,128]{3,2,1,0:T(8,128)S(1)} %shard_map.123), channel_id=1, source_target_pairs={{0,384},{128,0},{256,128},{384,256},{1,385},{129,1},{257,129},{385... | collective-permute-start | bytes 786440 | tf_op jit(solution)/shard_map/ppermute | solution.py:55
  47.7 2.2 %shard_map.121.slab0 = f32[4,4,32,128]{3,2,1,0:T(8,128)S(1)} custom-call(s32[6]{0:T(128)S(1)} %stack.15.place, f32[16]{0:T(128)S(1)} %copy-done.2, f32[4,2,16]{2,1,0:T(2,128)S(1)} %bitcast.16, f32[4,16]{1,0:T(4,128)S(1)} %bitcast.20, f32[7,2,16,32,128]{4,3,2,1,0:T(8,128)S(1)} %shard_map.119.shifted), custom_call_target="tpu_custom_call" | custom-call | tf_op jit(solution)/shard_map/pallas_call | solution.py:624
  49.9 2.6 %collective-permute-done.6.slab1 = f32[4,4,32,128]{3,2,1,0:T(8,128)S(1)} collective-permute-done((f32[4,4,32,128]{3,2,1,0:T(8,128)S(1)}, f32[4,4,32,128]{3,2,1,0:T(8,128)S(1)}, u32[]{:S(2)}, u32[]{:S(2)}) %collective-permute-start.6) | collective-permute-done | bytes 262176 | tf_op jit(solution)/shard_map/ppermute | solution.py:55
  52.5 1.6 %collective-permute-done.7.slab2 = f32[4,4,32,128]{3,2,1,0:T(8,128)S(1)} collective-permute-done((f32[4,4,32,128]{3,2,1,0:T(8,128)S(1)}, f32[4,4,32,128]{3,2,1,0:T(8,128)S(1)}, u32[]{:S(2)}, u32[]{:S(2)}) %collective-permute-start.7) | collective-permute-done | bytes 262176 | tf_op jit(solution)/shard_map/ppermute | solution.py:55
  54.1 3.4 %collective-permute-done.8.slab3 = f32[4,4,32,128]{3,2,1,0:T(8,128)S(1)} collective-permute-done((f32[4,4,32,128]{3,2,1,0:T(8,128)S(1)}, f32[4,4,32,128]{3,2,1,0:T(8,128)S(1)}, u32[]{:S(2)}, u32[]{:S(2)}) %collective-permute-start.8) | collective-permute-done | bytes 262176 | tf_op jit(solution)/shard_map/ppermute | solution.py:55
  57.5 0.0 copy-done.5
  57.5 1.0 %shard_map.124 = bf16[128,1152]{1,0:T(8,128)(2,1)S(1)} custom-call(s32[6]{0:T(128)S(1)} %stack.15.place, s32[4,16]{1,0:T(4,128)S(1)} %bitcast.23, bf16[256,128]{1,0:T(8,128)(2,1)S(1)} %get-tuple-element.36.select, s32[128,128]{1,0:T(8,128)S(1)} %get-tuple-element.37.lengths, f32[4,4,32,128]{3,2,1,0:T(8,128)S(1)} %shard_map.121.slab0, ...), custom_call_target="tpu_custom_call" | custom-call | tf_op jit(solution)/shard_map/pallas_call | solution.py:630
  58.5 33.6 %all_to_all.5 = bf16[16,8,1152]{2,1,0:T(8,128)(2,1)S(1)} all-to-all(bf16[16,8,1152]{2,1,0:T(8,128)(2,1)S(1)} %bitcast.11), channel_id=1, replica_groups=mesh['depth'=4,'row'=8,'col'=16] {'col'}, dimensions={0} | all-to-all | bytes 589824 | tf_op jit(solution)/shard_map/all_to_all | solution.py:636
  92.0 1.2 %shard_map.125 = f32[512,128]{1,0:T(8,128)} custom-call(bf16[128,1152]{1,0:T(8,128)(2,1)S(1)} %bitcast.12, bf16[4,128,128]{2,1,0:T(8,128)(2,1)S(1)} %get-tuple-element.39.warp), custom_call_target="tpu_custom_call" | custom-call | tf_op jit(solution)/shard_map/pallas_call | solution.py:643
Async XLA Ops:
  1.7 11.2 %copy-start.3 = (s32[4,1,32,1]{2,3,1,0:T(1,128)S(1)}, s32[4,1,32,1]{2,3,1,0:T(1,128)}, u32[]{:S(2)}) copy-start(s32[4,1,32,1]{2,3,1,0:T(1,128)} %param.18) | copy-start | bytes 1540
  1.7 11.2 %copy-start.4 = (s32[4,1,32]{2,1,0:T(1,128)S(1)}, s32[4,1,32]{2,1,0:T(1,128)}, u32[]{:S(2)}) copy-start(s32[4,1,32]{2,1,0:T(1,128)} %param.17) | copy-start | bytes 1540
  1.7 7.3 %collective-permute-start = (bf16[4,3,32,128]{3,2,1,0:T(8,128)(2,1)S(1)}, bf16[4,3,32,128]{3,2,1,0:T(8,128)(2,1)S(1)}, u32[]{:S(2)}, u32[]{:S(2)}) collective-permute-start(bf16[4,3,32,128]{3,2,1,0:T(8,128)(2,1)S(1)} %get-tuple-element.22), channel_id=1, source_target_pairs={{0,128},{128,256},{256,384},{1,129},{129,257},{257,385},{2,130},{1... | collective-permute-start | bytes 294920 | tf_op jit(solution)/shard_map/ppermute | solution.py:60
  3.0 6.8 %collective-permute-start.1 = (bf16[4,3,32,128]{3,2,1,0:T(8,128)(2,1)S(1)}, bf16[4,3,32,128]{3,2,1,0:T(8,128)(2,1)S(1)}, u32[]{:S(2)}, u32[]{:S(2)}) collective-permute-start(bf16[4,3,32,128]{3,2,1,0:T(8,128)(2,1)S(1)} %get-tuple-element.23), channel_id=1, source_target_pairs={{128,0},{256,128},{384,256},{129,1},{257,129},{385,257},{130,2},{2... | collective-permute-start | bytes 294920 | tf_op jit(solution)/shard_map/ppermute | solution.py:65
  9.8 4.9 %collective-permute-start.2 = (bf16[3,88,128]{2,1,0:T(8,128)(2,1)S(1)}, bf16[3,88,128]{2,1,0:T(8,128)(2,1)S(1)}, u32[]{:S(2)}, u32[]{:S(2)}) collective-permute-start(bf16[3,88,128]{2,1,0:T(8,128)(2,1)S(1)} %get-tuple-element.29), channel_id=1, source_target_pairs={{0,16},{16,32},{32,48},{48,64},{64,80},{80,96},{96,112},{112,0},{1... | collective-permute-start | bytes 202760 | tf_op jit(solution)/shard_map/ppermute | solution.py:55
  9.9 4.9 %collective-permute-start.3 = (bf16[3,88,128]{2,1,0:T(8,128)(2,1)S(1)}, bf16[3,88,128]{2,1,0:T(8,128)(2,1)S(1)}, u32[]{:S(2)}, u32[]{:S(2)}) collective-permute-start(bf16[3,88,128]{2,1,0:T(8,128)(2,1)S(1)} %get-tuple-element.30), channel_id=1, source_target_pairs={{0,112},{16,0},{32,16},{48,32},{64,48},{80,64},{96,80},{112,96},{1... | collective-permute-start | bytes 202760 | tf_op jit(solution)/shard_map/ppermute | solution.py:55
  15.7 10.5 %collective-permute-start.5 = (bf16[8,3584]{1,0:T(8,128)(2,1)S(1)}, bf16[8,3584]{1,0:T(8,128)(2,1)S(1)}, u32[]{:S(2)}, u32[]{:S(2)}) collective-permute-start(bf16[8,3584]{1,0:T(8,128)(2,1)S(1)} %get-tuple-element.33.low), channel_id=1, source_target_pairs={{1,0},{2,1},{3,2},{4,3},{5,4},{6,5},{7,6},{8,7},{9,8},{10,9},{11,1... | collective-permute-start | bytes 172040 | tf_op jit(solution)/shard_map/ppermute | solution.py:65
  17.0 9.2 %collective-permute-start.4 = (bf16[8,3584]{1,0:T(8,128)(2,1)S(1)}, bf16[8,3584]{1,0:T(8,128)(2,1)S(1)}, u32[]{:S(2)}, u32[]{:S(2)}) collective-permute-start(bf16[8,3584]{1,0:T(8,128)(2,1)S(1)} %get-tuple-element.34.high), channel_id=1, source_target_pairs={{0,1},{1,2},{2,3},{3,4},{4,5},{5,6},{6,7},{7,8},{8,9},{9,10},{10,1... | collective-permute-start | bytes 172040 | tf_op jit(solution)/shard_map/ppermute | solution.py:60
  26.2 2.6 %copy-start = (f32[16,4,2]{0,2,1:T(2,128)S(1)}, f32[16,4,2]{0,2,1:T(2,128)}, u32[]{:S(2)}) copy-start(f32[16,4,2]{0,2,1:T(2,128)} %param.14) | copy-start | bytes 1540
  26.2 2.6 %copy-start.1 = (f32[16,4]{0,1:T(4,128)S(1)}, f32[16,4]{0,1:T(4,128)}, u32[]{:S(2)}) copy-start(f32[16,4]{0,1:T(4,128)} %param.15) | copy-start | bytes 772
  26.2 2.6 %copy-start.2 = (f32[16]{0:T(128)S(1)}, f32[16]{0:T(128)}, u32[]{:S(2)}) copy-start(f32[16]{0:T(128)} %shear.7) | copy-start | bytes 196
  35.5 22.0 %copy-start.5 = (s32[16,4]{0,1:T(4,128)S(1)}, s32[16,4]{0,1:T(4,128)}, u32[]{:S(2)}) copy-start(s32[16,4]{0,1:T(4,128)} %param.16) | copy-start | bytes 772
  35.5 17.0 %collective-permute-start.6 = (f32[4,4,32,128]{3,2,1,0:T(8,128)S(1)}, f32[4,4,32,128]{3,2,1,0:T(8,128)S(1)}, u32[]{:S(2)}, u32[]{:S(2)}) collective-permute-start(f32[4,4,32,128]{3,2,1,0:T(8,128)S(1)} %get-tuple-element.38), channel_id=1, source_target_pairs={{0,128},{128,256},{256,384},{384,0},{1,129},{129,257},{257,385},{3... | collective-permute-start | bytes 786440 | tf_op jit(solution)/shard_map/ppermute | solution.py:55
  43.0 11.1 %collective-permute-start.7 = (f32[4,4,32,128]{3,2,1,0:T(8,128)S(1)}, f32[4,4,32,128]{3,2,1,0:T(8,128)S(1)}, u32[]{:S(2)}, u32[]{:S(2)}) collective-permute-start(f32[4,4,32,128]{3,2,1,0:T(8,128)S(1)} %shard_map.122), channel_id=1, source_target_pairs={{0,256},{128,384},{256,0},{384,128},{1,257},{129,385},{257,1},{385... | collective-permute-start | bytes 786440 | tf_op jit(solution)/shard_map/ppermute | solution.py:55
  44.9 12.5 %collective-permute-start.8 = (f32[4,4,32,128]{3,2,1,0:T(8,128)S(1)}, f32[4,4,32,128]{3,2,1,0:T(8,128)S(1)}, u32[]{:S(2)}, u32[]{:S(2)}) collective-permute-start(f32[4,4,32,128]{3,2,1,0:T(8,128)S(1)} %shard_map.123), channel_id=1, source_target_pairs={{0,384},{128,0},{256,128},{384,256},{1,385},{129,1},{257,129},{385... | collective-permute-start | bytes 786440 | tf_op jit(solution)/shard_map/ppermute | solution.py:55

commit v11 on v9

--- a/solution.py
+++ b/solution.py
@@ -400,8 +400,8 @@
         ]
         slope = shear[v]
 
-        for part in range(4):
-            strip = slice(part * 8, (part + 1) * 8)
+        for part in range(2):
+            strip = slice(part * 16, (part + 1) * 16)
 
             def march(k, state):
                 c0, c1, c2, total, through = state
@@ -422,7 +422,7 @@
                 c2 = c2 + part * jnp.tanh(logits[2])
                 return c0, c1, c2, total, after
 
-            zero = jnp.zeros((8, 128), F32)
+            zero = jnp.zeros((16, 128), F32)
             c0, c1, c2, _, through = lax.fori_loop(
                 0, depth_cells, march, (zero, zero, zero, zero, zero + 1.0), unroll=16
             )

time: 95 us -> 95 us (level)
  no operation moved by 1% of the time
where the time goes in v11:
time: 95 us; the launch traced here: 93.4 us
  blocking collectives  33.6 us (35%)
  starting transfers between devices  26.8 us (28%)
  Pallas kernels  23.1 us (24%)
  waiting for transfers between devices  8.9 us (9%)
    all_to_all x1, blocking collectives, body(): lax.all_to_all(outgoing.reshape(col_devices, -1, 1152), 'col', split_axis...  33.6 us
    ppermute x5, starting transfers between devices, turn_by(): return lax.ppermute(x, axis, [(i, (i + steps) % n) for i in range(n)])  15.1 us
    ppermute x5, waiting for transfers between devices, turn_by(): return lax.ppermute(x, axis, [(i, (i + steps) % n) for i in range(n)])  7.94 us
    pallas_call x3, Pallas kernels, body(): call(functools.partial(render, away), image, [SMEM_SPEC] * 4 + [VMEM_SPEC])  6.68 us
    ppermute x2, starting transfers between devices, shift_down(): return lax.ppermute(x, axis, [(i + 1, i) for i in range(n - 1)])  5.85 us
    ppermute x2, starting transfers between devices, shift_up(): return lax.ppermute(x, axis, [(i, i + 1) for i in range(n - 1)])  5.84 us
    pallas_call x1, Pallas kernels, body(): call(advance_own, (shifted_type, jax.ShapeDtypeStruct((16, 2 * LINES), F3...  4.7 us
    pallas_call x1, Pallas kernels, body(): call(advance_edges, shifted_type, [SMEM_SPEC] + [VMEM_SPEC] * 6, [pltpu.V...  2.53 us
  transfers between devices with their start and end apart: 9, of which 5 were waited for; matrix products, arithmetic and copies ran while one was open for 0% of the time, Pallas kernels for 10%

profile of v11, /device:TPU:6, one launch (start us, length us, event | category | flops | bytes accessed | tf_op | source)
XLA Modules:
  0.0 93.4 jit_solution(4779540722423447798)
XLA Ops:
  0.6 1.1 %shard_map.114 = (bf16[4,3,32,128]{3,2,1,0:T(8,128)(2,1)S(1)}, bf16[4,3,32,128]{3,2,1,0:T(8,128)(2,1)S(1)}) custom-call(f32[2,16,32,128]{3,2,1,0:T(8,128)} %species.3, f32[16,32,128]{2,1,0:T(8,128)} %diff.3, f32[16,32,128]{2,1,0:T(8,128)} %rate.3), custom_call_target="tpu_custom_call" | custom-call | tf_op jit(solution)/shard_map/pallas_call | solution.py:546
  1.7 1.3 %collective-permute-start = (bf16[4,3,32,128]{3,2,1,0:T(8,128)(2,1)S(1)}, bf16[4,3,32,128]{3,2,1,0:T(8,128)(2,1)S(1)}, u32[]{:S(2)}, u32[]{:S(2)}) collective-permute-start(bf16[4,3,32,128]{3,2,1,0:T(8,128)(2,1)S(1)} %get-tuple-element.21), channel_id=1, source_target_pairs={{0,128},{128,256},{256,384},{1,129},{129,257},{257,385},{2,130},{1... | collective-permute-start | bytes 294920 | tf_op jit(solution)/shard_map/ppermute | solution.py:60
  3.0 0.0 copy-start.3
  3.0 0.0 copy-start.4
  3.0 4.6 %collective-permute-start.1 = (bf16[4,3,32,128]{3,2,1,0:T(8,128)(2,1)S(1)}, bf16[4,3,32,128]{3,2,1,0:T(8,128)(2,1)S(1)}, u32[]{:S(2)}, u32[]{:S(2)}) collective-permute-start(bf16[4,3,32,128]{3,2,1,0:T(8,128)(2,1)S(1)} %get-tuple-element.22), channel_id=1, source_target_pairs={{128,0},{256,128},{384,256},{129,1},{257,129},{385,257},{130,2},{2... | collective-permute-start | bytes 294920 | tf_op jit(solution)/shard_map/ppermute | solution.py:65
  7.6 1.2 %shard_map.113.unused = f32[4,22,40,128]{3,2,1,0:T(8,128)S(1)} custom-call(f32[2,16,32,128]{3,2,1,0:T(8,128)} %species.3, f32[16,32,128]{2,1,0:T(8,128)} %diff.3, f32[16,32,128]{2,1,0:T(8,128)} %rate.3), custom_call_target="tpu_custom_call" | custom-call | tf_op jit(solution)/shard_map/pallas_call | solution.py:554
  8.8 0.0 collective-permute-done.before
  8.8 0.9 %collective-permute-done.1.after = bf16[4,3,32,128]{3,2,1,0:T(8,128)(2,1)S(1)} collective-permute-done((bf16[4,3,32,128]{3,2,1,0:T(8,128)(2,1)S(1)}, bf16[4,3,32,128]{3,2,1,0:T(8,128)(2,1)S(1)}, u32[]{:S(2)}, u32[]{:S(2)}) %collective-permute-start.1) | collective-permute-done | bytes 98336 | tf_op jit(solution)/shard_map/ppermute | solution.py:65
  9.8 0.1 shard_map.115
  9.8 0.0 collective-permute-start.2
  9.9 2.9 %collective-permute-start.3 = (bf16[3,88,128]{2,1,0:T(8,128)(2,1)S(1)}, bf16[3,88,128]{2,1,0:T(8,128)(2,1)S(1)}, u32[]{:S(2)}, u32[]{:S(2)}) collective-permute-start(bf16[3,88,128]{2,1,0:T(8,128)(2,1)S(1)} %get-tuple-element.29), channel_id=1, source_target_pairs={{0,112},{16,0},{32,16},{48,32},{64,48},{80,64},{96,80},{112,96},{1... | collective-permute-start | bytes 202760 | tf_op jit(solution)/shard_map/ppermute | solution.py:55
  12.8 0.1 stack.15.place
  12.9 0.0 copy-done.3
  12.9 0.0 copy-done.4
  12.9 1.5 %shard_map.116 = (bf16[256,128]{1,0:T(8,128)(2,1)S(1)}, s32[128,128]{1,0:T(8,128)S(1)}, bf16[4,128,128]{2,1,0:T(8,128)(2,1)S(1)}) custom-call(s32[6]{0:T(128)S(1)} %stack.15.place, s32[4,32]{1,0:T(4,128)S(1)} %bitcast.21, s32[4,32]{1,0:T(4,128)S(1)} %bitcast.22, bf16[16,128,128]{2,1,0:T(8,128)(2,1)} %warp.1), custom_call_target="tpu_custom_call" | custom-call | tf_op jit(solution)/shard_map/pallas_call | solution.py:562
  14.4 0.4 collective-permute-done.2.above
  14.8 0.0 collective-permute-done.3.below
  14.8 0.9 shard_map.117
  15.7 1.3 %collective-permute-start.5 = (bf16[8,3584]{1,0:T(8,128)(2,1)S(1)}, bf16[8,3584]{1,0:T(8,128)(2,1)S(1)}, u32[]{:S(2)}, u32[]{:S(2)}) collective-permute-start(bf16[8,3584]{1,0:T(8,128)(2,1)S(1)} %get-tuple-element.33.low), channel_id=1, source_target_pairs={{1,0},{2,1},{3,2},{4,3},{5,4},{6,5},{7,6},{8,7},{9,8},{10,9},{11,1... | collective-permute-start | bytes 172040 | tf_op jit(solution)/shard_map/ppermute | solution.py:65
  17.0 4.5 %collective-permute-start.4 = (bf16[8,3584]{1,0:T(8,128)(2,1)S(1)}, bf16[8,3584]{1,0:T(8,128)(2,1)S(1)}, u32[]{:S(2)}, u32[]{:S(2)}) collective-permute-start(bf16[8,3584]{1,0:T(8,128)(2,1)S(1)} %get-tuple-element.34.high), channel_id=1, source_target_pairs={{0,1},{1,2},{2,3},{3,4},{4,5},{5,6},{6,7},{7,8},{8,9},{9,10},{10,1... | collective-permute-start | bytes 172040 | tf_op jit(solution)/shard_map/ppermute | solution.py:60
  21.6 4.7 %shard_map.118 = (f32[7,2,16,32,128]{4,3,2,1,0:T(8,128)S(1)}, f32[16,1792]{1,0:T(8,128)S(1)}) custom-call(s32[6]{0:T(128)S(1)} %stack.15.place, f32[4,22,40,128]{3,2,1,0:T(8,128)S(1)} %get-tuple-element.30.brick), custom_call_target="tpu_custom_call" | custom-call | tf_op jit(solution)/shard_map/pallas_call | solution.py:584
  26.3 0.0 collective-permute-done.5.right
  26.3 0.0 collective-permute-done.4.left
  26.3 0.0 copy-start
  26.3 0.0 copy-start.1
  26.3 0.0 copy-start.2
  26.3 2.5 %shard_map.119.shifted = f32[7,2,16,32,128]{4,3,2,1,0:T(8,128)S(1)} custom-call(s32[6]{0:T(128)S(1)} %stack.15.place, f32[7,2,16,32,128]{4,3,2,1,0:T(8,128)S(1)} %get-tuple-element.31.unused, f32[16,1792]{1,0:T(8,128)S(1)} %get-tuple-element.32.edges, bf16[8,3584]{1,0:T(8,128)(2,1)S(1)} %get-tuple-element.33.low, ...), custom_call_target="tpu_custom_call", output_to_operand_aliasing={{}: (1, {})} | custom-call | tf_op jit(solution)/shard_map/pallas_call | solution.py:591
  28.9 0.0 copy-done
  28.9 0.0 copy-done.1
  28.9 0.0 copy-done.2
  28.9 2.2 %shard_map.123 = f32[4,4,32,128]{3,2,1,0:T(8,128)S(1)} custom-call(s32[6]{0:T(128)S(1)} %stack.15.place, f32[16]{0:T(128)S(1)} %copy-done.2, f32[4,2,16]{2,1,0:T(2,128)S(1)} %bitcast.13, f32[4,16]{1,0:T(4,128)S(1)} %bitcast.17, f32[7,2,16,32,128]{4,3,2,1,0:T(8,128)S(1)} %shard_map.119.shifted), custom_call_target="tpu_custom_call" | custom-call | tf_op jit(solution)/shard_map/pallas_call | solution.py:612
  31.1 2.2 %shard_map.122 = f32[4,4,32,128]{3,2,1,0:T(8,128)S(1)} custom-call(s32[6]{0:T(128)S(1)} %stack.15.place, f32[16]{0:T(128)S(1)} %copy-done.2, f32[4,2,16]{2,1,0:T(2,128)S(1)} %bitcast.14, f32[4,16]{1,0:T(4,128)S(1)} %bitcast.18, f32[7,2,16,32,128]{4,3,2,1,0:T(8,128)S(1)} %shard_map.119.shifted), custom_call_target="tpu_custom_call" | custom-call | tf_op jit(solution)/shard_map/pallas_call | solution.py:612
  33.4 2.2 %shard_map.120 = (f32[4,4,32,128]{3,2,1,0:T(8,128)S(1)}, f32[2,16,32,128]{3,2,1,0:T(8,128)}) custom-call(s32[6]{0:T(128)S(1)} %stack.15.place, f32[16]{0:T(128)S(1)} %copy-done.2, f32[4,2,16]{2,1,0:T(2,128)S(1)} %bitcast.15, f32[4,16]{1,0:T(4,128)S(1)} %bitcast.19, f32[7,2,16,32,128]{4,3,2,1,0:T(8,128)S(1)} %shard_map.119.shifted), custom_call_target="tpu_custom_call" | custom-call | tf_op jit(solution)/shard_map/pallas_call | solution.py:604
  35.6 0.0 copy-start.5
  35.6 7.5 %collective-permute-start.6 = (f32[4,4,32,128]{3,2,1,0:T(8,128)S(1)}, f32[4,4,32,128]{3,2,1,0:T(8,128)S(1)}, u32[]{:S(2)}, u32[]{:S(2)}) collective-permute-start(f32[4,4,32,128]{3,2,1,0:T(8,128)S(1)} %get-tuple-element.38), channel_id=1, source_target_pairs={{0,128},{128,256},{256,384},{384,0},{1,129},{129,257},{257,385},{3... | collective-permute-start | bytes 786440 | tf_op jit(solution)/shard_map/ppermute | solution.py:55
  43.1 1.9 %collective-permute-start.7 = (f32[4,4,32,128]{3,2,1,0:T(8,128)S(1)}, f32[4,4,32,128]{3,2,1,0:T(8,128)S(1)}, u32[]{:S(2)}, u32[]{:S(2)}) collective-permute-start(f32[4,4,32,128]{3,2,1,0:T(8,128)S(1)} %shard_map.122), channel_id=1, source_target_pairs={{0,256},{128,384},{256,0},{384,128},{1,257},{129,385},{257,1},{385... | collective-permute-start | bytes 786440 | tf_op jit(solution)/shard_map/ppermute | solution.py:55
  45.0 2.8 %collective-permute-start.8 = (f32[4,4,32,128]{3,2,1,0:T(8,128)S(1)}, f32[4,4,32,128]{3,2,1,0:T(8,128)S(1)}, u32[]{:S(2)}, u32[]{:S(2)}) collective-permute-start(f32[4,4,32,128]{3,2,1,0:T(8,128)S(1)} %shard_map.123), channel_id=1, source_target_pairs={{0,384},{128,0},{256,128},{384,256},{1,385},{129,1},{257,129},{385... | collective-permute-start | bytes 786440 | tf_op jit(solution)/shard_map/ppermute | solution.py:55
  47.8 2.2 %shard_map.121.slab0 = f32[4,4,32,128]{3,2,1,0:T(8,128)S(1)} custom-call(s32[6]{0:T(128)S(1)} %stack.15.place, f32[16]{0:T(128)S(1)} %copy-done.2, f32[4,2,16]{2,1,0:T(2,128)S(1)} %bitcast.16, f32[4,16]{1,0:T(4,128)S(1)} %bitcast.20, f32[7,2,16,32,128]{4,3,2,1,0:T(8,128)S(1)} %shard_map.119.shifted), custom_call_target="tpu_custom_call" | custom-call | tf_op jit(solution)/shard_map/pallas_call | solution.py:612
  50.0 2.6 %collective-permute-done.6.slab1 = f32[4,4,32,128]{3,2,1,0:T(8,128)S(1)} collective-permute-done((f32[4,4,32,128]{3,2,1,0:T(8,128)S(1)}, f32[4,4,32,128]{3,2,1,0:T(8,128)S(1)}, u32[]{:S(2)}, u32[]{:S(2)}) %collective-permute-start.6) | collective-permute-done | bytes 262176 | tf_op jit(solution)/shard_map/ppermute | solution.py:55
  52.6 1.6 %collective-permute-done.7.slab2 = f32[4,4,32,128]{3,2,1,0:T(8,128)S(1)} collective-permute-done((f32[4,4,32,128]{3,2,1,0:T(8,128)S(1)}, f32[4,4,32,128]{3,2,1,0:T(8,128)S(1)}, u32[]{:S(2)}, u32[]{:S(2)}) %collective-permute-start.7) | collective-permute-done | bytes 262176 | tf_op jit(solution)/shard_map/ppermute | solution.py:55
  54.2 3.4 %collective-permute-done.8.slab3 = f32[4,4,32,128]{3,2,1,0:T(8,128)S(1)} collective-permute-done((f32[4,4,32,128]{3,2,1,0:T(8,128)S(1)}, f32[4,4,32,128]{3,2,1,0:T(8,128)S(1)}, u32[]{:S(2)}, u32[]{:S(2)}) %collective-permute-start.8) | collective-permute-done | bytes 262176 | tf_op jit(solution)/shard_map/ppermute | solution.py:55
  57.6 0.0 copy-done.5
  57.6 1.0 %shard_map.124 = bf16[128,1152]{1,0:T(8,128)(2,1)S(1)} custom-call(s32[6]{0:T(128)S(1)} %stack.15.place, s32[4,16]{1,0:T(4,128)S(1)} %bitcast.23, bf16[256,128]{1,0:T(8,128)(2,1)S(1)} %get-tuple-element.36.select, s32[128,128]{1,0:T(8,128)S(1)} %get-tuple-element.37.lengths, f32[4,4,32,128]{3,2,1,0:T(8,128)S(1)} %shard_map.121.slab0, ...), custom_call_target="tpu_custom_call" | custom-call | tf_op jit(solution)/shard_map/pallas_call | solution.py:618
  58.6 33.6 %all_to_all.5 = bf16[16,8,1152]{2,1,0:T(8,128)(2,1)S(1)} all-to-all(bf16[16,8,1152]{2,1,0:T(8,128)(2,1)S(1)} %bitcast.11), channel_id=1, replica_groups=mesh['depth'=4,'row'=8,'col'=16] {'col'}, dimensions={0} | all-to-all | bytes 589824 | tf_op jit(solution)/shard_map/all_to_all | solution.py:624
  92.1 1.2 %shard_map.125 = f32[512,128]{1,0:T(8,128)} custom-call(bf16[128,1152]{1,0:T(8,128)(2,1)S(1)} %bitcast.12, bf16[4,128,128]{2,1,0:T(8,128)(2,1)S(1)} %get-tuple-element.39.warp), custom_call_target="tpu_custom_call" | custom-call | tf_op jit(solution)/shard_map/pallas_call | solution.py:631
Async XLA Ops:
  1.7 7.1 %collective-permute-start = (bf16[4,3,32,128]{3,2,1,0:T(8,128)(2,1)S(1)}, bf16[4,3,32,128]{3,2,1,0:T(8,128)(2,1)S(1)}, u32[]{:S(2)}, u32[]{:S(2)}) collective-permute-start(bf16[4,3,32,128]{3,2,1,0:T(8,128)(2,1)S(1)} %get-tuple-element.21), channel_id=1, source_target_pairs={{0,128},{128,256},{256,384},{1,129},{129,257},{257,385},{2,130},{1... | collective-permute-start | bytes 294920 | tf_op jit(solution)/shard_map/ppermute | solution.py:60
  3.0 9.9 %copy-start.3 = (s32[4,1,32,1]{2,3,1,0:T(1,128)S(1)}, s32[4,1,32,1]{2,3,1,0:T(1,128)}, u32[]{:S(2)}) copy-start(s32[4,1,32,1]{2,3,1,0:T(1,128)} %param.18) | copy-start | bytes 1540
  3.0 9.9 %copy-start.4 = (s32[4,1,32]{2,1,0:T(1,128)S(1)}, s32[4,1,32]{2,1,0:T(1,128)}, u32[]{:S(2)}) copy-start(s32[4,1,32]{2,1,0:T(1,128)} %param.17) | copy-start | bytes 1540
  3.0 6.8 %collective-permute-start.1 = (bf16[4,3,32,128]{3,2,1,0:T(8,128)(2,1)S(1)}, bf16[4,3,32,128]{3,2,1,0:T(8,128)(2,1)S(1)}, u32[]{:S(2)}, u32[]{:S(2)}) collective-permute-start(bf16[4,3,32,128]{3,2,1,0:T(8,128)(2,1)S(1)} %get-tuple-element.22), channel_id=1, source_target_pairs={{128,0},{256,128},{384,256},{129,1},{257,129},{385,257},{130,2},{2... | collective-permute-start | bytes 294920 | tf_op jit(solution)/shard_map/ppermute | solution.py:65
  9.8 4.9 %collective-permute-start.2 = (bf16[3,88,128]{2,1,0:T(8,128)(2,1)S(1)}, bf16[3,88,128]{2,1,0:T(8,128)(2,1)S(1)}, u32[]{:S(2)}, u32[]{:S(2)}) collective-permute-start(bf16[3,88,128]{2,1,0:T(8,128)(2,1)S(1)} %get-tuple-element.28), channel_id=1, source_target_pairs={{0,16},{16,32},{32,48},{48,64},{64,80},{80,96},{96,112},{112,0},{1... | collective-permute-start | bytes 202760 | tf_op jit(solution)/shard_map/ppermute | solution.py:55
  9.9 4.9 %collective-permute-start.3 = (bf16[3,88,128]{2,1,0:T(8,128)(2,1)S(1)}, bf16[3,88,128]{2,1,0:T(8,128)(2,1)S(1)}, u32[]{:S(2)}, u32[]{:S(2)}) collective-permute-start(bf16[3,88,128]{2,1,0:T(8,128)(2,1)S(1)} %get-tuple-element.29), channel_id=1, source_target_pairs={{0,112},{16,0},{32,16},{48,32},{64,48},{80,64},{96,80},{112,96},{1... | collective-permute-start | bytes 202760 | tf_op jit(solution)/shard_map/ppermute | solution.py:55
  15.7 10.6 %collective-permute-start.5 = (bf16[8,3584]{1,0:T(8,128)(2,1)S(1)}, bf16[8,3584]{1,0:T(8,128)(2,1)S(1)}, u32[]{:S(2)}, u32[]{:S(2)}) collective-permute-start(bf16[8,3584]{1,0:T(8,128)(2,1)S(1)} %get-tuple-element.33.low), channel_id=1, source_target_pairs={{1,0},{2,1},{3,2},{4,3},{5,4},{6,5},{7,6},{8,7},{9,8},{10,9},{11,1... | collective-permute-start | bytes 172040 | tf_op jit(solution)/shard_map/ppermute | solution.py:65
  17.0 9.3 %collective-permute-start.4 = (bf16[8,3584]{1,0:T(8,128)(2,1)S(1)}, bf16[8,3584]{1,0:T(8,128)(2,1)S(1)}, u32[]{:S(2)}, u32[]{:S(2)}) collective-permute-start(bf16[8,3584]{1,0:T(8,128)(2,1)S(1)} %get-tuple-element.34.high), channel_id=1, source_target_pairs={{0,1},{1,2},{2,3},{3,4},{4,5},{5,6},{6,7},{7,8},{8,9},{9,10},{10,1... | collective-permute-start | bytes 172040 | tf_op jit(solution)/shard_map/ppermute | solution.py:60
  26.3 2.6 %copy-start = (f32[16,4,2]{0,2,1:T(2,128)S(1)}, f32[16,4,2]{0,2,1:T(2,128)}, u32[]{:S(2)}) copy-start(f32[16,4,2]{0,2,1:T(2,128)} %param.14) | copy-start | bytes 1540
  26.3 2.6 %copy-start.1 = (f32[16,4]{0,1:T(4,128)S(1)}, f32[16,4]{0,1:T(4,128)}, u32[]{:S(2)}) copy-start(f32[16,4]{0,1:T(4,128)} %param.15) | copy-start | bytes 772
  26.3 2.6 %copy-start.2 = (f32[16]{0:T(128)S(1)}, f32[16]{0:T(128)}, u32[]{:S(2)}) copy-start(f32[16]{0:T(128)} %shear.7) | copy-start | bytes 196
  35.6 22.0 %copy-start.5 = (s32[16,4]{0,1:T(4,128)S(1)}, s32[16,4]{0,1:T(4,128)}, u32[]{:S(2)}) copy-start(s32[16,4]{0,1:T(4,128)} %param.16) | copy-start | bytes 772
  35.6 17.0 %collective-permute-start.6 = (f32[4,4,32,128]{3,2,1,0:T(8,128)S(1)}, f32[4,4,32,128]{3,2,1,0:T(8,128)S(1)}, u32[]{:S(2)}, u32[]{:S(2)}) collective-permute-start(f32[4,4,32,128]{3,2,1,0:T(8,128)S(1)} %get-tuple-element.38), channel_id=1, source_target_pairs={{0,128},{128,256},{256,384},{384,0},{1,129},{129,257},{257,385},{3... | collective-permute-start | bytes 786440 | tf_op jit(solution)/shard_map/ppermute | solution.py:55
  43.1 11.1 %collective-permute-start.7 = (f32[4,4,32,128]{3,2,1,0:T(8,128)S(1)}, f32[4,4,32,128]{3,2,1,0:T(8,128)S(1)}, u32[]{:S(2)}, u32[]{:S(2)}) collective-permute-start(f32[4,4,32,128]{3,2,1,0:T(8,128)S(1)} %shard_map.122), channel_id=1, source_target_pairs={{0,256},{128,384},{256,0},{384,128},{1,257},{129,385},{257,1},{385... | collective-permute-start | bytes 786440 | tf_op jit(solution)/shard_map/ppermute | solution.py:55
  45.0 12.5 %collective-permute-start.8 = (f32[4,4,32,128]{3,2,1,0:T(8,128)S(1)}, f32[4,4,32,128]{3,2,1,0:T(8,128)S(1)}, u32[]{:S(2)}, u32[]{:S(2)}) collective-permute-start(f32[4,4,32,128]{3,2,1,0:T(8,128)S(1)} %shard_map.123), channel_id=1, source_target_pairs={{0,384},{128,0},{256,128},{384,256},{1,385},{129,1},{257,129},{385... | collective-permute-start | bytes 786440 | tf_op jit(solution)/shard_map/ppermute | solution.py:55
